TPU v7x, 256 devices: a whole 4x4x8 slice. The times are simulated.
256 devices in a mesh: row: 16 (over z_lo, x), col: 16 (over z_hi, y, core).
Axes of the slice: x: 4, y: 4, z: 8 (z_hi: 2, z_lo: 4; z = z_hi * 4 + z_lo), core: 2. Of those that a mesh axis runs over, the one named last changes fastest.
Arguments:
- start_vector: float32 [12288, 12288], P('row', 'col'), may hold values from -6 to 6, as said below
- ham_blocks: bfloat16 [768, 128, 128], P('row'), may hold values from -0.1875 to 0.1875
- diagonal: float32 [12288], replicated, may hold values from -1 to 1
- pair_lists: int32 [3, 16, 64], replicated, may hold values from 0 to 47, as said below
- pair_counts: int32 [16], replicated, may hold values from 16 to 64, as said below
- hot_blocks: int32 [16, 2], replicated, may hold values from 0 to 5, as said below
- selection: int32 [16, 16], replicated, may hold values from 0 to 1
Outputs:
- first_iterate: float32 [12288, 12288], P('row', 'col')
- second_iterate: float32 [12288, 12288], P('row', 'col')
Inputs may be any that keep to these rules, and one draw needn't show every extreme that they name: start_vector is symmetric: entry (a, b) equals entry (b, a). `pair_lists`: component 0 is a tile (0 to 15), component 1 a block of a tile (0 to 5), component 2 a block id (0 to 47); slot k < 16 of every list has source tile k. `pair_counts`: some tile has all 64 slots live. `hot_blocks`: the 2 blocks of a tile are distinct.
All inputs are finite; a program needn't handle non-finite values.
Results may differ from a plain program's by a relative error of at most 0.0023.
Values may be sent and summed in bfloat16 or wider, within the bound.
No kernel may reach another device: no remote copies, remote signals or barrier semaphores. Data moves between devices by JAX's collectives and lax.ppermute only.
A program may use at most 128 MiB of HBM per device.

v0:
```python
import jax
import jax.numpy as jnp
from jax import lax
from jax.sharding import PartitionSpec as P

center = 0.25
half_width = 2.5


def from_root(block, axis, holder):
    block = jnp.where(lax.axis_index(axis) == holder, block, jnp.zeros_like(block))
    return lax.psum(block, axis)


def alpha_products(sources, hams, pair_table, live_count, block_count):
    block_size, col_width = (sources.shape[1], sources.shape[2])
    turn_count = (live_count + 15) // 16

    def alpha_turn(step_index, accumulated):
        first_pair = step_index * 16
        source_ids = lax.dynamic_slice_in_dim(pair_table[0], first_pair, 16)
        target_ids = lax.dynamic_slice_in_dim(pair_table[1], first_pair, 16)
        ham_ids = lax.dynamic_slice_in_dim(pair_table[2], first_pair, 16)
        is_live = first_pair + jnp.arange(16) < live_count
        picked = jnp.take(sources, source_ids, axis=0)
        hams_now = jnp.take(hams, ham_ids, axis=0)
        products = jnp.einsum("kij,kjn->kin", hams_now, picked, preferred_element_type=jnp.float32)
        products = jnp.where(is_live[:, None, None], products, 0.0)
        return accumulated.at[target_ids].add(products)

    summed = lax.fori_loop(
        0, turn_count, alpha_turn, jnp.zeros((block_count, block_size, col_width), jnp.float32)
    )
    return summed.reshape(block_count * block_size, col_width)


def beta_products(sources, hams, pair_table, live_count, block_count):
    row_height, block_size = (sources.shape[1], sources.shape[2])
    turn_count = (live_count + 15) // 16

    def beta_turn(step_index, accumulated):
        first_pair = step_index * 16
        source_ids = lax.dynamic_slice_in_dim(pair_table[0], first_pair, 16)
        target_ids = lax.dynamic_slice_in_dim(pair_table[1], first_pair, 16)
        ham_ids = lax.dynamic_slice_in_dim(pair_table[2], first_pair, 16)
        is_live = first_pair + jnp.arange(16) < live_count
        picked = jnp.take(sources, source_ids, axis=0)
        hams_now = jnp.take(hams, ham_ids, axis=0)
        products = jnp.einsum("kai,kji->kaj", picked, hams_now, preferred_element_type=jnp.float32)
        products = jnp.where(is_live[:, None, None], products, 0.0)
        return accumulated.at[target_ids].add(products)

    summed = lax.fori_loop(
        0, turn_count, beta_turn, jnp.zeros((block_count, row_height, block_size), jnp.float32)
    )
    return summed.transpose(1, 0, 2).reshape(row_height, block_count * block_size)


def body(start_vector, ham_blocks, diagonal, pair_lists, pair_counts, hot_blocks, selection):
    row_count = lax.axis_size("row")
    col_count = lax.axis_size("col")
    ratio = row_count // col_count
    tile_rows, tile_cols = start_vector.shape
    block_size = ham_blocks.shape[1]
    block_count = tile_rows // block_size
    hot_count = hot_blocks.shape[1]
    row_index = lax.axis_index("row")
    col_index = lax.axis_index("col")
    mirror_tiles = [col_index * ratio + 0]
    mirror_hams = [from_root(ham_blocks, "row", mirror) for mirror in mirror_tiles]
    mirror_pairs = [jnp.take(pair_lists, mirror, axis=1) for mirror in mirror_tiles]
    mirror_counts = [pair_counts[mirror] for mirror in mirror_tiles]
    own_pairs = jnp.take(pair_lists, row_index, axis=1)
    own_count = pair_counts[row_index]
    row_diag = lax.dynamic_slice_in_dim(diagonal, row_index * tile_rows, tile_rows)
    col_diag = lax.dynamic_slice_in_dim(diagonal, col_index * tile_cols, tile_cols)
    local_tiles = col_index * ratio + jnp.arange(ratio)
    tiles_all = jnp.arange(row_count)

    def operator(iterate):
        rounded = iterate.astype(jnp.bfloat16)
        row_pieces = rounded.reshape(block_count, block_size, tile_cols)
        col_pieces = rounded.reshape(tile_rows, ratio * block_count, block_size).transpose(1, 0, 2)
        own_hot = jnp.take(row_pieces, hot_blocks[row_index], axis=0)
        hot_rows = lax.all_gather(own_hot, "row", axis=0, tiled=True)
        alpha_source = jnp.take(hot_rows, tiles_all * hot_count + selection[row_index], axis=0)
        alpha_part = alpha_products(alpha_source, ham_blocks, own_pairs, own_count, block_count)
        col_ids = (jnp.arange(ratio)[:, None] * block_count + hot_blocks[local_tiles]).reshape(-1)
        own_cols = jnp.take(col_pieces, col_ids, axis=0)
        hot_cols = lax.all_gather(own_cols, "col", axis=0, tiled=True)
        beta_sources = [
            jnp.take(hot_cols, tiles_all * hot_count + selection[mirror], axis=0)
            for mirror in mirror_tiles
        ]
        beta_part = beta_products(
            beta_sources[0], mirror_hams[0], mirror_pairs[0], mirror_counts[0], block_count
        )
        return alpha_part + beta_part + (row_diag[:, None] + col_diag[None, :]) * iterate

    first_iterate = (operator(start_vector) - center * start_vector) / half_width
    second_iterate = (
        2.0 * (operator(first_iterate) - center * first_iterate) / half_width - start_vector
    )
    return (first_iterate, second_iterate)


def solution(mesh):
    in_specs = (P("row", "col"), P("row", None, None), P(), P(), P(), P(), P())
    out_specs = (P("row", "col"), P("row", "col"))
    return jax.shard_map(body, mesh=mesh, in_specs=in_specs, out_specs=out_specs, check_vma=False)
```

profile of v0, /device:TPU:51, one launch (start us, length us, event | category | flops | bytes accessed | tf_op | source)
XLA Modules:
  0.0 772.0 jit_solution(9004850609802576937)
XLA Ops:
  24.9 86.2 %all-gather.7.cloned.1.call-done = bf16[32,768,128]{2,1,0:T(8,128)(2,1)} async-done(((bf16[2,768,128]{2,1,0:T(8,128)(2,1)}), bf16[32,768,128]{2,1,0:T(8,128)(2,1)}) %all-gather.7.cloned.1.call-update) | async-done | bytes 6291472 | tf_op jit(solution)/shard_map/all_gather | solution.py:90
  117.0 104.6 %all-reduce.2.cloned.1.call-done = bf16[48,128,128]{2,1,0:T(8,128)(2,1)} async-done(((bf16[48,128,128]{2,1,0:T(8,128)(2,1)}), bf16[48,128,128]{2,1,0:T(8,128)(2,1)}) %all-reduce.2.cloned.1.call-update) | async-done | bytes 1572880 | tf_op jit(solution)/shard_map/psum | solution.py:12
  221.8 88.9 %while.43 = (s32[]{:T(128)}, f32[6,768,128]{2,1,0:T(8,128)S(1)}, s32[]{:T(128)}, s32[3,64]{1,0:T(4,128)S(1)}, s32[]{:T(128)}, /*index=5*/bf16[16,768,128]{2,1,0:...) while((s32[]{:T(128)}, f32[6,768,128]{2,1,0:T(8,128)S(1)}, ...), condition=%wide.region_6.15_spmd, body=%wide.region_4.14_spmd.sunk | while | flops 407636256 | bytes 36186576 | solution.py:53
  234.8 9.3 %scatter_fusion.1 = f32[6,768,128]{2,1,0:T(8,128)S(1)} fusion(f32[6,768,128]{2,1,0:T(8,128)S(1)} %get-tuple-element.542, s32[16]{0:T(128)S(1)} %fusion.100, f32[16,768,128]{2,1,0:T(8,128)} %broadcast_select_fusion.18), kind=kCustom, calls=%fused_computation.17.clone.1 | custom fusion | flops 1572864 | bytes 18874432 | tf_op jit(solution)/shard_map/while/body/scatter-add | solution.py:51
  257.1 9.2 %scatter_fusion.1 = f32[6,768,128]{2,1,0:T(8,128)S(1)} fusion(f32[6,768,128]{2,1,0:T(8,128)S(1)} %get-tuple-element.542, s32[16]{0:T(128)S(1)} %fusion.100, f32[16,768,128]{2,1,0:T(8,128)} %broadcast_select_fusion.18), kind=kCustom, calls=%fused_computation.17.clone.1 | custom fusion | flops 1572864 | bytes 18874432 | tf_op jit(solution)/shard_map/while/body/scatter-add | solution.py:51
  279.3 9.2 %scatter_fusion.1 = f32[6,768,128]{2,1,0:T(8,128)S(1)} fusion(f32[6,768,128]{2,1,0:T(8,128)S(1)} %get-tuple-element.542, s32[16]{0:T(128)S(1)} %fusion.100, f32[16,768,128]{2,1,0:T(8,128)} %broadcast_select_fusion.18), kind=kCustom, calls=%fused_computation.17.clone.1 | custom fusion | flops 1572864 | bytes 18874432 | tf_op jit(solution)/shard_map/while/body/scatter-add | solution.py:51
  301.5 9.3 %scatter_fusion.1 = f32[6,768,128]{2,1,0:T(8,128)S(1)} fusion(f32[6,768,128]{2,1,0:T(8,128)S(1)} %get-tuple-element.542, s32[16]{0:T(128)S(1)} %fusion.100, f32[16,768,128]{2,1,0:T(8,128)} %broadcast_select_fusion.18), kind=kCustom, calls=%fused_computation.17.clone.1 | custom fusion | flops 1572864 | bytes 18874432 | tf_op jit(solution)/shard_map/while/body/scatter-add | solution.py:51
  321.6 88.0 %while.42 = (s32[]{:T(128)}, f32[6,128,768]{2,1,0:T(8,128)S(1)}, s32[]{:T(128)}, s32[3,64]{1,0:T(4,128)S(1)}, s32[]{:T(128)}, /*index=5*/bf16[48,128,128]{2,1,0:...) while((s32[]{:T(128)}, f32[6,128,768]{2,1,0:T(8,128)S(1)}, ...), condition=%wide.region_2.8_spmd, body=%wide.region_0.7_spmd.sunk | while | flops 407636256 | bytes 36186576 | solution.py:31
  334.4 9.3 %scatter_fusion = f32[6,128,768]{2,1,0:T(8,128)S(1)} fusion(f32[6,128,768]{2,1,0:T(8,128)S(1)} %get-tuple-element.575, s32[16]{0:T(128)S(1)} %fusion.96, f32[16,128,768]{2,1,0:T(8,128)} %broadcast_select_fusion.17), kind=kCustom, calls=%fused_computation.16.clone.1 | custom fusion | flops 1572864 | bytes 18874432 | tf_op jit(solution)/shard_map/while/body/scatter-add | solution.py:29
  356.4 9.2 %scatter_fusion = f32[6,128,768]{2,1,0:T(8,128)S(1)} fusion(f32[6,128,768]{2,1,0:T(8,128)S(1)} %get-tuple-element.575, s32[16]{0:T(128)S(1)} %fusion.96, f32[16,128,768]{2,1,0:T(8,128)} %broadcast_select_fusion.17), kind=kCustom, calls=%fused_computation.16.clone.1 | custom fusion | flops 1572864 | bytes 18874432 | tf_op jit(solution)/shard_map/while/body/scatter-add | solution.py:29
  378.3 9.2 %scatter_fusion = f32[6,128,768]{2,1,0:T(8,128)S(1)} fusion(f32[6,128,768]{2,1,0:T(8,128)S(1)} %get-tuple-element.575, s32[16]{0:T(128)S(1)} %fusion.96, f32[16,128,768]{2,1,0:T(8,128)} %broadcast_select_fusion.17), kind=kCustom, calls=%fused_computation.16.clone.1 | custom fusion | flops 1572864 | bytes 18874432 | tf_op jit(solution)/shard_map/while/body/scatter-add | solution.py:29
  400.3 9.3 %scatter_fusion = f32[6,128,768]{2,1,0:T(8,128)S(1)} fusion(f32[6,128,768]{2,1,0:T(8,128)S(1)} %get-tuple-element.575, s32[16]{0:T(128)S(1)} %fusion.96, f32[16,128,768]{2,1,0:T(8,128)} %broadcast_select_fusion.17), kind=kCustom, calls=%fused_computation.16.clone.1 | custom fusion | flops 1572864 | bytes 18874432 | tf_op jit(solution)/shard_map/while/body/scatter-add | solution.py:29
  425.8 82.8 %all-gather.11.cloned.1.call-done = bf16[32,768,128]{2,1,0:T(8,128)(2,1)} async-done(((bf16[2,768,128]{2,1,0:T(8,128)(2,1)}), bf16[32,768,128]{2,1,0:T(8,128)(2,1)}) %all-gather.11.cloned.1.call-update) | async-done | bytes 6291472 | tf_op jit(solution)/shard_map/all_gather | solution.py:90
  519.6 111.0 %while.45 = (s32[]{:T(128)}, f32[6,768,128]{2,1,0:T(8,128)}, s32[]{:T(128)}, s32[3,64]{1,0:T(4,128)S(1)}, s32[]{:T(128)}, /*index=5*/bf16[16,768,128]{2,1,0:T(8,...) while((s32[]{:T(128)}, f32[6,768,128]{2,1,0:T(8,128)}, ...), condition=%wide.region_12.21_spmd, body=%wide.region_10.20_spmd.sunk | while | flops 407636256 | bytes 36186576 | solution.py:53
  532.6 15.0 %scatter_fusion.3 = f32[6,768,128]{2,1,0:T(8,128)} fusion(f32[6,768,128]{2,1,0:T(8,128)} %get-tuple-element.608, s32[16]{0:T(128)S(1)} %fusion.108, f32[16,768,128]{2,1,0:T(8,128)} %broadcast_select_fusion.20), kind=kCustom, calls=%fused_computation.19.clone.1 | custom fusion | flops 1572864 | bytes 18874432 | tf_op jit(solution)/shard_map/while/body/scatter-add | solution.py:51
  560.6 14.6 %scatter_fusion.3 = f32[6,768,128]{2,1,0:T(8,128)} fusion(f32[6,768,128]{2,1,0:T(8,128)} %get-tuple-element.608, s32[16]{0:T(128)S(1)} %fusion.108, f32[16,768,128]{2,1,0:T(8,128)} %broadcast_select_fusion.20), kind=kCustom, calls=%fused_computation.19.clone.1 | custom fusion | flops 1572864 | bytes 18874432 | tf_op jit(solution)/shard_map/while/body/scatter-add | solution.py:51
  588.2 14.5 %scatter_fusion.3 = f32[6,768,128]{2,1,0:T(8,128)} fusion(f32[6,768,128]{2,1,0:T(8,128)} %get-tuple-element.608, s32[16]{0:T(128)S(1)} %fusion.108, f32[16,768,128]{2,1,0:T(8,128)} %broadcast_select_fusion.20), kind=kCustom, calls=%fused_computation.19.clone.1 | custom fusion | flops 1572864 | bytes 18874432 | tf_op jit(solution)/shard_map/while/body/scatter-add | solution.py:51
  615.6 15.0 %scatter_fusion.3 = f32[6,768,128]{2,1,0:T(8,128)} fusion(f32[6,768,128]{2,1,0:T(8,128)} %get-tuple-element.608, s32[16]{0:T(128)S(1)} %fusion.108, f32[16,768,128]{2,1,0:T(8,128)} %broadcast_select_fusion.20), kind=kCustom, calls=%fused_computation.19.clone.1 | custom fusion | flops 1572864 | bytes 18874432 | tf_op jit(solution)/shard_map/while/body/scatter-add | solution.py:51
  647.7 110.3 %while.44 = (s32[]{:T(128)}, f32[6,128,768]{2,1,0:T(8,128)}, s32[]{:T(128)}, s32[3,64]{1,0:T(4,128)S(1)}, s32[]{:T(128)}, /*index=5*/bf16[48,128,128]{2,1,0:T(8,...) while((s32[]{:T(128)}, f32[6,128,768]{2,1,0:T(8,128)}, ...), condition=%wide.region_9.18_spmd, body=%wide.region_7.17_spmd.sunk | while | flops 407636256 | bytes 36186576 | solution.py:31
  660.5 15.0 %scatter_fusion.2 = f32[6,128,768]{2,1,0:T(8,128)} fusion(f32[6,128,768]{2,1,0:T(8,128)} %get-tuple-element.641, s32[16]{0:T(128)S(1)} %fusion.104, f32[16,128,768]{2,1,0:T(8,128)} %broadcast_select_fusion.19), kind=kCustom, calls=%fused_computation.18.clone.1 | custom fusion | flops 1572864 | bytes 18874432 | tf_op jit(solution)/shard_map/while/body/scatter-add | solution.py:29
  688.2 14.6 %scatter_fusion.2 = f32[6,128,768]{2,1,0:T(8,128)} fusion(f32[6,128,768]{2,1,0:T(8,128)} %get-tuple-element.641, s32[16]{0:T(128)S(1)} %fusion.104, f32[16,128,768]{2,1,0:T(8,128)} %broadcast_select_fusion.19), kind=kCustom, calls=%fused_computation.18.clone.1 | custom fusion | flops 1572864 | bytes 18874432 | tf_op jit(solution)/shard_map/while/body/scatter-add | solution.py:29
  715.5 14.7 %scatter_fusion.2 = f32[6,128,768]{2,1,0:T(8,128)} fusion(f32[6,128,768]{2,1,0:T(8,128)} %get-tuple-element.641, s32[16]{0:T(128)S(1)} %fusion.104, f32[16,128,768]{2,1,0:T(8,128)} %broadcast_select_fusion.19), kind=kCustom, calls=%fused_computation.18.clone.1 | custom fusion | flops 1572864 | bytes 18874432 | tf_op jit(solution)/shard_map/while/body/scatter-add | solution.py:29
  742.9 15.1 %scatter_fusion.2 = f32[6,128,768]{2,1,0:T(8,128)} fusion(f32[6,128,768]{2,1,0:T(8,128)} %get-tuple-element.641, s32[16]{0:T(128)S(1)} %fusion.104, f32[16,128,768]{2,1,0:T(8,128)} %broadcast_select_fusion.19), kind=kCustom, calls=%fused_computation.18.clone.1 | custom fusion | flops 1572864 | bytes 18874432 | tf_op jit(solution)/shard_map/while/body/scatter-add | solution.py:29
  758.0 6.9 fusion.61
  (226 shorter events, 281.8 us)
Async XLA Ops:
  8.0 103.0 %all-gather.7.cloned.1.call-start = ((), (), s32[]{:S(2)}) async-start(), calls=%async_computation.1 | async-start | bytes 6684672 | tf_op jit(solution)/shard_map/all_gather | solution.py:90
  9.0 7.5 copy-start.10
  10.8 6.7 copy-start
  14.7 4.1 copy-start.3
  17.5 204.2 %all-reduce.2.cloned.1.call-start = ((), (), s32[]{:S(2)}) async-start(), calls=%async_computation.2 | async-start | bytes 3145728 | tf_op jit(solution)/shard_map/psum | solution.py:12
  17.5 2.9 copy-start.9
  18.8 296.9 %all-gather.5.cloned.1.call-start = ((), (), s32[]{:S(2)}) async-start(), calls=%async_computation | async-start | bytes 6684672 | tf_op jit(solution)/shard_map/all_gather | solution.py:85
  18.9 5.9 copy-start.4
  19.5 2.8 copy-start.11
  20.4 488.2 %all-gather.11.cloned.1.call-start = ((), (), s32[]{:S(2)}) async-start(), calls=%async_computation.4 | async-start | bytes 6684672 | tf_op jit(solution)/shard_map/all_gather | solution.py:90
  23.1 91.9 %copy-start.7 = (pred[16]{0:T(512)(128)(4,1)}, pred[16]{0:T(512)(128)(4,1)S(1)}, u32[]{:S(2)}) copy-start(pred[16]{0:T(512)(128)(4,1)S(1)} %get-tuple-element.294) | copy-start | bytes 52
  23.1 296.2 %copy-start.5 = (pred[16]{0:T(512)(128)(4,1)}, pred[16]{0:T(512)(128)(4,1)S(1)}, u32[]{:S(2)}) copy-start(pred[16]{0:T(512)(128)(4,1)S(1)} %get-tuple-element.266) | copy-start | bytes 52
  23.9 91.1 %copy-start.2 = (s32[1024]{0:T(1024)}, s32[1024]{0:T(1024)S(1)}, u32[]{:S(2)}) copy-start(s32[1024]{0:T(1024)S(1)} %pad_clamp_fusion.8) | copy-start | bytes 12292
  24.0 291.8 %copy-start.1 = (s32[1024]{0:T(1024)}, s32[1024]{0:T(1024)S(1)}, u32[]{:S(2)}) copy-start(s32[1024]{0:T(1024)S(1)} %pad_clamp_fusion.10) | copy-start | bytes 12292
  422.4 214.4 %all-gather.9.cloned.1.call-start = ((), (), s32[]{:S(2)}) async-start(), calls=%async_computation.3 | async-start | bytes 6684672 | tf_op jit(solution)/shard_map/all_gather | solution.py:85
  425.8 88.3 %copy-start.8 = (pred[16]{0:T(512)(128)(4,1)S(1)}, pred[16]{0:T(512)(128)(4,1)}, u32[]{:S(2)}) copy-start(pred[16]{0:T(512)(128)(4,1)} %copy-done.7) | copy-start | bytes 52
  636.8 5.4 copy-start.6
Sparse Core Ops, SparseCore 0:
  17.6 93.3 all-gather.6
  112.9 84.2 all-gather.4
  422.6 86.0 all-gather.10
  510.4 75.4 all-gather.8
Sparse Core Ops, SparseCore 1:
  21.2 200.5 all-reduce.1
where the time goes:
time: 776 us; the launch traced here: 772 us
  waiting for transfers between devices  274 us (35%)
  other arithmetic  237 us (31%)
  local copies, waits for them, and re-layouts  154 us (20%)
  matrix products  89.5 us (12%)
  between operations  16.7 us (2%)
    all_gather x2, waiting for transfers between devices, operator(): hot_cols = lax.all_gather(own_cols, 'col', axis=0, tiled=True)  169 us
    psum x1, waiting for transfers between devices, from_root(): return lax.psum(block, axis)  105 us
    scatter-add x8, other arithmetic, alpha_turn(): return accumulated.at[target_ids].add(products)  96.3 us
    scatter-add x8, other arithmetic, beta_turn(): return accumulated.at[target_ids].add(products)  96 us
    dot_general x8, matrix products, beta_turn(): jnp.einsum('kai,kji->kaj', picked, hams_now, preferred_element_type=jnp.f...  44.8 us
    dot_general x8, matrix products, alpha_turn(): jnp.einsum('kij,kjn->kin', hams_now, picked, preferred_element_type=jnp.f...  44.8 us
    gather x8, local copies, waits for them, and re-layouts, beta_turn(): picked = jnp.take(sources, source_ids, axis=0)  36 us
    gather x8, local copies, waits for them, and re-layouts, alpha_turn(): picked = jnp.take(sources, source_ids, axis=0)  34.5 us
  transfers between devices with their start and end apart: 5, of which 3 were waited for; matrix products, arithmetic and copies ran while one was open for 31% of the time, Pallas kernels for 0%

commit v1 on v0

v1 whole, which is shorter than its diff:
```python
import jax
import jax.numpy as jnp
from jax import lax
from jax.experimental import pallas as pl
from jax.experimental.pallas import tpu as pltpu
from jax.sharding import Mesh, PartitionSpec as P
import numpy as np

center = 0.25
scale = 1.0 / 2.5
axes = ("zl", "x", "zh", "y", "k")
sizes = (4, 4, 2, 4, 2)
B = 128
T = 768
R = 256
bf16 = jnp.bfloat16
f32 = jnp.float32


def permute(value, target):
    places = list(np.ndindex(*sizes))
    pairs = [
        (int(np.ravel_multi_index(p, sizes)), int(np.ravel_multi_index(target(*p), sizes)))
        for p in places
    ]
    return lax.ppermute(value, axes, pairs)


def z_xor(n):
    return lambda zl, x, zh, y, k: (zl ^ n, x, zh, y, k)


def y_shift(n):
    return lambda zl, x, zh, y, k: (zl, x, zh, (y + n) % 4, k)


def zh_flip(zl, x, zh, y, k):
    return (zl, x, 1 - zh, y, k)


def k_flip(zl, x, zh, y, k):
    return (zl, x, zh, y, 1 - k)


def mirror(zl, x, zh, y, k):
    r, c = zl * 4 + x, zh * 8 + y * 2 + k
    return (c // 4, c % 4, r // 8, (r % 8) // 2, r % 2)


def barrier(*values):
    return lax.optimization_barrier(values)


def start(block):
    return pl.multiple_of(block * B, B)


def call(kernel, scalars, grid, in_specs, out_specs, out_shape, args, scratch=(), flops=0, moved=0):
    return pl.pallas_call(
        kernel,
        grid_spec=pltpu.PrefetchScalarGridSpec(
            num_scalar_prefetch=len(scalars),
            grid=grid,
            in_specs=in_specs,
            out_specs=out_specs,
            scratch_shapes=list(scratch),
        ),
        out_shape=out_shape,
        cost_estimate=pl.CostEstimate(flops=flops, bytes_accessed=moved, transcendentals=0),
    )(*scalars, *args)


def shape(dims, kind=bf16):
    return jax.ShapeDtypeStruct(dims, kind)


pack_shapes = (shape((2, B, T)), shape((2, T, B)), shape((4, B, T)))


def pack_kernel(ids, hot, sel, x_ref, row_ref, col_ref, near_ref):
    r, c = ids[0], ids[1]
    for h in range(2):
        row_ref[h] = x_ref[pl.ds(start(hot[r, h]), B), :].astype(bf16)
        col_ref[h] = x_ref[:, pl.ds(start(hot[c, h]), B)].astype(bf16)
    for j in range(4):
        block = hot[r, sel[(r // 4) * 4 + j, r]]
        near_ref[j] = x_ref[pl.ds(start(block), B), :].astype(bf16)


def pack(ids, hot, sel, value):
    def whole(dims):
        return pl.BlockSpec(dims, lambda i, *_: (0,) * len(dims))

    return call(
        pack_kernel,
        (ids, hot, sel),
        (1,),
        [whole((T, T))],
        [whole((2, B, T)), whole((2, T, B)), whole((4, B, T))],
        pack_shapes,
        (value,),
        moved=5 << 20,
    )


def choose(ids, sel, slabs, steps):
    def kernel(ids, sel, *refs):
        for n in range(len(slabs)):
            refs[-1][n] = refs[n][0]

    def reader(step):
        def index(j, ids, sel):
            zl, x = ids[0] // 4, ids[0] % 4
            return (sel[zl * 4 + j, (zl ^ step) * 4 + x], 0, 0)

        return pl.BlockSpec((1, B, T), index)

    count = len(slabs)
    return call(
        kernel,
        (ids, sel),
        (4,),
        [reader(step) for step in steps],
        pl.BlockSpec((count, B, T), lambda j, *_: (j, 0, 0)),
        shape((4 * count, B, T)),
        slabs,
        moved=count << 21,
    )


def over_x(payload):
    return lax.all_to_all(payload, "x", 0, 0, tiled=True)


def dense_kernel(mirrored):
    def kernel(ids, lists, counts, ham_ref, out_ref, total):
        r, c = ids[0], ids[1]
        tile = c if mirrored else r
        zl = r // 4

        def clear(i, carry):
            total[i] = jnp.zeros((B, B), f32)
            return carry

        lax.fori_loop(0, 96, clear, 0)

        def add(slot, carry):
            q = lists[0, tile, slot]
            t = lists[1, tile, slot]
            b = lists[2, tile, slot]
            if mirrored:
                zh, y, k = c // 8, (c // 2) % 4, c % 2
                qzh, qy, qk = q // 8, (q // 2) % 4, q % 2
                place = ((qk ^ k) * 4 + ((y - qy + 4) % 4)) * 2 + (qzh ^ zh)
                piece = b // 3
                b = ((piece % 4) * 4 + ((piece // 4) ^ zl)) * 3 + b % 3
            else:
                n, j = (q // 4) ^ zl, q % 4
                place = jnp.where(n < 2, n * 4 + j, 8 + j * 2 + (n - 2))
            at = t * 16 + place
            total[at] = total[at] + ham_ref[b].astype(f32)
            return carry

        lax.fori_loop(0, counts[tile], add, 0)
        for t in range(6):
            for place in range(16):
                block = total[t * 16 + place].astype(bf16)
                if mirrored:
                    out_ref[place * B : (place + 1) * B, t * B : (t + 1) * B] = block
                else:
                    out_ref[t * B : (t + 1) * B, place * B : (place + 1) * B] = block

    return kernel


def dense(ids, lists, counts, hams, mirrored):
    dims = (2048, T) if mirrored else (T, 2048)
    return call(
        dense_kernel(mirrored),
        (ids, lists, counts),
        (1,),
        [pl.BlockSpec((48, B, B), lambda i, *_: (0, 0, 0))],
        pl.BlockSpec(dims, lambda i, *_: (0, 0)),
        shape(dims),
        (hams,),
        scratch=[pltpu.VMEM((96, B, B), f32)],
        flops=1 << 22,
        moved=5 << 20,
    )


def first_products_kernel(ids, sel, ham_t_ref, ham_ref, near_ref, next_ref, *refs):
    slabs, out_ref, wide = refs[:8], refs[8], refs[9]
    c = ids[1]
    zh, y, k = c // 8, (c // 2) % 4, c % 2
    for place in range(16):
        m, flip = place // 2, place % 2
        q = (zh ^ flip) * 8 + ((y - m % 4 + 4) % 4) * 2 + (k ^ (m // 4))
        wide[:, place * B : (place + 1) * B] = slabs[m][flip * 2 + sel[c, q]]
    out_ref[...] = (
        jnp.dot(wide[...], ham_t_ref[...], preferred_element_type=f32)
        + jnp.dot(ham_ref[:, :512], near_ref[...], preferred_element_type=f32)
        + jnp.dot(ham_ref[:, 512:], next_ref[...], preferred_element_type=f32)
    )


def first_products(ids, sel, ham_t, ham, near, following, slabs):
    return call(
        first_products_kernel,
        (ids, sel),
        (T // R,),
        [
            pl.BlockSpec((2048, T), lambda i, *_: (0, 0)),
            pl.BlockSpec((R, 1024), lambda i, *_: (i, 0)),
            pl.BlockSpec((512, T), lambda i, *_: (0, 0)),
            pl.BlockSpec((512, T), lambda i, *_: (0, 0)),
        ]
        + [pl.BlockSpec((4, R, B), lambda i, *_: (0, i, 0))] * 8,
        pl.BlockSpec((R, T), lambda i, *_: (i, 0)),
        shape((T, T), f32),
        (ham_t, ham, near, following, *slabs),
        scratch=[pltpu.VMEM((R, 2048), bf16)],
        flops=2 * T * T * 3072,
        moved=18 << 20,
    )


def finish_kernel(second):
    def kernel(ids, hot, sel, part_ref, ham_ref, far_ref, x_ref, dr_ref, dc_ref, *refs):
        total = part_ref[...] + jnp.dot(ham_ref[...], far_ref[...], preferred_element_type=f32)
        value = x_ref[...]
        applied = total + (dr_ref[...] + dc_ref[...]) * value
        stepped = (applied - center * value) * scale
        if second:
            refs[1][...] = 2.0 * stepped - refs[0][...]
            return
        out_ref, row_ref, col_ref, near_ref = refs
        out_ref[...] = stepped
        i, r, c = pl.program_id(0), ids[0], ids[1]
        for h in range(2):
            col_ref[h] = out_ref[:, pl.ds(start(hot[c, h]), B)].astype(bf16)
            block = hot[r, h]

            @pl.when(block // 2 == i)
            def _(h=h, block=block):
                row_ref[h] = out_ref[pl.ds(start(block % 2), B), :].astype(bf16)

        for j in range(4):
            block = hot[r, sel[(r // 4) * 4 + j, r]]

            @pl.when(block // 2 == i)
            def _(j=j, block=block):
                near_ref[j] = out_ref[pl.ds(start(block % 2), B), :].astype(bf16)

    return kernel


def finish(ids, hot, sel, part, ham, far, value, dr, dc, before=None):
    second = before is not None
    rows = pl.BlockSpec((R, T), lambda i, *_: (i, 0))
    in_specs = [
        rows,
        pl.BlockSpec((R, 1024), lambda i, *_: (i, 1)),
        pl.BlockSpec((1024, T), lambda i, *_: (0, 0)),
        rows,
        pl.BlockSpec((R, 1), lambda i, *_: (i, 0)),
        pl.BlockSpec((1, T), lambda i, *_: (0, 0)),
    ]
    args = (part, ham, far, value, dr, dc)
    if second:
        in_specs, args = in_specs + [rows], args + (before,)
        out_specs, out_shape = rows, shape((T, T), f32)
    else:
        out_specs = [
            rows,
            pl.BlockSpec((2, B, T), lambda i, *_: (0, 0, 0)),
            pl.BlockSpec((2, R, B), lambda i, *_: (0, i, 0)),
            pl.BlockSpec((4, B, T), lambda i, *_: (0, 0, 0)),
        ]
        out_shape = (shape((T, T), f32),) + pack_shapes
    return call(
        finish_kernel(second),
        (ids, hot, sel),
        (T // R,),
        in_specs,
        out_specs,
        out_shape,
        args,
        flops=2 * T * T * 1024,
        moved=12 << 20,
    )


def body(start_vector, ham_blocks, diagonal, lists, counts, hot, sel):
    row_index = lax.axis_index("zl") * 4 + lax.axis_index("x")
    col_index = (lax.axis_index("zh") * 4 + lax.axis_index("y")) * 2 + lax.axis_index("k")
    ids = jnp.stack([row_index, col_index]).astype(jnp.int32)
    dr = lax.dynamic_slice_in_dim(diagonal, row_index * T, T).reshape(T, 1)
    dc = lax.dynamic_slice_in_dim(diagonal, col_index * T, T).reshape(1, T)

    piece = lax.dynamic_slice_in_dim(ham_blocks, col_index * 3, 3).transpose(0, 2, 1)
    piece = permute(piece, mirror)
    row, col, near_out = pack(ids, hot, sel, start_vector)
    ham = dense(ids, lists, counts, ham_blocks, False)

    ham_t = None
    outs = []
    value, before = start_vector, None
    for step in range(2):
        row, col, near_out, piece = barrier(row, col, near_out, piece)
        z1 = permute(row, z_xor(1))
        zh = permute(col, zh_flip)
        near = over_x(near_out)
        pieces = [permute(piece, z_xor(n)) for n in (1, 2, 3)] if step == 0 else []
        row, col, z1, zh, near, *pieces = barrier(row, col, z1, zh, near, *pieces)
        both = jnp.concatenate([col, zh])
        z2 = permute(row, z_xor(2))
        z3 = permute(row, z_xor(3))
        ys = [permute(both, y_shift(n)) for n in (1, 2, 3)]
        following = over_x(choose(ids, sel, (z1,), (1,)))
        extra = []
        if step == 0:
            joined = jnp.stack([piece] + pieces)
            extra = [over_x(jnp.broadcast_to(joined[None], (4, 4, 3, B, B)).reshape(48, B, B))]
        z2, z3, following, both, *rest = barrier(z2, z3, following, both, *ys, *extra)
        mine = [both] + rest[:3]
        others = [permute(m, k_flip) for m in mine]
        far = over_x(choose(ids, sel, (z2, z3), (2, 3)))
        if step == 0:
            ham_t = dense(ids, lists, counts, rest[3], True)
        part = first_products(
            ids, sel, ham_t, ham, near.reshape(512, T), following.reshape(512, T), mine + others
        )
        far = far.reshape(1024, T)
        if step == 0:
            value, row, col, near_out = finish(ids, hot, sel, part, ham, far, value, dr, dc)
            outs.append(value)
        else:
            outs.append(finish(ids, hot, sel, part, ham, far, value, dr, dc, start_vector))
    return tuple(outs)


def solution(mesh):
    fine = Mesh(mesh.devices.reshape(sizes), axes)
    rows, cols = ("zl", "x"), ("zh", "y", "k")
    in_specs = (P(rows, cols), P(rows, None, None), P(), P(), P(), P(), P())
    out_specs = (P(rows, cols), P(rows, cols))
    return jax.shard_map(body, mesh=fine, in_specs=in_specs, out_specs=out_specs, check_vma=False)
```

time: 776 us -> 285 us (0.37)
  the two profiles are of different devices: /device:TPU:51 before, /device:TPU:8 now
where the time goes in v1:
time: 285 us; the launch traced here: 283 us
  waiting for transfers between devices  117 us (41%)
  starting transfers between devices  83.3 us (29%)
  Pallas kernels  67.9 us (24%)
  local copies, waits for them, and re-layouts  13.6 us (5%)
    ppermute x26, waiting for transfers between devices, permute(): return lax.ppermute(value, axes, pairs)  102 us
    pallas_call x11, Pallas kernels, call(): pl.pallas_call(kernel, grid_spec=pltpu.PrefetchScalarGridSpec(num_scalar_...  67.9 us
    ppermute x26, starting transfers between devices, permute(): return lax.ppermute(value, axes, pairs)  52.5 us
    all_to_all x7, starting transfers between devices, over_x(): return lax.all_to_all(payload, 'x', 0, 0, tiled=True)  30.9 us
    all_to_all x7, waiting for transfers between devices, over_x(): return lax.all_to_all(payload, 'x', 0, 0, tiled=True)  14.6 us
    unnamed x55, local copies, waits for them, and re-layouts  8.45 us
  transfers between devices with their start and end apart: 33, of which 14 were waited for; matrix products, arithmetic and copies ran while one was open for 2% of the time, Pallas kernels for 14%

profile of v1, /device:TPU:8, one launch (start us, length us, event | category | flops | bytes accessed | tf_op | source)
XLA Modules:
  0.0 283.1 jit_solution(3292459832218939727)
XLA Ops:
  1.5 4.8 %collective-permute-start = (bf16[3,128,128]{1,2,0:T(8,128)(2,1)S(1)}, bf16[3,128,128]{1,2,0:T(8,128)(2,1)S(1)}, u32[]{:S(2)}, u32[]{:S(2)}) collective-permute-start(bf16[3,128,128]{1,2,0:T(8,128)(2,1)S(1)} %dynamic-slice_bitcast_fusion), channel_id=1, source_target_pairs={{0,0},{1,16},{2,32},{3,48},{4,64},{5,80},{6,96},{7,112},{8,128},{9... | collective-permute-start | bytes 294920 | tf_op jit(solution)/shard_map/ppermute | solution.py:26
  18.7 8.8 %collective-permute-start.2 = (bf16[2,768,128]{2,1,0:T(8,128)(2,1)S(1)}, bf16[2,768,128]{2,1,0:T(8,128)(2,1)S(1)}, u32[]{:S(2)}, u32[]{:S(2)}) collective-permute-start(bf16[2,768,128]{2,1,0:T(8,128)(2,1)S(1)} %copy-done.15), channel_id=1, source_target_pairs={{0,8},{1,9},{2,10},{3,11},{4,12},{5,13},{6,14},{7,15},{8,0},{9,1},... | collective-permute-start | bytes 1179656 | tf_op jit(solution)/shard_map/ppermute | solution.py:26
  31.9 17.6 %collective-permute-done.5 = bf16[3,128,128]{1,2,0:T(8,128)(2,1)S(1)} collective-permute-done((bf16[3,128,128]{1,2,0:T(8,128)(2,1)S(1)}, bf16[3,128,128]{1,2,0:T(8,128)(2,1)S(1)}, u32[]{:S(2)}, u32[]{:S(2)}) %collective-permute-start.5) | collective-permute-done | bytes 98336 | tf_op jit(solution)/shard_map/ppermute | solution.py:26
  55.8 4.4 %all-to-all-start.1 = ((bf16[4,128,768]{2,1,0:T(8,128)(2,1)}), bf16[4,128,768]{2,1,0:T(8,128)(2,1)S(1)}, u32[]{:S(2)}, u32[]{:S(2)}) async-start(bf16[4,128,768]{2,1,0:T(8,128)(2,1)} %shard_map.87), calls=%async_computation.1 | async-start | bytes 1572864 | tf_op jit(solution)/shard_map/all_to_all | solution.py:132
  60.5 9.6 %all-to-all-done.1 = bf16[4,128,768]{2,1,0:T(8,128)(2,1)S(1)} async-done(((bf16[4,128,768]{2,1,0:T(8,128)(2,1)}), bf16[4,128,768]{2,1,0:T(8,128)(2,1)S(1)}, u32[]{:S(2)}, u32[]{:S(2)}) %all-to-all-start.1) | async-done | bytes 786464 | tf_op jit(solution)/shard_map/all_to_all | solution.py:132
  81.9 6.4 %collective-permute-start.7 = (bf16[2,128,768]{2,1,0:T(8,128)(2,1)}, bf16[2,128,768]{2,1,0:T(8,128)(2,1)S(1)}, u32[]{:S(2)}, u32[]{:S(2)}) collective-permute-start(bf16[2,128,768]{2,1,0:T(8,128)(2,1)} %get-tuple-element.51), channel_id=1, source_target_pairs={{0,192},{1,193},{2,194},{3,195},{4,196},{5,197},{6,198},{7,199},{8... | collective-permute-start | bytes 1179656 | tf_op jit(solution)/shard_map/ppermute | solution.py:26
  89.7 8.4 %collective-permute-done.7.refs_1_ = bf16[2,128,768]{2,1,0:T(8,128)(2,1)S(1)} collective-permute-done((bf16[2,128,768]{2,1,0:T(8,128)(2,1)}, bf16[2,128,768]{2,1,0:T(8,128)(2,1)S(1)}, u32[]{:S(2)}, u32[]{:S(2)}) %collective-permute-start.7) | collective-permute-done | bytes 393248 | tf_op jit(solution)/shard_map/ppermute | solution.py:26
  98.1 21.0 %collective-permute-done.6.refs_0_ = bf16[2,128,768]{2,1,0:T(8,128)(2,1)S(1)} collective-permute-done((bf16[2,128,768]{2,1,0:T(8,128)(2,1)}, bf16[2,128,768]{2,1,0:T(8,128)(2,1)S(1)}, u32[]{:S(2)}, u32[]{:S(2)}) %collective-permute-start.6) | collective-permute-done | bytes 393248 | tf_op jit(solution)/shard_map/ppermute | solution.py:26
  125.0 4.7 %all-to-all-start.3 = ((bf16[8,128,768]{2,1,0:T(8,128)(2,1)}), bf16[8,128,768]{2,1,0:T(8,128)(2,1)S(1)}, u32[]{:S(2)}, u32[]{:S(2)}) async-start(bf16[8,128,768]{2,1,0:T(8,128)(2,1)} %shard_map.91), calls=%async_computation.3 | async-start | bytes 3145728 | tf_op jit(solution)/shard_map/all_to_all | solution.py:132
  133.1 5.7 %shard_map.89.ham_ref = bf16[768,2048]{1,0:T(8,128)(2,1)} custom-call(s32[2]{0:T(128)} %pad_add_fusion.ids, s32[3,16,64]{2,1,0:T(8,128)} %lists.3, s32[16]{0:T(128)} %counts.3, bf16[48,128,128]{2,1,0:T(8,128)(2,1)} %ham_ref.1), custom_call_target="tpu_custom_call" | custom-call | flops 4194304 | bytes 5242880 | tf_op jit(solution)/shard_map/pallas_call | solution.py:59
  138.8 6.3 %shard_map.88.ham_t_ref = bf16[2048,768]{1,0:T(8,128)(2,1)} custom-call(s32[2]{0:T(128)} %pad_add_fusion.ids, s32[3,16,64]{2,1,0:T(8,128)} %lists.3, s32[16]{0:T(128)} %counts.3, bf16[48,128,128]{2,1,0:T(8,128)(2,1)} %copy-done), custom_call_target="tpu_custom_call" | custom-call | flops 4194304 | bytes 5242880 | tf_op jit(solution)/shard_map/pallas_call | solution.py:59
  146.3 9.5 %shard_map.90.part_ref = f32[768,768]{1,0:T(8,128)} custom-call(s32[2]{0:T(128)} %pad_add_fusion.ids, s32[16,16]{1,0:T(8,128)} %sel.17, bf16[2048,768]{1,0:T(8,128)(2,1)} %shard_map.88.ham_t_ref, bf16[768,2048]{1,0:T(8,128)(2,1)} %shard_map.89.ham_ref, bf16[512,768]{1,0:T(8,128)(2,1)} %bitcast.17, bf16[512,768]{1,0:T(8,128)(2,1)} %bitcast.18, ...), custom_call_target="tpu_custom_call" | custom-call | flops 3623878656 | bytes 18874368 | tf_op jit(solution)/shard_map/pallas_call | solution.py:59
  157.1 8.4 %shard_map.92 = (f32[768,768]{1,0:T(8,128)}, bf16[2,128,768]{2,1,0:T(8,128)(2,1)}, bf16[2,768,128]{2,1,0:T(8,128)(2,1)}, bf16[4,128,768]{2,1,0:T(8,128)(2,1)}) custom-call(s32[2]{0:T(128)} %pad_add_fusion.ids, s32[16,2]{1,0:T(8,128)} %copy.15.hot, s32[16,16]{1,0:T(8,128)} %sel.17, f32[768,768]{1,0:T(8,128)} %shard_map.90.part_ref, ...), custom_call_target="tpu_custom_call" | custom-call | flops 1207959552 | bytes 12582912 | tf_op jit(solution)/shard_map/pallas_call | solution.py:59
  165.5 5.0 %all-to-all-start.4 = ((bf16[4,128,768]{2,1,0:T(8,128)(2,1)}), bf16[4,128,768]{2,1,0:T(8,128)(2,1)S(1)}, u32[]{:S(2)}, u32[]{:S(2)}) async-start(bf16[4,128,768]{2,1,0:T(8,128)(2,1)} %get-tuple-element.73), calls=%async_computation.4 | async-start | bytes 1572864 | tf_op jit(solution)/shard_map/all_to_all | solution.py:132
  174.6 16.2 %collective-permute-done.15.refs_0_ = bf16[2,128,768]{2,1,0:T(8,128)(2,1)S(1)} collective-permute-done((bf16[2,128,768]{2,1,0:T(8,128)(2,1)S(1)}, bf16[2,128,768]{2,1,0:T(8,128)(2,1)S(1)}, u32[]{:S(2)}, u32[]{:S(2)}) %collective-permute-start.15) | collective-permute-done | bytes 393248 | tf_op jit(solution)/shard_map/ppermute | solution.py:26
  190.8 4.7 %collective-permute-done.16 = bf16[2,768,128]{2,1,0:T(8,128)(2,1)S(1)} collective-permute-done((bf16[2,768,128]{2,1,0:T(8,128)(2,1)S(1)}, bf16[2,768,128]{2,1,0:T(8,128)(2,1)S(1)}, u32[]{:S(2)}, u32[]{:S(2)}) %collective-permute-start.16) | collective-permute-done | bytes 393248 | tf_op jit(solution)/shard_map/ppermute | solution.py:26
  203.9 4.7 %all-to-all-start.5 = ((bf16[4,128,768]{2,1,0:T(8,128)(2,1)}), bf16[4,128,768]{2,1,0:T(8,128)(2,1)S(1)}, u32[]{:S(2)}, u32[]{:S(2)}) async-start(bf16[4,128,768]{2,1,0:T(8,128)(2,1)} %shard_map.93), calls=%async_computation.5 | async-start | bytes 1572864 | tf_op jit(solution)/shard_map/all_to_all | solution.py:132
  208.6 7.0 %collective-permute-start.17 = (bf16[2,128,768]{2,1,0:T(8,128)(2,1)S(1)}, bf16[2,128,768]{2,1,0:T(8,128)(2,1)S(1)}, u32[]{:S(2)}, u32[]{:S(2)}) collective-permute-start(bf16[2,128,768]{2,1,0:T(8,128)(2,1)S(1)} %copy-done.25), channel_id=1, source_target_pairs={{0,128},{1,129},{2,130},{3,131},{4,132},{5,133},{6,134},{7,135},{8... | collective-permute-start | bytes 1179656 | tf_op jit(solution)/shard_map/ppermute | solution.py:26
  215.6 6.3 %collective-permute-done.18.refs_1_ = bf16[2,128,768]{2,1,0:T(8,128)(2,1)S(1)} collective-permute-done((bf16[2,128,768]{2,1,0:T(8,128)(2,1)S(1)}, bf16[2,128,768]{2,1,0:T(8,128)(2,1)S(1)}, u32[]{:S(2)}, u32[]{:S(2)}) %collective-permute-start.18) | collective-permute-done | bytes 393248 | tf_op jit(solution)/shard_map/ppermute | solution.py:26
  221.9 21.5 %collective-permute-done.17.refs_0_ = bf16[2,128,768]{2,1,0:T(8,128)(2,1)S(1)} collective-permute-done((bf16[2,128,768]{2,1,0:T(8,128)(2,1)S(1)}, bf16[2,128,768]{2,1,0:T(8,128)(2,1)S(1)}, u32[]{:S(2)}, u32[]{:S(2)}) %collective-permute-start.17) | collective-permute-done | bytes 393248 | tf_op jit(solution)/shard_map/ppermute | solution.py:26
  248.5 4.8 %all-to-all-start.6 = ((bf16[8,128,768]{2,1,0:T(8,128)(2,1)}), bf16[8,128,768]{2,1,0:T(8,128)(2,1)S(1)}, u32[]{:S(2)}, u32[]{:S(2)}) async-start(bf16[8,128,768]{2,1,0:T(8,128)(2,1)} %shard_map.95), calls=%async_computation.6 | async-start | bytes 3145728 | tf_op jit(solution)/shard_map/all_to_all | solution.py:132
  259.3 9.6 %shard_map.94.part_ref = f32[768,768]{1,0:T(8,128)} custom-call(s32[2]{0:T(128)} %pad_add_fusion.ids, s32[16,16]{1,0:T(8,128)} %sel.17, bf16[2048,768]{1,0:T(8,128)(2,1)} %shard_map.88.ham_t_ref, bf16[768,2048]{1,0:T(8,128)(2,1)} %shard_map.89.ham_ref, bf16[512,768]{1,0:T(8,128)(2,1)} %bitcast.19, bf16[512,768]{1,0:T(8,128)(2,1)} %bitcast.20, ...), custom_call_target="tpu_custom_call" | custom-call | flops 3623878656 | bytes 18874368 | tf_op jit(solution)/shard_map/pallas_call | solution.py:59
  268.9 4.9 %all-to-all-done.6 = bf16[8,128,768]{2,1,0:T(8,128)(2,1)S(1)} async-done(((bf16[8,128,768]{2,1,0:T(8,128)(2,1)}), bf16[8,128,768]{2,1,0:T(8,128)(2,1)S(1)}, u32[]{:S(2)}, u32[]{:S(2)}) %all-to-all-start.6) | async-done | bytes 1572896 | tf_op jit(solution)/shard_map/all_to_all | solution.py:132
  275.1 8.1 %shard_map.96 = f32[768,768]{1,0:T(8,128)} custom-call(s32[2]{0:T(128)} %pad_add_fusion.ids, s32[16,2]{1,0:T(8,128)} %copy.15.hot, s32[16,16]{1,0:T(8,128)} %sel.17, f32[768,768]{1,0:T(8,128)} %shard_map.94.part_ref, bf16[768,2048]{1,0:T(8,128)(2,1)} %shard_map.89.ham_ref, bf16[1024,768]{1,0:T(8,128)(2,1)} %bitcast.16, f32[768,768]{1,0:T(8,128)} %get-tuple-element.42.x_ref, ...), custom_call_target="tpu_custom_call" | custom-call | flops 1207959552 | bytes 12582912 | tf_op jit(solution)/shard_map/pallas_call | solution.py:59
  (118 shorter events, 73.8 us)
Async XLA Ops:
  12.2 38.8 %all-to-all-start = ((bf16[4,128,768]{2,1,0:T(8,128)(2,1)}), bf16[4,128,768]{2,1,0:T(8,128)(2,1)S(1)}, u32[]{:S(2)}, u32[]{:S(2)}) async-start(bf16[4,128,768]{2,1,0:T(8,128)(2,1)} %get-tuple-element.49), calls=%async_computation | async-start | bytes 1572864 | tf_op jit(solution)/shard_map/all_to_all | solution.py:132
  15.8 35.2 %collective-permute-start.1 = (bf16[2,128,768]{2,1,0:T(8,128)(2,1)}, bf16[2,128,768]{2,1,0:T(8,128)(2,1)S(1)}, u32[]{:S(2)}, u32[]{:S(2)}) collective-permute-start(bf16[2,128,768]{2,1,0:T(8,128)(2,1)} %get-tuple-element.51), channel_id=1, source_target_pairs={{0,64},{1,65},{2,66},{3,67},{4,68},{5,69},{6,70},{7,71},{8,72},{9,... | collective-permute-start | bytes 1179656 | tf_op jit(solution)/shard_map/ppermute | solution.py:26
  18.7 32.4 %collective-permute-start.2 = (bf16[2,768,128]{2,1,0:T(8,128)(2,1)S(1)}, bf16[2,768,128]{2,1,0:T(8,128)(2,1)S(1)}, u32[]{:S(2)}, u32[]{:S(2)}) collective-permute-start(bf16[2,768,128]{2,1,0:T(8,128)(2,1)S(1)} %copy-done.15), channel_id=1, source_target_pairs={{0,8},{1,9},{2,10},{3,11},{4,12},{5,13},{6,14},{7,15},{8,0},{9,1},... | collective-permute-start | bytes 1179656 | tf_op jit(solution)/shard_map/ppermute | solution.py:26
  27.5 22.0 %collective-permute-start.5 = (bf16[3,128,128]{1,2,0:T(8,128)(2,1)S(1)}, bf16[3,128,128]{1,2,0:T(8,128)(2,1)S(1)}, u32[]{:S(2)}, u32[]{:S(2)}) collective-permute-start(bf16[3,128,128]{1,2,0:T(8,128)(2,1)S(1)} %collective-permute-done), channel_id=1, source_target_pairs={{0,192},{1,193},{2,194},{3,195},{4,196},{5,197},{6,198},{7,199},{8... | collective-permute-start | bytes 294920 | tf_op jit(solution)/shard_map/ppermute | solution.py:26
  27.5 22.0 %collective-permute-start.4 = (bf16[3,128,128]{1,2,0:T(8,128)(2,1)S(1)}, bf16[3,128,128]{1,2,0:T(8,128)(2,1)S(1)}, u32[]{:S(2)}, u32[]{:S(2)}) collective-permute-start(bf16[3,128,128]{1,2,0:T(8,128)(2,1)S(1)} %collective-permute-done), channel_id=1, source_target_pairs={{0,128},{1,129},{2,130},{3,131},{4,132},{5,133},{6,134},{7,135},{8... | collective-permute-start | bytes 294920 | tf_op jit(solution)/shard_map/ppermute | solution.py:26
  29.5 21.5 %collective-permute-start.3 = (bf16[3,128,128]{1,2,0:T(8,128)(2,1)S(1)}, bf16[3,128,128]{1,2,0:T(8,128)(2,1)S(1)}, u32[]{:S(2)}, u32[]{:S(2)}) collective-permute-start(bf16[3,128,128]{1,2,0:T(8,128)(2,1)S(1)} %collective-permute-done), channel_id=1, source_target_pairs={{0,64},{1,65},{2,66},{3,67},{4,68},{5,69},{6,70},{7,71},{8,72},{9,... | collective-permute-start | bytes 294920 | tf_op jit(solution)/shard_map/ppermute | solution.py:26
  71.7 49.2 %all-to-all-start.2 = ((bf16[48,128,128]{2,1,0:T(8,128)(2,1)}), bf16[48,128,128]{2,1,0:T(8,128)(2,1)S(1)}, u32[]{:S(2)}, u32[]{:S(2)}) async-start(bf16[48,128,128]{2,1,0:T(8,128)(2,1)} %bitcast.7), calls=%async_computation.2 | async-start | bytes 3145728 | tf_op jit(solution)/shard_map/all_to_all | solution.py:132
  75.5 43.5 %collective-permute-start.10 = (bf16[4,768,128]{2,1,0:T(8,128)(2,1)S(1)}, bf16[4,768,128]{2,1,0:T(8,128)(2,1)S(1)}, u32[]{:S(2)}, u32[]{:S(2)}) collective-permute-start(bf16[4,768,128]{2,1,0:T(8,128)(2,1)S(1)} %constant_dynamic-update-slice_fusion.refs_0_), channel_id=1, source_target_pairs={{0,6},{1,7},{2,0},{3,1},{4,2},{5,3},{6,4},{7,5},{8,14},{9,15},{10,... | collective-permute-start | bytes 2359304 | tf_op jit(solution)/shard_map/ppermute | solution.py:26
  76.4 42.6 %collective-permute-start.9 = (bf16[4,768,128]{2,1,0:T(8,128)(2,1)S(1)}, bf16[4,768,128]{2,1,0:T(8,128)(2,1)S(1)}, u32[]{:S(2)}, u32[]{:S(2)}) collective-permute-start(bf16[4,768,128]{2,1,0:T(8,128)(2,1)S(1)} %constant_dynamic-update-slice_fusion.refs_0_), channel_id=1, source_target_pairs={{0,4},{1,5},{2,6},{3,7},{4,0},{5,1},{6,2},{7,3},{8,12},{9,13},{10,... | collective-permute-start | bytes 2359304 | tf_op jit(solution)/shard_map/ppermute | solution.py:26
  80.2 40.7 %collective-permute-start.8 = (bf16[4,768,128]{2,1,0:T(8,128)(2,1)S(1)}, bf16[4,768,128]{2,1,0:T(8,128)(2,1)}, u32[]{:S(2)}, u32[]{:S(2)}) collective-permute-start(bf16[4,768,128]{2,1,0:T(8,128)(2,1)S(1)} %constant_dynamic-update-slice_fusion.refs_0_), channel_id=1, source_target_pairs={{0,2},{1,3},{2,4},{3,5},{4,6},{5,7},{6,0},{7,1},{8,10},{9,11},{10,... | collective-permute-start | bytes 2359304 | tf_op jit(solution)/shard_map/ppermute | solution.py:26
  81.9 16.2 %collective-permute-start.7 = (bf16[2,128,768]{2,1,0:T(8,128)(2,1)}, bf16[2,128,768]{2,1,0:T(8,128)(2,1)S(1)}, u32[]{:S(2)}, u32[]{:S(2)}) collective-permute-start(bf16[2,128,768]{2,1,0:T(8,128)(2,1)} %get-tuple-element.51), channel_id=1, source_target_pairs={{0,192},{1,193},{2,194},{3,195},{4,196},{5,197},{6,198},{7,199},{8... | collective-permute-start | bytes 1179656 | tf_op jit(solution)/shard_map/ppermute | solution.py:26
  88.3 30.8 %collective-permute-start.6 = (bf16[2,128,768]{2,1,0:T(8,128)(2,1)}, bf16[2,128,768]{2,1,0:T(8,128)(2,1)S(1)}, u32[]{:S(2)}, u32[]{:S(2)}) collective-permute-start(bf16[2,128,768]{2,1,0:T(8,128)(2,1)} %get-tuple-element.51), channel_id=1, source_target_pairs={{0,128},{1,129},{2,130},{3,131},{4,132},{5,133},{6,134},{7,135},{8... | collective-permute-start | bytes 1179656 | tf_op jit(solution)/shard_map/ppermute | solution.py:26
  125.0 30.8 %all-to-all-start.3 = ((bf16[8,128,768]{2,1,0:T(8,128)(2,1)}), bf16[8,128,768]{2,1,0:T(8,128)(2,1)S(1)}, u32[]{:S(2)}, u32[]{:S(2)}) async-start(bf16[8,128,768]{2,1,0:T(8,128)(2,1)} %shard_map.91), calls=%async_computation.3 | async-start | bytes 3145728 | tf_op jit(solution)/shard_map/all_to_all | solution.py:132
  129.7 15.4 %collective-permute-start.11 = (bf16[4,768,128]{2,1,0:T(8,128)(2,1)}, bf16[4,768,128]{2,1,0:T(8,128)(2,1)S(1)}, u32[]{:S(2)}, u32[]{:S(2)}) collective-permute-start(bf16[4,768,128]{2,1,0:T(8,128)(2,1)} %copy-done.7), channel_id=1, source_target_pairs={{0,1},{1,0},{2,3},{3,2},{4,5},{5,4},{6,7},{7,6},{8,9},{9,8},{10,11... | collective-permute-start | bytes 2359304 | tf_op jit(solution)/shard_map/ppermute | solution.py:26
  129.7 15.4 %collective-permute-start.12 = (bf16[4,768,128]{2,1,0:T(8,128)(2,1)}, bf16[4,768,128]{2,1,0:T(8,128)(2,1)S(1)}, u32[]{:S(2)}, u32[]{:S(2)}) collective-permute-start(bf16[4,768,128]{2,1,0:T(8,128)(2,1)} %collective-permute-done.8.refs_1_), channel_id=1, source_target_pairs={{0,1},{1,0},{2,3},{3,2},{4,5},{5,4},{6,7},{7,6},{8,9},{9,8},{10,11... | collective-permute-start | bytes 2359304 | tf_op jit(solution)/shard_map/ppermute | solution.py:26
  165.5 30.0 %all-to-all-start.4 = ((bf16[4,128,768]{2,1,0:T(8,128)(2,1)}), bf16[4,128,768]{2,1,0:T(8,128)(2,1)S(1)}, u32[]{:S(2)}, u32[]{:S(2)}) async-start(bf16[4,128,768]{2,1,0:T(8,128)(2,1)} %get-tuple-element.73), calls=%async_computation.4 | async-start | bytes 1572864 | tf_op jit(solution)/shard_map/all_to_all | solution.py:132
  170.5 20.4 %collective-permute-start.15 = (bf16[2,128,768]{2,1,0:T(8,128)(2,1)S(1)}, bf16[2,128,768]{2,1,0:T(8,128)(2,1)S(1)}, u32[]{:S(2)}, u32[]{:S(2)}) collective-permute-start(bf16[2,128,768]{2,1,0:T(8,128)(2,1)S(1)} %copy-done.25), channel_id=1, source_target_pairs={{0,64},{1,65},{2,66},{3,67},{4,68},{5,69},{6,70},{7,71},{8,72},{9,... | collective-permute-start | bytes 1179656 | tf_op jit(solution)/shard_map/ppermute | solution.py:26
  170.5 25.0 %collective-permute-start.16 = (bf16[2,768,128]{2,1,0:T(8,128)(2,1)S(1)}, bf16[2,768,128]{2,1,0:T(8,128)(2,1)S(1)}, u32[]{:S(2)}, u32[]{:S(2)}) collective-permute-start(bf16[2,768,128]{2,1,0:T(8,128)(2,1)S(1)} %copy-done.18), channel_id=1, source_target_pairs={{0,8},{1,9},{2,10},{3,11},{4,12},{5,13},{6,14},{7,15},{8,0},{9,1},... | collective-permute-start | bytes 1179656 | tf_op jit(solution)/shard_map/ppermute | solution.py:26
  195.6 47.8 %collective-permute-start.21 = (bf16[4,768,128]{2,1,0:T(8,128)(2,1)S(1)}, bf16[4,768,128]{2,1,0:T(8,128)(2,1)S(1)}, u32[]{:S(2)}, u32[]{:S(2)}) collective-permute-start(bf16[4,768,128]{2,1,0:T(8,128)(2,1)S(1)} %constant_dynamic-update-slice_fusion.2.refs_0_), channel_id=1, source_target_pairs={{0,6},{1,7},{2,0},{3,1},{4,2},{5,3},{6,4},{7,5},{8,14},{9,15},{10,... | collective-permute-start | bytes 2359304 | tf_op jit(solution)/shard_map/ppermute | solution.py:26
  196.5 46.9 %collective-permute-start.20 = (bf16[4,768,128]{2,1,0:T(8,128)(2,1)S(1)}, bf16[4,768,128]{2,1,0:T(8,128)(2,1)}, u32[]{:S(2)}, u32[]{:S(2)}) collective-permute-start(bf16[4,768,128]{2,1,0:T(8,128)(2,1)S(1)} %constant_dynamic-update-slice_fusion.2.refs_0_), channel_id=1, source_target_pairs={{0,4},{1,5},{2,6},{3,7},{4,0},{5,1},{6,2},{7,3},{8,12},{9,13},{10,... | collective-permute-start | bytes 2359304 | tf_op jit(solution)/shard_map/ppermute | solution.py:26
  197.3 46.2 %collective-permute-start.19 = (bf16[4,768,128]{2,1,0:T(8,128)(2,1)S(1)}, bf16[4,768,128]{2,1,0:T(8,128)(2,1)}, u32[]{:S(2)}, u32[]{:S(2)}) collective-permute-start(bf16[4,768,128]{2,1,0:T(8,128)(2,1)S(1)} %constant_dynamic-update-slice_fusion.2.refs_0_), channel_id=1, source_target_pairs={{0,2},{1,3},{2,4},{3,5},{4,6},{5,7},{6,0},{7,1},{8,10},{9,11},{10,... | collective-permute-start | bytes 2359304 | tf_op jit(solution)/shard_map/ppermute | solution.py:26
  203.9 39.6 %all-to-all-start.5 = ((bf16[4,128,768]{2,1,0:T(8,128)(2,1)}), bf16[4,128,768]{2,1,0:T(8,128)(2,1)S(1)}, u32[]{:S(2)}, u32[]{:S(2)}) async-start(bf16[4,128,768]{2,1,0:T(8,128)(2,1)} %shard_map.93), calls=%async_computation.5 | async-start | bytes 1572864 | tf_op jit(solution)/shard_map/all_to_all | solution.py:132
  208.6 34.8 %collective-permute-start.17 = (bf16[2,128,768]{2,1,0:T(8,128)(2,1)S(1)}, bf16[2,128,768]{2,1,0:T(8,128)(2,1)S(1)}, u32[]{:S(2)}, u32[]{:S(2)}) collective-permute-start(bf16[2,128,768]{2,1,0:T(8,128)(2,1)S(1)} %copy-done.25), channel_id=1, source_target_pairs={{0,128},{1,129},{2,130},{3,131},{4,132},{5,133},{6,134},{7,135},{8... | collective-permute-start | bytes 1179656 | tf_op jit(solution)/shard_map/ppermute | solution.py:26
  248.5 25.3 %all-to-all-start.6 = ((bf16[8,128,768]{2,1,0:T(8,128)(2,1)}), bf16[8,128,768]{2,1,0:T(8,128)(2,1)S(1)}, u32[]{:S(2)}, u32[]{:S(2)}) async-start(bf16[8,128,768]{2,1,0:T(8,128)(2,1)} %shard_map.95), calls=%async_computation.6 | async-start | bytes 3145728 | tf_op jit(solution)/shard_map/all_to_all | solution.py:132
  (35 other events, 309.8 us)

commit v2 on v1

v2 whole, which is shorter than its diff:
```python
import jax
import jax.numpy as jnp
from jax import lax
from jax.experimental import pallas as pl
from jax.experimental.pallas import tpu as pltpu
from jax.sharding import Mesh, PartitionSpec as P
import numpy as np

center = 0.25
scale = 1.0 / 2.5
axes = ("zl", "x", "zh", "y", "k")
sizes = (4, 4, 2, 4, 2)
B = 128
T = 768
R = 256
bf16 = jnp.bfloat16
f32 = jnp.float32


def permute(value, target):
    places = list(np.ndindex(*sizes))
    pairs = [
        (int(np.ravel_multi_index(p, sizes)), int(np.ravel_multi_index(target(*p), sizes)))
        for p in places
    ]
    return lax.ppermute(value, axes, pairs)


def z_xor(n):
    return lambda zl, x, zh, y, k: (zl ^ n, x, zh, y, k)


def x_shift(n):
    return lambda zl, x, zh, y, k: (zl, (x + n) % 4, zh, y, k)


def zh_flip(zl, x, zh, y, k):
    return (zl, x, 1 - zh, y, k)


def mirror(zl, x, zh, y, k):
    r, c = zl * 4 + x, zh * 8 + y * 2 + k
    return (c // 4, c % 4, r // 8, (r % 8) // 2, r % 2)


def barrier(*values):
    return lax.optimization_barrier(values)


def start(block):
    return pl.multiple_of(block * B, B)


def call(kernel, scalars, grid, in_specs, out_specs, out_shape, args, scratch=(), flops=0, moved=0, room=1):
    return pl.pallas_call(
        kernel,
        grid_spec=pltpu.PrefetchScalarGridSpec(
            num_scalar_prefetch=len(scalars),
            grid=grid,
            in_specs=in_specs,
            out_specs=out_specs,
            scratch_shapes=list(scratch),
        ),
        out_shape=out_shape,
        compiler_params=pltpu.CompilerParams(vmem_limit_bytes=room << 20),
        cost_estimate=pl.CostEstimate(flops=flops, bytes_accessed=moved, transcendentals=0),
    )(*scalars, *args)


def shape(dims, kind=bf16):
    return jax.ShapeDtypeStruct(dims, kind)


pack_shapes = (shape((2, B, T)), shape((2, T, B)))


def pack_kernel(ids, hot, x_ref, row_ref, col_ref):
    r, c = ids[0], ids[1]
    for h in range(2):
        row_ref[h] = x_ref[pl.ds(start(hot[r, h]), B), :].astype(bf16)
        col_ref[h] = x_ref[:, pl.ds(start(hot[c, h]), B)].astype(bf16)

def pack(ids, hot, value):
    def whole(dims):
        return pl.BlockSpec(dims, lambda i, *_: (0,) * len(dims))

    return call(
        pack_kernel,
        (ids, hot),
        (1,),
        [whole((T, T))],
        [whole((2, B, T)), whole((2, T, B))],
        pack_shapes,
        (value,),
        moved=5 << 20,
        room=16,
    )


anywhere = pl.BlockSpec(memory_space=pl.ANY)


def copy_all(pairs, done):
    copies = [
        pltpu.make_async_copy(source, target, done.at[i])
        for i, (source, target) in enumerate(pairs)
    ]
    for copy in copies:
        copy.start()
    for copy in copies:
        copy.wait()


def over_x(ids, sel, slabs, step):
    def kernel(ids, sel, slabs_ref, *refs):
        zl, x = ids[0] // 4, ids[0] % 4
        q = (zl ^ step) * 4 + x
        copy_all(
            [(slabs_ref.at[sel[zl * 4 + (x + n) % 4, q]], refs[n].at[0]) for n in range(4)],
            refs[4],
        )

    chosen = call(
        kernel,
        (ids, sel),
        (1,),
        [anywhere],
        [anywhere] * 4,
        [shape((1, B, T))] * 4,
        (slabs,),
        scratch=[pltpu.SemaphoreType.DMA((4,))],
        moved=256 << 20,
    )
    return [chosen[0]] + [permute(chosen[n], x_shift(n)) for n in (1, 2, 3)]


def over_yk(ids, sel, slabs, flip):
    def kernel(ids, sel, slabs_ref, out_ref, done):
        zh, q = ids[1] // 8, ids[1] ^ (8 * flip)
        copy_all(
            [(slabs_ref.at[sel[zh * 8 + i, q]], out_ref.at[i]) for i in range(8)], done
        )

    chosen = call(
        kernel,
        (ids, sel),
        (1,),
        [anywhere],
        anywhere,
        shape((8, T, B)),
        (slabs,),
        scratch=[pltpu.SemaphoreType.DMA((8,))],
        moved=256 << 20,
    )
    return lax.all_to_all(chosen, ("y", "k"), 0, 0, tiled=True)


def dense_kernel(mirrored):
    def kernel(ids, lists, counts, ham_ref, out_ref, total):
        r, c = ids[0], ids[1]
        tile = c if mirrored else r
        zl = r // 4

        def clear(i, carry):
            total[i] = jnp.zeros((B, B), f32)
            return carry

        lax.fori_loop(0, 96, clear, 0)

        def add(slot, carry):
            q = lists[0, tile, slot]
            t = lists[1, tile, slot]
            b = lists[2, tile, slot]
            if mirrored:
                place = q ^ (c // 8 * 8)
                piece = b // 3
                b = ((piece % 4) * 4 + ((piece // 4) ^ zl)) * 3 + b % 3
            else:
                place = ((q // 4) ^ zl) * 4 + (r + 4 - q % 4) % 4
            at = t * 16 + place
            total[at] = total[at] + ham_ref[b].astype(f32)
            return carry

        lax.fori_loop(0, counts[tile], add, 0)
        for t in range(6):
            for place in range(16):
                block = total[t * 16 + place].astype(bf16)
                if mirrored:
                    out_ref[place * B : (place + 1) * B, t * B : (t + 1) * B] = block
                else:
                    out_ref[t * B : (t + 1) * B, place * B : (place + 1) * B] = block

    return kernel


def dense(ids, lists, counts, hams, mirrored):
    dims = (2048, T) if mirrored else (T, 2048)
    return call(
        dense_kernel(mirrored),
        (ids, lists, counts),
        (1,),
        [pl.BlockSpec((48, B, B), lambda i, *_: (0, 0, 0))],
        pl.BlockSpec(dims, lambda i, *_: (0, 0)),
        shape(dims),
        (hams,),
        scratch=[pltpu.VMEM((96, B, B), f32)],
        flops=1 << 22,
        moved=5 << 20,
        room=28,
    )


def first_products_kernel(second):
    def kernel(ham_t_ref, ham_ref, x_ref, dr_ref, dc_ref, yk0_ref, yk1_ref, *refs):
        slabs, out_ref, wide = refs[:8], refs[-2], refs[-1]
        for i in range(8):
            wide[:, i * B : (i + 1) * B] = yk0_ref[i]
            wide[:, (8 + i) * B : (9 + i) * B] = yk1_ref[i]
        stacked = jnp.concatenate([slab[0] for slab in slabs], axis=0)
        total = jnp.dot(wide[...], ham_t_ref[...], preferred_element_type=f32) + jnp.dot(
            ham_ref[...], stacked, preferred_element_type=f32
        )
        total = total + (dr_ref[...] + dc_ref[...] - center) * x_ref[...]
        if second:
            total = total - refs[8][...] * (0.5 / scale)
        out_ref[...] = total

    return kernel


rows = pl.BlockSpec((R, T), lambda i, *_: (i, 0))
slab = pl.BlockSpec((1, B, T), lambda i, *_: (0, 0, 0))


def first_products(ham_t, ham, value, dr, dc, yk0, yk1, slabs, before=None):
    extra = () if before is None else (before,)
    return call(
        first_products_kernel(before is not None),
        (),
        (T // R,),
        [
            pl.BlockSpec((2048, T), lambda i, *_: (0, 0)),
            pl.BlockSpec((R, 1024), lambda i, *_: (i, 0)),
            rows,
            pl.BlockSpec((R, 1), lambda i, *_: (i, 0)),
            pl.BlockSpec((1, T), lambda i, *_: (0, 0)),
        ]
        + [pl.BlockSpec((8, R, B), lambda i, *_: (0, i, 0))] * 2
        + [slab] * 8
        + [rows] * len(extra),
        rows,
        shape((T, T), f32),
        (ham_t, ham, value, dr, dc, yk0, yk1, *slabs, *extra),
        scratch=[pltpu.VMEM((R, 2048), bf16)],
        flops=2 * T * T * 3072,
        moved=18 << 20,
        room=32,
    )


def finish_kernel(second):
    def kernel(ids, hot, part_ref, ham_ref, *refs):
        stacked = jnp.concatenate([ref[0] for ref in refs[:8]], axis=0)
        out_ref = refs[8]
        total = part_ref[...] + jnp.dot(ham_ref[...], stacked, preferred_element_type=f32)
        if second:
            out_ref[...] = total * (2.0 * scale)
            return
        row_ref, col_ref = refs[9:]
        out_ref[...] = total * scale
        i, r, c = pl.program_id(0), ids[0], ids[1]
        for h in range(2):
            col_ref[h] = out_ref[:, pl.ds(start(hot[c, h]), B)].astype(bf16)
            block = hot[r, h]

            @pl.when(block // 2 == i)
            def _(h=h, block=block):
                row_ref[h] = out_ref[pl.ds(start(block % 2), B), :].astype(bf16)

    return kernel


def finish(ids, hot, part, ham, slabs, second):
    out_specs, out_shape = rows, shape((T, T), f32)
    if not second:
        out_specs = [
            rows,
            pl.BlockSpec((2, B, T), lambda i, *_: (0, 0, 0)),
            pl.BlockSpec((2, R, B), lambda i, *_: (0, i, 0)),
        ]
        out_shape = (out_shape,) + pack_shapes
    return call(
        finish_kernel(second),
        (ids, hot),
        (T // R,),
        [rows, pl.BlockSpec((R, 1024), lambda i, *_: (i, 1))] + [slab] * 8,
        out_specs,
        out_shape,
        (part, ham, *slabs),
        flops=2 * T * T * 1024,
        moved=8 << 20,
        room=24,
    )


def spread(pieces):
    count = len(pieces)

    def kernel(*refs):
        out_ref = refs[count]
        copy_all(
            [(refs[n], out_ref.at[j, n]) for j in range(4) for n in range(count)], refs[-1]
        )

    return call(
        kernel,
        (),
        (1,),
        [anywhere] * count,
        anywhere,
        shape((4, count) + pieces[0].shape),
        pieces,
        scratch=[pltpu.SemaphoreType.DMA((4 * count,))],
        moved=256 << 20,
    )


def body(start_vector, ham_blocks, diagonal, lists, counts, hot, sel):
    row_index = lax.axis_index("zl") * 4 + lax.axis_index("x")
    col_index = (lax.axis_index("zh") * 4 + lax.axis_index("y")) * 2 + lax.axis_index("k")
    ids = jnp.stack([row_index, col_index]).astype(jnp.int32)
    dr = lax.dynamic_slice_in_dim(diagonal, row_index * T, T).reshape(T, 1)
    dc = lax.dynamic_slice_in_dim(diagonal, col_index * T, T).reshape(1, T)

    piece = lax.dynamic_slice_in_dim(ham_blocks, col_index * 3, 3).transpose(0, 2, 1)
    piece = permute(piece, mirror)
    row, col = pack(ids, hot, start_vector)
    ham_t = ham = None
    outs = []
    value = start_vector
    for step in range(2):
        first = step == 0
        row, col, piece = barrier(row, col, piece)
        z1 = permute(row, z_xor(1))
        zh = permute(col, zh_flip)
        pieces = [permute(piece, z_xor(n)) for n in (1, 2, 3)] if first else []
        x0 = over_x(ids, sel, row, 0)
        yk0 = over_yk(ids, sel, col, 0)
        if first:
            ham = dense(ids, lists, counts, ham_blocks, False)
        row, z1, zh, x0, yk0, ham, dr, dc, pieces = barrier(
            row, z1, zh, x0, yk0, ham, dr, dc, pieces
        )
        z2 = permute(row, z_xor(2))
        x1 = over_x(ids, sel, z1, 1)
        if first:
            hams = spread([piece] + pieces).reshape(48, B, B)
            hams = lax.all_to_all(hams, "x", 0, 0, tiled=True)
            row, zh, z2, x1, hams = barrier(row, zh, z2, x1, hams)
        else:
            yk1 = over_yk(ids, sel, zh, 1)
            row, z2, x1, yk1 = barrier(row, z2, x1, yk1)
        z3 = permute(row, z_xor(3))
        x2 = over_x(ids, sel, z2, 2)
        if first:
            yk1 = over_yk(ids, sel, zh, 1)
            ham_t = dense(ids, lists, counts, hams, True)
            z3, x2, yk1, ham_t = barrier(z3, x2, yk1, ham_t)
            part = first_products(ham_t, ham, value, dr, dc, yk0, yk1, x0 + x1)
        else:
            part = first_products(ham_t, ham, value, dr, dc, yk0, yk1, x0 + x1, start_vector)
            z3, x2, part = barrier(z3, x2, part)
        x3 = over_x(ids, sel, z3, 3)
        result = finish(ids, hot, part, ham, x2 + x3, not first)
        if first:
            value, row, col = result
            result = value
        outs.append(result)
    return tuple(outs)


def solution(mesh):
    fine = Mesh(mesh.devices.reshape(sizes), axes)
    rows, cols = ("zl", "x"), ("zh", "y", "k")
    in_specs = (P(rows, cols), P(rows, None, None), P(), P(), P(), P(), P())
    out_specs = (P(rows, cols), P(rows, cols))
    return jax.shard_map(body, mesh=fine, in_specs=in_specs, out_specs=out_specs, check_vma=False)
```

time: 285 us -> 334 us (1.17)
  waiting for transfers between devices: 117 us -> 57.3 us
  Pallas kernels: 67.9 us -> 120 us
  local copies, waits for them, and re-layouts: 13.6 us -> 57.1 us
  starting transfers between devices: 83.3 us -> 96.7 us
    pallas_call x11 -> x20, Pallas kernels: 67.9 us -> 120 us  [call(): pl.pallas_call(kernel, grid_spec=pltpu.PrefetchScalarGridSpec(num_scalar_...]
    ppermute x26 -> x36, waiting for transfers between devices: 102 us -> 55.8 us  [permute(): return lax.ppermute(value, axes, pairs)]
    unnamed x55 -> x126, local copies, waits for them, and re-layouts: 8.45 us -> 53.1 us
    ppermute x26 -> x36, starting transfers between devices: 52.5 us -> 70.8 us  [permute(): return lax.ppermute(value, axes, pairs)]
    all_to_all x7 -> x5, waiting for transfers between devices: 14.6 us -> 1.52 us  [the longest x4 1.51 us: over_yk(): return lax.all_to_all(chosen, ('y', 'k'), 0, 0, tiled=True)]
    all_to_all x7 -> x5, starting transfers between devices: 30.9 us -> 25.9 us  [the longest x4 21.6 us: over_yk(): return lax.all_to_all(chosen, ('y', 'k'), 0, 0, tiled=True)]
  transfers between devices with their start and end apart: 33 -> 41, of which waited for: 14 -> 14; matrix products, arithmetic and copies ran while one was open for 2% -> 1% of each run, Pallas kernels for 14% -> 15%
where the time goes in v2:
time: 334 us; the launch traced here: 333 us
  Pallas kernels  120 us (36%)
  starting transfers between devices  96.7 us (29%)
  waiting for transfers between devices  57.3 us (17%)
  local copies, waits for them, and re-layouts  57.1 us (17%)
    pallas_call x20, Pallas kernels, call(): pl.pallas_call(kernel, grid_spec=pltpu.PrefetchScalarGridSpec(num_scalar_...  120 us
    ppermute x36, starting transfers between devices, permute(): return lax.ppermute(value, axes, pairs)  70.8 us
    ppermute x36, waiting for transfers between devices, permute(): return lax.ppermute(value, axes, pairs)  55.8 us
    unnamed x126, local copies, waits for them, and re-layouts  53.1 us
    all_to_all x4, starting transfers between devices, over_yk(): return lax.all_to_all(chosen, ('y', 'k'), 0, 0, tiled=True)  21.6 us
  transfers between devices with their start and end apart: 41, of which 14 were waited for; matrix products, arithmetic and copies ran while one was open for 1% of the time, Pallas kernels for 15%

profile of v2, /device:TPU:8, one launch (start us, length us, event | category | flops | bytes accessed | tf_op | source)
XLA Modules:
  0.0 332.5 jit_solution(1785971983843533095)
XLA Ops:
  1.7 4.8 %collective-permute-start = (bf16[3,128,128]{2,1,0:T(8,128)(2,1)S(1)}, bf16[3,128,128]{2,1,0:T(8,128)(2,1)S(1)}, u32[]{:S(2)}, u32[]{:S(2)}) collective-permute-start(bf16[3,128,128]{2,1,0:T(8,128)(2,1)S(1)} %bitcast.5), channel_id=1, source_target_pairs={{0,0},{1,16},{2,32},{3,48},{4,64},{5,80},{6,96},{7,112},{8,128},{9... | collective-permute-start | bytes 294920 | tf_op jit(solution)/shard_map/ppermute | solution.py:26
  11.7 49.5 %shard_map.88 = bf16[8,768,128]{2,1,0:T(8,128)(2,1)} custom-call(s32[2]{0:T(128)S(1)} %pad_add_fusion.ids, s32[16,16]{1,0:T(8,128)S(1)} %copy-done.12, bf16[2,768,128]{2,1,0:T(8,128)(2,1)} %get-tuple-element.100.slabs_ref), custom_call_target="tpu_custom_call" | custom-call | bytes 268435456 | tf_op jit(solution)/shard_map/pallas_call | solution.py:55
  61.2 6.3 %all-to-all-start = ((bf16[8,768,128]{2,1,0:T(8,128)(2,1)}), bf16[8,768,128]{2,1,0:T(8,128)(2,1)}, u32[]{:S(2)}, u32[]{:S(2)}) async-start(bf16[8,768,128]{2,1,0:T(8,128)(2,1)} %shard_map.88), calls=%async_computation | async-start | bytes 3145728 | tf_op jit(solution)/shard_map/all_to_all | solution.py:155
  67.5 10.0 %collective-permute-start.2 = (bf16[2,768,128]{2,1,0:T(8,128)(2,1)}, bf16[2,768,128]{2,1,0:T(8,128)(2,1)}, u32[]{:S(2)}, u32[]{:S(2)}) collective-permute-start(bf16[2,768,128]{2,1,0:T(8,128)(2,1)} %get-tuple-element.100.slabs_ref), channel_id=1, source_target_pairs={{0,8},{1,9},{2,10},{3,11},{4,12},{5,13},{6,14},{7,15},{8,0},{9,1},... | collective-permute-start | bytes 1179656 | tf_op jit(solution)/shard_map/ppermute | solution.py:26
  83.1 19.7 %shard_map.87 = (bf16[1,128,768]{2,1,0:T(8,128)(2,1)S(1)}, bf16[1,128,768]{2,1,0:T(8,128)(2,1)}, bf16[1,128,768]{2,1,0:T(8,128)(2,1)}, bf16[1,128,768]{2,1,0:T(8,128)(2,1)}) custom-call(s32[2]{0:T(128)S(1)} %pad_add_fusion.ids, s32[16,16]{1,0:T(8,128)S(1)} %copy-done.12, bf16[2,128,768]{2,1,0:T(8,128)(2,1)} %get-tuple-element.116.slabs_ref), custom_call_target="tpu_custom_call" | custom-call | bytes 268435456 | tf_op jit(solution)/shard_map/pallas_call | solution.py:55
  127.0 4.4 %all-to-all-start.1 = ((bf16[48,128,128]{2,1,0:T(8,128)(2,1)}), bf16[48,128,128]{2,1,0:T(8,128)(2,1)}, u32[]{:S(2)}, u32[]{:S(2)}) async-start(bf16[48,128,128]{2,1,0:T(8,128)(2,1)} %bitcast.4), calls=%async_computation.1 | async-start | bytes 3145728 | tf_op jit(solution)/shard_map/all_to_all | solution.py:358
  138.3 2.7 collective-permute-start.11
  142.5 14.3 %collective-permute-done.10.refs_5_ = bf16[1,128,768]{2,1,0:T(8,128)(2,1)S(1)} collective-permute-done((bf16[1,128,768]{2,1,0:T(8,128)(2,1)S(1)}, bf16[1,128,768]{2,1,0:T(8,128)(2,1)S(1)}, u32[]{:S(2)}, u32[]{:S(2)}) %collective-permute-start.10) | collective-permute-done | bytes 196640 | tf_op jit(solution)/shard_map/ppermute | solution.py:26
  164.9 4.9 %all-to-all-start.2 = ((bf16[8,768,128]{2,1,0:T(8,128)(2,1)}), bf16[8,768,128]{2,1,0:T(8,128)(2,1)}, u32[]{:S(2)}, u32[]{:S(2)}) async-start(bf16[8,768,128]{2,1,0:T(8,128)(2,1)} %copy-done.7), calls=%async_computation.2 | async-start | bytes 3145728 | tf_op jit(solution)/shard_map/all_to_all | solution.py:155
  169.8 3.2 collective-permute-start.13
  182.3 3.9 %shard_map.94.ham_t_ref = bf16[2048,768]{1,0:T(8,128)(2,1)S(1)} custom-call(s32[2]{0:T(128)S(1)} %pad_add_fusion.ids, s32[3,16,64]{2,1,0:T(8,128)S(1)} %copy-done.59, s32[16]{0:T(128)S(1)} %copy-done.61, bf16[48,128,128]{2,1,0:T(8,128)(2,1)} %all-to-all-done.1.ham_ref), custom_call_target="tpu_custom_call" | custom-call | flops 4194304 | bytes 5242880 | tf_op jit(solution)/shard_map/pallas_call | solution.py:55
  204.3 5.8 %shard_map.95.part_ref = f32[768,768]{1,0:T(8,128)S(1)} custom-call(bf16[2048,768]{1,0:T(8,128)(2,1)S(1)} %copy-done.1, bf16[768,2048]{1,0:T(8,128)(2,1)S(1)} %shard_map.89.ham_ref, f32[768,768]{1,0:T(8,128)S(1)} %copy-done.4, f32[768,1]{1,0:T(8,128)S(1)} %copy.15.dr_ref, f32[1,768]{1,0:T(1,128)S(1)} %reshape.14.dc_ref, ...), custom_call_target="tpu_custom_call" | custom-call | flops 3623878656 | bytes 18874368 | tf_op jit(solution)/shard_map/pallas_call | solution.py:55
  210.1 5.1 %shard_map.97 = (f32[768,768]{1,0:T(8,128)}, bf16[2,128,768]{2,1,0:T(8,128)(2,1)}, bf16[2,768,128]{2,1,0:T(8,128)(2,1)}) custom-call(s32[2]{0:T(128)S(1)} %pad_add_fusion.ids, s32[16,2]{1,0:T(8,128)S(1)} %copy-done.48, f32[768,768]{1,0:T(8,128)S(1)} %shard_map.95.part_ref, bf16[768,2048]{1,0:T(8,128)(2,1)S(1)} %shard_map.89.ham_ref, ...), custom_call_target="tpu_custom_call" | custom-call | flops 1207959552 | bytes 8388608 | tf_op jit(solution)/shard_map/pallas_call | solution.py:55
  218.8 5.6 %all-to-all-start.3 = ((bf16[8,768,128]{2,1,0:T(8,128)(2,1)}), bf16[8,768,128]{2,1,0:T(8,128)(2,1)}, u32[]{:S(2)}, u32[]{:S(2)}) async-start(bf16[8,768,128]{2,1,0:T(8,128)(2,1)} %copy-done.6), calls=%async_computation.3 | async-start | bytes 3145728 | tf_op jit(solution)/shard_map/all_to_all | solution.py:155
  224.3 4.0 %collective-permute-start.21 = (bf16[2,768,128]{2,1,0:T(8,128)(2,1)}, bf16[2,768,128]{2,1,0:T(8,128)(2,1)S(1)}, u32[]{:S(2)}, u32[]{:S(2)}) collective-permute-start(bf16[2,768,128]{2,1,0:T(8,128)(2,1)} %get-tuple-element.151.slabs_ref), channel_id=1, source_target_pairs={{0,8},{1,9},{2,10},{3,11},{4,12},{5,13},{6,14},{7,15},{8,0},{9,1},... | collective-permute-start | bytes 1179656 | tf_op jit(solution)/shard_map/ppermute | solution.py:26
  237.4 6.9 %collective-permute-done.22.refs_1_ = bf16[1,128,768]{2,1,0:T(8,128)(2,1)S(1)} collective-permute-done((bf16[1,128,768]{2,1,0:T(8,128)(2,1)S(1)}, bf16[1,128,768]{2,1,0:T(8,128)(2,1)S(1)}, u32[]{:S(2)}, u32[]{:S(2)}) %collective-permute-start.22) | collective-permute-done | bytes 196640 | tf_op jit(solution)/shard_map/ppermute | solution.py:26
  247.1 8.6 %collective-permute-done.20.slabs_ref = bf16[2,128,768]{2,1,0:T(8,128)(2,1)S(1)} collective-permute-done((bf16[2,128,768]{2,1,0:T(8,128)(2,1)}, bf16[2,128,768]{2,1,0:T(8,128)(2,1)S(1)}, u32[]{:S(2)}, u32[]{:S(2)}) %collective-permute-start.20) | collective-permute-done | bytes 393248 | tf_op jit(solution)/shard_map/ppermute | solution.py:26
  256.7 2.8 shard_map.101
  260.7 4.8 %all-to-all-start.4 = ((bf16[8,768,128]{2,1,0:T(8,128)(2,1)}), bf16[8,768,128]{2,1,0:T(8,128)(2,1)}, u32[]{:S(2)}, u32[]{:S(2)}) async-start(bf16[8,768,128]{2,1,0:T(8,128)(2,1)} %copy-done.8), calls=%async_computation.4 | async-start | bytes 3145728 | tf_op jit(solution)/shard_map/all_to_all | solution.py:155
  272.8 7.8 %collective-permute-done.26.refs_5_ = bf16[1,128,768]{2,1,0:T(8,128)(2,1)S(1)} collective-permute-done((bf16[1,128,768]{2,1,0:T(8,128)(2,1)S(1)}, bf16[1,128,768]{2,1,0:T(8,128)(2,1)S(1)}, u32[]{:S(2)}, u32[]{:S(2)}) %collective-permute-start.26) | collective-permute-done | bytes 196640 | tf_op jit(solution)/shard_map/ppermute | solution.py:26
  282.7 3.5 %collective-permute-done.25.slabs_ref = bf16[2,128,768]{2,1,0:T(8,128)(2,1)S(1)} collective-permute-done((bf16[2,128,768]{2,1,0:T(8,128)(2,1)}, bf16[2,128,768]{2,1,0:T(8,128)(2,1)S(1)}, u32[]{:S(2)}, u32[]{:S(2)}) %collective-permute-start.25) | collective-permute-done | bytes 393248 | tf_op jit(solution)/shard_map/ppermute | solution.py:26
  309.3 5.6 %shard_map.103.part_ref = f32[768,768]{1,0:T(8,128)S(1)} custom-call(bf16[2048,768]{1,0:T(8,128)(2,1)S(1)} %copy-done.2, bf16[768,2048]{1,0:T(8,128)(2,1)S(1)} %shard_map.89.ham_ref, f32[768,768]{1,0:T(8,128)S(1)} %copy-done.10, f32[768,1]{1,0:T(8,128)S(1)} %copy.17.dr_ref, f32[1,768]{1,0:T(1,128)S(1)} %reshape.14.dc_ref, ...), custom_call_target="tpu_custom_call" | custom-call | flops 3623878656 | bytes 18874368 | tf_op jit(solution)/shard_map/pallas_call | solution.py:55
  321.3 6.9 %collective-permute-done.33.refs_5_ = bf16[1,128,768]{2,1,0:T(8,128)(2,1)S(1)} collective-permute-done((bf16[1,128,768]{2,1,0:T(8,128)(2,1)S(1)}, bf16[1,128,768]{2,1,0:T(8,128)(2,1)S(1)}, u32[]{:S(2)}, u32[]{:S(2)}) %collective-permute-start.33) | collective-permute-done | bytes 196640 | tf_op jit(solution)/shard_map/ppermute | solution.py:26
  328.8 3.7 %shard_map.105 = f32[768,768]{1,0:T(8,128)} custom-call(s32[2]{0:T(128)S(1)} %pad_add_fusion.ids, s32[16,2]{1,0:T(8,128)S(1)} %copy-done.49, f32[768,768]{1,0:T(8,128)S(1)} %shard_map.103.part_ref, bf16[768,2048]{1,0:T(8,128)(2,1)S(1)} %shard_map.89.ham_ref, bf16[1,128,768]{2,1,0:T(8,128)(2,1)S(1)} %get-tuple-element.183.refs_0_, ...), custom_call_target="tpu_custom_call" | custom-call | flops 1207959552 | bytes 8388608 | tf_op jit(solution)/shard_map/pallas_call | solution.py:55
  (211 shorter events, 136.5 us)
Async XLA Ops:
  61.2 58.8 %all-to-all-start = ((bf16[8,768,128]{2,1,0:T(8,128)(2,1)}), bf16[8,768,128]{2,1,0:T(8,128)(2,1)}, u32[]{:S(2)}, u32[]{:S(2)}) async-start(bf16[8,768,128]{2,1,0:T(8,128)(2,1)} %shard_map.88), calls=%async_computation | async-start | bytes 3145728 | tf_op jit(solution)/shard_map/all_to_all | solution.py:155
  67.5 52.6 %collective-permute-start.2 = (bf16[2,768,128]{2,1,0:T(8,128)(2,1)}, bf16[2,768,128]{2,1,0:T(8,128)(2,1)}, u32[]{:S(2)}, u32[]{:S(2)}) collective-permute-start(bf16[2,768,128]{2,1,0:T(8,128)(2,1)} %get-tuple-element.100.slabs_ref), channel_id=1, source_target_pairs={{0,8},{1,9},{2,10},{3,11},{4,12},{5,13},{6,14},{7,15},{8,0},{9,1},... | collective-permute-start | bytes 1179656 | tf_op jit(solution)/shard_map/ppermute | solution.py:26
  77.5 42.6 %collective-permute-start.1 = (bf16[2,128,768]{2,1,0:T(8,128)(2,1)}, bf16[2,128,768]{2,1,0:T(8,128)(2,1)S(1)}, u32[]{:S(2)}, u32[]{:S(2)}) collective-permute-start(bf16[2,128,768]{2,1,0:T(8,128)(2,1)} %get-tuple-element.116.slabs_ref), channel_id=1, source_target_pairs={{0,64},{1,65},{2,66},{3,67},{4,68},{5,69},{6,70},{7,71},{8,72},{9,... | collective-permute-start | bytes 1179656 | tf_op jit(solution)/shard_map/ppermute | solution.py:26
  78.7 27.1 %collective-permute-start.8 = (bf16[3,128,128]{2,1,0:T(8,128)(2,1)}, bf16[3,128,128]{2,1,0:T(8,128)(2,1)S(1)}, u32[]{:S(2)}, u32[]{:S(2)}) collective-permute-start(bf16[3,128,128]{2,1,0:T(8,128)(2,1)} %copy-done.50), channel_id=1, source_target_pairs={{0,192},{1,193},{2,194},{3,195},{4,196},{5,197},{6,198},{7,199},{8... | collective-permute-start | bytes 294920 | tf_op jit(solution)/shard_map/ppermute | solution.py:26
  78.7 29.2 %collective-permute-start.7 = (bf16[3,128,128]{2,1,0:T(8,128)(2,1)}, bf16[3,128,128]{2,1,0:T(8,128)(2,1)S(1)}, u32[]{:S(2)}, u32[]{:S(2)}) collective-permute-start(bf16[3,128,128]{2,1,0:T(8,128)(2,1)} %copy-done.50), channel_id=1, source_target_pairs={{0,128},{1,129},{2,130},{3,131},{4,132},{5,133},{6,134},{7,135},{8... | collective-permute-start | bytes 294920 | tf_op jit(solution)/shard_map/ppermute | solution.py:26
  81.0 30.1 %collective-permute-start.6 = (bf16[3,128,128]{2,1,0:T(8,128)(2,1)}, bf16[3,128,128]{2,1,0:T(8,128)(2,1)S(1)}, u32[]{:S(2)}, u32[]{:S(2)}) collective-permute-start(bf16[3,128,128]{2,1,0:T(8,128)(2,1)} %copy-done.50), channel_id=1, source_target_pairs={{0,64},{1,65},{2,66},{3,67},{4,68},{5,69},{6,70},{7,71},{8,72},{9,... | collective-permute-start | bytes 294920 | tf_op jit(solution)/shard_map/ppermute | solution.py:26
  127.0 34.4 %all-to-all-start.1 = ((bf16[48,128,128]{2,1,0:T(8,128)(2,1)}), bf16[48,128,128]{2,1,0:T(8,128)(2,1)}, u32[]{:S(2)}, u32[]{:S(2)}) async-start(bf16[48,128,128]{2,1,0:T(8,128)(2,1)} %bitcast.4), calls=%async_computation.1 | async-start | bytes 3145728 | tf_op jit(solution)/shard_map/all_to_all | solution.py:358
  131.3 29.2 %collective-permute-start.9 = (bf16[2,128,768]{2,1,0:T(8,128)(2,1)}, bf16[2,128,768]{2,1,0:T(8,128)(2,1)S(1)}, u32[]{:S(2)}, u32[]{:S(2)}) collective-permute-start(bf16[2,128,768]{2,1,0:T(8,128)(2,1)} %get-tuple-element.116.slabs_ref), channel_id=1, source_target_pairs={{0,128},{1,129},{2,130},{3,131},{4,132},{5,133},{6,134},{7,135},{8... | collective-permute-start | bytes 1179656 | tf_op jit(solution)/shard_map/ppermute | solution.py:26
  136.4 20.3 %collective-permute-start.10 = (bf16[1,128,768]{2,1,0:T(8,128)(2,1)S(1)}, bf16[1,128,768]{2,1,0:T(8,128)(2,1)S(1)}, u32[]{:S(2)}, u32[]{:S(2)}) collective-permute-start(bf16[1,128,768]{2,1,0:T(8,128)(2,1)S(1)} %get-tuple-element.110), channel_id=1, source_target_pairs={{0,16},{1,17},{2,18},{3,19},{4,20},{5,21},{6,22},{7,23},{8,24},{9,... | collective-permute-start | bytes 589832 | tf_op jit(solution)/shard_map/ppermute | solution.py:26
  138.3 20.9 %collective-permute-start.11 = (bf16[1,128,768]{2,1,0:T(8,128)(2,1)S(1)}, bf16[1,128,768]{2,1,0:T(8,128)(2,1)S(1)}, u32[]{:S(2)}, u32[]{:S(2)}) collective-permute-start(bf16[1,128,768]{2,1,0:T(8,128)(2,1)S(1)} %get-tuple-element.111), channel_id=1, source_target_pairs={{0,32},{1,33},{2,34},{3,35},{4,36},{5,37},{6,38},{7,39},{8,40},{9,... | collective-permute-start | bytes 589832 | tf_op jit(solution)/shard_map/ppermute | solution.py:26
  141.0 18.9 %collective-permute-start.12 = (bf16[1,128,768]{2,1,0:T(8,128)(2,1)S(1)}, bf16[1,128,768]{2,1,0:T(8,128)(2,1)S(1)}, u32[]{:S(2)}, u32[]{:S(2)}) collective-permute-start(bf16[1,128,768]{2,1,0:T(8,128)(2,1)S(1)} %get-tuple-element.112), channel_id=1, source_target_pairs={{0,48},{1,49},{2,50},{3,51},{4,52},{5,53},{6,54},{7,55},{8,56},{9,... | collective-permute-start | bytes 589832 | tf_op jit(solution)/shard_map/ppermute | solution.py:26
  164.9 25.2 %all-to-all-start.2 = ((bf16[8,768,128]{2,1,0:T(8,128)(2,1)}), bf16[8,768,128]{2,1,0:T(8,128)(2,1)}, u32[]{:S(2)}, u32[]{:S(2)}) async-start(bf16[8,768,128]{2,1,0:T(8,128)(2,1)} %copy-done.7), calls=%async_computation.2 | async-start | bytes 3145728 | tf_op jit(solution)/shard_map/all_to_all | solution.py:155
  169.8 18.8 %collective-permute-start.13 = (bf16[2,128,768]{2,1,0:T(8,128)(2,1)}, bf16[2,128,768]{2,1,0:T(8,128)(2,1)}, u32[]{:S(2)}, u32[]{:S(2)}) collective-permute-start(bf16[2,128,768]{2,1,0:T(8,128)(2,1)} %get-tuple-element.116.slabs_ref), channel_id=1, source_target_pairs={{0,192},{1,193},{2,194},{3,195},{4,196},{5,197},{6,198},{7,199},{8... | collective-permute-start | bytes 1179656 | tf_op jit(solution)/shard_map/ppermute | solution.py:26
  192.0 18.0 %collective-permute-start.17 = (bf16[1,128,768]{2,1,0:T(8,128)(2,1)S(1)}, bf16[1,128,768]{2,1,0:T(8,128)(2,1)S(1)}, u32[]{:S(2)}, u32[]{:S(2)}) collective-permute-start(bf16[1,128,768]{2,1,0:T(8,128)(2,1)S(1)} %get-tuple-element.144), channel_id=1, source_target_pairs={{0,16},{1,17},{2,18},{3,19},{4,20},{5,21},{6,22},{7,23},{8,24},{9,... | collective-permute-start | bytes 589832 | tf_op jit(solution)/shard_map/ppermute | solution.py:26
  192.1 18.0 %collective-permute-start.18 = (bf16[1,128,768]{2,1,0:T(8,128)(2,1)S(1)}, bf16[1,128,768]{2,1,0:T(8,128)(2,1)S(1)}, u32[]{:S(2)}, u32[]{:S(2)}) collective-permute-start(bf16[1,128,768]{2,1,0:T(8,128)(2,1)S(1)} %get-tuple-element.145), channel_id=1, source_target_pairs={{0,32},{1,33},{2,34},{3,35},{4,36},{5,37},{6,38},{7,39},{8,40},{9,... | collective-permute-start | bytes 589832 | tf_op jit(solution)/shard_map/ppermute | solution.py:26
  218.8 37.0 %all-to-all-start.3 = ((bf16[8,768,128]{2,1,0:T(8,128)(2,1)}), bf16[8,768,128]{2,1,0:T(8,128)(2,1)}, u32[]{:S(2)}, u32[]{:S(2)}) async-start(bf16[8,768,128]{2,1,0:T(8,128)(2,1)} %copy-done.6), calls=%async_computation.3 | async-start | bytes 3145728 | tf_op jit(solution)/shard_map/all_to_all | solution.py:155
  224.3 22.0 %collective-permute-start.21 = (bf16[2,768,128]{2,1,0:T(8,128)(2,1)}, bf16[2,768,128]{2,1,0:T(8,128)(2,1)S(1)}, u32[]{:S(2)}, u32[]{:S(2)}) collective-permute-start(bf16[2,768,128]{2,1,0:T(8,128)(2,1)} %get-tuple-element.151.slabs_ref), channel_id=1, source_target_pairs={{0,8},{1,9},{2,10},{3,11},{4,12},{5,13},{6,14},{7,15},{8,0},{9,1},... | collective-permute-start | bytes 1179656 | tf_op jit(solution)/shard_map/ppermute | solution.py:26
  228.4 27.4 %collective-permute-start.20 = (bf16[2,128,768]{2,1,0:T(8,128)(2,1)}, bf16[2,128,768]{2,1,0:T(8,128)(2,1)S(1)}, u32[]{:S(2)}, u32[]{:S(2)}) collective-permute-start(bf16[2,128,768]{2,1,0:T(8,128)(2,1)} %get-tuple-element.163.slabs_ref), channel_id=1, source_target_pairs={{0,64},{1,65},{2,66},{3,67},{4,68},{5,69},{6,70},{7,71},{8,72},{9,... | collective-permute-start | bytes 1179656 | tf_op jit(solution)/shard_map/ppermute | solution.py:26
  260.7 26.3 %all-to-all-start.4 = ((bf16[8,768,128]{2,1,0:T(8,128)(2,1)}), bf16[8,768,128]{2,1,0:T(8,128)(2,1)}, u32[]{:S(2)}, u32[]{:S(2)}) async-start(bf16[8,768,128]{2,1,0:T(8,128)(2,1)} %copy-done.8), calls=%async_computation.4 | async-start | bytes 3145728 | tf_op jit(solution)/shard_map/all_to_all | solution.py:155
  265.5 20.7 %collective-permute-start.25 = (bf16[2,128,768]{2,1,0:T(8,128)(2,1)}, bf16[2,128,768]{2,1,0:T(8,128)(2,1)S(1)}, u32[]{:S(2)}, u32[]{:S(2)}) collective-permute-start(bf16[2,128,768]{2,1,0:T(8,128)(2,1)} %get-tuple-element.163.slabs_ref), channel_id=1, source_target_pairs={{0,128},{1,129},{2,130},{3,131},{4,132},{5,133},{6,134},{7,135},{8... | collective-permute-start | bytes 1179656 | tf_op jit(solution)/shard_map/ppermute | solution.py:26
  287.0 27.9 %collective-permute-start.29 = (bf16[2,128,768]{2,1,0:T(8,128)(2,1)}, bf16[2,128,768]{2,1,0:T(8,128)(2,1)}, u32[]{:S(2)}, u32[]{:S(2)}) collective-permute-start(bf16[2,128,768]{2,1,0:T(8,128)(2,1)} %get-tuple-element.163.slabs_ref), channel_id=1, source_target_pairs={{0,192},{1,193},{2,194},{3,195},{4,196},{5,197},{6,198},{7,199},{8... | collective-permute-start | bytes 1179656 | tf_op jit(solution)/shard_map/ppermute | solution.py:26
  291.9 23.1 %collective-permute-start.30 = (bf16[1,128,768]{2,1,0:T(8,128)(2,1)S(1)}, bf16[1,128,768]{2,1,0:T(8,128)(2,1)S(1)}, u32[]{:S(2)}, u32[]{:S(2)}) collective-permute-start(bf16[1,128,768]{2,1,0:T(8,128)(2,1)S(1)} %get-tuple-element.166), channel_id=1, source_target_pairs={{0,16},{1,17},{2,18},{3,19},{4,20},{5,21},{6,22},{7,23},{8,24},{9,... | collective-permute-start | bytes 589832 | tf_op jit(solution)/shard_map/ppermute | solution.py:26
  292.2 22.8 %collective-permute-start.31 = (bf16[1,128,768]{2,1,0:T(8,128)(2,1)S(1)}, bf16[1,128,768]{2,1,0:T(8,128)(2,1)S(1)}, u32[]{:S(2)}, u32[]{:S(2)}) collective-permute-start(bf16[1,128,768]{2,1,0:T(8,128)(2,1)S(1)} %get-tuple-element.167), channel_id=1, source_target_pairs={{0,32},{1,33},{2,34},{3,35},{4,36},{5,37},{6,38},{7,39},{8,40},{9,... | collective-permute-start | bytes 589832 | tf_op jit(solution)/shard_map/ppermute | solution.py:26
  294.1 20.8 %collective-permute-start.32 = (bf16[1,128,768]{2,1,0:T(8,128)(2,1)S(1)}, bf16[1,128,768]{2,1,0:T(8,128)(2,1)S(1)}, u32[]{:S(2)}, u32[]{:S(2)}) collective-permute-start(bf16[1,128,768]{2,1,0:T(8,128)(2,1)S(1)} %get-tuple-element.168), channel_id=1, source_target_pairs={{0,48},{1,49},{2,50},{3,51},{4,52},{5,53},{6,54},{7,55},{8,56},{9,... | collective-permute-start | bytes 589832 | tf_op jit(solution)/shard_map/ppermute | solution.py:26
  (79 other events, 405.5 us)

commit v3 on v2

v3 whole, which is shorter than its diff:
```python
import jax
import jax.numpy as jnp
from jax import lax
from jax.experimental import pallas as pl
from jax.experimental.pallas import tpu as pltpu
from jax.sharding import Mesh, PartitionSpec as P
import numpy as np

center = 0.25
scale = 1.0 / 2.5
axes = ("zl", "x", "zh", "y", "k")
sizes = (4, 4, 2, 4, 2)
B = 128
T = 768
R = 256
bf16 = jnp.bfloat16
f32 = jnp.float32


def permute(value, target):
    places = list(np.ndindex(*sizes))
    pairs = [
        (int(np.ravel_multi_index(p, sizes)), int(np.ravel_multi_index(target(*p), sizes)))
        for p in places
    ]
    return lax.ppermute(value, axes, pairs)


def z_xor(n):
    return lambda zl, x, zh, y, k: (zl ^ n, x, zh, y, k)


def x_shift(n):
    return lambda zl, x, zh, y, k: (zl, (x + n) % 4, zh, y, k)


def zh_flip(zl, x, zh, y, k):
    return (zl, x, 1 - zh, y, k)


def mirror(zl, x, zh, y, k):
    r, c = zl * 4 + x, zh * 8 + y * 2 + k
    return (c // 4, c % 4, r // 8, (r % 8) // 2, r % 2)


def barrier(*values):
    return lax.optimization_barrier(values)


def start(block):
    return pl.multiple_of(block * B, B)


def call(kernel, scalars, grid, in_specs, out_specs, out_shape, args, scratch=(), flops=0, moved=0, room=1, pinned=False):
    return pl.pallas_call(
        kernel,
        grid_spec=pltpu.PrefetchScalarGridSpec(
            num_scalar_prefetch=len(scalars),
            grid=grid,
            in_specs=in_specs,
            out_specs=out_specs,
            scratch_shapes=list(scratch),
        ),
        out_shape=out_shape,
        compiler_params=pltpu.CompilerParams(vmem_limit_bytes=room << 20),
        cost_estimate=pl.CostEstimate(flops=flops, bytes_accessed=moved, transcendentals=0),
    )(*scalars, *(pltpu.with_memory_space_constraint(arg, pltpu.HBM) if pinned else arg for arg in args))


def shape(dims, kind=bf16):
    return pltpu.HBM(dims, kind)


def free_shape(dims, kind=bf16):
    return jax.ShapeDtypeStruct(dims, kind)


def whole(dims):
    return pl.BlockSpec(dims, lambda i, *_: (0,) * len(dims))


send_shapes = (
    [shape((2, B, T)), shape((2, T, B))] + [shape((1, B, T))] * 4 + [shape((8, T, B))]
)


def choose_rows(ids, sel, step, slabs_ref, refs):
    zl, x = ids[0] // 4, ids[0] % 4
    for n in range(4):
        refs[n][0] = slabs_ref[sel[zl * 4 + (x + n) % 4, (zl ^ step) * 4 + x]]


def choose_cols(ids, sel, flip, slabs_ref, out_ref, stride=1, offset=0):
    zh, q = ids[1] // 8, ids[1] ^ (8 * flip)
    for i in range(8):
        out_ref[i * stride + offset] = slabs_ref[sel[zh * 8 + i, q]]


def pack_kernel(ids, hot, sel, x_ref, row_ref, col_ref, *refs):
    r, c = ids[0], ids[1]
    for h in range(2):
        row_ref[h] = x_ref[pl.ds(start(hot[r, h]), B), :].astype(bf16)
        col_ref[h] = x_ref[:, pl.ds(start(hot[c, h]), B)].astype(bf16)
    choose_rows(ids, sel, 0, row_ref, refs[:4])
    choose_cols(ids, sel, 0, col_ref, refs[4])


def pack(ids, hot, sel, value):
    return call(
        pack_kernel,
        (ids, hot, sel),
        (1,),
        [whole((T, T))],
        [whole(s.shape) for s in send_shapes],
        send_shapes,
        (value,),
        moved=5 << 20,
        room=32,
    )


def next_slabs(ids, sel, rows, step, *cols):
    def kernel(ids, sel, *refs):
        outs = refs[1 + len(cols) :]
        choose_rows(ids, sel, step, refs[0], outs[:4])
        if len(cols) == 1:
            choose_cols(ids, sel, 1, refs[1], outs[4])
        if len(cols) == 2:
            choose_cols(ids, sel, 0, refs[1], outs[4], 2, 0)
            choose_cols(ids, sel, 1, refs[2], outs[4], 2, 1)

    out_shapes = send_shapes[2:6] + [shape((8 * len(cols), T, B))] * (len(cols) > 0)
    args = (rows, *cols)
    return call(
        kernel,
        (ids, sel),
        (1,),
        [whole(arg.shape) for arg in args],
        [whole(s.shape) for s in out_shapes],
        out_shapes,
        args,
        moved=4 << 20,
        room=32,
    )


def over_x(chosen):
    return [chosen[0]] + [permute(chosen[n], x_shift(n)) for n in (1, 2, 3)]


def over_yk(chosen):
    return lax.all_to_all(chosen, ("y", "k"), 0, 0, tiled=True)


def dense_kernel(mirrored):
    def kernel(ids, lists, counts, ham_ref, out_ref, total):
        r, c = ids[0], ids[1]
        tile = c if mirrored else r
        zl = r // 4

        def clear(i, carry):
            total[i] = jnp.zeros((B, B), f32)
            return carry

        lax.fori_loop(0, 96, clear, 0)

        def add(slot, carry):
            q = lists[0, tile, slot]
            t = lists[1, tile, slot]
            b = lists[2, tile, slot]
            if mirrored:
                place = q ^ (c // 8 * 8)
                piece = b // 3
                b = ((piece % 4) * 4 + ((piece // 4) ^ zl)) * 3 + b % 3
            else:
                place = ((q // 4) ^ zl) * 4 + (r + 4 - q % 4) % 4
            at = t * 16 + place
            total[at] = total[at] + ham_ref[b].astype(f32)
            return carry

        lax.fori_loop(0, counts[tile], add, 0)
        for t in range(6):
            for place in range(16):
                block = total[t * 16 + place].astype(bf16)
                if mirrored:
                    out_ref[place * B : (place + 1) * B, t * B : (t + 1) * B] = block
                else:
                    out_ref[t * B : (t + 1) * B, place * B : (place + 1) * B] = block

    return kernel


def dense(ids, lists, counts, hams, mirrored):
    dims = (2048, T) if mirrored else (T, 2048)
    return call(
        dense_kernel(mirrored),
        (ids, lists, counts),
        (1,),
        [pl.BlockSpec((48, B, B), lambda i, *_: (0, 0, 0))],
        pl.BlockSpec(dims, lambda i, *_: (0, 0)),
        shape(dims),
        (hams,),
        scratch=[pltpu.VMEM((96, B, B), f32)],
        flops=1 << 22,
        moved=5 << 20,
        room=28,
    )


def first_products_kernel(second, arrays):
    def kernel(ham_t_ref, ham_ref, x_ref, dr_ref, dc_ref, *refs):
        slabs, out_ref, wide = refs[:8], refs[-2], refs[-1]
        yk = refs[8 : 8 + arrays]
        for i in range(8):
            wide[:, i * B : (i + 1) * B] = yk[0][i] if arrays == 2 else yk[0][2 * i]
            wide[:, (8 + i) * B : (9 + i) * B] = yk[1][i] if arrays == 2 else yk[0][2 * i + 1]
        stacked = jnp.concatenate([slab[0] for slab in slabs], axis=0)
        total = jnp.dot(wide[...], ham_t_ref[...], preferred_element_type=f32) + jnp.dot(
            ham_ref[...], stacked, preferred_element_type=f32
        )
        total = total + (dr_ref[...] + dc_ref[...] - center) * x_ref[...]
        if second:
            total = total - refs[8 + arrays][...] * (0.5 / scale)
        out_ref[...] = total

    return kernel


rows = pl.BlockSpec((R, T), lambda i, *_: (i, 0))
slab = pl.BlockSpec((1, B, T), lambda i, *_: (0, 0, 0))


def first_products(ham_t, ham, value, dr, dc, yk, slabs, before=None):
    extra = () if before is None else (before,)
    return call(
        first_products_kernel(before is not None, len(yk)),
        (),
        (T // R,),
        [
            pl.BlockSpec((2048, T), lambda i, *_: (0, 0)),
            pl.BlockSpec((R, 1024), lambda i, *_: (i, 0)),
            rows,
            pl.BlockSpec((R, 1), lambda i, *_: (i, 0)),
            pl.BlockSpec((1, T), lambda i, *_: (0, 0)),
        ]
        + [slab] * 8
        + [pl.BlockSpec((a.shape[0], R, B), lambda i, *_: (0, i, 0)) for a in yk]
        + [rows] * len(extra),
        rows,
        free_shape((T, T), f32),
        (ham_t, ham, value, dr, dc, *slabs, *yk, *extra),
        scratch=[pltpu.VMEM((R, 2048), bf16)],
        flops=2 * T * T * 3072,
        moved=18 << 20,
        room=32,
        pinned=True,
    )


def finish_kernel(second):
    def kernel(ids, hot, sel, part_ref, ham_ref, *refs):
        stacked = jnp.concatenate([ref[0] for ref in refs[:8]], axis=0)
        out_ref = refs[8]
        total = part_ref[...] + jnp.dot(ham_ref[...], stacked, preferred_element_type=f32)
        if second:
            out_ref[...] = total * (2.0 * scale)
            return
        row_ref, col_ref = refs[9:11]
        out_ref[...] = total * scale
        i, r, c = pl.program_id(0), ids[0], ids[1]
        for h in range(2):
            col_ref[h] = out_ref[:, pl.ds(start(hot[c, h]), B)].astype(bf16)
            block = hot[r, h]

            @pl.when(block // 2 == i)
            def _(h=h, block=block):
                row_ref[h] = out_ref[pl.ds(start(block % 2), B), :].astype(bf16)

        @pl.when(i == T // R - 1)
        def _():
            choose_rows(ids, sel, 0, row_ref, refs[11:15])

    return kernel


def finish(ids, hot, sel, part, ham, slabs, second):
    out_specs, out_shape = rows, shape((T, T), f32)
    if not second:
        out_specs = [rows, whole((2, B, T)), pl.BlockSpec((2, R, B), lambda i, *_: (0, i, 0))]
        out_specs += [whole((1, B, T))] * 4
        out_shape = [out_shape] + send_shapes[:6]
    return call(
        finish_kernel(second),
        (ids, hot, sel),
        (T // R,),
        [rows, pl.BlockSpec((R, 1024), lambda i, *_: (i, 1))] + [slab] * 8,
        out_specs,
        out_shape,
        (part, ham, *slabs),
        flops=2 * T * T * 1024,
        moved=8 << 20,
        room=32,
    )


def spread(pieces):
    def kernel(*refs):
        for n in range(4):
            refs[4][0, n] = refs[n][...]

    dims = pieces[0].shape
    return call(
        kernel,
        (),
        (4,),
        [whole(dims)] * 4,
        pl.BlockSpec((1, 4) + dims, lambda i: (i, 0, 0, 0, 0)),
        shape((4, 4) + dims),
        pieces,
        moved=4 << 20,
        room=16,
    )


def body(start_vector, ham_blocks, diagonal, lists, counts, hot, sel):
    row_index = lax.axis_index("zl") * 4 + lax.axis_index("x")
    col_index = (lax.axis_index("zh") * 4 + lax.axis_index("y")) * 2 + lax.axis_index("k")
    ids = jnp.stack([row_index, col_index]).astype(jnp.int32)
    dr = lax.dynamic_slice_in_dim(diagonal, row_index * T, T).reshape(T, 1)
    dc = lax.dynamic_slice_in_dim(diagonal, col_index * T, T).reshape(1, T)

    piece = lax.dynamic_slice_in_dim(ham_blocks, col_index * 3, 3).transpose(0, 2, 1)
    piece = permute(piece, mirror)
    row, col, *sends = pack(ids, hot, sel, start_vector)
    ham_t = ham = None
    outs = []
    value = start_vector
    for step in range(2):
        first = step == 0
        row, col, sends, piece = barrier(row, col, sends, piece)
        z1 = permute(row, z_xor(1))
        zh = permute(col, zh_flip)
        x0 = over_x(sends[:4])
        if first:
            pieces = [piece] + [permute(piece, z_xor(n)) for n in (1, 2, 3)]
            yk0 = over_yk(sends[4])
            sends = next_slabs(ids, sel, z1, 1, zh)
            ham = dense(ids, lists, counts, ham_blocks, False)
            hams = spread(pieces)
            row, sends, x0, yk0, ham, dr, dc, hams = barrier(
                row, sends, x0, yk0, ham, dr, dc, hams
            )
        else:
            sends = next_slabs(ids, sel, z1, 1, col, zh)
            row, sends, x0 = barrier(row, sends, x0)
        z2 = permute(row, z_xor(2))
        x1 = over_x(sends[:4])
        later = sends[4]
        sends = next_slabs(ids, sel, z2, 2)
        if first:
            hams = lax.all_to_all(hams.reshape(48, B, B), "x", 0, 0, tiled=True)
            row, sends, x1, hams, later = barrier(row, sends, x1, hams, later)
            yk = [yk0, over_yk(later)]
        else:
            yk = [over_yk(later)]
            row, sends, x1 = barrier(row, sends, x1)
        z3 = permute(row, z_xor(3))
        x2 = over_x(sends)
        sends = next_slabs(ids, sel, z3, 3)
        if first:
            ham_t = dense(ids, lists, counts, hams, True)
        sends, x2, yk, ham_t = barrier(sends, x2, yk, ham_t)
        x3 = over_x(sends)
        before = () if first else (start_vector,)
        part = first_products(ham_t, ham, value, dr, dc, yk, x0 + x1, *before)
        result = finish(ids, hot, sel, part, ham, x2 + x3, not first)
        if first:
            value, row, col, *sends = result
            result = value
        outs.append(result)
    return tuple(outs)


def solution(mesh):
    fine = Mesh(mesh.devices.reshape(sizes), axes)
    rows, cols = ("zl", "x"), ("zh", "y", "k")
    in_specs = (P(rows, cols), P(rows, None, None), P(), P(), P(), P(), P())
    out_specs = (P(rows, cols), P(rows, cols))
    return jax.shard_map(body, mesh=fine, in_specs=in_specs, out_specs=out_specs, check_vma=False)
```

time: 334 us -> 246 us (0.74)
  Pallas kernels: 120 us -> 49.5 us
  local copies, waits for them, and re-layouts: 57.1 us -> 9.06 us
  waiting for transfers between devices: 57.3 us -> 95 us
  starting transfers between devices: 96.7 us -> 87.3 us
    pallas_call x20 -> x14, Pallas kernels: 120 us -> 49.5 us  [call(): pl.pallas_call(kernel, grid_spec=pltpu.PrefetchScalarGridSpec(num_scalar_...]
    unnamed x126 -> x76, local copies, waits for them, and re-layouts: 53.1 us -> 5.77 us
    ppermute x36, waiting for transfers between devices: 55.8 us -> 90.4 us  [permute(): return lax.ppermute(value, axes, pairs)]
    all_to_all x4 -> x3, starting transfers between devices: 21.6 us -> 15.8 us  [over_yk(): return lax.all_to_all(chosen, ('y', 'k'), 0, 0, tiled=True)]
  transfers between devices with their start and end apart: 41 -> 40, of which waited for: 14 -> 15; matrix products, arithmetic and copies ran while one was open for 1% -> 1% of each run, Pallas kernels for 15% -> 17%
where the time goes in v3:
time: 246 us; the launch traced here: 242 us
  waiting for transfers between devices  95 us (39%)
  starting transfers between devices  87.3 us (35%)
  Pallas kernels  49.5 us (20%)
  local copies, waits for them, and re-layouts  9.06 us (4%)
    ppermute x36, waiting for transfers between devices, permute(): return lax.ppermute(value, axes, pairs)  90.4 us
    ppermute x36, starting transfers between devices, permute(): return lax.ppermute(value, axes, pairs)  67.8 us
    pallas_call x14, Pallas kernels, call(): pl.pallas_call(kernel, grid_spec=pltpu.PrefetchScalarGridSpec(num_scalar_...  49.5 us
    all_to_all x3, starting transfers between devices, over_yk(): return lax.all_to_all(chosen, ('y', 'k'), 0, 0, tiled=True)  15.8 us
    unnamed x76, local copies, waits for them, and re-layouts  5.77 us
  transfers between devices with their start and end apart: 40, of which 15 were waited for; matrix products, arithmetic and copies ran while one was open for 1% of the time, Pallas kernels for 17%

profile of v3, /device:TPU:8, one launch (start us, length us, event | category | flops | bytes accessed | tf_op | source)
XLA Modules:
  0.0 242.0 jit_solution(4189198106260332585)
XLA Ops:
  1.7 4.8 %collective-permute-start = (bf16[3,128,128]{2,1,0:T(8,128)(2,1)S(1)}, bf16[3,128,128]{2,1,0:T(8,128)(2,1)S(1)}, u32[]{:S(2)}, u32[]{:S(2)}) collective-permute-start(bf16[3,128,128]{2,1,0:T(8,128)(2,1)S(1)} %bitcast.5), channel_id=1, source_target_pairs={{0,0},{1,16},{2,32},{3,48},{4,64},{5,80},{6,96},{7,112},{8,128},{9... | collective-permute-start | bytes 294920 | tf_op jit(solution)/shard_map/ppermute | solution.py:26
  12.3 5.9 %all-to-all-start = ((bf16[8,768,128]{2,1,0:T(8,128)(2,1)}), bf16[8,768,128]{2,1,0:T(8,128)(2,1)}, u32[]{:S(2)}, u32[]{:S(2)}) async-start(bf16[8,768,128]{2,1,0:T(8,128)(2,1)} %get-tuple-element.140), calls=%async_computation | async-start | bytes 3145728 | tf_op jit(solution)/shard_map/all_to_all | solution.py:152
  18.1 9.8 %collective-permute-start.2 = (bf16[2,768,128]{2,1,0:T(8,128)(2,1)}, bf16[2,768,128]{2,1,0:T(8,128)(2,1)S(1)}, u32[]{:S(2)}, u32[]{:S(2)}) collective-permute-start(bf16[2,768,128]{2,1,0:T(8,128)(2,1)} %get-tuple-element.130), channel_id=1, source_target_pairs={{0,8},{1,9},{2,10},{3,11},{4,12},{5,13},{6,14},{7,15},{8,0},{9,1},... | collective-permute-start | bytes 1179656 | tf_op jit(solution)/shard_map/ppermute | solution.py:26
  33.5 22.9 %collective-permute-done.8.refs_3_ = bf16[3,128,128]{2,1,0:T(8,128)(2,1)S(1)} collective-permute-done((bf16[3,128,128]{2,1,0:T(8,128)(2,1)S(1)}, bf16[3,128,128]{2,1,0:T(8,128)(2,1)S(1)}, u32[]{:S(2)}, u32[]{:S(2)}) %collective-permute-start.8) | collective-permute-done | bytes 98336 | tf_op jit(solution)/shard_map/ppermute | solution.py:26
  63.8 4.7 %shard_map.88.ham_ref = bf16[768,2048]{1,0:T(8,128)(2,1)} custom-call(s32[2]{0:T(128)S(1)} %pad_add_fusion.ids, s32[3,16,64]{2,1,0:T(8,128)S(1)} %copy-done.13, s32[16]{0:T(128)S(1)} %copy-done.17, bf16[48,128,128]{2,1,0:T(8,128)(2,1)S(1)} %copy-done.3), custom_call_target="tpu_custom_call" | custom-call | flops 4194304 | bytes 5242880 | tf_op jit(solution)/shard_map/pallas_call | solution.py:55
  72.4 3.7 %all-to-all-start.1 = ((bf16[48,128,128]{2,1,0:T(8,128)(2,1)}), bf16[48,128,128]{2,1,0:T(8,128)(2,1)S(1)}, u32[]{:S(2)}, u32[]{:S(2)}) async-start(bf16[48,128,128]{2,1,0:T(8,128)(2,1)} %bitcast.4), calls=%async_computation.1 | async-start | bytes 3145728 | tf_op jit(solution)/shard_map/all_to_all | solution.py:361
  84.0 11.8 %collective-permute-done.9.refs_0_ = bf16[2,128,768]{2,1,0:T(8,128)(2,1)S(1)} collective-permute-done((bf16[2,128,768]{2,1,0:T(8,128)(2,1)}, bf16[2,128,768]{2,1,0:T(8,128)(2,1)S(1)}, u32[]{:S(2)}, u32[]{:S(2)}) %collective-permute-start.9) | collective-permute-done | bytes 393248 | tf_op jit(solution)/shard_map/ppermute | solution.py:26
  97.4 4.4 %collective-permute-done.10.refs_5_ = bf16[1,128,768]{2,1,0:T(8,128)(2,1)S(1)} collective-permute-done((bf16[1,128,768]{2,1,0:T(8,128)(2,1)}, bf16[1,128,768]{2,1,0:T(8,128)(2,1)S(1)}, u32[]{:S(2)}, u32[]{:S(2)}) %collective-permute-start.10) | collective-permute-done | bytes 196640 | tf_op jit(solution)/shard_map/ppermute | solution.py:26
  104.8 4.9 %all-to-all-start.2 = ((bf16[8,768,128]{2,1,0:T(8,128)(2,1)}), bf16[8,768,128]{2,1,0:T(8,128)(2,1)}, u32[]{:S(2)}, u32[]{:S(2)}) async-start(bf16[8,768,128]{2,1,0:T(8,128)(2,1)} %get-tuple-element.163), calls=%async_computation.2 | async-start | bytes 3145728 | tf_op jit(solution)/shard_map/all_to_all | solution.py:152
  116.3 4.8 %shard_map.92.ham_t_ref = bf16[2048,768]{1,0:T(8,128)(2,1)} custom-call(s32[2]{0:T(128)S(1)} %pad_add_fusion.ids, s32[3,16,64]{2,1,0:T(8,128)S(1)} %copy-done.13, s32[16]{0:T(128)S(1)} %copy-done.17, bf16[48,128,128]{2,1,0:T(8,128)(2,1)S(1)} %all-to-all-done.1.ham_ref), custom_call_target="tpu_custom_call" | custom-call | flops 4194304 | bytes 5242880 | tf_op jit(solution)/shard_map/pallas_call | solution.py:55
  125.3 4.6 %all-to-all-done.2.refs_9_ = bf16[8,768,128]{2,1,0:T(8,128)(2,1)} async-done(((bf16[8,768,128]{2,1,0:T(8,128)(2,1)}), bf16[8,768,128]{2,1,0:T(8,128)(2,1)}, u32[]{:S(2)}, u32[]{:S(2)}) %all-to-all-start.2) | async-done | bytes 1572896 | tf_op jit(solution)/shard_map/all_to_all | solution.py:152
  133.8 7.5 %shard_map.93.part_ref = f32[768,768]{1,0:T(8,128)S(1)} custom-call(bf16[2048,768]{1,0:T(8,128)(2,1)} %shard_map.92.ham_t_ref, bf16[768,2048]{1,0:T(8,128)(2,1)} %shard_map.88.ham_ref, f32[768,768]{1,0:T(8,128)} %refs_9_.1, f32[768,1]{1,0:T(8,128)} %copy.15.dr_ref, f32[1,768]{1,0:T(1,128)} %reshape.14.dc_ref, ...), custom_call_target="tpu_custom_call" | custom-call | flops 3623878656 | bytes 18874368 | tf_op jit(solution)/shard_map/pallas_call | solution.py:55
  142.8 4.5 %shard_map.94 = (f32[768,768]{1,0:T(8,128)}, bf16[2,128,768]{2,1,0:T(8,128)(2,1)}, bf16[2,768,128]{2,1,0:T(8,128)(2,1)}, bf16[1,128,768]{2,1,0:T(8,128)(2,1)}, b...) custom-call(s32[2]{0:T(128)S(1)} %copy-done.15, s32[16,2]{1,0:T(8,128)S(1)} %copy.16.hot, ...), custom_call_target="tpu_custom_call" | custom-call | flops 1207959552 | bytes 8388608 | tf_op jit(solution)/shard_map/pallas_call | solution.py:55
  152.8 3.6 %collective-permute-start.23 = (bf16[1,128,768]{2,1,0:T(8,128)(2,1)}, bf16[1,128,768]{2,1,0:T(8,128)(2,1)S(1)}, u32[]{:S(2)}, u32[]{:S(2)}) collective-permute-start(bf16[1,128,768]{2,1,0:T(8,128)(2,1)} %get-tuple-element.203), channel_id=1, source_target_pairs={{0,32},{1,33},{2,34},{3,35},{4,36},{5,37},{6,38},{7,39},{8,40},{9,... | collective-permute-start | bytes 589832 | tf_op jit(solution)/shard_map/ppermute | solution.py:26
  156.4 6.5 %collective-permute-done.20.refs_0_ = bf16[2,128,768]{2,1,0:T(8,128)(2,1)S(1)} collective-permute-done((bf16[2,128,768]{2,1,0:T(8,128)(2,1)}, bf16[2,128,768]{2,1,0:T(8,128)(2,1)S(1)}, u32[]{:S(2)}, u32[]{:S(2)}) %collective-permute-start.20) | collective-permute-done | bytes 393248 | tf_op jit(solution)/shard_map/ppermute | solution.py:26
  162.9 14.5 %collective-permute-done.21.refs_2_ = bf16[2,768,128]{2,1,0:T(8,128)(2,1)S(1)} collective-permute-done((bf16[2,768,128]{2,1,0:T(8,128)(2,1)}, bf16[2,768,128]{2,1,0:T(8,128)(2,1)S(1)}, u32[]{:S(2)}, u32[]{:S(2)}) %collective-permute-start.21) | collective-permute-done | bytes 393248 | tf_op jit(solution)/shard_map/ppermute | solution.py:26
  182.1 5.0 %all-to-all-start.3 = ((bf16[16,768,128]{2,1,0:T(8,128)(2,1)}), bf16[16,768,128]{2,1,0:T(8,128)(2,1)}, u32[]{:S(2)}, u32[]{:S(2)}) async-start(bf16[16,768,128]{2,1,0:T(8,128)(2,1)} %get-tuple-element.223), calls=%async_computation.3 | async-start | bytes 6291456 | tf_op jit(solution)/shard_map/all_to_all | solution.py:152
  188.7 3.6 %collective-permute-start.27 = (bf16[1,128,768]{2,1,0:T(8,128)(2,1)S(1)}, bf16[1,128,768]{2,1,0:T(8,128)(2,1)S(1)}, u32[]{:S(2)}, u32[]{:S(2)}) collective-permute-start(bf16[1,128,768]{2,1,0:T(8,128)(2,1)S(1)} %copy-done.35), channel_id=1, source_target_pairs={{0,32},{1,33},{2,34},{3,35},{4,36},{5,37},{6,38},{7,39},{8,40},{9,... | collective-permute-start | bytes 589832 | tf_op jit(solution)/shard_map/ppermute | solution.py:26
  192.3 14.7 %collective-permute-done.25.refs_0_ = bf16[2,128,768]{2,1,0:T(8,128)(2,1)S(1)} collective-permute-done((bf16[2,128,768]{2,1,0:T(8,128)(2,1)S(1)}, bf16[2,128,768]{2,1,0:T(8,128)(2,1)S(1)}, u32[]{:S(2)}, u32[]{:S(2)}) %collective-permute-start.25) | collective-permute-done | bytes 393248 | tf_op jit(solution)/shard_map/ppermute | solution.py:26
  212.0 3.6 %collective-permute-start.31 = (bf16[1,128,768]{2,1,0:T(8,128)(2,1)}, bf16[1,128,768]{2,1,0:T(8,128)(2,1)S(1)}, u32[]{:S(2)}, u32[]{:S(2)}) collective-permute-start(bf16[1,128,768]{2,1,0:T(8,128)(2,1)} %get-tuple-element.221), channel_id=1, source_target_pairs={{0,32},{1,33},{2,34},{3,35},{4,36},{5,37},{6,38},{7,39},{8,40},{9,... | collective-permute-start | bytes 589832 | tf_op jit(solution)/shard_map/ppermute | solution.py:26
  215.6 6.1 %collective-permute-done.29.refs_0_ = bf16[2,128,768]{2,1,0:T(8,128)(2,1)S(1)} collective-permute-done((bf16[2,128,768]{2,1,0:T(8,128)(2,1)S(1)}, bf16[2,128,768]{2,1,0:T(8,128)(2,1)S(1)}, u32[]{:S(2)}, u32[]{:S(2)}) %collective-permute-start.29) | collective-permute-done | bytes 393248 | tf_op jit(solution)/shard_map/ppermute | solution.py:26
  225.7 3.6 %collective-permute-start.34 = (bf16[1,128,768]{2,1,0:T(8,128)(2,1)}, bf16[1,128,768]{2,1,0:T(8,128)(2,1)S(1)}, u32[]{:S(2)}, u32[]{:S(2)}) collective-permute-start(bf16[1,128,768]{2,1,0:T(8,128)(2,1)} %get-tuple-element.240), channel_id=1, source_target_pairs={{0,32},{1,33},{2,34},{3,35},{4,36},{5,37},{6,38},{7,39},{8,40},{9,... | collective-permute-start | bytes 589832 | tf_op jit(solution)/shard_map/ppermute | solution.py:26
  229.3 8.2 %shard_map.98.part_ref = f32[768,768]{1,0:T(8,128)S(1)} custom-call(bf16[2048,768]{1,0:T(8,128)(2,1)} %shard_map.92.ham_t_ref, bf16[768,2048]{1,0:T(8,128)(2,1)} %shard_map.88.ham_ref, f32[768,768]{1,0:T(8,128)} %get-tuple-element.120.x_ref, f32[768,1]{1,0:T(8,128)} %copy.15.dr_ref, f32[1,768]{1,0:T(1,128)} %reshape.14.dc_ref, ...), custom_call_target="tpu_custom_call" | custom-call | flops 3623878656 | bytes 18874368 | tf_op jit(solution)/shard_map/pallas_call | solution.py:55
  238.2 3.8 %shard_map.99 = f32[768,768]{1,0:T(8,128)} custom-call(s32[2]{0:T(128)S(1)} %copy-done.16, s32[16,2]{1,0:T(8,128)S(1)} %copy.16.hot, s32[16,16]{1,0:T(8,128)S(1)} %copy-done.5, f32[768,768]{1,0:T(8,128)S(1)} %shard_map.98.part_ref, bf16[768,2048]{1,0:T(8,128)(2,1)S(1)} %copy-done.1, bf16[1,128,768]{2,1,0:T(8,128)(2,1)S(1)} %copy-done.11, ...), custom_call_target="tpu_custom_call" | custom-call | flops 1207959552 | bytes 8388608 | tf_op jit(solution)/shard_map/pallas_call | solution.py:55
  (152 shorter events, 73.3 us)
Async XLA Ops:
  12.3 60.2 %all-to-all-start = ((bf16[8,768,128]{2,1,0:T(8,128)(2,1)}), bf16[8,768,128]{2,1,0:T(8,128)(2,1)}, u32[]{:S(2)}, u32[]{:S(2)}) async-start(bf16[8,768,128]{2,1,0:T(8,128)(2,1)} %get-tuple-element.140), calls=%async_computation | async-start | bytes 3145728 | tf_op jit(solution)/shard_map/all_to_all | solution.py:152
  18.1 52.0 %collective-permute-start.2 = (bf16[2,768,128]{2,1,0:T(8,128)(2,1)}, bf16[2,768,128]{2,1,0:T(8,128)(2,1)S(1)}, u32[]{:S(2)}, u32[]{:S(2)}) collective-permute-start(bf16[2,768,128]{2,1,0:T(8,128)(2,1)} %get-tuple-element.130), channel_id=1, source_target_pairs={{0,8},{1,9},{2,10},{3,11},{4,12},{5,13},{6,14},{7,15},{8,0},{9,1},... | collective-permute-start | bytes 1179656 | tf_op jit(solution)/shard_map/ppermute | solution.py:26
  27.9 42.2 %collective-permute-start.1 = (bf16[2,128,768]{2,1,0:T(8,128)(2,1)}, bf16[2,128,768]{2,1,0:T(8,128)(2,1)S(1)}, u32[]{:S(2)}, u32[]{:S(2)}) collective-permute-start(bf16[2,128,768]{2,1,0:T(8,128)(2,1)} %get-tuple-element.153), channel_id=1, source_target_pairs={{0,64},{1,65},{2,66},{3,67},{4,68},{5,69},{6,70},{7,71},{8,72},{9,... | collective-permute-start | bytes 1179656 | tf_op jit(solution)/shard_map/ppermute | solution.py:26
  29.2 27.3 %collective-permute-start.8 = (bf16[3,128,128]{2,1,0:T(8,128)(2,1)S(1)}, bf16[3,128,128]{2,1,0:T(8,128)(2,1)S(1)}, u32[]{:S(2)}, u32[]{:S(2)}) collective-permute-start(bf16[3,128,128]{2,1,0:T(8,128)(2,1)S(1)} %collective-permute-done.refs_0_), channel_id=1, source_target_pairs={{0,192},{1,193},{2,194},{3,195},{4,196},{5,197},{6,198},{7,199},{8... | collective-permute-start | bytes 294920 | tf_op jit(solution)/shard_map/ppermute | solution.py:26
  29.2 29.2 %collective-permute-start.7 = (bf16[3,128,128]{2,1,0:T(8,128)(2,1)S(1)}, bf16[3,128,128]{2,1,0:T(8,128)(2,1)S(1)}, u32[]{:S(2)}, u32[]{:S(2)}) collective-permute-start(bf16[3,128,128]{2,1,0:T(8,128)(2,1)S(1)} %collective-permute-done.refs_0_), channel_id=1, source_target_pairs={{0,128},{1,129},{2,130},{3,131},{4,132},{5,133},{6,134},{7,135},{8... | collective-permute-start | bytes 294920 | tf_op jit(solution)/shard_map/ppermute | solution.py:26
  31.4 29.2 %collective-permute-start.6 = (bf16[3,128,128]{2,1,0:T(8,128)(2,1)S(1)}, bf16[3,128,128]{2,1,0:T(8,128)(2,1)S(1)}, u32[]{:S(2)}, u32[]{:S(2)}) collective-permute-start(bf16[3,128,128]{2,1,0:T(8,128)(2,1)S(1)} %collective-permute-done.refs_0_), channel_id=1, source_target_pairs={{0,64},{1,65},{2,66},{3,67},{4,68},{5,69},{6,70},{7,71},{8,72},{9,... | collective-permute-start | bytes 294920 | tf_op jit(solution)/shard_map/ppermute | solution.py:26
  56.5 15.9 %collective-permute-start.3 = (bf16[1,128,768]{2,1,0:T(8,128)(2,1)}, bf16[1,128,768]{2,1,0:T(8,128)(2,1)S(1)}, u32[]{:S(2)}, u32[]{:S(2)}) collective-permute-start(bf16[1,128,768]{2,1,0:T(8,128)(2,1)} %get-tuple-element.137), channel_id=1, source_target_pairs={{0,16},{1,17},{2,18},{3,19},{4,20},{5,21},{6,22},{7,23},{8,24},{9,... | collective-permute-start | bytes 589832 | tf_op jit(solution)/shard_map/ppermute | solution.py:26
  58.4 14.0 %collective-permute-start.4 = (bf16[1,128,768]{2,1,0:T(8,128)(2,1)}, bf16[1,128,768]{2,1,0:T(8,128)(2,1)S(1)}, u32[]{:S(2)}, u32[]{:S(2)}) collective-permute-start(bf16[1,128,768]{2,1,0:T(8,128)(2,1)} %get-tuple-element.138), channel_id=1, source_target_pairs={{0,32},{1,33},{2,34},{3,35},{4,36},{5,37},{6,38},{7,39},{8,40},{9,... | collective-permute-start | bytes 589832 | tf_op jit(solution)/shard_map/ppermute | solution.py:26
  72.4 32.3 %all-to-all-start.1 = ((bf16[48,128,128]{2,1,0:T(8,128)(2,1)}), bf16[48,128,128]{2,1,0:T(8,128)(2,1)S(1)}, u32[]{:S(2)}, u32[]{:S(2)}) async-start(bf16[48,128,128]{2,1,0:T(8,128)(2,1)} %bitcast.4), calls=%async_computation.1 | async-start | bytes 3145728 | tf_op jit(solution)/shard_map/all_to_all | solution.py:361
  76.1 19.6 %collective-permute-start.9 = (bf16[2,128,768]{2,1,0:T(8,128)(2,1)}, bf16[2,128,768]{2,1,0:T(8,128)(2,1)S(1)}, u32[]{:S(2)}, u32[]{:S(2)}) collective-permute-start(bf16[2,128,768]{2,1,0:T(8,128)(2,1)} %get-tuple-element.153), channel_id=1, source_target_pairs={{0,128},{1,129},{2,130},{3,131},{4,132},{5,133},{6,134},{7,135},{8... | collective-permute-start | bytes 1179656 | tf_op jit(solution)/shard_map/ppermute | solution.py:26
  78.0 23.9 %collective-permute-start.10 = (bf16[1,128,768]{2,1,0:T(8,128)(2,1)}, bf16[1,128,768]{2,1,0:T(8,128)(2,1)S(1)}, u32[]{:S(2)}, u32[]{:S(2)}) collective-permute-start(bf16[1,128,768]{2,1,0:T(8,128)(2,1)} %get-tuple-element.148), channel_id=1, source_target_pairs={{0,16},{1,17},{2,18},{3,19},{4,20},{5,21},{6,22},{7,23},{8,24},{9,... | collective-permute-start | bytes 589832 | tf_op jit(solution)/shard_map/ppermute | solution.py:26
  79.9 24.9 %collective-permute-start.11 = (bf16[1,128,768]{2,1,0:T(8,128)(2,1)S(1)}, bf16[1,128,768]{2,1,0:T(8,128)(2,1)S(1)}, u32[]{:S(2)}, u32[]{:S(2)}) collective-permute-start(bf16[1,128,768]{2,1,0:T(8,128)(2,1)S(1)} %copy-done.33), channel_id=1, source_target_pairs={{0,32},{1,33},{2,34},{3,35},{4,36},{5,37},{6,38},{7,39},{8,40},{9,... | collective-permute-start | bytes 589832 | tf_op jit(solution)/shard_map/ppermute | solution.py:26
  82.5 22.2 %collective-permute-start.12 = (bf16[1,128,768]{2,1,0:T(8,128)(2,1)S(1)}, bf16[1,128,768]{2,1,0:T(8,128)(2,1)S(1)}, u32[]{:S(2)}, u32[]{:S(2)}) collective-permute-start(bf16[1,128,768]{2,1,0:T(8,128)(2,1)S(1)} %copy-done.32), channel_id=1, source_target_pairs={{0,48},{1,49},{2,50},{3,51},{4,52},{5,53},{6,54},{7,55},{8,56},{9,... | collective-permute-start | bytes 589832 | tf_op jit(solution)/shard_map/ppermute | solution.py:26
  104.8 25.2 %all-to-all-start.2 = ((bf16[8,768,128]{2,1,0:T(8,128)(2,1)}), bf16[8,768,128]{2,1,0:T(8,128)(2,1)}, u32[]{:S(2)}, u32[]{:S(2)}) async-start(bf16[8,768,128]{2,1,0:T(8,128)(2,1)} %get-tuple-element.163), calls=%async_computation.2 | async-start | bytes 3145728 | tf_op jit(solution)/shard_map/all_to_all | solution.py:152
  147.3 15.6 %collective-permute-start.20 = (bf16[2,128,768]{2,1,0:T(8,128)(2,1)}, bf16[2,128,768]{2,1,0:T(8,128)(2,1)S(1)}, u32[]{:S(2)}, u32[]{:S(2)}) collective-permute-start(bf16[2,128,768]{2,1,0:T(8,128)(2,1)} %get-tuple-element.214), channel_id=1, source_target_pairs={{0,64},{1,65},{2,66},{3,67},{4,68},{5,69},{6,70},{7,71},{8,72},{9,... | collective-permute-start | bytes 1179656 | tf_op jit(solution)/shard_map/ppermute | solution.py:26
  150.5 26.8 %collective-permute-start.21 = (bf16[2,768,128]{2,1,0:T(8,128)(2,1)}, bf16[2,768,128]{2,1,0:T(8,128)(2,1)S(1)}, u32[]{:S(2)}, u32[]{:S(2)}) collective-permute-start(bf16[2,768,128]{2,1,0:T(8,128)(2,1)} %get-tuple-element.195.refs_1_), channel_id=1, source_target_pairs={{0,8},{1,9},{2,10},{3,11},{4,12},{5,13},{6,14},{7,15},{8,0},{9,1},... | collective-permute-start | bytes 1179656 | tf_op jit(solution)/shard_map/ppermute | solution.py:26
  152.3 29.0 %collective-permute-start.22 = (bf16[1,128,768]{2,1,0:T(8,128)(2,1)}, bf16[1,128,768]{2,1,0:T(8,128)(2,1)S(1)}, u32[]{:S(2)}, u32[]{:S(2)}) collective-permute-start(bf16[1,128,768]{2,1,0:T(8,128)(2,1)} %get-tuple-element.202), channel_id=1, source_target_pairs={{0,16},{1,17},{2,18},{3,19},{4,20},{5,21},{6,22},{7,23},{8,24},{9,... | collective-permute-start | bytes 589832 | tf_op jit(solution)/shard_map/ppermute | solution.py:26
  152.8 28.5 %collective-permute-start.23 = (bf16[1,128,768]{2,1,0:T(8,128)(2,1)}, bf16[1,128,768]{2,1,0:T(8,128)(2,1)S(1)}, u32[]{:S(2)}, u32[]{:S(2)}) collective-permute-start(bf16[1,128,768]{2,1,0:T(8,128)(2,1)} %get-tuple-element.203), channel_id=1, source_target_pairs={{0,32},{1,33},{2,34},{3,35},{4,36},{5,37},{6,38},{7,39},{8,40},{9,... | collective-permute-start | bytes 589832 | tf_op jit(solution)/shard_map/ppermute | solution.py:26
  156.4 25.0 %collective-permute-start.24 = (bf16[1,128,768]{2,1,0:T(8,128)(2,1)}, bf16[1,128,768]{2,1,0:T(8,128)(2,1)S(1)}, u32[]{:S(2)}, u32[]{:S(2)}) collective-permute-start(bf16[1,128,768]{2,1,0:T(8,128)(2,1)} %get-tuple-element.204), channel_id=1, source_target_pairs={{0,48},{1,49},{2,50},{3,51},{4,52},{5,53},{6,54},{7,55},{8,56},{9,... | collective-permute-start | bytes 589832 | tf_op jit(solution)/shard_map/ppermute | solution.py:26
  182.1 42.5 %all-to-all-start.3 = ((bf16[16,768,128]{2,1,0:T(8,128)(2,1)}), bf16[16,768,128]{2,1,0:T(8,128)(2,1)}, u32[]{:S(2)}, u32[]{:S(2)}) async-start(bf16[16,768,128]{2,1,0:T(8,128)(2,1)} %get-tuple-element.223), calls=%async_computation.3 | async-start | bytes 6291456 | tf_op jit(solution)/shard_map/all_to_all | solution.py:152
  187.2 19.9 %collective-permute-start.25 = (bf16[2,128,768]{2,1,0:T(8,128)(2,1)S(1)}, bf16[2,128,768]{2,1,0:T(8,128)(2,1)S(1)}, u32[]{:S(2)}, u32[]{:S(2)}) collective-permute-start(bf16[2,128,768]{2,1,0:T(8,128)(2,1)S(1)} %copy-done.30), channel_id=1, source_target_pairs={{0,128},{1,129},{2,130},{3,131},{4,132},{5,133},{6,134},{7,135},{8... | collective-permute-start | bytes 1179656 | tf_op jit(solution)/shard_map/ppermute | solution.py:26
  187.2 21.5 %collective-permute-start.26 = (bf16[1,128,768]{2,1,0:T(8,128)(2,1)S(1)}, bf16[1,128,768]{2,1,0:T(8,128)(2,1)S(1)}, u32[]{:S(2)}, u32[]{:S(2)}) collective-permute-start(bf16[1,128,768]{2,1,0:T(8,128)(2,1)S(1)} %copy-done.36), channel_id=1, source_target_pairs={{0,16},{1,17},{2,18},{3,19},{4,20},{5,21},{6,22},{7,23},{8,24},{9,... | collective-permute-start | bytes 589832 | tf_op jit(solution)/shard_map/ppermute | solution.py:26
  188.7 20.0 %collective-permute-start.27 = (bf16[1,128,768]{2,1,0:T(8,128)(2,1)S(1)}, bf16[1,128,768]{2,1,0:T(8,128)(2,1)S(1)}, u32[]{:S(2)}, u32[]{:S(2)}) collective-permute-start(bf16[1,128,768]{2,1,0:T(8,128)(2,1)S(1)} %copy-done.35), channel_id=1, source_target_pairs={{0,32},{1,33},{2,34},{3,35},{4,36},{5,37},{6,38},{7,39},{8,40},{9,... | collective-permute-start | bytes 589832 | tf_op jit(solution)/shard_map/ppermute | solution.py:26
  192.3 16.4 %collective-permute-start.28 = (bf16[1,128,768]{2,1,0:T(8,128)(2,1)S(1)}, bf16[1,128,768]{2,1,0:T(8,128)(2,1)S(1)}, u32[]{:S(2)}, u32[]{:S(2)}) collective-permute-start(bf16[1,128,768]{2,1,0:T(8,128)(2,1)S(1)} %copy-done.34), channel_id=1, source_target_pairs={{0,48},{1,49},{2,50},{3,51},{4,52},{5,53},{6,54},{7,55},{8,56},{9,... | collective-permute-start | bytes 589832 | tf_op jit(solution)/shard_map/ppermute | solution.py:26
  (53 other events, 847.6 us)

commit v4 on v3

v4 whole, which is shorter than its diff:
```python
import jax
import jax.numpy as jnp
from jax import lax
from jax.experimental import pallas as pl
from jax.experimental.pallas import tpu as pltpu
from jax.sharding import Mesh, PartitionSpec as P
import numpy as np

center = 0.25
scale = 1.0 / 2.5
axes = ("zl", "x", "zh", "y", "k")
sizes = (4, 4, 2, 4, 2)
B = 128
T = 768
R = 256
bf16 = jnp.bfloat16
f32 = jnp.float32


def permute(value, target):
    places = list(np.ndindex(*sizes))
    pairs = [
        (int(np.ravel_multi_index(p, sizes)), int(np.ravel_multi_index(target(*p), sizes)))
        for p in places
    ]
    return lax.ppermute(value, axes, pairs)


def z_xor(n):
    return lambda zl, x, zh, y, k: (zl ^ n, x, zh, y, k)


def x_shift(n):
    return lambda zl, x, zh, y, k: (zl, (x + n) % 4, zh, y, k)


def zh_flip(zl, x, zh, y, k):
    return (zl, x, 1 - zh, y, k)


def mirror(zl, x, zh, y, k):
    r, c = zl * 4 + x, zh * 8 + y * 2 + k
    return (c // 4, c % 4, r // 8, (r % 8) // 2, r % 2)


def barrier(*values):
    return lax.optimization_barrier(values)


def start(block):
    return pl.multiple_of(block * B, B)


def call(kernel, scalars, grid, in_specs, out_specs, out_shape, args, scratch=(), flops=0, moved=0, room=1, pinned=False):
    return pl.pallas_call(
        kernel,
        grid_spec=pltpu.PrefetchScalarGridSpec(
            num_scalar_prefetch=len(scalars),
            grid=grid,
            in_specs=in_specs,
            out_specs=out_specs,
            scratch_shapes=list(scratch),
        ),
        out_shape=out_shape,
        compiler_params=pltpu.CompilerParams(vmem_limit_bytes=room << 20),
        cost_estimate=pl.CostEstimate(flops=flops, bytes_accessed=moved, transcendentals=0),
    )(*scalars, *(pltpu.with_memory_space_constraint(arg, pltpu.HBM) if pinned else arg for arg in args))


def shape(dims, kind=bf16):
    return pltpu.HBM(dims, kind)


def free_shape(dims, kind=bf16):
    return jax.ShapeDtypeStruct(dims, kind)


def whole(dims):
    return pl.BlockSpec(dims, lambda i, *_: (0,) * len(dims))


send_shapes = (
    [shape((2, B, T)), shape((2, T, B))] + [shape((1, B, T))] * 4 + [shape((8, T, B))]
)


def choose_rows(ids, sel, step, slabs_ref, refs, at=0):
    zl, x = ids[0] // 4, ids[0] % 4
    for n in range(4):
        refs[n][at] = slabs_ref[sel[zl * 4 + (x + n) % 4, (zl ^ step) * 4 + x]]


def choose_cols(ids, sel, flip, slabs_ref, out_ref):
    zh, q = ids[1] // 8, ids[1] ^ (8 * flip)
    for i in range(8):
        out_ref[i] = slabs_ref[sel[zh * 8 + i, q]]


def pack_kernel(ids, hot, sel, x_ref, row_ref, col_ref, *refs):
    r, c = ids[0], ids[1]
    for h in range(2):
        row_ref[h] = x_ref[pl.ds(start(hot[r, h]), B), :].astype(bf16)
        col_ref[h] = x_ref[:, pl.ds(start(hot[c, h]), B)].astype(bf16)
    choose_rows(ids, sel, 0, row_ref, refs[:4])
    choose_cols(ids, sel, 0, col_ref, refs[4])


def pack(ids, hot, sel, value):
    return call(
        pack_kernel,
        (ids, hot, sel),
        (1,),
        [whole((T, T))],
        [whole(s.shape) for s in send_shapes],
        send_shapes,
        (value,),
        moved=5 << 20,
        room=32,
    )


def next_slabs(ids, sel, rows, steps, cols=None):
    count = len(rows)

    def kernel(ids, sel, *refs):
        outs = refs[count + (cols is not None) :]
        for m in range(count):
            choose_rows(ids, sel, steps[m], refs[m], outs[:4], m)
        if cols is not None:
            choose_cols(ids, sel, 1, refs[count], outs[4])

    out_shapes = [shape((count, B, T))] * 4 + [shape((8, T, B))] * (cols is not None)
    args = rows if cols is None else rows + [cols]
    return call(
        kernel,
        (ids, sel),
        (1,),
        [whole(arg.shape) for arg in args],
        [whole(s.shape) for s in out_shapes],
        out_shapes,
        args,
        moved=4 << 20,
        room=32,
    )


def over_x(chosen):
    return [chosen[0]] + [permute(chosen[n], x_shift(n)) for n in (1, 2, 3)]


def over_yk(chosen):
    return lax.all_to_all(chosen, ("y", "k"), 0, 0, tiled=True)


def dense_kernel(mirrored):
    def kernel(ids, lists, counts, *refs):
        out_ref, held, total = refs[-3:]
        ham_ref = refs[0]
        r, c = ids[0], ids[1]
        tile = c if mirrored else r
        if mirrored:
            ham_ref = held
            for n in range(4):
                ham_ref[n * 12 : (n + 1) * 12] = refs[n][...]

        def clear(i, carry):
            total[i] = jnp.zeros((B, B), f32)
            return carry

        lax.fori_loop(0, 96, clear, 0)

        def add(slot, carry):
            q = lists[0, tile, slot]
            t = lists[1, tile, slot]
            b = lists[2, tile, slot]
            if mirrored:
                place = q ^ (c // 8 * 8)
                piece = b // 3
                b = ((r + 4 - piece % 4) % 4 * 4 + ((piece // 4) ^ (r // 4))) * 3 + b % 3
            else:
                place = ((q // 4) ^ (r // 4)) * 4 + (r + 4 - q % 4) % 4
            at = t * 16 + place
            total[at] = total[at] + ham_ref[b].astype(f32)
            return carry

        lax.fori_loop(0, counts[tile], add, 0)
        for t in range(6):
            for place in range(16):
                block = total[t * 16 + place].astype(bf16)
                if mirrored:
                    out_ref[place * B : (place + 1) * B, t * B : (t + 1) * B] = block
                else:
                    out_ref[t * B : (t + 1) * B, place * B : (place + 1) * B] = block

    return kernel


def dense(ids, lists, counts, hams, mirrored):
    dims = (2048, T) if mirrored else (T, 2048)
    return call(
        dense_kernel(mirrored),
        (ids, lists, counts),
        (1,),
        [whole(h.shape) for h in hams],
        whole(dims),
        shape(dims),
        hams,
        scratch=[pltpu.VMEM((48, B, B), bf16), pltpu.VMEM((96, B, B), f32)],
        flops=1 << 22,
        moved=5 << 20,
        room=32,
    )


rows = pl.BlockSpec((R, T), lambda i, *_: (i, 0))


def first_products_kernel(second):
    def kernel(ham_t_ref, ham_ref, x_ref, dr_ref, dc_ref, *refs):
        yk0_ref, yk1_ref = refs[8:10]
        out_ref, wide = refs[-2:]
        for i in range(8):
            wide[:, i * B : (i + 1) * B] = yk0_ref[i]
            wide[:, (8 + i) * B : (9 + i) * B] = yk1_ref[i]
        near = jnp.concatenate(
            [ref[0] for ref in refs[:4]] + [ref[m] for m in range(2) for ref in refs[4:8]], axis=0
        )
        total = jnp.dot(wide[...], ham_t_ref[...], preferred_element_type=f32) + jnp.dot(
            ham_ref[...], near, preferred_element_type=f32
        )
        total = total + (dr_ref[...] + dc_ref[...] - center) * x_ref[...]
        if second:
            total = total - refs[10][...] * (0.5 / scale)
        out_ref[...] = total

    return kernel


def first_products(ham_t, ham, value, dr, dc, x0, x12, yk0, yk1, before=None):
    extra = () if before is None else (before,)
    return call(
        first_products_kernel(before is not None),
        (),
        (T // R,),
        [
            whole((2048, T)),
            pl.BlockSpec((R, 1536), lambda i, *_: (i, 0)),
            rows,
            pl.BlockSpec((R, 1), lambda i, *_: (i, 0)),
            whole((1, T)),
        ]
        + [whole(s.shape) for s in x0 + x12]
        + [pl.BlockSpec((8, R, B), lambda i, *_: (0, i, 0))] * 2
        + [rows] * len(extra),
        rows,
        free_shape((T, T), f32),
        (ham_t, ham, value, dr, dc, *x0, *x12, yk0, yk1, *extra),
        scratch=[pltpu.VMEM((R, 2048), bf16)],
        flops=2 * T * T * 3584,
        moved=20 << 20,
        room=36,
        pinned=True,
    )


def finish_kernel(second):
    def kernel(ids, hot, sel, part_ref, ham_ref, *refs):
        stacked = jnp.concatenate([ref[0] for ref in refs[:4]], axis=0)
        out_ref = refs[4]
        total = part_ref[...] + jnp.dot(ham_ref[...], stacked, preferred_element_type=f32)
        if second:
            out_ref[...] = total * (2.0 * scale)
            return
        row_ref, col_ref = refs[5:7]
        out_ref[...] = total * scale
        i, r, c = pl.program_id(0), ids[0], ids[1]
        for h in range(2):
            col_ref[h] = out_ref[:, pl.ds(start(hot[c, h]), B)].astype(bf16)
            block = hot[r, h]

            @pl.when(block // 2 == i)
            def _(h=h, block=block):
                row_ref[h] = out_ref[pl.ds(start(block % 2), B), :].astype(bf16)

        choose_cols(ids, sel, 0, col_ref, refs[11])

        @pl.when(i == T // R - 1)
        def _():
            choose_rows(ids, sel, 0, row_ref, refs[7:11])

    return kernel


def finish(ids, hot, sel, part, ham, slabs, second):
    out_specs, out_shape = rows, shape((T, T), f32)
    if not second:
        out_specs = [rows, whole((2, B, T)), pl.BlockSpec((2, R, B), lambda i, *_: (0, i, 0))]
        out_specs += [whole((1, B, T))] * 4 + [pl.BlockSpec((8, R, B), lambda i, *_: (0, i, 0))]
        out_shape = [out_shape] + send_shapes
    return call(
        finish_kernel(second),
        (ids, hot, sel),
        (T // R,),
        [rows, pl.BlockSpec((R, 512), lambda i, *_: (i, 3))] + [whole((1, B, T))] * 4,
        out_specs,
        out_shape,
        (part, ham, *slabs),
        flops=2 * T * T * 512,
        moved=6 << 20,
        room=32,
    )


def body(start_vector, ham_blocks, diagonal, lists, counts, hot, sel):
    row_index = lax.axis_index("zl") * 4 + lax.axis_index("x")
    col_index = (lax.axis_index("zh") * 4 + lax.axis_index("y")) * 2 + lax.axis_index("k")
    ids = jnp.stack([row_index, col_index]).astype(jnp.int32)
    dr = lax.dynamic_slice_in_dim(diagonal, row_index * T, T).reshape(T, 1)
    dc = lax.dynamic_slice_in_dim(diagonal, col_index * T, T).reshape(1, T)

    piece = lax.dynamic_slice_in_dim(ham_blocks, col_index * 3, 3).transpose(0, 2, 1)
    piece = permute(piece, mirror)
    pieces = [piece] + [permute(piece, z_xor(n)) for n in (1, 2, 3)]
    row, col, *sends = pack(ids, hot, sel, start_vector)
    ham = dense(ids, lists, counts, (ham_blocks,), False)
    near = over_x(sends[:4])
    quarter, row, col, sends, near, ham, dr, dc = barrier(
        jnp.concatenate(pieces), row, col, sends, near, ham, dr, dc
    )
    ham_t = None
    outs = []
    value = start_vector
    for step in range(2):
        first = step == 0
        z1 = permute(row, z_xor(1))
        z2 = permute(row, z_xor(2))
        zh = permute(col, zh_flip)
        yk0 = over_yk(sends[4])
        if first:
            hams = [quarter] + [permute(quarter, x_shift(n)) for n in (1, 2)]
            sends = next_slabs(ids, sel, [z1, z2], (1, 2), zh)
            row, sends, near, yk0, hams = barrier(row, sends, near, yk0, hams)
            hams.append(permute(quarter, x_shift(3)))
        else:
            last = sends[3]
            near = [sends[0]] + [permute(sends[n], x_shift(n)) for n in (1, 2)]
            sends = next_slabs(ids, sel, [z1, z2], (1, 2), zh)
            row, sends, near, yk0, last = barrier(row, sends, near, yk0, last)
            near.append(permute(last, x_shift(3)))
        z3 = permute(row, z_xor(3))
        x12 = over_x(sends[:4])
        yk1 = over_yk(sends[4])
        if first:
            ham_t = dense(ids, lists, counts, hams, True)
        sends = next_slabs(ids, sel, [z3], (3,))
        sends, x12, yk1, near, ham_t = barrier(sends, x12, yk1, near, ham_t)
        x3 = over_x(sends)
        before = () if first else (start_vector,)
        part = first_products(ham_t, ham, value, dr, dc, near, x12, yk0, yk1, *before)
        result = finish(ids, hot, sel, part, ham, x3, not first)
        if first:
            value, *sent = result
            row, col, sends = barrier(sent[0], sent[1], sent[2:])
            result = value
        outs.append(result)
    return tuple(outs)


def solution(mesh):
    fine = Mesh(mesh.devices.reshape(sizes), axes)
    rows, cols = ("zl", "x"), ("zh", "y", "k")
    in_specs = (P(rows, cols), P(rows, None, None), P(), P(), P(), P(), P())
    out_specs = (P(rows, cols), P(rows, cols))
    return jax.shard_map(body, mesh=fine, in_specs=in_specs, out_specs=out_specs, check_vma=False)
```

time: 246 us -> 236 us (0.959); the launches traced: 242 us -> 235 us
  starting transfers between devices: 87.3 us -> 81.1 us
  Pallas kernels: 49.5 us -> 45.9 us
  waiting for transfers between devices: 95 us -> 98.5 us
    ppermute x36 -> x33, waiting for transfers between devices: 90.4 us -> 98.5 us  [permute(): return lax.ppermute(value, axes, pairs)]
    ppermute x36 -> x33, starting transfers between devices: 67.8 us -> 61.6 us  [permute(): return lax.ppermute(value, axes, pairs)]
    all_to_all x3 -> x4, waiting for transfers between devices: 4.64 us -> 0.01 us  [over_yk(): return lax.all_to_all(chosen, ('y', 'k'), 0, 0, tiled=True)]
    all_to_all x1 -> x0, starting transfers between devices: 3.71 us -> none  [body(): hams = lax.all_to_all(hams.reshape(48, B, B), 'x', 0, 0, tiled=True)]
    all_to_all x3 -> x4, starting transfers between devices: 15.8 us -> 19.5 us  [over_yk(): return lax.all_to_all(chosen, ('y', 'k'), 0, 0, tiled=True)]
    pallas_call x14 -> x11, Pallas kernels: 49.5 us -> 45.9 us  [call(): pl.pallas_call(kernel, grid_spec=pltpu.PrefetchScalarGridSpec(num_scalar_...]
    unnamed x76 -> x58, local copies, waits for them, and re-layouts: 5.77 us -> 5.3 us
  transfers between devices with their start and end apart: 40 -> 37, of which waited for: 15 -> 11; matrix products, arithmetic and copies ran while one was open for 1% -> 1% of each run, Pallas kernels for 17% -> 16%
where the time goes in v4:
time: 236 us; the launch traced here: 235 us
  waiting for transfers between devices  98.5 us (42%)
  starting transfers between devices  81.1 us (34%)
  Pallas kernels  45.9 us (19%)
  local copies, waits for them, and re-layouts  8.57 us (4%)
    ppermute x33, waiting for transfers between devices, permute(): return lax.ppermute(value, axes, pairs)  98.5 us
    ppermute x33, starting transfers between devices, permute(): return lax.ppermute(value, axes, pairs)  61.6 us
    pallas_call x11, Pallas kernels, call(): pl.pallas_call(kernel, grid_spec=pltpu.PrefetchScalarGridSpec(num_scalar_...  45.9 us
    all_to_all x4, starting transfers between devices, over_yk(): return lax.all_to_all(chosen, ('y', 'k'), 0, 0, tiled=True)  19.5 us
    unnamed x58, local copies, waits for them, and re-layouts  5.3 us
  transfers between devices with their start and end apart: 37, of which 11 were waited for; matrix products, arithmetic and copies ran while one was open for 1% of the time, Pallas kernels for 16%

profile of v4, /device:TPU:8, one launch (start us, length us, event | category | flops | bytes accessed | tf_op | source)
XLA Modules:
  0.0 235.2 jit_solution(10876981820190569928)
XLA Ops:
  1.7 4.8 %collective-permute-start = (bf16[3,128,128]{2,1,0:T(8,128)(2,1)S(1)}, bf16[3,128,128]{2,1,0:T(8,128)(2,1)S(1)}, u32[]{:S(2)}, u32[]{:S(2)}) collective-permute-start(bf16[3,128,128]{2,1,0:T(8,128)(2,1)S(1)} %bitcast.3), channel_id=1, source_target_pairs={{0,0},{1,16},{2,32},{3,48},{4,64},{5,80},{6,96},{7,112},{8,128},{9... | collective-permute-start | bytes 294920 | tf_op jit(solution)/shard_map/ppermute | solution.py:26
  7.3 4.4 %collective-permute-done = bf16[3,128,128]{2,1,0:T(8,128)(2,1)S(1)} collective-permute-done((bf16[3,128,128]{2,1,0:T(8,128)(2,1)S(1)}, bf16[3,128,128]{2,1,0:T(8,128)(2,1)S(1)}, u32[]{:S(2)}, u32[]{:S(2)}) %collective-permute-start) | collective-permute-done | bytes 98336 | tf_op jit(solution)/shard_map/ppermute | solution.py:26
  11.7 8.7 %collective-permute-start.3 = (bf16[3,128,128]{2,1,0:T(8,128)(2,1)S(1)}, bf16[3,128,128]{2,1,0:T(8,128)(2,1)S(1)}, u32[]{:S(2)}, u32[]{:S(2)}) collective-permute-start(bf16[3,128,128]{2,1,0:T(8,128)(2,1)S(1)} %collective-permute-done), channel_id=1, source_target_pairs={{0,192},{1,193},{2,194},{3,195},{4,196},{5,197},{6,198},{7,199},{8... | collective-permute-start | bytes 294920 | tf_op jit(solution)/shard_map/ppermute | solution.py:26
  25.4 4.7 %collective-permute-start.5 = (bf16[1,128,768]{2,1,0:T(8,128)(2,1)}, bf16[1,128,768]{2,1,0:T(8,128)(2,1)S(1)}, u32[]{:S(2)}, u32[]{:S(2)}) collective-permute-start(bf16[1,128,768]{2,1,0:T(8,128)(2,1)} %get-tuple-element.109), channel_id=1, source_target_pairs={{0,32},{1,33},{2,34},{3,35},{4,36},{5,37},{6,38},{7,39},{8,40},{9,... | collective-permute-start | bytes 589832 | tf_op jit(solution)/shard_map/ppermute | solution.py:26
  33.5 5.3 %shard_map.87.ham_ref = bf16[768,2048]{1,0:T(8,128)(2,1)} custom-call(s32[2]{0:T(128)S(1)} %pad_add_fusion.ids, s32[3,16,64]{2,1,0:T(8,128)S(1)} %copy-done.8, s32[16]{0:T(128)S(1)} %copy-done.9, bf16[48,128,128]{2,1,0:T(8,128)(2,1)S(1)} %copy-done.3), custom_call_target="tpu_custom_call" | custom-call | flops 4194304 | bytes 5242880 | tf_op jit(solution)/shard_map/pallas_call | solution.py:55
  39.7 4.9 %all-to-all-start = ((bf16[8,768,128]{2,1,0:T(8,128)(2,1)}), bf16[8,768,128]{2,1,0:T(8,128)(2,1)}, u32[]{:S(2)}, u32[]{:S(2)}) async-start(bf16[8,768,128]{2,1,0:T(8,128)(2,1)} %get-tuple-element.124), calls=%async_computation | async-start | bytes 3145728 | tf_op jit(solution)/shard_map/all_to_all | solution.py:152
  44.6 5.1 %collective-permute-start.9 = (bf16[2,768,128]{2,1,0:T(8,128)(2,1)S(1)}, bf16[2,768,128]{2,1,0:T(8,128)(2,1)S(1)}, u32[]{:S(2)}, u32[]{:S(2)}) collective-permute-start(bf16[2,768,128]{2,1,0:T(8,128)(2,1)S(1)} %copy-done.23), channel_id=1, source_target_pairs={{0,8},{1,9},{2,10},{3,11},{4,12},{5,13},{6,14},{7,15},{8,0},{9,1},... | collective-permute-start | bytes 1179656 | tf_op jit(solution)/shard_map/ppermute | solution.py:26
  54.0 15.0 %collective-permute-done.9.refs_2_ = bf16[2,768,128]{2,1,0:T(8,128)(2,1)S(1)} collective-permute-done((bf16[2,768,128]{2,1,0:T(8,128)(2,1)S(1)}, bf16[2,768,128]{2,1,0:T(8,128)(2,1)S(1)}, u32[]{:S(2)}, u32[]{:S(2)}) %collective-permute-start.9) | collective-permute-done | bytes 393248 | tf_op jit(solution)/shard_map/ppermute | solution.py:26
  69.1 15.6 %collective-permute-done.8.refs_1_ = bf16[2,128,768]{2,1,0:T(8,128)(2,1)S(1)} collective-permute-done((bf16[2,128,768]{2,1,0:T(8,128)(2,1)}, bf16[2,128,768]{2,1,0:T(8,128)(2,1)S(1)}, u32[]{:S(2)}, u32[]{:S(2)}) %collective-permute-start.8) | collective-permute-done | bytes 393248 | tf_op jit(solution)/shard_map/ppermute | solution.py:26
  87.2 4.8 %all-to-all-start.1 = ((bf16[8,768,128]{2,1,0:T(8,128)(2,1)}), bf16[8,768,128]{2,1,0:T(8,128)(2,1)}, u32[]{:S(2)}, u32[]{:S(2)}) async-start(bf16[8,768,128]{2,1,0:T(8,128)(2,1)} %get-tuple-element.135), calls=%async_computation.1 | async-start | bytes 3145728 | tf_op jit(solution)/shard_map/all_to_all | solution.py:152
  100.1 4.0 %collective-permute-done.16.refs_3_ = bf16[12,128,128]{2,1,0:T(8,128)(2,1)S(1)} collective-permute-done((bf16[12,128,128]{2,1,0:T(8,128)(2,1)S(1)}, bf16[12,128,128]{2,1,0:T(8,128)(2,1)S(1)}, u32[]{:S(2)}, u32[]{:S(2)}) %collective-permute-start.16) | collective-permute-done | bytes 393248 | tf_op jit(solution)/shard_map/ppermute | solution.py:26
  104.0 4.5 %shard_map.90.ham_t_ref = bf16[2048,768]{1,0:T(8,128)(2,1)} custom-call(s32[2]{0:T(128)S(1)} %pad_add_fusion.ids, s32[3,16,64]{2,1,0:T(8,128)S(1)} %copy-done.8, s32[16]{0:T(128)S(1)} %copy-done.9, bf16[12,128,128]{2,1,0:T(8,128)(2,1)S(1)} %pad_maximum_fusion.refs_0_, bf16[12,128,128]{2,1,0:T(8,128)(2,1)S(1)} %collective-permute-done.10.refs_1_, ...), custom_call_target="tpu_custom_call" | custom-call | flops 4194304 | bytes 5242880 | tf_op jit(solution)/shard_map/pallas_call | solution.py:55
  110.1 5.0 %collective-permute-done.13.refs_5_ = bf16[2,128,768]{2,1,0:T(8,128)(2,1)S(1)} collective-permute-done((bf16[2,128,768]{2,1,0:T(8,128)(2,1)}, bf16[2,128,768]{2,1,0:T(8,128)(2,1)S(1)}, u32[]{:S(2)}, u32[]{:S(2)}) %collective-permute-start.13) | collective-permute-done | bytes 393248 | tf_op jit(solution)/shard_map/ppermute | solution.py:26
  115.2 5.0 %collective-permute-done.15.refs_7_ = bf16[2,128,768]{2,1,0:T(8,128)(2,1)S(1)} collective-permute-done((bf16[2,128,768]{2,1,0:T(8,128)(2,1)}, bf16[2,128,768]{2,1,0:T(8,128)(2,1)S(1)}, u32[]{:S(2)}, u32[]{:S(2)}) %collective-permute-start.15) | collective-permute-done | bytes 393248 | tf_op jit(solution)/shard_map/ppermute | solution.py:26
  123.7 8.4 %shard_map.91.part_ref = f32[768,768]{1,0:T(8,128)S(1)} custom-call(bf16[2048,768]{1,0:T(8,128)(2,1)} %shard_map.90.ham_t_ref, bf16[768,2048]{1,0:T(8,128)(2,1)} %shard_map.87.ham_ref, f32[768,768]{1,0:T(8,128)} %refs_10_.1, f32[768,1]{1,0:T(8,128)} %copy.15.dr_ref, f32[1,768]{1,0:T(1,128)} %reshape.11.dc_ref, ...), custom_call_target="tpu_custom_call" | custom-call | flops 4227858432 | bytes 20971520 | tf_op jit(solution)/shard_map/pallas_call | solution.py:55
  132.6 4.4 %shard_map.92 = (f32[768,768]{1,0:T(8,128)}, bf16[2,128,768]{2,1,0:T(8,128)(2,1)}, bf16[2,768,128]{2,1,0:T(8,128)(2,1)}, bf16[1,128,768]{2,1,0:T(8,128)(2,1)}, b...) custom-call(s32[2]{0:T(128)S(1)} %pad_add_fusion.ids, ...), custom_call_target="tpu_custom_call" | custom-call | flops 603979776 | bytes 6291456 | tf_op jit(solution)/shard_map/pallas_call | solution.py:55
  137.0 4.9 %all-to-all-start.2 = ((bf16[8,768,128]{2,1,0:T(8,128)(2,1)}), bf16[8,768,128]{2,1,0:T(8,128)(2,1)S(1)}, u32[]{:S(2)}, u32[]{:S(2)}) async-start(bf16[8,768,128]{2,1,0:T(8,128)(2,1)} %get-tuple-element.179), calls=%async_computation.2 | async-start | bytes 3145728 | tf_op jit(solution)/shard_map/all_to_all | solution.py:152
  150.8 15.6 %collective-permute-done.22.refs_2_ = bf16[2,768,128]{2,1,0:T(8,128)(2,1)S(1)} collective-permute-done((bf16[2,768,128]{2,1,0:T(8,128)(2,1)S(1)}, bf16[2,768,128]{2,1,0:T(8,128)(2,1)S(1)}, u32[]{:S(2)}, u32[]{:S(2)}) %collective-permute-start.22) | collective-permute-done | bytes 393248 | tf_op jit(solution)/shard_map/ppermute | solution.py:26
  166.4 14.7 %collective-permute-done.21.refs_1_ = bf16[2,128,768]{2,1,0:T(8,128)(2,1)S(1)} collective-permute-done((bf16[2,128,768]{2,1,0:T(8,128)(2,1)S(1)}, bf16[2,128,768]{2,1,0:T(8,128)(2,1)S(1)}, u32[]{:S(2)}, u32[]{:S(2)}) %collective-permute-start.21) | collective-permute-done | bytes 393248 | tf_op jit(solution)/shard_map/ppermute | solution.py:26
  184.8 4.8 %all-to-all-start.3 = ((bf16[8,768,128]{2,1,0:T(8,128)(2,1)}), bf16[8,768,128]{2,1,0:T(8,128)(2,1)S(1)}, u32[]{:S(2)}, u32[]{:S(2)}) async-start(bf16[8,768,128]{2,1,0:T(8,128)(2,1)} %get-tuple-element.190), calls=%async_computation.3 | async-start | bytes 3145728 | tf_op jit(solution)/shard_map/all_to_all | solution.py:152
  197.2 5.7 %collective-permute-done.25.refs_0_ = bf16[2,128,768]{2,1,0:T(8,128)(2,1)S(1)} collective-permute-done((bf16[2,128,768]{2,1,0:T(8,128)(2,1)}, bf16[2,128,768]{2,1,0:T(8,128)(2,1)S(1)}, u32[]{:S(2)}, u32[]{:S(2)}) %collective-permute-start.25) | collective-permute-done | bytes 393248 | tf_op jit(solution)/shard_map/ppermute | solution.py:26
  204.6 13.0 %collective-permute-done.29.refs_3_ = bf16[1,128,768]{2,1,0:T(8,128)(2,1)S(1)} collective-permute-done((bf16[1,128,768]{2,1,0:T(8,128)(2,1)}, bf16[1,128,768]{2,1,0:T(8,128)(2,1)S(1)}, u32[]{:S(2)}, u32[]{:S(2)}) %collective-permute-start.29) | collective-permute-done | bytes 196640 | tf_op jit(solution)/shard_map/ppermute | solution.py:26
  222.8 9.0 %shard_map.95.part_ref = f32[768,768]{1,0:T(8,128)S(1)} custom-call(bf16[2048,768]{1,0:T(8,128)(2,1)} %shard_map.90.ham_t_ref, bf16[768,2048]{1,0:T(8,128)(2,1)} %shard_map.87.ham_ref, f32[768,768]{1,0:T(8,128)} %get-tuple-element.104.x_ref, f32[768,1]{1,0:T(8,128)} %copy.15.dr_ref, f32[1,768]{1,0:T(1,128)} %reshape.11.dc_ref, ...), custom_call_target="tpu_custom_call" | custom-call | flops 4227858432 | bytes 20971520 | tf_op jit(solution)/shard_map/pallas_call | solution.py:55
  231.9 3.4 %shard_map.96 = f32[768,768]{1,0:T(8,128)} custom-call(s32[2]{0:T(128)S(1)} %pad_add_fusion.ids, s32[16,2]{1,0:T(8,128)S(1)} %copy.16.hot, s32[16,16]{1,0:T(8,128)S(1)} %copy-done.5, f32[768,768]{1,0:T(8,128)S(1)} %shard_map.95.part_ref, bf16[768,2048]{1,0:T(8,128)(2,1)S(1)} %copy-done.1, bf16[1,128,768]{2,1,0:T(8,128)(2,1)S(1)} %copy-done.7, ...), custom_call_target="tpu_custom_call" | custom-call | flops 603979776 | bytes 6291456 | tf_op jit(solution)/shard_map/pallas_call | solution.py:55
  (126 shorter events, 58.3 us)
Async XLA Ops:
  11.7 19.7 %collective-permute-start.3 = (bf16[3,128,128]{2,1,0:T(8,128)(2,1)S(1)}, bf16[3,128,128]{2,1,0:T(8,128)(2,1)S(1)}, u32[]{:S(2)}, u32[]{:S(2)}) collective-permute-start(bf16[3,128,128]{2,1,0:T(8,128)(2,1)S(1)} %collective-permute-done), channel_id=1, source_target_pairs={{0,192},{1,193},{2,194},{3,195},{4,196},{5,197},{6,198},{7,199},{8... | collective-permute-start | bytes 294920 | tf_op jit(solution)/shard_map/ppermute | solution.py:26
  39.7 47.5 %all-to-all-start = ((bf16[8,768,128]{2,1,0:T(8,128)(2,1)}), bf16[8,768,128]{2,1,0:T(8,128)(2,1)}, u32[]{:S(2)}, u32[]{:S(2)}) async-start(bf16[8,768,128]{2,1,0:T(8,128)(2,1)} %get-tuple-element.124), calls=%async_computation | async-start | bytes 3145728 | tf_op jit(solution)/shard_map/all_to_all | solution.py:152
  44.6 24.4 %collective-permute-start.9 = (bf16[2,768,128]{2,1,0:T(8,128)(2,1)S(1)}, bf16[2,768,128]{2,1,0:T(8,128)(2,1)S(1)}, u32[]{:S(2)}, u32[]{:S(2)}) collective-permute-start(bf16[2,768,128]{2,1,0:T(8,128)(2,1)S(1)} %copy-done.23), channel_id=1, source_target_pairs={{0,8},{1,9},{2,10},{3,11},{4,12},{5,13},{6,14},{7,15},{8,0},{9,1},... | collective-permute-start | bytes 1179656 | tf_op jit(solution)/shard_map/ppermute | solution.py:26
  49.8 34.9 %collective-permute-start.8 = (bf16[2,128,768]{2,1,0:T(8,128)(2,1)}, bf16[2,128,768]{2,1,0:T(8,128)(2,1)S(1)}, u32[]{:S(2)}, u32[]{:S(2)}) collective-permute-start(bf16[2,128,768]{2,1,0:T(8,128)(2,1)} %get-tuple-element.126), channel_id=1, source_target_pairs={{0,128},{1,129},{2,130},{3,131},{4,132},{5,133},{6,134},{7,135},{8... | collective-permute-start | bytes 1179656 | tf_op jit(solution)/shard_map/ppermute | solution.py:26
  49.8 34.9 %collective-permute-start.7 = (bf16[2,128,768]{2,1,0:T(8,128)(2,1)}, bf16[2,128,768]{2,1,0:T(8,128)(2,1)S(1)}, u32[]{:S(2)}, u32[]{:S(2)}) collective-permute-start(bf16[2,128,768]{2,1,0:T(8,128)(2,1)} %get-tuple-element.126), channel_id=1, source_target_pairs={{0,64},{1,65},{2,66},{3,67},{4,68},{5,69},{6,70},{7,71},{8,72},{9,... | collective-permute-start | bytes 1179656 | tf_op jit(solution)/shard_map/ppermute | solution.py:26
  50.8 36.5 %collective-permute-start.11 = (bf16[12,128,128]{2,1,0:T(8,128)(2,1)S(1)}, bf16[12,128,128]{2,1,0:T(8,128)(2,1)S(1)}, u32[]{:S(2)}, u32[]{:S(2)}) collective-permute-start(bf16[12,128,128]{2,1,0:T(8,128)(2,1)S(1)} %pad_maximum_fusion.refs_0_), channel_id=1, source_target_pairs={{0,32},{1,33},{2,34},{3,35},{4,36},{5,37},{6,38},{7,39},{8,40},{9,... | collective-permute-start | bytes 1179656 | tf_op jit(solution)/shard_map/ppermute | solution.py:26
  52.3 34.9 %collective-permute-start.10 = (bf16[12,128,128]{2,1,0:T(8,128)(2,1)S(1)}, bf16[12,128,128]{2,1,0:T(8,128)(2,1)S(1)}, u32[]{:S(2)}, u32[]{:S(2)}) collective-permute-start(bf16[12,128,128]{2,1,0:T(8,128)(2,1)S(1)} %pad_maximum_fusion.refs_0_), channel_id=1, source_target_pairs={{0,16},{1,17},{2,18},{3,19},{4,20},{5,21},{6,22},{7,23},{8,24},{9,... | collective-permute-start | bytes 1179656 | tf_op jit(solution)/shard_map/ppermute | solution.py:26
  87.2 32.9 %all-to-all-start.1 = ((bf16[8,768,128]{2,1,0:T(8,128)(2,1)}), bf16[8,768,128]{2,1,0:T(8,128)(2,1)}, u32[]{:S(2)}, u32[]{:S(2)}) async-start(bf16[8,768,128]{2,1,0:T(8,128)(2,1)} %get-tuple-element.135), calls=%async_computation.1 | async-start | bytes 3145728 | tf_op jit(solution)/shard_map/all_to_all | solution.py:152
  92.7 15.8 %collective-permute-start.12 = (bf16[2,128,768]{2,1,0:T(8,128)(2,1)}, bf16[2,128,768]{2,1,0:T(8,128)(2,1)S(1)}, u32[]{:S(2)}, u32[]{:S(2)}) collective-permute-start(bf16[2,128,768]{2,1,0:T(8,128)(2,1)} %get-tuple-element.126), channel_id=1, source_target_pairs={{0,192},{1,193},{2,194},{3,195},{4,196},{5,197},{6,198},{7,199},{8... | collective-permute-start | bytes 1179656 | tf_op jit(solution)/shard_map/ppermute | solution.py:26
  94.7 20.5 %collective-permute-start.13 = (bf16[2,128,768]{2,1,0:T(8,128)(2,1)}, bf16[2,128,768]{2,1,0:T(8,128)(2,1)S(1)}, u32[]{:S(2)}, u32[]{:S(2)}) collective-permute-start(bf16[2,128,768]{2,1,0:T(8,128)(2,1)} %get-tuple-element.132), channel_id=1, source_target_pairs={{0,16},{1,17},{2,18},{3,19},{4,20},{5,21},{6,22},{7,23},{8,24},{9,... | collective-permute-start | bytes 1179656 | tf_op jit(solution)/shard_map/ppermute | solution.py:26
  96.5 18.7 %collective-permute-start.14 = (bf16[2,128,768]{2,1,0:T(8,128)(2,1)}, bf16[2,128,768]{2,1,0:T(8,128)(2,1)S(1)}, u32[]{:S(2)}, u32[]{:S(2)}) collective-permute-start(bf16[2,128,768]{2,1,0:T(8,128)(2,1)} %get-tuple-element.133), channel_id=1, source_target_pairs={{0,32},{1,33},{2,34},{3,35},{4,36},{5,37},{6,38},{7,39},{8,40},{9,... | collective-permute-start | bytes 1179656 | tf_op jit(solution)/shard_map/ppermute | solution.py:26
  96.5 23.7 %collective-permute-start.15 = (bf16[2,128,768]{2,1,0:T(8,128)(2,1)}, bf16[2,128,768]{2,1,0:T(8,128)(2,1)S(1)}, u32[]{:S(2)}, u32[]{:S(2)}) collective-permute-start(bf16[2,128,768]{2,1,0:T(8,128)(2,1)} %get-tuple-element.134), channel_id=1, source_target_pairs={{0,48},{1,49},{2,50},{3,51},{4,52},{5,53},{6,54},{7,55},{8,56},{9,... | collective-permute-start | bytes 1179656 | tf_op jit(solution)/shard_map/ppermute | solution.py:26
  137.0 46.6 %all-to-all-start.2 = ((bf16[8,768,128]{2,1,0:T(8,128)(2,1)}), bf16[8,768,128]{2,1,0:T(8,128)(2,1)S(1)}, u32[]{:S(2)}, u32[]{:S(2)}) async-start(bf16[8,768,128]{2,1,0:T(8,128)(2,1)} %get-tuple-element.179), calls=%async_computation.2 | async-start | bytes 3145728 | tf_op jit(solution)/shard_map/all_to_all | solution.py:152
  142.0 24.4 %collective-permute-start.22 = (bf16[2,768,128]{2,1,0:T(8,128)(2,1)S(1)}, bf16[2,768,128]{2,1,0:T(8,128)(2,1)S(1)}, u32[]{:S(2)}, u32[]{:S(2)}) collective-permute-start(bf16[2,768,128]{2,1,0:T(8,128)(2,1)S(1)} %copy-done.25), channel_id=1, source_target_pairs={{0,8},{1,9},{2,10},{3,11},{4,12},{5,13},{6,14},{7,15},{8,0},{9,1},... | collective-permute-start | bytes 1179656 | tf_op jit(solution)/shard_map/ppermute | solution.py:26
  145.2 35.9 %collective-permute-start.21 = (bf16[2,128,768]{2,1,0:T(8,128)(2,1)S(1)}, bf16[2,128,768]{2,1,0:T(8,128)(2,1)S(1)}, u32[]{:S(2)}, u32[]{:S(2)}) collective-permute-start(bf16[2,128,768]{2,1,0:T(8,128)(2,1)S(1)} %copy-done.24), channel_id=1, source_target_pairs={{0,128},{1,129},{2,130},{3,131},{4,132},{5,133},{6,134},{7,135},{8... | collective-permute-start | bytes 1179656 | tf_op jit(solution)/shard_map/ppermute | solution.py:26
  146.3 34.8 %collective-permute-start.20 = (bf16[2,128,768]{2,1,0:T(8,128)(2,1)S(1)}, bf16[2,128,768]{2,1,0:T(8,128)(2,1)S(1)}, u32[]{:S(2)}, u32[]{:S(2)}) collective-permute-start(bf16[2,128,768]{2,1,0:T(8,128)(2,1)S(1)} %copy-done.24), channel_id=1, source_target_pairs={{0,64},{1,65},{2,66},{3,67},{4,68},{5,69},{6,70},{7,71},{8,72},{9,... | collective-permute-start | bytes 1179656 | tf_op jit(solution)/shard_map/ppermute | solution.py:26
  147.2 36.4 %collective-permute-start.23 = (bf16[1,128,768]{2,1,0:T(8,128)(2,1)S(1)}, bf16[1,128,768]{2,1,0:T(8,128)(2,1)S(1)}, u32[]{:S(2)}, u32[]{:S(2)}) collective-permute-start(bf16[1,128,768]{2,1,0:T(8,128)(2,1)S(1)} %copy-done.27), channel_id=1, source_target_pairs={{0,16},{1,17},{2,18},{3,19},{4,20},{5,21},{6,22},{7,23},{8,24},{9,... | collective-permute-start | bytes 589832 | tf_op jit(solution)/shard_map/ppermute | solution.py:26
  149.2 34.5 %collective-permute-start.24 = (bf16[1,128,768]{2,1,0:T(8,128)(2,1)S(1)}, bf16[1,128,768]{2,1,0:T(8,128)(2,1)}, u32[]{:S(2)}, u32[]{:S(2)}) collective-permute-start(bf16[1,128,768]{2,1,0:T(8,128)(2,1)S(1)} %copy-done.26), channel_id=1, source_target_pairs={{0,32},{1,33},{2,34},{3,35},{4,36},{5,37},{6,38},{7,39},{8,40},{9,... | collective-permute-start | bytes 589832 | tf_op jit(solution)/shard_map/ppermute | solution.py:26
  184.8 32.8 %all-to-all-start.3 = ((bf16[8,768,128]{2,1,0:T(8,128)(2,1)}), bf16[8,768,128]{2,1,0:T(8,128)(2,1)S(1)}, u32[]{:S(2)}, u32[]{:S(2)}) async-start(bf16[8,768,128]{2,1,0:T(8,128)(2,1)} %get-tuple-element.190), calls=%async_computation.3 | async-start | bytes 3145728 | tf_op jit(solution)/shard_map/all_to_all | solution.py:152
  192.0 25.6 %collective-permute-start.26 = (bf16[2,128,768]{2,1,0:T(8,128)(2,1)}, bf16[2,128,768]{2,1,0:T(8,128)(2,1)S(1)}, u32[]{:S(2)}, u32[]{:S(2)}) collective-permute-start(bf16[2,128,768]{2,1,0:T(8,128)(2,1)} %get-tuple-element.187), channel_id=1, source_target_pairs={{0,16},{1,17},{2,18},{3,19},{4,20},{5,21},{6,22},{7,23},{8,24},{9,... | collective-permute-start | bytes 1179656 | tf_op jit(solution)/shard_map/ppermute | solution.py:26
  193.1 24.5 %collective-permute-start.27 = (bf16[2,128,768]{2,1,0:T(8,128)(2,1)}, bf16[2,128,768]{2,1,0:T(8,128)(2,1)S(1)}, u32[]{:S(2)}, u32[]{:S(2)}) collective-permute-start(bf16[2,128,768]{2,1,0:T(8,128)(2,1)} %get-tuple-element.188), channel_id=1, source_target_pairs={{0,32},{1,33},{2,34},{3,35},{4,36},{5,37},{6,38},{7,39},{8,40},{9,... | collective-permute-start | bytes 1179656 | tf_op jit(solution)/shard_map/ppermute | solution.py:26
  195.9 21.8 %collective-permute-start.28 = (bf16[2,128,768]{2,1,0:T(8,128)(2,1)}, bf16[2,128,768]{2,1,0:T(8,128)(2,1)S(1)}, u32[]{:S(2)}, u32[]{:S(2)}) collective-permute-start(bf16[2,128,768]{2,1,0:T(8,128)(2,1)} %get-tuple-element.189), channel_id=1, source_target_pairs={{0,48},{1,49},{2,50},{3,51},{4,52},{5,53},{6,54},{7,55},{8,56},{9,... | collective-permute-start | bytes 1179656 | tf_op jit(solution)/shard_map/ppermute | solution.py:26
  196.8 20.8 %collective-permute-start.29 = (bf16[1,128,768]{2,1,0:T(8,128)(2,1)}, bf16[1,128,768]{2,1,0:T(8,128)(2,1)S(1)}, u32[]{:S(2)}, u32[]{:S(2)}) collective-permute-start(bf16[1,128,768]{2,1,0:T(8,128)(2,1)} %get-tuple-element.194), channel_id=1, source_target_pairs={{0,48},{1,49},{2,50},{3,51},{4,52},{5,53},{6,54},{7,55},{8,56},{9,... | collective-permute-start | bytes 589832 | tf_op jit(solution)/shard_map/ppermute | solution.py:26
  217.7 14.1 %collective-permute-start.30 = (bf16[1,128,768]{2,1,0:T(8,128)(2,1)}, bf16[1,128,768]{2,1,0:T(8,128)(2,1)S(1)}, u32[]{:S(2)}, u32[]{:S(2)}) collective-permute-start(bf16[1,128,768]{2,1,0:T(8,128)(2,1)} %get-tuple-element.207), channel_id=1, source_target_pairs={{0,16},{1,17},{2,18},{3,19},{4,20},{5,21},{6,22},{7,23},{8,24},{9,... | collective-permute-start | bytes 589832 | tf_op jit(solution)/shard_map/ppermute | solution.py:26
  (41 other events, 396.7 us)

commit v5 on v4

--- a/solution.py
+++ b/solution.py
@@ -45,6 +45,10 @@
 
 def barrier(*values):
     return lax.optimization_barrier(values)
+
+
+def after(value, earlier):
+    return barrier(value, earlier)[0]
 
 
 def start(block):
@@ -320,12 +324,16 @@
 
     piece = lax.dynamic_slice_in_dim(ham_blocks, col_index * 3, 3).transpose(0, 2, 1)
     piece = permute(piece, mirror)
-    pieces = [piece] + [permute(piece, z_xor(n)) for n in (1, 2, 3)]
     row, col, *sends = pack(ids, hot, sel, start_vector)
+    zh = permute(col, zh_flip)
+    piece, row, sends = barrier(piece, row, sends)
+    near = [sends[0]] + [permute(sends[n], x_shift(n)) for n in (1, 2)]
+    near.append(permute(after(sends[3], near[2]), x_shift(3)))
+    pieces = [piece, permute(after(piece, near[1]), z_xor(1))]
+    pieces += [permute(piece, z_xor(n)) for n in (2, 3)]
     ham = dense(ids, lists, counts, (ham_blocks,), False)
-    near = over_x(sends[:4])
-    quarter, row, col, sends, near, ham, dr, dc = barrier(
-        jnp.concatenate(pieces), row, col, sends, near, ham, dr, dc
+    quarter, row, zh, sends, near, ham, dr, dc = barrier(
+        jnp.concatenate(pieces), row, zh, sends, near, ham, dr, dc
     )
     ham_t = None
     outs = []
@@ -334,19 +342,16 @@
         first = step == 0
         z1 = permute(row, z_xor(1))
         z2 = permute(row, z_xor(2))
-        zh = permute(col, zh_flip)
         yk0 = over_yk(sends[4])
         if first:
-            hams = [quarter] + [permute(quarter, x_shift(n)) for n in (1, 2)]
-            sends = next_slabs(ids, sel, [z1, z2], (1, 2), zh)
-            row, sends, near, yk0, hams = barrier(row, sends, near, yk0, hams)
-            hams.append(permute(quarter, x_shift(3)))
+            hams = [quarter] + [permute(quarter, x_shift(n)) for n in (1, 2, 3)]
         else:
-            last = sends[3]
+            zh = permute(col, zh_flip)
             near = [sends[0]] + [permute(sends[n], x_shift(n)) for n in (1, 2)]
-            sends = next_slabs(ids, sel, [z1, z2], (1, 2), zh)
-            row, sends, near, yk0, last = barrier(row, sends, near, yk0, last)
-            near.append(permute(last, x_shift(3)))
+            near.append(permute(after(sends[3], near[1]), x_shift(3)))
+            hams = []
+        sends = next_slabs(ids, sel, [z1, z2], (1, 2), zh)
+        row, sends, near, yk0, hams = barrier(row, sends, near, yk0, hams)
         z3 = permute(row, z_xor(3))
         x12 = over_x(sends[:4])
         yk1 = over_yk(sends[4])

time: 236 us -> 223 us (0.945)
  waiting for transfers between devices: 98.5 us -> 86 us
    ppermute x33, waiting for transfers between devices: 98.5 us -> 86 us  [permute(): return lax.ppermute(value, axes, pairs)]
    unnamed x58 -> x60, local copies, waits for them, and re-layouts: 5.3 us -> 5.23 us
  transfers between devices with their start and end apart: 37 -> 37, of which waited for: 11 -> 16; matrix products, arithmetic and copies ran while one was open for 1% -> 1% of each run, Pallas kernels for 16% -> 17%
where the time goes in v5:
time: 223 us; the launch traced here: 222 us
  waiting for transfers between devices  86 us (39%)
  starting transfers between devices  81.4 us (37%)
  Pallas kernels  44.9 us (20%)
  local copies, waits for them, and re-layouts  8.5 us (4%)
    ppermute x33, waiting for transfers between devices, permute(): return lax.ppermute(value, axes, pairs)  86 us
    ppermute x33, starting transfers between devices, permute(): return lax.ppermute(value, axes, pairs)  61 us
    pallas_call x11, Pallas kernels, call(): pl.pallas_call(kernel, grid_spec=pltpu.PrefetchScalarGridSpec(num_scalar_...  44.9 us
    all_to_all x4, starting transfers between devices, over_yk(): return lax.all_to_all(chosen, ('y', 'k'), 0, 0, tiled=True)  20.4 us
    unnamed x60, local copies, waits for them, and re-layouts  5.23 us
  transfers between devices with their start and end apart: 37, of which 16 were waited for; matrix products, arithmetic and copies ran while one was open for 1% of the time, Pallas kernels for 17%

profile of v5, /device:TPU:8, one launch (start us, length us, event | category | flops | bytes accessed | tf_op | source)
XLA Modules:
  0.0 222.0 jit_solution(2762180142317952715)
XLA Ops:
  1.7 4.8 %collective-permute-start = (bf16[3,128,128]{2,1,0:T(8,128)(2,1)S(1)}, bf16[3,128,128]{2,1,0:T(8,128)(2,1)S(1)}, u32[]{:S(2)}, u32[]{:S(2)}) collective-permute-start(bf16[3,128,128]{2,1,0:T(8,128)(2,1)S(1)} %bitcast.3), channel_id=1, source_target_pairs={{0,0},{1,16},{2,32},{3,48},{4,64},{5,80},{6,96},{7,112},{8,128},{9... | collective-permute-start | bytes 294920 | tf_op jit(solution)/shard_map/ppermute | solution.py:26
  13.8 9.3 %collective-permute-start.5 = (bf16[2,768,128]{2,1,0:T(8,128)(2,1)}, bf16[2,768,128]{2,1,0:T(8,128)(2,1)S(1)}, u32[]{:S(2)}, u32[]{:S(2)}) collective-permute-start(bf16[2,768,128]{2,1,0:T(8,128)(2,1)} %get-tuple-element.127), channel_id=1, source_target_pairs={{0,8},{1,9},{2,10},{3,11},{4,12},{5,13},{6,14},{7,15},{8,0},{9,1},... | collective-permute-start | bytes 1179656 | tf_op jit(solution)/shard_map/ppermute | solution.py:26
  25.3 3.6 %collective-permute-start.3 = (bf16[3,128,128]{2,1,0:T(8,128)(2,1)S(1)}, bf16[3,128,128]{2,1,0:T(8,128)(2,1)S(1)}, u32[]{:S(2)}, u32[]{:S(2)}) collective-permute-start(bf16[3,128,128]{2,1,0:T(8,128)(2,1)S(1)} %collective-permute-done), channel_id=1, source_target_pairs={{0,128},{1,129},{2,130},{3,131},{4,132},{5,133},{6,134},{7,135},{8... | collective-permute-start | bytes 294920 | tf_op jit(solution)/shard_map/ppermute | solution.py:26
  32.1 4.2 %shard_map.87.ham_ref = bf16[768,2048]{1,0:T(8,128)(2,1)} custom-call(s32[2]{0:T(128)S(1)} %pad_add_fusion.ids, s32[3,16,64]{2,1,0:T(8,128)S(1)} %copy-done.8, s32[16]{0:T(128)S(1)} %copy-done.9, bf16[48,128,128]{2,1,0:T(8,128)(2,1)S(1)} %copy-done.3), custom_call_target="tpu_custom_call" | custom-call | flops 4194304 | bytes 5242880 | tf_op jit(solution)/shard_map/pallas_call | solution.py:59
  36.3 9.1 %collective-permute-done.4 = bf16[3,128,128]{2,1,0:T(8,128)(2,1)S(1)} collective-permute-done((bf16[3,128,128]{2,1,0:T(8,128)(2,1)S(1)}, bf16[3,128,128]{2,1,0:T(8,128)(2,1)S(1)}, u32[]{:S(2)}, u32[]{:S(2)}) %collective-permute-start.4) | collective-permute-done | bytes 98336 | tf_op jit(solution)/shard_map/ppermute | solution.py:26
  45.4 5.5 %collective-permute-done.3 = bf16[3,128,128]{2,1,0:T(8,128)(2,1)S(1)} collective-permute-done((bf16[3,128,128]{2,1,0:T(8,128)(2,1)S(1)}, bf16[3,128,128]{2,1,0:T(8,128)(2,1)S(1)}, u32[]{:S(2)}, u32[]{:S(2)}) %collective-permute-start.3) | collective-permute-done | bytes 98336 | tf_op jit(solution)/shard_map/ppermute | solution.py:26
  51.6 5.9 %all-to-all-start = ((bf16[8,768,128]{2,1,0:T(8,128)(2,1)}), bf16[8,768,128]{2,1,0:T(8,128)(2,1)}, u32[]{:S(2)}, u32[]{:S(2)}) async-start(bf16[8,768,128]{2,1,0:T(8,128)(2,1)} %get-tuple-element.144), calls=%async_computation | async-start | bytes 3145728 | tf_op jit(solution)/shard_map/all_to_all | solution.py:156
  57.7 3.5 %collective-permute-start.8 = (bf16[2,128,768]{2,1,0:T(8,128)(2,1)}, bf16[2,128,768]{2,1,0:T(8,128)(2,1)S(1)}, u32[]{:S(2)}, u32[]{:S(2)}) collective-permute-start(bf16[2,128,768]{2,1,0:T(8,128)(2,1)} %get-tuple-element.146), channel_id=1, source_target_pairs={{0,64},{1,65},{2,66},{3,67},{4,68},{5,69},{6,70},{7,71},{8,72},{9,... | collective-permute-start | bytes 1179656 | tf_op jit(solution)/shard_map/ppermute | solution.py:26
  64.0 14.3 %collective-permute-done.9.refs_1_ = bf16[2,128,768]{2,1,0:T(8,128)(2,1)S(1)} collective-permute-done((bf16[2,128,768]{2,1,0:T(8,128)(2,1)}, bf16[2,128,768]{2,1,0:T(8,128)(2,1)S(1)}, u32[]{:S(2)}, u32[]{:S(2)}) %collective-permute-start.9) | collective-permute-done | bytes 393248 | tf_op jit(solution)/shard_map/ppermute | solution.py:26
  82.2 4.8 %all-to-all-start.1 = ((bf16[8,768,128]{2,1,0:T(8,128)(2,1)}), bf16[8,768,128]{2,1,0:T(8,128)(2,1)}, u32[]{:S(2)}, u32[]{:S(2)}) async-start(bf16[8,768,128]{2,1,0:T(8,128)(2,1)} %get-tuple-element.155), calls=%async_computation.1 | async-start | bytes 3145728 | tf_op jit(solution)/shard_map/all_to_all | solution.py:156
  93.3 4.6 %shard_map.90.ham_t_ref = bf16[2048,768]{1,0:T(8,128)(2,1)} custom-call(s32[2]{0:T(128)S(1)} %pad_add_fusion.ids, s32[3,16,64]{2,1,0:T(8,128)S(1)} %copy-done.8, s32[16]{0:T(128)S(1)} %copy-done.9, bf16[12,128,128]{2,1,0:T(8,128)(2,1)S(1)} %pad_maximum_fusion.refs_0_, bf16[12,128,128]{2,1,0:T(8,128)(2,1)S(1)} %collective-permute-done.10.refs_1_, ...), custom_call_target="tpu_custom_call" | custom-call | flops 4194304 | bytes 5242880 | tf_op jit(solution)/shard_map/pallas_call | solution.py:59
  101.9 6.8 %collective-permute-done.14.refs_5_ = bf16[2,128,768]{2,1,0:T(8,128)(2,1)S(1)} collective-permute-done((bf16[2,128,768]{2,1,0:T(8,128)(2,1)}, bf16[2,128,768]{2,1,0:T(8,128)(2,1)S(1)}, u32[]{:S(2)}, u32[]{:S(2)}) %collective-permute-start.14) | collective-permute-done | bytes 393248 | tf_op jit(solution)/shard_map/ppermute | solution.py:26
  110.5 3.1 %collective-permute-start.18 = (bf16[1,128,768]{2,1,0:T(8,128)(2,1)}, bf16[1,128,768]{2,1,0:T(8,128)(2,1)S(1)}, u32[]{:S(2)}, u32[]{:S(2)}) collective-permute-start(bf16[1,128,768]{2,1,0:T(8,128)(2,1)} %get-tuple-element.180), channel_id=1, source_target_pairs={{0,32},{1,33},{2,34},{3,35},{4,36},{5,37},{6,38},{7,39},{8,40},{9,... | collective-permute-start | bytes 589832 | tf_op jit(solution)/shard_map/ppermute | solution.py:26
  113.8 8.4 %shard_map.91.part_ref = f32[768,768]{1,0:T(8,128)S(1)} custom-call(bf16[2048,768]{1,0:T(8,128)(2,1)} %shard_map.90.ham_t_ref, bf16[768,2048]{1,0:T(8,128)(2,1)} %shard_map.87.ham_ref, f32[768,768]{1,0:T(8,128)} %refs_10_.1, f32[768,1]{1,0:T(8,128)} %copy.15.dr_ref, f32[1,768]{1,0:T(1,128)} %reshape.11.dc_ref, ...), custom_call_target="tpu_custom_call" | custom-call | flops 4227858432 | bytes 20971520 | tf_op jit(solution)/shard_map/pallas_call | solution.py:59
  122.8 4.4 %shard_map.92 = (f32[768,768]{1,0:T(8,128)}, bf16[2,128,768]{2,1,0:T(8,128)(2,1)}, bf16[2,768,128]{2,1,0:T(8,128)(2,1)}, bf16[1,128,768]{2,1,0:T(8,128)(2,1)}, b...) custom-call(s32[2]{0:T(128)S(1)} %pad_add_fusion.ids, ...), custom_call_target="tpu_custom_call" | custom-call | flops 603979776 | bytes 6291456 | tf_op jit(solution)/shard_map/pallas_call | solution.py:59
  127.3 4.9 %all-to-all-start.2 = ((bf16[8,768,128]{2,1,0:T(8,128)(2,1)}), bf16[8,768,128]{2,1,0:T(8,128)(2,1)S(1)}, u32[]{:S(2)}, u32[]{:S(2)}) async-start(bf16[8,768,128]{2,1,0:T(8,128)(2,1)} %get-tuple-element.202), calls=%async_computation.2 | async-start | bytes 3145728 | tf_op jit(solution)/shard_map/all_to_all | solution.py:156
  141.3 15.0 %collective-permute-done.22.refs_2_ = bf16[2,768,128]{2,1,0:T(8,128)(2,1)S(1)} collective-permute-done((bf16[2,768,128]{2,1,0:T(8,128)(2,1)S(1)}, bf16[2,768,128]{2,1,0:T(8,128)(2,1)S(1)}, u32[]{:S(2)}, u32[]{:S(2)}) %collective-permute-start.22) | collective-permute-done | bytes 393248 | tf_op jit(solution)/shard_map/ppermute | solution.py:26
  156.4 15.3 %collective-permute-done.21.refs_1_ = bf16[2,128,768]{2,1,0:T(8,128)(2,1)S(1)} collective-permute-done((bf16[2,128,768]{2,1,0:T(8,128)(2,1)S(1)}, bf16[2,128,768]{2,1,0:T(8,128)(2,1)S(1)}, u32[]{:S(2)}, u32[]{:S(2)}) %collective-permute-start.21) | collective-permute-done | bytes 393248 | tf_op jit(solution)/shard_map/ppermute | solution.py:26
  175.5 4.8 %all-to-all-start.3 = ((bf16[8,768,128]{2,1,0:T(8,128)(2,1)}), bf16[8,768,128]{2,1,0:T(8,128)(2,1)S(1)}, u32[]{:S(2)}, u32[]{:S(2)}) async-start(bf16[8,768,128]{2,1,0:T(8,128)(2,1)} %get-tuple-element.212), calls=%async_computation.3 | async-start | bytes 3145728 | tf_op jit(solution)/shard_map/all_to_all | solution.py:156
  183.4 3.0 %collective-permute-start.28 = (bf16[2,128,768]{2,1,0:T(8,128)(2,1)}, bf16[2,128,768]{2,1,0:T(8,128)(2,1)S(1)}, u32[]{:S(2)}, u32[]{:S(2)}) collective-permute-start(bf16[2,128,768]{2,1,0:T(8,128)(2,1)} %get-tuple-element.210), channel_id=1, source_target_pairs={{0,32},{1,33},{2,34},{3,35},{4,36},{5,37},{6,38},{7,39},{8,40},{9,... | collective-permute-start | bytes 1179656 | tf_op jit(solution)/shard_map/ppermute | solution.py:26
  187.8 5.7 %collective-permute-done.26.refs_0_ = bf16[2,128,768]{2,1,0:T(8,128)(2,1)S(1)} collective-permute-done((bf16[2,128,768]{2,1,0:T(8,128)(2,1)}, bf16[2,128,768]{2,1,0:T(8,128)(2,1)S(1)}, u32[]{:S(2)}, u32[]{:S(2)}) %collective-permute-start.26) | collective-permute-done | bytes 393248 | tf_op jit(solution)/shard_map/ppermute | solution.py:26
  196.3 7.5 %collective-permute-done.28.refs_6_ = bf16[2,128,768]{2,1,0:T(8,128)(2,1)S(1)} collective-permute-done((bf16[2,128,768]{2,1,0:T(8,128)(2,1)}, bf16[2,128,768]{2,1,0:T(8,128)(2,1)S(1)}, u32[]{:S(2)}, u32[]{:S(2)}) %collective-permute-start.28) | collective-permute-done | bytes 393248 | tf_op jit(solution)/shard_map/ppermute | solution.py:26
  209.5 9.0 %shard_map.95.part_ref = f32[768,768]{1,0:T(8,128)S(1)} custom-call(bf16[2048,768]{1,0:T(8,128)(2,1)} %shard_map.90.ham_t_ref, bf16[768,2048]{1,0:T(8,128)(2,1)} %shard_map.87.ham_ref, f32[768,768]{1,0:T(8,128)} %get-tuple-element.115.x_ref, f32[768,1]{1,0:T(8,128)} %copy.15.dr_ref, f32[1,768]{1,0:T(1,128)} %reshape.11.dc_ref, ...), custom_call_target="tpu_custom_call" | custom-call | flops 4227858432 | bytes 20971520 | tf_op jit(solution)/shard_map/pallas_call | solution.py:59
  218.6 3.4 %shard_map.96 = f32[768,768]{1,0:T(8,128)} custom-call(s32[2]{0:T(128)S(1)} %pad_add_fusion.ids, s32[16,2]{1,0:T(8,128)S(1)} %copy.16.hot, s32[16,16]{1,0:T(8,128)S(1)} %copy-done.5, f32[768,768]{1,0:T(8,128)S(1)} %shard_map.95.part_ref, bf16[768,2048]{1,0:T(8,128)(2,1)S(1)} %copy-done.1, bf16[1,128,768]{2,1,0:T(8,128)(2,1)S(1)} %copy-done.7, ...), custom_call_target="tpu_custom_call" | custom-call | flops 603979776 | bytes 6291456 | tf_op jit(solution)/shard_map/pallas_call | solution.py:59
  (128 shorter events, 59.9 us)
Async XLA Ops:
  13.8 37.1 %collective-permute-start.5 = (bf16[2,768,128]{2,1,0:T(8,128)(2,1)}, bf16[2,768,128]{2,1,0:T(8,128)(2,1)S(1)}, u32[]{:S(2)}, u32[]{:S(2)}) collective-permute-start(bf16[2,768,128]{2,1,0:T(8,128)(2,1)} %get-tuple-element.127), channel_id=1, source_target_pairs={{0,8},{1,9},{2,10},{3,11},{4,12},{5,13},{6,14},{7,15},{8,0},{9,1},... | collective-permute-start | bytes 1179656 | tf_op jit(solution)/shard_map/ppermute | solution.py:26
  23.1 22.2 %collective-permute-start.4 = (bf16[3,128,128]{2,1,0:T(8,128)(2,1)S(1)}, bf16[3,128,128]{2,1,0:T(8,128)(2,1)S(1)}, u32[]{:S(2)}, u32[]{:S(2)}) collective-permute-start(bf16[3,128,128]{2,1,0:T(8,128)(2,1)S(1)} %collective-permute-done), channel_id=1, source_target_pairs={{0,192},{1,193},{2,194},{3,195},{4,196},{5,197},{6,198},{7,199},{8... | collective-permute-start | bytes 294920 | tf_op jit(solution)/shard_map/ppermute | solution.py:26
  25.3 25.5 %collective-permute-start.3 = (bf16[3,128,128]{2,1,0:T(8,128)(2,1)S(1)}, bf16[3,128,128]{2,1,0:T(8,128)(2,1)S(1)}, u32[]{:S(2)}, u32[]{:S(2)}) collective-permute-start(bf16[3,128,128]{2,1,0:T(8,128)(2,1)S(1)} %collective-permute-done), channel_id=1, source_target_pairs={{0,128},{1,129},{2,130},{3,131},{4,132},{5,133},{6,134},{7,135},{8... | collective-permute-start | bytes 294920 | tf_op jit(solution)/shard_map/ppermute | solution.py:26
  28.9 21.9 %collective-permute-start.2 = (bf16[3,128,128]{2,1,0:T(8,128)(2,1)S(1)}, bf16[3,128,128]{2,1,0:T(8,128)(2,1)S(1)}, u32[]{:S(2)}, u32[]{:S(2)}) collective-permute-start(bf16[3,128,128]{2,1,0:T(8,128)(2,1)S(1)} %collective-permute-done), channel_id=1, source_target_pairs={{0,64},{1,65},{2,66},{3,67},{4,68},{5,69},{6,70},{7,71},{8,72},{9,... | collective-permute-start | bytes 294920 | tf_op jit(solution)/shard_map/ppermute | solution.py:26
  29.0 22.0 %collective-permute-start.7 = (bf16[1,128,768]{2,1,0:T(8,128)(2,1)}, bf16[1,128,768]{2,1,0:T(8,128)(2,1)S(1)}, u32[]{:S(2)}, u32[]{:S(2)}) collective-permute-start(bf16[1,128,768]{2,1,0:T(8,128)(2,1)} %get-tuple-element.132), channel_id=1, source_target_pairs={{0,48},{1,49},{2,50},{3,51},{4,52},{5,53},{6,54},{7,55},{8,56},{9,... | collective-permute-start | bytes 589832 | tf_op jit(solution)/shard_map/ppermute | solution.py:26
  51.6 30.6 %all-to-all-start = ((bf16[8,768,128]{2,1,0:T(8,128)(2,1)}), bf16[8,768,128]{2,1,0:T(8,128)(2,1)}, u32[]{:S(2)}, u32[]{:S(2)}) async-start(bf16[8,768,128]{2,1,0:T(8,128)(2,1)} %get-tuple-element.144), calls=%async_computation | async-start | bytes 3145728 | tf_op jit(solution)/shard_map/all_to_all | solution.py:156
  57.5 20.8 %collective-permute-start.9 = (bf16[2,128,768]{2,1,0:T(8,128)(2,1)}, bf16[2,128,768]{2,1,0:T(8,128)(2,1)S(1)}, u32[]{:S(2)}, u32[]{:S(2)}) collective-permute-start(bf16[2,128,768]{2,1,0:T(8,128)(2,1)} %get-tuple-element.146), channel_id=1, source_target_pairs={{0,128},{1,129},{2,130},{3,131},{4,132},{5,133},{6,134},{7,135},{8... | collective-permute-start | bytes 1179656 | tf_op jit(solution)/shard_map/ppermute | solution.py:26
  57.7 20.7 %collective-permute-start.8 = (bf16[2,128,768]{2,1,0:T(8,128)(2,1)}, bf16[2,128,768]{2,1,0:T(8,128)(2,1)S(1)}, u32[]{:S(2)}, u32[]{:S(2)}) collective-permute-start(bf16[2,128,768]{2,1,0:T(8,128)(2,1)} %get-tuple-element.146), channel_id=1, source_target_pairs={{0,64},{1,65},{2,66},{3,67},{4,68},{5,69},{6,70},{7,71},{8,72},{9,... | collective-permute-start | bytes 1179656 | tf_op jit(solution)/shard_map/ppermute | solution.py:26
  61.2 19.7 %collective-permute-start.12 = (bf16[12,128,128]{2,1,0:T(8,128)(2,1)S(1)}, bf16[12,128,128]{2,1,0:T(8,128)(2,1)S(1)}, u32[]{:S(2)}, u32[]{:S(2)}) collective-permute-start(bf16[12,128,128]{2,1,0:T(8,128)(2,1)S(1)} %pad_maximum_fusion.refs_0_), channel_id=1, source_target_pairs={{0,48},{1,49},{2,50},{3,51},{4,52},{5,53},{6,54},{7,55},{8,56},{9,... | collective-permute-start | bytes 1179656 | tf_op jit(solution)/shard_map/ppermute | solution.py:26
  61.9 19.0 %collective-permute-start.11 = (bf16[12,128,128]{2,1,0:T(8,128)(2,1)S(1)}, bf16[12,128,128]{2,1,0:T(8,128)(2,1)S(1)}, u32[]{:S(2)}, u32[]{:S(2)}) collective-permute-start(bf16[12,128,128]{2,1,0:T(8,128)(2,1)S(1)} %pad_maximum_fusion.refs_0_), channel_id=1, source_target_pairs={{0,32},{1,33},{2,34},{3,35},{4,36},{5,37},{6,38},{7,39},{8,40},{9,... | collective-permute-start | bytes 1179656 | tf_op jit(solution)/shard_map/ppermute | solution.py:26
  64.0 18.2 %collective-permute-start.10 = (bf16[12,128,128]{2,1,0:T(8,128)(2,1)S(1)}, bf16[12,128,128]{2,1,0:T(8,128)(2,1)S(1)}, u32[]{:S(2)}, u32[]{:S(2)}) collective-permute-start(bf16[12,128,128]{2,1,0:T(8,128)(2,1)S(1)} %pad_maximum_fusion.refs_0_), channel_id=1, source_target_pairs={{0,16},{1,17},{2,18},{3,19},{4,20},{5,21},{6,22},{7,23},{8,24},{9,... | collective-permute-start | bytes 1179656 | tf_op jit(solution)/shard_map/ppermute | solution.py:26
  82.2 27.2 %all-to-all-start.1 = ((bf16[8,768,128]{2,1,0:T(8,128)(2,1)}), bf16[8,768,128]{2,1,0:T(8,128)(2,1)}, u32[]{:S(2)}, u32[]{:S(2)}) async-start(bf16[8,768,128]{2,1,0:T(8,128)(2,1)} %get-tuple-element.155), calls=%async_computation.1 | async-start | bytes 3145728 | tf_op jit(solution)/shard_map/all_to_all | solution.py:156
  88.1 20.7 %collective-permute-start.14 = (bf16[2,128,768]{2,1,0:T(8,128)(2,1)}, bf16[2,128,768]{2,1,0:T(8,128)(2,1)S(1)}, u32[]{:S(2)}, u32[]{:S(2)}) collective-permute-start(bf16[2,128,768]{2,1,0:T(8,128)(2,1)} %get-tuple-element.152), channel_id=1, source_target_pairs={{0,16},{1,17},{2,18},{3,19},{4,20},{5,21},{6,22},{7,23},{8,24},{9,... | collective-permute-start | bytes 1179656 | tf_op jit(solution)/shard_map/ppermute | solution.py:26
  88.5 20.3 %collective-permute-start.15 = (bf16[2,128,768]{2,1,0:T(8,128)(2,1)}, bf16[2,128,768]{2,1,0:T(8,128)(2,1)S(1)}, u32[]{:S(2)}, u32[]{:S(2)}) collective-permute-start(bf16[2,128,768]{2,1,0:T(8,128)(2,1)} %get-tuple-element.153), channel_id=1, source_target_pairs={{0,32},{1,33},{2,34},{3,35},{4,36},{5,37},{6,38},{7,39},{8,40},{9,... | collective-permute-start | bytes 1179656 | tf_op jit(solution)/shard_map/ppermute | solution.py:26
  90.1 19.3 %collective-permute-start.16 = (bf16[2,128,768]{2,1,0:T(8,128)(2,1)}, bf16[2,128,768]{2,1,0:T(8,128)(2,1)S(1)}, u32[]{:S(2)}, u32[]{:S(2)}) collective-permute-start(bf16[2,128,768]{2,1,0:T(8,128)(2,1)} %get-tuple-element.154), channel_id=1, source_target_pairs={{0,48},{1,49},{2,50},{3,51},{4,52},{5,53},{6,54},{7,55},{8,56},{9,... | collective-permute-start | bytes 1179656 | tf_op jit(solution)/shard_map/ppermute | solution.py:26
  127.3 46.9 %all-to-all-start.2 = ((bf16[8,768,128]{2,1,0:T(8,128)(2,1)}), bf16[8,768,128]{2,1,0:T(8,128)(2,1)S(1)}, u32[]{:S(2)}, u32[]{:S(2)}) async-start(bf16[8,768,128]{2,1,0:T(8,128)(2,1)} %get-tuple-element.202), calls=%async_computation.2 | async-start | bytes 3145728 | tf_op jit(solution)/shard_map/all_to_all | solution.py:156
  133.6 22.8 %collective-permute-start.22 = (bf16[2,768,128]{2,1,0:T(8,128)(2,1)S(1)}, bf16[2,768,128]{2,1,0:T(8,128)(2,1)S(1)}, u32[]{:S(2)}, u32[]{:S(2)}) collective-permute-start(bf16[2,768,128]{2,1,0:T(8,128)(2,1)S(1)} %copy-done.25), channel_id=1, source_target_pairs={{0,8},{1,9},{2,10},{3,11},{4,12},{5,13},{6,14},{7,15},{8,0},{9,1},... | collective-permute-start | bytes 1179656 | tf_op jit(solution)/shard_map/ppermute | solution.py:26
  136.3 35.4 %collective-permute-start.21 = (bf16[2,128,768]{2,1,0:T(8,128)(2,1)S(1)}, bf16[2,128,768]{2,1,0:T(8,128)(2,1)S(1)}, u32[]{:S(2)}, u32[]{:S(2)}) collective-permute-start(bf16[2,128,768]{2,1,0:T(8,128)(2,1)S(1)} %copy-done.24), channel_id=1, source_target_pairs={{0,128},{1,129},{2,130},{3,131},{4,132},{5,133},{6,134},{7,135},{8... | collective-permute-start | bytes 1179656 | tf_op jit(solution)/shard_map/ppermute | solution.py:26
  136.3 35.4 %collective-permute-start.20 = (bf16[2,128,768]{2,1,0:T(8,128)(2,1)S(1)}, bf16[2,128,768]{2,1,0:T(8,128)(2,1)S(1)}, u32[]{:S(2)}, u32[]{:S(2)}) collective-permute-start(bf16[2,128,768]{2,1,0:T(8,128)(2,1)S(1)} %copy-done.24), channel_id=1, source_target_pairs={{0,64},{1,65},{2,66},{3,67},{4,68},{5,69},{6,70},{7,71},{8,72},{9,... | collective-permute-start | bytes 1179656 | tf_op jit(solution)/shard_map/ppermute | solution.py:26
  138.1 36.1 %collective-permute-start.24 = (bf16[1,128,768]{2,1,0:T(8,128)(2,1)S(1)}, bf16[1,128,768]{2,1,0:T(8,128)(2,1)S(1)}, u32[]{:S(2)}, u32[]{:S(2)}) collective-permute-start(bf16[1,128,768]{2,1,0:T(8,128)(2,1)S(1)} %copy-done.27), channel_id=1, source_target_pairs={{0,32},{1,33},{2,34},{3,35},{4,36},{5,37},{6,38},{7,39},{8,40},{9,... | collective-permute-start | bytes 589832 | tf_op jit(solution)/shard_map/ppermute | solution.py:26
  140.4 33.8 %collective-permute-start.25 = (bf16[1,128,768]{2,1,0:T(8,128)(2,1)S(1)}, bf16[1,128,768]{2,1,0:T(8,128)(2,1)S(1)}, u32[]{:S(2)}, u32[]{:S(2)}) collective-permute-start(bf16[1,128,768]{2,1,0:T(8,128)(2,1)S(1)} %copy-done.26), channel_id=1, source_target_pairs={{0,48},{1,49},{2,50},{3,51},{4,52},{5,53},{6,54},{7,55},{8,56},{9,... | collective-permute-start | bytes 589832 | tf_op jit(solution)/shard_map/ppermute | solution.py:26
  175.5 28.9 %all-to-all-start.3 = ((bf16[8,768,128]{2,1,0:T(8,128)(2,1)}), bf16[8,768,128]{2,1,0:T(8,128)(2,1)S(1)}, u32[]{:S(2)}, u32[]{:S(2)}) async-start(bf16[8,768,128]{2,1,0:T(8,128)(2,1)} %get-tuple-element.212), calls=%async_computation.3 | async-start | bytes 3145728 | tf_op jit(solution)/shard_map/all_to_all | solution.py:156
  183.4 20.5 %collective-permute-start.28 = (bf16[2,128,768]{2,1,0:T(8,128)(2,1)}, bf16[2,128,768]{2,1,0:T(8,128)(2,1)S(1)}, u32[]{:S(2)}, u32[]{:S(2)}) collective-permute-start(bf16[2,128,768]{2,1,0:T(8,128)(2,1)} %get-tuple-element.210), channel_id=1, source_target_pairs={{0,32},{1,33},{2,34},{3,35},{4,36},{5,37},{6,38},{7,39},{8,40},{9,... | collective-permute-start | bytes 1179656 | tf_op jit(solution)/shard_map/ppermute | solution.py:26
  186.3 18.0 %collective-permute-start.29 = (bf16[2,128,768]{2,1,0:T(8,128)(2,1)}, bf16[2,128,768]{2,1,0:T(8,128)(2,1)S(1)}, u32[]{:S(2)}, u32[]{:S(2)}) collective-permute-start(bf16[2,128,768]{2,1,0:T(8,128)(2,1)} %get-tuple-element.211), channel_id=1, source_target_pairs={{0,48},{1,49},{2,50},{3,51},{4,52},{5,53},{6,54},{7,55},{8,56},{9,... | collective-permute-start | bytes 1179656 | tf_op jit(solution)/shard_map/ppermute | solution.py:26
  (42 other events, 458.5 us)

commit v6 on v5

--- a/solution.py
+++ b/solution.py
@@ -83,21 +83,13 @@
     return pl.BlockSpec(dims, lambda i, *_: (0,) * len(dims))
 
 
-send_shapes = (
-    [shape((2, B, T)), shape((2, T, B))] + [shape((1, B, T))] * 4 + [shape((8, T, B))]
-)
+send_shapes = [shape((2, B, T)), shape((2, T, B))] + [shape((1, B, T))] * 4
 
 
 def choose_rows(ids, sel, step, slabs_ref, refs, at=0):
     zl, x = ids[0] // 4, ids[0] % 4
     for n in range(4):
         refs[n][at] = slabs_ref[sel[zl * 4 + (x + n) % 4, (zl ^ step) * 4 + x]]
-
-
-def choose_cols(ids, sel, flip, slabs_ref, out_ref):
-    zh, q = ids[1] // 8, ids[1] ^ (8 * flip)
-    for i in range(8):
-        out_ref[i] = slabs_ref[sel[zh * 8 + i, q]]
 
 
 def pack_kernel(ids, hot, sel, x_ref, row_ref, col_ref, *refs):
@@ -105,8 +97,7 @@
     for h in range(2):
         row_ref[h] = x_ref[pl.ds(start(hot[r, h]), B), :].astype(bf16)
         col_ref[h] = x_ref[:, pl.ds(start(hot[c, h]), B)].astype(bf16)
-    choose_rows(ids, sel, 0, row_ref, refs[:4])
-    choose_cols(ids, sel, 0, col_ref, refs[4])
+    choose_rows(ids, sel, 0, row_ref, refs)
 
 
 def pack(ids, hot, sel, value):
@@ -123,26 +114,41 @@
     )
 
 
-def next_slabs(ids, sel, rows, steps, cols=None):
+def next_rows(ids, sel, rows, steps):
     count = len(rows)
 
     def kernel(ids, sel, *refs):
-        outs = refs[count + (cols is not None) :]
         for m in range(count):
-            choose_rows(ids, sel, steps[m], refs[m], outs[:4], m)
-        if cols is not None:
-            choose_cols(ids, sel, 1, refs[count], outs[4])
-
-    out_shapes = [shape((count, B, T))] * 4 + [shape((8, T, B))] * (cols is not None)
-    args = rows if cols is None else rows + [cols]
+            choose_rows(ids, sel, steps[m], refs[m], refs[count:], m)
+
     return call(
         kernel,
         (ids, sel),
         (1,),
-        [whole(arg.shape) for arg in args],
-        [whole(s.shape) for s in out_shapes],
-        out_shapes,
-        args,
+        [whole(arg.shape) for arg in rows],
+        [whole((count, B, T))] * 4,
+        [shape((count, B, T))] * 4,
+        rows,
+        moved=4 << 20,
+        room=32,
+    )
+
+
+def choose_cols(ids, sel, here, there):
+    def kernel(ids, sel, here_ref, there_ref, out_ref):
+        zh, q = ids[1] // 8, ids[1]
+        for i in range(8):
+            out_ref[2 * i] = here_ref[sel[zh * 8 + i, q]]
+            out_ref[2 * i + 1] = there_ref[sel[zh * 8 + i, q ^ 8]]
+
+    return call(
+        kernel,
+        (ids, sel),
+        (1,),
+        [whole(here.shape)] * 2,
+        whole((16, T, B)),
+        shape((16, T, B)),
+        (here, there),
         moved=4 << 20,
         room=32,
     )
@@ -221,11 +227,11 @@
 
 def first_products_kernel(second):
     def kernel(ham_t_ref, ham_ref, x_ref, dr_ref, dc_ref, *refs):
-        yk0_ref, yk1_ref = refs[8:10]
+        yk_ref = refs[8]
         out_ref, wide = refs[-2:]
-        for i in range(8):
-            wide[:, i * B : (i + 1) * B] = yk0_ref[i]
-            wide[:, (8 + i) * B : (9 + i) * B] = yk1_ref[i]
+        for i in range(16):
+            at = i % 2 * 8 + i // 2
+            wide[:, at * B : (at + 1) * B] = yk_ref[i]
         near = jnp.concatenate(
             [ref[0] for ref in refs[:4]] + [ref[m] for m in range(2) for ref in refs[4:8]], axis=0
         )
@@ -234,13 +240,13 @@
         )
         total = total + (dr_ref[...] + dc_ref[...] - center) * x_ref[...]
         if second:
-            total = total - refs[10][...] * (0.5 / scale)
+            total = total - refs[9][...] * (0.5 / scale)
         out_ref[...] = total
 
     return kernel
 
 
-def first_products(ham_t, ham, value, dr, dc, x0, x12, yk0, yk1, before=None):
+def first_products(ham_t, ham, value, dr, dc, x0, x12, yk, before=None):
     extra = () if before is None else (before,)
     return call(
         first_products_kernel(before is not None),
@@ -254,11 +260,11 @@
             whole((1, T)),
         ]
         + [whole(s.shape) for s in x0 + x12]
-        + [pl.BlockSpec((8, R, B), lambda i, *_: (0, i, 0))] * 2
+        + [pl.BlockSpec((16, R, B), lambda i, *_: (0, i, 0))]
         + [rows] * len(extra),
         rows,
         free_shape((T, T), f32),
-        (ham_t, ham, value, dr, dc, *x0, *x12, yk0, yk1, *extra),
+        (ham_t, ham, value, dr, dc, *x0, *x12, yk, *extra),
         scratch=[pltpu.VMEM((R, 2048), bf16)],
         flops=2 * T * T * 3584,
         moved=20 << 20,
@@ -286,8 +292,6 @@
             def _(h=h, block=block):
                 row_ref[h] = out_ref[pl.ds(start(block % 2), B), :].astype(bf16)
 
-        choose_cols(ids, sel, 0, col_ref, refs[11])
-
         @pl.when(i == T // R - 1)
         def _():
             choose_rows(ids, sel, 0, row_ref, refs[7:11])
@@ -299,7 +303,7 @@
     out_specs, out_shape = rows, shape((T, T), f32)
     if not second:
         out_specs = [rows, whole((2, B, T)), pl.BlockSpec((2, R, B), lambda i, *_: (0, i, 0))]
-        out_specs += [whole((1, B, T))] * 4 + [pl.BlockSpec((8, R, B), lambda i, *_: (0, i, 0))]
+        out_specs += [whole((1, B, T))] * 4
         out_shape = [out_shape] + send_shapes
     return call(
         finish_kernel(second),
@@ -332,36 +336,33 @@
     pieces = [piece, permute(after(piece, near[1]), z_xor(1))]
     pieces += [permute(piece, z_xor(n)) for n in (2, 3)]
     ham = dense(ids, lists, counts, (ham_blocks,), False)
-    quarter, row, zh, sends, near, ham, dr, dc = barrier(
-        jnp.concatenate(pieces), row, zh, sends, near, ham, dr, dc
+    quarter, row, col, zh, near, ham, dr, dc = barrier(
+        jnp.concatenate(pieces), row, col, zh, near, ham, dr, dc
     )
     ham_t = None
     outs = []
     value = start_vector
     for step in range(2):
         first = step == 0
+        if not first:
+            zh = permute(col, zh_flip)
+            near = over_x(sends)
+            row, col, zh, near = barrier(row, col, zh, near)
         z1 = permute(row, z_xor(1))
         z2 = permute(row, z_xor(2))
-        yk0 = over_yk(sends[4])
-        if first:
-            hams = [quarter] + [permute(quarter, x_shift(n)) for n in (1, 2, 3)]
-        else:
-            zh = permute(col, zh_flip)
-            near = [sends[0]] + [permute(sends[n], x_shift(n)) for n in (1, 2)]
-            near.append(permute(after(sends[3], near[1]), x_shift(3)))
-            hams = []
-        sends = next_slabs(ids, sel, [z1, z2], (1, 2), zh)
-        row, sends, near, yk0, hams = barrier(row, sends, near, yk0, hams)
+        yk = over_yk(choose_cols(ids, sel, col, zh))
+        hams = over_x([quarter] * 4) if first else []
+        far = next_rows(ids, sel, [z1, z2], (1, 2))
+        row, far, hams = barrier(row, far, hams)
         z3 = permute(row, z_xor(3))
-        x12 = over_x(sends[:4])
-        yk1 = over_yk(sends[4])
+        x12 = over_x(far)
         if first:
             ham_t = dense(ids, lists, counts, hams, True)
-        sends = next_slabs(ids, sel, [z3], (3,))
-        sends, x12, yk1, near, ham_t = barrier(sends, x12, yk1, near, ham_t)
-        x3 = over_x(sends)
+        far = next_rows(ids, sel, [z3], (3,))
+        far, x12, ham_t = barrier(far, x12, ham_t)
+        x3 = over_x(far)
         before = () if first else (start_vector,)
-        part = first_products(ham_t, ham, value, dr, dc, near, x12, yk0, yk1, *before)
+        part = first_products(ham_t, ham, value, dr, dc, near, x12, yk, *before)
         result = finish(ids, hot, sel, part, ham, x3, not first)
         if first:
             value, *sent = result

time: 223 us -> 219 us (0.982)
  waiting for transfers between devices: 86 us -> 77.1 us
  Pallas kernels: 44.9 us -> 49.8 us
    ppermute x33, starting transfers between devices: 61 us -> 70.6 us  [permute(): return lax.ppermute(value, axes, pairs)]
    all_to_all x4 -> x2, starting transfers between devices: 20.4 us -> 11.1 us  [over_yk(): return lax.all_to_all(chosen, ('y', 'k'), 0, 0, tiled=True)]
    ppermute x33, waiting for transfers between devices: 86 us -> 77.1 us  [permute(): return lax.ppermute(value, axes, pairs)]
    pallas_call x11 -> x13, Pallas kernels: 44.9 us -> 49.8 us  [call(): pl.pallas_call(kernel, grid_spec=pltpu.PrefetchScalarGridSpec(num_scalar_...]
    unnamed x60 -> x58, local copies, waits for them, and re-layouts: 5.23 us -> 5.08 us
  transfers between devices with their start and end apart: 37 -> 35, of which waited for: 16 -> 16; matrix products, arithmetic and copies ran while one was open for 1% -> 2% of each run, Pallas kernels for 17% -> 17%
where the time goes in v6:
time: 219 us; the launch traced here: 218 us
  starting transfers between devices  81.7 us (37%)
  waiting for transfers between devices  77.1 us (35%)
  Pallas kernels  49.8 us (23%)
  local copies, waits for them, and re-layouts  8.39 us (4%)
    ppermute x33, waiting for transfers between devices, permute(): return lax.ppermute(value, axes, pairs)  77.1 us
    ppermute x33, starting transfers between devices, permute(): return lax.ppermute(value, axes, pairs)  70.6 us
    pallas_call x13, Pallas kernels, call(): pl.pallas_call(kernel, grid_spec=pltpu.PrefetchScalarGridSpec(num_scalar_...  49.8 us
    all_to_all x2, starting transfers between devices, over_yk(): return lax.all_to_all(chosen, ('y', 'k'), 0, 0, tiled=True)  11.1 us
    unnamed x58, local copies, waits for them, and re-layouts  5.08 us
  transfers between devices with their start and end apart: 35, of which 16 were waited for; matrix products, arithmetic and copies ran while one was open for 2% of the time, Pallas kernels for 17%

profile of v6, /device:TPU:8, one launch (start us, length us, event | category | flops | bytes accessed | tf_op | source)
XLA Modules:
  0.0 218.0 jit_solution(1499402049975640390)
XLA Ops:
  1.7 4.8 %collective-permute-start = (bf16[3,128,128]{2,1,0:T(8,128)(2,1)S(1)}, bf16[3,128,128]{2,1,0:T(8,128)(2,1)S(1)}, u32[]{:S(2)}, u32[]{:S(2)}) collective-permute-start(bf16[3,128,128]{2,1,0:T(8,128)(2,1)S(1)} %bitcast.3), channel_id=1, source_target_pairs={{0,0},{1,16},{2,32},{3,48},{4,64},{5,80},{6,96},{7,112},{8,128},{9... | collective-permute-start | bytes 294920 | tf_op jit(solution)/shard_map/ppermute | solution.py:26
  12.7 9.9 %collective-permute-start.5 = (bf16[2,768,128]{2,1,0:T(8,128)(2,1)}, bf16[2,768,128]{2,1,0:T(8,128)(2,1)S(1)}, u32[]{:S(2)}, u32[]{:S(2)}) collective-permute-start(bf16[2,768,128]{2,1,0:T(8,128)(2,1)} %get-tuple-element.140.here_ref), channel_id=1, source_target_pairs={{0,8},{1,9},{2,10},{3,11},{4,12},{5,13},{6,14},{7,15},{8,0},{9,1},... | collective-permute-start | bytes 1179656 | tf_op jit(solution)/shard_map/ppermute | solution.py:26
  22.6 6.6 %collective-permute-start.4 = (bf16[3,128,128]{2,1,0:T(8,128)(2,1)S(1)}, bf16[3,128,128]{2,1,0:T(8,128)(2,1)S(1)}, u32[]{:S(2)}, u32[]{:S(2)}) collective-permute-start(bf16[3,128,128]{2,1,0:T(8,128)(2,1)S(1)} %collective-permute-done), channel_id=1, source_target_pairs={{0,192},{1,193},{2,194},{3,195},{4,196},{5,197},{6,198},{7,199},{8... | collective-permute-start | bytes 294920 | tf_op jit(solution)/shard_map/ppermute | solution.py:26
  33.5 5.0 %shard_map.87.ham_ref = bf16[768,2048]{1,0:T(8,128)(2,1)} custom-call(s32[2]{0:T(128)S(1)} %pad_add_fusion.ids, s32[3,16,64]{2,1,0:T(8,128)S(1)} %copy-done.10, s32[16]{0:T(128)S(1)} %copy-done.14, bf16[48,128,128]{2,1,0:T(8,128)(2,1)S(1)} %copy-done.3), custom_call_target="tpu_custom_call" | custom-call | flops 4194304 | bytes 5242880 | tf_op jit(solution)/shard_map/pallas_call | solution.py:59
  38.6 9.7 %collective-permute-done.3 = bf16[3,128,128]{2,1,0:T(8,128)(2,1)S(1)} collective-permute-done((bf16[3,128,128]{2,1,0:T(8,128)(2,1)S(1)}, bf16[3,128,128]{2,1,0:T(8,128)(2,1)S(1)}, u32[]{:S(2)}, u32[]{:S(2)}) %collective-permute-start.3) | collective-permute-done | bytes 98336 | tf_op jit(solution)/shard_map/ppermute | solution.py:26
  51.0 6.0 %all-to-all-start = ((bf16[16,768,128]{2,1,0:T(8,128)(2,1)}), bf16[16,768,128]{2,1,0:T(8,128)(2,1)}, u32[]{:S(2)}, u32[]{:S(2)}) async-start(bf16[16,768,128]{2,1,0:T(8,128)(2,1)} %shard_map.91), calls=%async_computation | async-start | bytes 6291456 | tf_op jit(solution)/shard_map/all_to_all | solution.py:162
  65.6 12.0 %collective-permute-done.8.refs_0_ = bf16[2,128,768]{2,1,0:T(8,128)(2,1)S(1)} collective-permute-done((bf16[2,128,768]{2,1,0:T(8,128)(2,1)}, bf16[2,128,768]{2,1,0:T(8,128)(2,1)S(1)}, u32[]{:S(2)}, u32[]{:S(2)}) %collective-permute-start.8) | collective-permute-done | bytes 393248 | tf_op jit(solution)/shard_map/ppermute | solution.py:26
  90.5 4.5 %shard_map.90.ham_t_ref = bf16[2048,768]{1,0:T(8,128)(2,1)} custom-call(s32[2]{0:T(128)S(1)} %pad_add_fusion.ids, s32[3,16,64]{2,1,0:T(8,128)S(1)} %copy-done.10, s32[16]{0:T(128)S(1)} %copy-done.14, bf16[12,128,128]{2,1,0:T(8,128)(2,1)S(1)} %pad_maximum_fusion.refs_0_, bf16[12,128,128]{2,1,0:T(8,128)(2,1)S(1)} %collective-permute-done.10.refs_1_, ...), custom_call_target="tpu_custom_call" | custom-call | flops 4194304 | bytes 5242880 | tf_op jit(solution)/shard_map/pallas_call | solution.py:59
  97.4 8.1 %collective-permute-done.15.refs_6_ = bf16[2,128,768]{2,1,0:T(8,128)(2,1)S(1)} collective-permute-done((bf16[2,128,768]{2,1,0:T(8,128)(2,1)}, bf16[2,128,768]{2,1,0:T(8,128)(2,1)S(1)}, u32[]{:S(2)}, u32[]{:S(2)}) %collective-permute-start.15) | collective-permute-done | bytes 393248 | tf_op jit(solution)/shard_map/ppermute | solution.py:26
  107.3 3.2 %collective-permute-start.18 = (bf16[1,128,768]{2,1,0:T(8,128)(2,1)}, bf16[1,128,768]{2,1,0:T(8,128)(2,1)}, u32[]{:S(2)}, u32[]{:S(2)}) collective-permute-start(bf16[1,128,768]{2,1,0:T(8,128)(2,1)} %get-tuple-element.144), channel_id=1, source_target_pairs={{0,32},{1,33},{2,34},{3,35},{4,36},{5,37},{6,38},{7,39},{8,40},{9,... | collective-permute-start | bytes 589832 | tf_op jit(solution)/shard_map/ppermute | solution.py:26
  110.6 8.4 %shard_map.92.part_ref = f32[768,768]{1,0:T(8,128)S(1)} custom-call(bf16[2048,768]{1,0:T(8,128)(2,1)} %shard_map.90.ham_t_ref, bf16[768,2048]{1,0:T(8,128)(2,1)} %shard_map.87.ham_ref, f32[768,768]{1,0:T(8,128)} %refs_9_.1, f32[768,1]{1,0:T(8,128)} %copy.15.dr_ref, f32[1,768]{1,0:T(1,128)} %reshape.11.dc_ref, ...), custom_call_target="tpu_custom_call" | custom-call | flops 4227858432 | bytes 20971520 | tf_op jit(solution)/shard_map/pallas_call | solution.py:59
  119.8 5.0 %shard_map.93 = (f32[768,768]{1,0:T(8,128)}, bf16[2,128,768]{2,1,0:T(8,128)(2,1)}, bf16[2,768,128]{2,1,0:T(8,128)(2,1)}, bf16[1,128,768]{2,1,0:T(8,128)(2,1)}, b...) custom-call(s32[2]{0:T(128)S(1)} %copy-done.12, s32[16,2]{1,0:T(8,128)S(1)} %copy.16.hot, ...), custom_call_target="tpu_custom_call" | custom-call | flops 603979776 | bytes 6291456 | tf_op jit(solution)/shard_map/pallas_call | solution.py:59
  133.2 5.2 %collective-permute-done.22.refs_2_ = bf16[1,128,768]{2,1,0:T(8,128)(2,1)S(1)} collective-permute-done((bf16[1,128,768]{2,1,0:T(8,128)(2,1)}, bf16[1,128,768]{2,1,0:T(8,128)(2,1)S(1)}, u32[]{:S(2)}, u32[]{:S(2)}) %collective-permute-start.22) | collective-permute-done | bytes 196640 | tf_op jit(solution)/shard_map/ppermute | solution.py:26
  138.4 5.7 %collective-permute-done.20.there_ref = bf16[2,768,128]{2,1,0:T(8,128)(2,1)S(1)} collective-permute-done((bf16[2,768,128]{2,1,0:T(8,128)(2,1)}, bf16[2,768,128]{2,1,0:T(8,128)(2,1)S(1)}, u32[]{:S(2)}, u32[]{:S(2)}) %collective-permute-start.20) | collective-permute-done | bytes 393248 | tf_op jit(solution)/shard_map/ppermute | solution.py:26
  147.8 5.0 %all-to-all-start.1 = ((bf16[16,768,128]{2,1,0:T(8,128)(2,1)}), bf16[16,768,128]{2,1,0:T(8,128)(2,1)}, u32[]{:S(2)}, u32[]{:S(2)}) async-start(bf16[16,768,128]{2,1,0:T(8,128)(2,1)} %shard_map.96), calls=%async_computation.1 | async-start | bytes 6291456 | tf_op jit(solution)/shard_map/all_to_all | solution.py:162
  152.8 5.4 %collective-permute-start.25 = (bf16[2,128,768]{2,1,0:T(8,128)(2,1)S(1)}, bf16[2,128,768]{2,1,0:T(8,128)(2,1)S(1)}, u32[]{:S(2)}, u32[]{:S(2)}) collective-permute-start(bf16[2,128,768]{2,1,0:T(8,128)(2,1)S(1)} %copy-done.27), channel_id=1, source_target_pairs={{0,128},{1,129},{2,130},{3,131},{4,132},{5,133},{6,134},{7,135},{8... | collective-permute-start | bytes 1179656 | tf_op jit(solution)/shard_map/ppermute | solution.py:26
  158.2 14.2 %collective-permute-done.24.refs_0_ = bf16[2,128,768]{2,1,0:T(8,128)(2,1)S(1)} collective-permute-done((bf16[2,128,768]{2,1,0:T(8,128)(2,1)S(1)}, bf16[2,128,768]{2,1,0:T(8,128)(2,1)S(1)}, u32[]{:S(2)}, u32[]{:S(2)}) %collective-permute-start.24) | collective-permute-done | bytes 393248 | tf_op jit(solution)/shard_map/ppermute | solution.py:26
  174.3 6.7 %collective-permute-start.26 = (bf16[2,128,768]{2,1,0:T(8,128)(2,1)S(1)}, bf16[2,128,768]{2,1,0:T(8,128)(2,1)S(1)}, u32[]{:S(2)}, u32[]{:S(2)}) collective-permute-start(bf16[2,128,768]{2,1,0:T(8,128)(2,1)S(1)} %copy-done.27), channel_id=1, source_target_pairs={{0,192},{1,193},{2,194},{3,195},{4,196},{5,197},{6,198},{7,199},{8... | collective-permute-start | bytes 1179656 | tf_op jit(solution)/shard_map/ppermute | solution.py:26
  182.2 3.1 %collective-permute-start.28 = (bf16[2,128,768]{2,1,0:T(8,128)(2,1)}, bf16[2,128,768]{2,1,0:T(8,128)(2,1)S(1)}, u32[]{:S(2)}, u32[]{:S(2)}) collective-permute-start(bf16[2,128,768]{2,1,0:T(8,128)(2,1)} %get-tuple-element.171), channel_id=1, source_target_pairs={{0,32},{1,33},{2,34},{3,35},{4,36},{5,37},{6,38},{7,39},{8,40},{9,... | collective-permute-start | bytes 1179656 | tf_op jit(solution)/shard_map/ppermute | solution.py:26
  185.3 4.1 %collective-permute-done.26.refs_0_ = bf16[2,128,768]{2,1,0:T(8,128)(2,1)S(1)} collective-permute-done((bf16[2,128,768]{2,1,0:T(8,128)(2,1)S(1)}, bf16[2,128,768]{2,1,0:T(8,128)(2,1)S(1)}, u32[]{:S(2)}, u32[]{:S(2)}) %collective-permute-start.26) | collective-permute-done | bytes 393248 | tf_op jit(solution)/shard_map/ppermute | solution.py:26
  193.4 8.3 %collective-permute-done.28.refs_6_ = bf16[2,128,768]{2,1,0:T(8,128)(2,1)S(1)} collective-permute-done((bf16[2,128,768]{2,1,0:T(8,128)(2,1)}, bf16[2,128,768]{2,1,0:T(8,128)(2,1)S(1)}, u32[]{:S(2)}, u32[]{:S(2)}) %collective-permute-start.28) | collective-permute-done | bytes 393248 | tf_op jit(solution)/shard_map/ppermute | solution.py:26
  202.1 3.2 %collective-permute-start.31 = (bf16[1,128,768]{2,1,0:T(8,128)(2,1)}, bf16[1,128,768]{2,1,0:T(8,128)(2,1)S(1)}, u32[]{:S(2)}, u32[]{:S(2)}) collective-permute-start(bf16[1,128,768]{2,1,0:T(8,128)(2,1)} %get-tuple-element.186), channel_id=1, source_target_pairs={{0,32},{1,33},{2,34},{3,35},{4,36},{5,37},{6,38},{7,39},{8,40},{9,... | collective-permute-start | bytes 589832 | tf_op jit(solution)/shard_map/ppermute | solution.py:26
  205.4 9.0 %shard_map.97.part_ref = f32[768,768]{1,0:T(8,128)S(1)} custom-call(bf16[2048,768]{1,0:T(8,128)(2,1)} %shard_map.90.ham_t_ref, bf16[768,2048]{1,0:T(8,128)(2,1)} %shard_map.87.ham_ref, f32[768,768]{1,0:T(8,128)} %get-tuple-element.93.x_ref, f32[768,1]{1,0:T(8,128)} %copy.15.dr_ref, f32[1,768]{1,0:T(1,128)} %reshape.11.dc_ref, ...), custom_call_target="tpu_custom_call" | custom-call | flops 4227858432 | bytes 20971520 | tf_op jit(solution)/shard_map/pallas_call | solution.py:59
  214.6 3.4 %shard_map.98 = f32[768,768]{1,0:T(8,128)} custom-call(s32[2]{0:T(128)S(1)} %copy-done.13, s32[16,2]{1,0:T(8,128)S(1)} %copy.16.hot, s32[16,16]{1,0:T(8,128)S(1)} %copy-done.5, f32[768,768]{1,0:T(8,128)S(1)} %shard_map.97.part_ref, bf16[768,2048]{1,0:T(8,128)(2,1)S(1)} %copy-done.1, bf16[1,128,768]{2,1,0:T(8,128)(2,1)S(1)} %copy-done.9, ...), custom_call_target="tpu_custom_call" | custom-call | flops 603979776 | bytes 6291456 | tf_op jit(solution)/shard_map/pallas_call | solution.py:59
  (124 shorter events, 60.3 us)
Async XLA Ops:
  11.7 17.5 %collective-permute-start.6 = (bf16[1,128,768]{2,1,0:T(8,128)(2,1)}, bf16[1,128,768]{2,1,0:T(8,128)(2,1)S(1)}, u32[]{:S(2)}, u32[]{:S(2)}) collective-permute-start(bf16[1,128,768]{2,1,0:T(8,128)(2,1)} %get-tuple-element.106), channel_id=1, source_target_pairs={{0,32},{1,33},{2,34},{3,35},{4,36},{5,37},{6,38},{7,39},{8,40},{9,... | collective-permute-start | bytes 589832 | tf_op jit(solution)/shard_map/ppermute | solution.py:26
  11.7 20.3 %collective-permute-start.1 = (bf16[1,128,768]{2,1,0:T(8,128)(2,1)}, bf16[1,128,768]{2,1,0:T(8,128)(2,1)S(1)}, u32[]{:S(2)}, u32[]{:S(2)}) collective-permute-start(bf16[1,128,768]{2,1,0:T(8,128)(2,1)} %get-tuple-element.101), channel_id=1, source_target_pairs={{0,16},{1,17},{2,18},{3,19},{4,20},{5,21},{6,22},{7,23},{8,24},{9,... | collective-permute-start | bytes 589832 | tf_op jit(solution)/shard_map/ppermute | solution.py:26
  12.7 35.6 %collective-permute-start.5 = (bf16[2,768,128]{2,1,0:T(8,128)(2,1)}, bf16[2,768,128]{2,1,0:T(8,128)(2,1)S(1)}, u32[]{:S(2)}, u32[]{:S(2)}) collective-permute-start(bf16[2,768,128]{2,1,0:T(8,128)(2,1)} %get-tuple-element.140.here_ref), channel_id=1, source_target_pairs={{0,8},{1,9},{2,10},{3,11},{4,12},{5,13},{6,14},{7,15},{8,0},{9,1},... | collective-permute-start | bytes 1179656 | tf_op jit(solution)/shard_map/ppermute | solution.py:26
  22.6 25.6 %collective-permute-start.3 = (bf16[3,128,128]{2,1,0:T(8,128)(2,1)S(1)}, bf16[3,128,128]{2,1,0:T(8,128)(2,1)S(1)}, u32[]{:S(2)}, u32[]{:S(2)}) collective-permute-start(bf16[3,128,128]{2,1,0:T(8,128)(2,1)S(1)} %collective-permute-done), channel_id=1, source_target_pairs={{0,128},{1,129},{2,130},{3,131},{4,132},{5,133},{6,134},{7,135},{8... | collective-permute-start | bytes 294920 | tf_op jit(solution)/shard_map/ppermute | solution.py:26
  22.6 25.6 %collective-permute-start.4 = (bf16[3,128,128]{2,1,0:T(8,128)(2,1)S(1)}, bf16[3,128,128]{2,1,0:T(8,128)(2,1)S(1)}, u32[]{:S(2)}, u32[]{:S(2)}) collective-permute-start(bf16[3,128,128]{2,1,0:T(8,128)(2,1)S(1)} %collective-permute-done), channel_id=1, source_target_pairs={{0,192},{1,193},{2,194},{3,195},{4,196},{5,197},{6,198},{7,199},{8... | collective-permute-start | bytes 294920 | tf_op jit(solution)/shard_map/ppermute | solution.py:26
  29.2 19.1 %collective-permute-start.7 = (bf16[1,128,768]{2,1,0:T(8,128)(2,1)}, bf16[1,128,768]{2,1,0:T(8,128)(2,1)S(1)}, u32[]{:S(2)}, u32[]{:S(2)}) collective-permute-start(bf16[1,128,768]{2,1,0:T(8,128)(2,1)} %get-tuple-element.108), channel_id=1, source_target_pairs={{0,48},{1,49},{2,50},{3,51},{4,52},{5,53},{6,54},{7,55},{8,56},{9,... | collective-permute-start | bytes 589832 | tf_op jit(solution)/shard_map/ppermute | solution.py:26
  32.0 16.2 %collective-permute-start.2 = (bf16[3,128,128]{2,1,0:T(8,128)(2,1)S(1)}, bf16[3,128,128]{2,1,0:T(8,128)(2,1)S(1)}, u32[]{:S(2)}, u32[]{:S(2)}) collective-permute-start(bf16[3,128,128]{2,1,0:T(8,128)(2,1)S(1)} %collective-permute-done), channel_id=1, source_target_pairs={{0,64},{1,65},{2,66},{3,67},{4,68},{5,69},{6,70},{7,71},{8,72},{9,... | collective-permute-start | bytes 294920 | tf_op jit(solution)/shard_map/ppermute | solution.py:26
  51.0 59.6 %all-to-all-start = ((bf16[16,768,128]{2,1,0:T(8,128)(2,1)}), bf16[16,768,128]{2,1,0:T(8,128)(2,1)}, u32[]{:S(2)}, u32[]{:S(2)}) async-start(bf16[16,768,128]{2,1,0:T(8,128)(2,1)} %shard_map.91), calls=%async_computation | async-start | bytes 6291456 | tf_op jit(solution)/shard_map/all_to_all | solution.py:162
  57.1 20.6 %collective-permute-start.8 = (bf16[2,128,768]{2,1,0:T(8,128)(2,1)}, bf16[2,128,768]{2,1,0:T(8,128)(2,1)S(1)}, u32[]{:S(2)}, u32[]{:S(2)}) collective-permute-start(bf16[2,128,768]{2,1,0:T(8,128)(2,1)} %get-tuple-element.115), channel_id=1, source_target_pairs={{0,64},{1,65},{2,66},{3,67},{4,68},{5,69},{6,70},{7,71},{8,72},{9,... | collective-permute-start | bytes 1179656 | tf_op jit(solution)/shard_map/ppermute | solution.py:26
  59.6 18.1 %collective-permute-start.9 = (bf16[2,128,768]{2,1,0:T(8,128)(2,1)}, bf16[2,128,768]{2,1,0:T(8,128)(2,1)S(1)}, u32[]{:S(2)}, u32[]{:S(2)}) collective-permute-start(bf16[2,128,768]{2,1,0:T(8,128)(2,1)} %get-tuple-element.115), channel_id=1, source_target_pairs={{0,128},{1,129},{2,130},{3,131},{4,132},{5,133},{6,134},{7,135},{8... | collective-permute-start | bytes 1179656 | tf_op jit(solution)/shard_map/ppermute | solution.py:26
  61.4 20.5 %collective-permute-start.10 = (bf16[12,128,128]{2,1,0:T(8,128)(2,1)S(1)}, bf16[12,128,128]{2,1,0:T(8,128)(2,1)S(1)}, u32[]{:S(2)}, u32[]{:S(2)}) collective-permute-start(bf16[12,128,128]{2,1,0:T(8,128)(2,1)S(1)} %pad_maximum_fusion.refs_0_), channel_id=1, source_target_pairs={{0,16},{1,17},{2,18},{3,19},{4,20},{5,21},{6,22},{7,23},{8,24},{9,... | collective-permute-start | bytes 1179656 | tf_op jit(solution)/shard_map/ppermute | solution.py:26
  61.5 20.4 %collective-permute-start.11 = (bf16[12,128,128]{2,1,0:T(8,128)(2,1)S(1)}, bf16[12,128,128]{2,1,0:T(8,128)(2,1)S(1)}, u32[]{:S(2)}, u32[]{:S(2)}) collective-permute-start(bf16[12,128,128]{2,1,0:T(8,128)(2,1)S(1)} %pad_maximum_fusion.refs_0_), channel_id=1, source_target_pairs={{0,32},{1,33},{2,34},{3,35},{4,36},{5,37},{6,38},{7,39},{8,40},{9,... | collective-permute-start | bytes 1179656 | tf_op jit(solution)/shard_map/ppermute | solution.py:26
  64.2 18.4 %collective-permute-start.12 = (bf16[12,128,128]{2,1,0:T(8,128)(2,1)S(1)}, bf16[12,128,128]{2,1,0:T(8,128)(2,1)S(1)}, u32[]{:S(2)}, u32[]{:S(2)}) collective-permute-start(bf16[12,128,128]{2,1,0:T(8,128)(2,1)S(1)} %pad_maximum_fusion.refs_0_), channel_id=1, source_target_pairs={{0,48},{1,49},{2,50},{3,51},{4,52},{5,53},{6,54},{7,55},{8,56},{9,... | collective-permute-start | bytes 1179656 | tf_op jit(solution)/shard_map/ppermute | solution.py:26
  85.5 20.0 %collective-permute-start.15 = (bf16[2,128,768]{2,1,0:T(8,128)(2,1)}, bf16[2,128,768]{2,1,0:T(8,128)(2,1)S(1)}, u32[]{:S(2)}, u32[]{:S(2)}) collective-permute-start(bf16[2,128,768]{2,1,0:T(8,128)(2,1)} %get-tuple-element.122), channel_id=1, source_target_pairs={{0,32},{1,33},{2,34},{3,35},{4,36},{5,37},{6,38},{7,39},{8,40},{9,... | collective-permute-start | bytes 1179656 | tf_op jit(solution)/shard_map/ppermute | solution.py:26
  88.1 17.5 %collective-permute-start.16 = (bf16[2,128,768]{2,1,0:T(8,128)(2,1)}, bf16[2,128,768]{2,1,0:T(8,128)(2,1)S(1)}, u32[]{:S(2)}, u32[]{:S(2)}) collective-permute-start(bf16[2,128,768]{2,1,0:T(8,128)(2,1)} %get-tuple-element.123), channel_id=1, source_target_pairs={{0,48},{1,49},{2,50},{3,51},{4,52},{5,53},{6,54},{7,55},{8,56},{9,... | collective-permute-start | bytes 1179656 | tf_op jit(solution)/shard_map/ppermute | solution.py:26
  106.4 12.6 %collective-permute-start.17 = (bf16[1,128,768]{2,1,0:T(8,128)(2,1)}, bf16[1,128,768]{2,1,0:T(8,128)(2,1)S(1)}, u32[]{:S(2)}, u32[]{:S(2)}) collective-permute-start(bf16[1,128,768]{2,1,0:T(8,128)(2,1)} %get-tuple-element.143), channel_id=1, source_target_pairs={{0,16},{1,17},{2,18},{3,19},{4,20},{5,21},{6,22},{7,23},{8,24},{9,... | collective-permute-start | bytes 589832 | tf_op jit(solution)/shard_map/ppermute | solution.py:26
  124.8 19.3 %collective-permute-start.20 = (bf16[2,768,128]{2,1,0:T(8,128)(2,1)}, bf16[2,768,128]{2,1,0:T(8,128)(2,1)S(1)}, u32[]{:S(2)}, u32[]{:S(2)}) collective-permute-start(bf16[2,768,128]{2,1,0:T(8,128)(2,1)} %get-tuple-element.182.here_ref), channel_id=1, source_target_pairs={{0,8},{1,9},{2,10},{3,11},{4,12},{5,13},{6,14},{7,15},{8,0},{9,1},... | collective-permute-start | bytes 1179656 | tf_op jit(solution)/shard_map/ppermute | solution.py:26
  147.8 57.6 %all-to-all-start.1 = ((bf16[16,768,128]{2,1,0:T(8,128)(2,1)}), bf16[16,768,128]{2,1,0:T(8,128)(2,1)}, u32[]{:S(2)}, u32[]{:S(2)}) async-start(bf16[16,768,128]{2,1,0:T(8,128)(2,1)} %shard_map.96), calls=%async_computation.1 | async-start | bytes 6291456 | tf_op jit(solution)/shard_map/all_to_all | solution.py:162
  152.8 19.6 %collective-permute-start.24 = (bf16[2,128,768]{2,1,0:T(8,128)(2,1)S(1)}, bf16[2,128,768]{2,1,0:T(8,128)(2,1)S(1)}, u32[]{:S(2)}, u32[]{:S(2)}) collective-permute-start(bf16[2,128,768]{2,1,0:T(8,128)(2,1)S(1)} %copy-done.27), channel_id=1, source_target_pairs={{0,64},{1,65},{2,66},{3,67},{4,68},{5,69},{6,70},{7,71},{8,72},{9,... | collective-permute-start | bytes 1179656 | tf_op jit(solution)/shard_map/ppermute | solution.py:26
  152.8 19.6 %collective-permute-start.25 = (bf16[2,128,768]{2,1,0:T(8,128)(2,1)S(1)}, bf16[2,128,768]{2,1,0:T(8,128)(2,1)S(1)}, u32[]{:S(2)}, u32[]{:S(2)}) collective-permute-start(bf16[2,128,768]{2,1,0:T(8,128)(2,1)S(1)} %copy-done.27), channel_id=1, source_target_pairs={{0,128},{1,129},{2,130},{3,131},{4,132},{5,133},{6,134},{7,135},{8... | collective-permute-start | bytes 1179656 | tf_op jit(solution)/shard_map/ppermute | solution.py:26
  174.3 15.1 %collective-permute-start.26 = (bf16[2,128,768]{2,1,0:T(8,128)(2,1)S(1)}, bf16[2,128,768]{2,1,0:T(8,128)(2,1)S(1)}, u32[]{:S(2)}, u32[]{:S(2)}) collective-permute-start(bf16[2,128,768]{2,1,0:T(8,128)(2,1)S(1)} %copy-done.27), channel_id=1, source_target_pairs={{0,192},{1,193},{2,194},{3,195},{4,196},{5,197},{6,198},{7,199},{8... | collective-permute-start | bytes 1179656 | tf_op jit(solution)/shard_map/ppermute | solution.py:26
  182.2 19.5 %collective-permute-start.28 = (bf16[2,128,768]{2,1,0:T(8,128)(2,1)}, bf16[2,128,768]{2,1,0:T(8,128)(2,1)S(1)}, u32[]{:S(2)}, u32[]{:S(2)}) collective-permute-start(bf16[2,128,768]{2,1,0:T(8,128)(2,1)} %get-tuple-element.171), channel_id=1, source_target_pairs={{0,32},{1,33},{2,34},{3,35},{4,36},{5,37},{6,38},{7,39},{8,40},{9,... | collective-permute-start | bytes 1179656 | tf_op jit(solution)/shard_map/ppermute | solution.py:26
  185.3 16.4 %collective-permute-start.29 = (bf16[2,128,768]{2,1,0:T(8,128)(2,1)}, bf16[2,128,768]{2,1,0:T(8,128)(2,1)S(1)}, u32[]{:S(2)}, u32[]{:S(2)}) collective-permute-start(bf16[2,128,768]{2,1,0:T(8,128)(2,1)} %get-tuple-element.172), channel_id=1, source_target_pairs={{0,48},{1,49},{2,50},{3,51},{4,52},{5,53},{6,54},{7,55},{8,56},{9,... | collective-permute-start | bytes 1179656 | tf_op jit(solution)/shard_map/ppermute | solution.py:26
  201.7 12.7 %collective-permute-start.30 = (bf16[1,128,768]{2,1,0:T(8,128)(2,1)}, bf16[1,128,768]{2,1,0:T(8,128)(2,1)S(1)}, u32[]{:S(2)}, u32[]{:S(2)}) collective-permute-start(bf16[1,128,768]{2,1,0:T(8,128)(2,1)} %get-tuple-element.185), channel_id=1, source_target_pairs={{0,16},{1,17},{2,18},{3,19},{4,20},{5,21},{6,22},{7,23},{8,24},{9,... | collective-permute-start | bytes 589832 | tf_op jit(solution)/shard_map/ppermute | solution.py:26
  (39 other events, 485.1 us)

commit v7 on v6

--- a/solution.py
+++ b/solution.py
@@ -327,13 +327,12 @@
     dc = lax.dynamic_slice_in_dim(diagonal, col_index * T, T).reshape(1, T)
 
     piece = lax.dynamic_slice_in_dim(ham_blocks, col_index * 3, 3).transpose(0, 2, 1)
-    piece = permute(piece, mirror)
     row, col, *sends = pack(ids, hot, sel, start_vector)
     zh = permute(col, zh_flip)
-    piece, row, sends = barrier(piece, row, sends)
+    piece = permute(after(piece, row), mirror)
     near = [sends[0]] + [permute(sends[n], x_shift(n)) for n in (1, 2)]
-    near.append(permute(after(sends[3], near[2]), x_shift(3)))
-    pieces = [piece, permute(after(piece, near[1]), z_xor(1))]
+    near.append(permute(after(sends[3], near[1]), x_shift(3)))
+    pieces = [piece, permute(after(piece, zh), z_xor(1))]
     pieces += [permute(piece, z_xor(n)) for n in (2, 3)]
     ham = dense(ids, lists, counts, (ham_blocks,), False)
     quarter, row, col, zh, near, ham, dr, dc = barrier(

time: 219 us -> 215 us (0.982)
  waiting for transfers between devices: 77.1 us -> 73.4 us
  starting transfers between devices: 81.7 us -> 84.1 us
    ppermute x33, waiting for transfers between devices: 77.1 us -> 73.4 us  [permute(): return lax.ppermute(value, axes, pairs)]
    ppermute x33, starting transfers between devices: 70.6 us -> 74.1 us  [permute(): return lax.ppermute(value, axes, pairs)]
  transfers between devices with their start and end apart: 35 -> 35, of which waited for: 16 -> 15; matrix products, arithmetic and copies ran while one was open for 2% -> 1% of each run, Pallas kernels for 17% -> 15%
where the time goes in v7:
time: 215 us
  starting transfers between devices  84.1 us (39%)
  waiting for transfers between devices  73.4 us (34%)
  Pallas kernels  48.9 us (23%)
  local copies, waits for them, and re-layouts  7.58 us (4%)
    ppermute x33, starting transfers between devices, permute(): return lax.ppermute(value, axes, pairs)  74.1 us
    ppermute x33, waiting for transfers between devices, permute(): return lax.ppermute(value, axes, pairs)  73.4 us
    pallas_call x13, Pallas kernels, call(): pl.pallas_call(kernel, grid_spec=pltpu.PrefetchScalarGridSpec(num_scalar_...  48.9 us
    all_to_all x2, starting transfers between devices, over_yk(): return lax.all_to_all(chosen, ('y', 'k'), 0, 0, tiled=True)  9.99 us
    unnamed x58, local copies, waits for them, and re-layouts  5.18 us
  transfers between devices with their start and end apart: 35, of which 15 were waited for; matrix products, arithmetic and copies ran while one was open for 1% of the time, Pallas kernels for 15%

profile of v7, /device:TPU:8, one launch (start us, length us, event | category | flops | bytes accessed | tf_op | source)
XLA Modules:
  0.0 215.0 jit_solution(18400769680010340438)
XLA Ops:
  5.8 7.2 %collective-permute-start.1 = (bf16[2,768,128]{2,1,0:T(8,128)(2,1)}, bf16[2,768,128]{2,1,0:T(8,128)(2,1)S(1)}, u32[]{:S(2)}, u32[]{:S(2)}) collective-permute-start(bf16[2,768,128]{2,1,0:T(8,128)(2,1)} %get-tuple-element.130.here_ref), channel_id=1, source_target_pairs={{0,8},{1,9},{2,10},{3,11},{4,12},{5,13},{6,14},{7,15},{8,0},{9,1},... | collective-permute-start | bytes 1179656 | tf_op jit(solution)/shard_map/ppermute | solution.py:26
  14.7 4.5 %collective-permute-start = (bf16[3,128,128]{2,1,0:T(8,128)(2,1)S(1)}, bf16[3,128,128]{2,1,0:T(8,128)(2,1)S(1)}, u32[]{:S(2)}, u32[]{:S(2)}) collective-permute-start(bf16[3,128,128]{2,1,0:T(8,128)(2,1)S(1)} %bitcast.3), channel_id=1, source_target_pairs={{0,0},{1,16},{2,32},{3,48},{4,64},{5,80},{6,96},{7,112},{8,128},{9... | collective-permute-start | bytes 294920 | tf_op jit(solution)/shard_map/ppermute | solution.py:26
  19.3 5.3 %collective-permute-done = bf16[3,128,128]{2,1,0:T(8,128)(2,1)S(1)} collective-permute-done((bf16[3,128,128]{2,1,0:T(8,128)(2,1)S(1)}, bf16[3,128,128]{2,1,0:T(8,128)(2,1)S(1)}, u32[]{:S(2)}, u32[]{:S(2)}) %collective-permute-start) | collective-permute-done | bytes 98336 | tf_op jit(solution)/shard_map/ppermute | solution.py:26
  24.6 14.4 %collective-permute-start.3 = (bf16[3,128,128]{2,1,0:T(8,128)(2,1)S(1)}, bf16[3,128,128]{2,1,0:T(8,128)(2,1)S(1)}, u32[]{:S(2)}, u32[]{:S(2)}) collective-permute-start(bf16[3,128,128]{2,1,0:T(8,128)(2,1)S(1)} %collective-permute-done), channel_id=1, source_target_pairs={{0,128},{1,129},{2,130},{3,131},{4,132},{5,133},{6,134},{7,135},{8... | collective-permute-start | bytes 294920 | tf_op jit(solution)/shard_map/ppermute | solution.py:26
  42.8 4.2 %shard_map.87.ham_ref = bf16[768,2048]{1,0:T(8,128)(2,1)} custom-call(s32[2]{0:T(128)S(1)} %pad_add_fusion.ids, s32[3,16,64]{2,1,0:T(8,128)S(1)} %copy-done.10, s32[16]{0:T(128)S(1)} %copy-done.14, bf16[48,128,128]{2,1,0:T(8,128)(2,1)S(1)} %copy-done.3), custom_call_target="tpu_custom_call" | custom-call | flops 4194304 | bytes 5242880 | tf_op jit(solution)/shard_map/pallas_call | solution.py:59
  50.2 4.9 %all-to-all-start = ((bf16[16,768,128]{2,1,0:T(8,128)(2,1)}), bf16[16,768,128]{2,1,0:T(8,128)(2,1)}, u32[]{:S(2)}, u32[]{:S(2)}) async-start(bf16[16,768,128]{2,1,0:T(8,128)(2,1)} %shard_map.91), calls=%async_computation | async-start | bytes 6291456 | tf_op jit(solution)/shard_map/all_to_all | solution.py:162
  59.5 3.3 %collective-permute-start.11 = (bf16[12,128,128]{2,1,0:T(8,128)(2,1)S(1)}, bf16[12,128,128]{2,1,0:T(8,128)(2,1)S(1)}, u32[]{:S(2)}, u32[]{:S(2)}) collective-permute-start(bf16[12,128,128]{2,1,0:T(8,128)(2,1)S(1)} %pad_maximum_fusion.refs_0_), channel_id=1, source_target_pairs={{0,32},{1,33},{2,34},{3,35},{4,36},{5,37},{6,38},{7,39},{8,40},{9,... | collective-permute-start | bytes 1179656 | tf_op jit(solution)/shard_map/ppermute | solution.py:26
  63.8 11.1 %collective-permute-done.8.refs_0_ = bf16[2,128,768]{2,1,0:T(8,128)(2,1)S(1)} collective-permute-done((bf16[2,128,768]{2,1,0:T(8,128)(2,1)}, bf16[2,128,768]{2,1,0:T(8,128)(2,1)S(1)}, u32[]{:S(2)}, u32[]{:S(2)}) %collective-permute-start.8) | collective-permute-done | bytes 393248 | tf_op jit(solution)/shard_map/ppermute | solution.py:26
  82.1 3.2 %collective-permute-start.15 = (bf16[2,128,768]{2,1,0:T(8,128)(2,1)}, bf16[2,128,768]{2,1,0:T(8,128)(2,1)S(1)}, u32[]{:S(2)}, u32[]{:S(2)}) collective-permute-start(bf16[2,128,768]{2,1,0:T(8,128)(2,1)} %get-tuple-element.112), channel_id=1, source_target_pairs={{0,32},{1,33},{2,34},{3,35},{4,36},{5,37},{6,38},{7,39},{8,40},{9,... | collective-permute-start | bytes 1179656 | tf_op jit(solution)/shard_map/ppermute | solution.py:26
  88.0 4.6 %shard_map.90.ham_t_ref = bf16[2048,768]{1,0:T(8,128)(2,1)} custom-call(s32[2]{0:T(128)S(1)} %pad_add_fusion.ids, s32[3,16,64]{2,1,0:T(8,128)S(1)} %copy-done.10, s32[16]{0:T(128)S(1)} %copy-done.14, bf16[12,128,128]{2,1,0:T(8,128)(2,1)S(1)} %pad_maximum_fusion.refs_0_, bf16[12,128,128]{2,1,0:T(8,128)(2,1)S(1)} %collective-permute-done.10.refs_1_, ...), custom_call_target="tpu_custom_call" | custom-call | flops 4194304 | bytes 5242880 | tf_op jit(solution)/shard_map/pallas_call | solution.py:59
  94.3 7.6 %collective-permute-done.15.refs_6_ = bf16[2,128,768]{2,1,0:T(8,128)(2,1)S(1)} collective-permute-done((bf16[2,128,768]{2,1,0:T(8,128)(2,1)}, bf16[2,128,768]{2,1,0:T(8,128)(2,1)S(1)}, u32[]{:S(2)}, u32[]{:S(2)}) %collective-permute-start.15) | collective-permute-done | bytes 393248 | tf_op jit(solution)/shard_map/ppermute | solution.py:26
  108.1 8.4 %shard_map.92.part_ref = f32[768,768]{1,0:T(8,128)S(1)} custom-call(bf16[2048,768]{1,0:T(8,128)(2,1)} %shard_map.90.ham_t_ref, bf16[768,2048]{1,0:T(8,128)(2,1)} %shard_map.87.ham_ref, f32[768,768]{1,0:T(8,128)} %refs_9_.1, f32[768,1]{1,0:T(8,128)} %copy.15.dr_ref, f32[1,768]{1,0:T(1,128)} %reshape.11.dc_ref, ...), custom_call_target="tpu_custom_call" | custom-call | flops 4227858432 | bytes 20971520 | tf_op jit(solution)/shard_map/pallas_call | solution.py:59
  116.6 5.0 %shard_map.93 = (f32[768,768]{1,0:T(8,128)}, bf16[2,128,768]{2,1,0:T(8,128)(2,1)}, bf16[2,768,128]{2,1,0:T(8,128)(2,1)}, bf16[1,128,768]{2,1,0:T(8,128)(2,1)}, b...) custom-call(s32[2]{0:T(128)S(1)} %copy-done.12, s32[16,2]{1,0:T(8,128)S(1)} %copy.16.hot, ...), custom_call_target="tpu_custom_call" | custom-call | flops 603979776 | bytes 6291456 | tf_op jit(solution)/shard_map/pallas_call | solution.py:59
  121.6 5.0 %collective-permute-start.20 = (bf16[2,768,128]{2,1,0:T(8,128)(2,1)}, bf16[2,768,128]{2,1,0:T(8,128)(2,1)S(1)}, u32[]{:S(2)}, u32[]{:S(2)}) collective-permute-start(bf16[2,768,128]{2,1,0:T(8,128)(2,1)} %get-tuple-element.172.here_ref), channel_id=1, source_target_pairs={{0,8},{1,9},{2,10},{3,11},{4,12},{5,13},{6,14},{7,15},{8,0},{9,1},... | collective-permute-start | bytes 1179656 | tf_op jit(solution)/shard_map/ppermute | solution.py:26
  131.1 3.8 %collective-permute-done.21.refs_1_ = bf16[1,128,768]{2,1,0:T(8,128)(2,1)S(1)} collective-permute-done((bf16[1,128,768]{2,1,0:T(8,128)(2,1)}, bf16[1,128,768]{2,1,0:T(8,128)(2,1)S(1)}, u32[]{:S(2)}, u32[]{:S(2)}) %collective-permute-start.21) | collective-permute-done | bytes 196640 | tf_op jit(solution)/shard_map/ppermute | solution.py:26
  134.9 3.6 %collective-permute-done.22.refs_2_ = bf16[1,128,768]{2,1,0:T(8,128)(2,1)S(1)} collective-permute-done((bf16[1,128,768]{2,1,0:T(8,128)(2,1)}, bf16[1,128,768]{2,1,0:T(8,128)(2,1)S(1)}, u32[]{:S(2)}, u32[]{:S(2)}) %collective-permute-start.22) | collective-permute-done | bytes 196640 | tf_op jit(solution)/shard_map/ppermute | solution.py:26
  138.5 5.5 %collective-permute-done.20.there_ref = bf16[2,768,128]{2,1,0:T(8,128)(2,1)S(1)} collective-permute-done((bf16[2,768,128]{2,1,0:T(8,128)(2,1)}, bf16[2,768,128]{2,1,0:T(8,128)(2,1)S(1)}, u32[]{:S(2)}, u32[]{:S(2)}) %collective-permute-start.20) | collective-permute-done | bytes 393248 | tf_op jit(solution)/shard_map/ppermute | solution.py:26
  147.7 5.1 %all-to-all-start.1 = ((bf16[16,768,128]{2,1,0:T(8,128)(2,1)}), bf16[16,768,128]{2,1,0:T(8,128)(2,1)}, u32[]{:S(2)}, u32[]{:S(2)}) async-start(bf16[16,768,128]{2,1,0:T(8,128)(2,1)} %shard_map.96), calls=%async_computation.1 | async-start | bytes 6291456 | tf_op jit(solution)/shard_map/all_to_all | solution.py:162
  155.8 16.4 %collective-permute-done.24.refs_0_ = bf16[2,128,768]{2,1,0:T(8,128)(2,1)S(1)} collective-permute-done((bf16[2,128,768]{2,1,0:T(8,128)(2,1)S(1)}, bf16[2,128,768]{2,1,0:T(8,128)(2,1)S(1)}, u32[]{:S(2)}, u32[]{:S(2)}) %collective-permute-start.24) | collective-permute-done | bytes 393248 | tf_op jit(solution)/shard_map/ppermute | solution.py:26
  181.9 4.6 %collective-permute-done.26.refs_0_ = bf16[2,128,768]{2,1,0:T(8,128)(2,1)S(1)} collective-permute-done((bf16[2,128,768]{2,1,0:T(8,128)(2,1)S(1)}, bf16[2,128,768]{2,1,0:T(8,128)(2,1)S(1)}, u32[]{:S(2)}, u32[]{:S(2)}) %collective-permute-start.26) | collective-permute-done | bytes 393248 | tf_op jit(solution)/shard_map/ppermute | solution.py:26
  190.4 8.2 %collective-permute-done.28.refs_6_ = bf16[2,128,768]{2,1,0:T(8,128)(2,1)S(1)} collective-permute-done((bf16[2,128,768]{2,1,0:T(8,128)(2,1)}, bf16[2,128,768]{2,1,0:T(8,128)(2,1)S(1)}, u32[]{:S(2)}, u32[]{:S(2)}) %collective-permute-start.28) | collective-permute-done | bytes 393248 | tf_op jit(solution)/shard_map/ppermute | solution.py:26
  199.1 3.3 %collective-permute-start.31 = (bf16[1,128,768]{2,1,0:T(8,128)(2,1)}, bf16[1,128,768]{2,1,0:T(8,128)(2,1)S(1)}, u32[]{:S(2)}, u32[]{:S(2)}) collective-permute-start(bf16[1,128,768]{2,1,0:T(8,128)(2,1)} %get-tuple-element.176), channel_id=1, source_target_pairs={{0,32},{1,33},{2,34},{3,35},{4,36},{5,37},{6,38},{7,39},{8,40},{9,... | collective-permute-start | bytes 589832 | tf_op jit(solution)/shard_map/ppermute | solution.py:26
  202.5 9.0 %shard_map.97.part_ref = f32[768,768]{1,0:T(8,128)S(1)} custom-call(bf16[2048,768]{1,0:T(8,128)(2,1)} %shard_map.90.ham_t_ref, bf16[768,2048]{1,0:T(8,128)(2,1)} %shard_map.87.ham_ref, f32[768,768]{1,0:T(8,128)} %get-tuple-element.88.x_ref, f32[768,1]{1,0:T(8,128)} %copy.15.dr_ref, f32[1,768]{1,0:T(1,128)} %reshape.11.dc_ref, ...), custom_call_target="tpu_custom_call" | custom-call | flops 4227858432 | bytes 20971520 | tf_op jit(solution)/shard_map/pallas_call | solution.py:59
  211.6 3.4 %shard_map.98 = f32[768,768]{1,0:T(8,128)} custom-call(s32[2]{0:T(128)S(1)} %copy-done.13, s32[16,2]{1,0:T(8,128)S(1)} %copy.16.hot, s32[16,16]{1,0:T(8,128)S(1)} %copy-done.5, f32[768,768]{1,0:T(8,128)S(1)} %shard_map.97.part_ref, bf16[768,2048]{1,0:T(8,128)(2,1)S(1)} %copy-done.1, bf16[1,128,768]{2,1,0:T(8,128)(2,1)S(1)} %copy-done.9, ...), custom_call_target="tpu_custom_call" | custom-call | flops 603979776 | bytes 6291456 | tf_op jit(solution)/shard_map/pallas_call | solution.py:59
  (124 shorter events, 62.5 us)
Async XLA Ops:
  5.8 34.9 %collective-permute-start.1 = (bf16[2,768,128]{2,1,0:T(8,128)(2,1)}, bf16[2,768,128]{2,1,0:T(8,128)(2,1)S(1)}, u32[]{:S(2)}, u32[]{:S(2)}) collective-permute-start(bf16[2,768,128]{2,1,0:T(8,128)(2,1)} %get-tuple-element.130.here_ref), channel_id=1, source_target_pairs={{0,8},{1,9},{2,10},{3,11},{4,12},{5,13},{6,14},{7,15},{8,0},{9,1},... | collective-permute-start | bytes 1179656 | tf_op jit(solution)/shard_map/ppermute | solution.py:26
  13.0 27.5 %collective-permute-start.5 = (bf16[1,128,768]{2,1,0:T(8,128)(2,1)}, bf16[1,128,768]{2,1,0:T(8,128)(2,1)S(1)}, u32[]{:S(2)}, u32[]{:S(2)}) collective-permute-start(bf16[1,128,768]{2,1,0:T(8,128)(2,1)} %get-tuple-element.95), channel_id=1, source_target_pairs={{0,16},{1,17},{2,18},{3,19},{4,20},{5,21},{6,22},{7,23},{8,24},{9,... | collective-permute-start | bytes 589832 | tf_op jit(solution)/shard_map/ppermute | solution.py:26
  19.2 28.3 %collective-permute-start.6 = (bf16[1,128,768]{2,1,0:T(8,128)(2,1)}, bf16[1,128,768]{2,1,0:T(8,128)(2,1)S(1)}, u32[]{:S(2)}, u32[]{:S(2)}) collective-permute-start(bf16[1,128,768]{2,1,0:T(8,128)(2,1)} %get-tuple-element.96), channel_id=1, source_target_pairs={{0,32},{1,33},{2,34},{3,35},{4,36},{5,37},{6,38},{7,39},{8,40},{9,... | collective-permute-start | bytes 589832 | tf_op jit(solution)/shard_map/ppermute | solution.py:26
  24.6 22.4 %collective-permute-start.3 = (bf16[3,128,128]{2,1,0:T(8,128)(2,1)S(1)}, bf16[3,128,128]{2,1,0:T(8,128)(2,1)S(1)}, u32[]{:S(2)}, u32[]{:S(2)}) collective-permute-start(bf16[3,128,128]{2,1,0:T(8,128)(2,1)S(1)} %collective-permute-done), channel_id=1, source_target_pairs={{0,128},{1,129},{2,130},{3,131},{4,132},{5,133},{6,134},{7,135},{8... | collective-permute-start | bytes 294920 | tf_op jit(solution)/shard_map/ppermute | solution.py:26
  50.2 57.9 %all-to-all-start = ((bf16[16,768,128]{2,1,0:T(8,128)(2,1)}), bf16[16,768,128]{2,1,0:T(8,128)(2,1)}, u32[]{:S(2)}, u32[]{:S(2)}) async-start(bf16[16,768,128]{2,1,0:T(8,128)(2,1)} %shard_map.91), calls=%async_computation | async-start | bytes 6291456 | tf_op jit(solution)/shard_map/all_to_all | solution.py:162
  55.1 19.8 %collective-permute-start.8 = (bf16[2,128,768]{2,1,0:T(8,128)(2,1)}, bf16[2,128,768]{2,1,0:T(8,128)(2,1)S(1)}, u32[]{:S(2)}, u32[]{:S(2)}) collective-permute-start(bf16[2,128,768]{2,1,0:T(8,128)(2,1)} %get-tuple-element.105), channel_id=1, source_target_pairs={{0,64},{1,65},{2,66},{3,67},{4,68},{5,69},{6,70},{7,71},{8,72},{9,... | collective-permute-start | bytes 1179656 | tf_op jit(solution)/shard_map/ppermute | solution.py:26
  56.2 18.7 %collective-permute-start.9 = (bf16[2,128,768]{2,1,0:T(8,128)(2,1)}, bf16[2,128,768]{2,1,0:T(8,128)(2,1)S(1)}, u32[]{:S(2)}, u32[]{:S(2)}) collective-permute-start(bf16[2,128,768]{2,1,0:T(8,128)(2,1)} %get-tuple-element.105), channel_id=1, source_target_pairs={{0,128},{1,129},{2,130},{3,131},{4,132},{5,133},{6,134},{7,135},{8... | collective-permute-start | bytes 1179656 | tf_op jit(solution)/shard_map/ppermute | solution.py:26
  59.1 17.8 %collective-permute-start.10 = (bf16[12,128,128]{2,1,0:T(8,128)(2,1)S(1)}, bf16[12,128,128]{2,1,0:T(8,128)(2,1)S(1)}, u32[]{:S(2)}, u32[]{:S(2)}) collective-permute-start(bf16[12,128,128]{2,1,0:T(8,128)(2,1)S(1)} %pad_maximum_fusion.refs_0_), channel_id=1, source_target_pairs={{0,16},{1,17},{2,18},{3,19},{4,20},{5,21},{6,22},{7,23},{8,24},{9,... | collective-permute-start | bytes 1179656 | tf_op jit(solution)/shard_map/ppermute | solution.py:26
  59.5 20.3 %collective-permute-start.11 = (bf16[12,128,128]{2,1,0:T(8,128)(2,1)S(1)}, bf16[12,128,128]{2,1,0:T(8,128)(2,1)S(1)}, u32[]{:S(2)}, u32[]{:S(2)}) collective-permute-start(bf16[12,128,128]{2,1,0:T(8,128)(2,1)S(1)} %pad_maximum_fusion.refs_0_), channel_id=1, source_target_pairs={{0,32},{1,33},{2,34},{3,35},{4,36},{5,37},{6,38},{7,39},{8,40},{9,... | collective-permute-start | bytes 1179656 | tf_op jit(solution)/shard_map/ppermute | solution.py:26
  62.8 17.2 %collective-permute-start.12 = (bf16[12,128,128]{2,1,0:T(8,128)(2,1)S(1)}, bf16[12,128,128]{2,1,0:T(8,128)(2,1)S(1)}, u32[]{:S(2)}, u32[]{:S(2)}) collective-permute-start(bf16[12,128,128]{2,1,0:T(8,128)(2,1)S(1)} %pad_maximum_fusion.refs_0_), channel_id=1, source_target_pairs={{0,48},{1,49},{2,50},{3,51},{4,52},{5,53},{6,54},{7,55},{8,56},{9,... | collective-permute-start | bytes 1179656 | tf_op jit(solution)/shard_map/ppermute | solution.py:26
  79.9 12.7 %collective-permute-start.13 = (bf16[2,128,768]{2,1,0:T(8,128)(2,1)}, bf16[2,128,768]{2,1,0:T(8,128)(2,1)S(1)}, u32[]{:S(2)}, u32[]{:S(2)}) collective-permute-start(bf16[2,128,768]{2,1,0:T(8,128)(2,1)} %get-tuple-element.105), channel_id=1, source_target_pairs={{0,192},{1,193},{2,194},{3,195},{4,196},{5,197},{6,198},{7,199},{8... | collective-permute-start | bytes 1179656 | tf_op jit(solution)/shard_map/ppermute | solution.py:26
  81.8 12.5 %collective-permute-start.14 = (bf16[2,128,768]{2,1,0:T(8,128)(2,1)}, bf16[2,128,768]{2,1,0:T(8,128)(2,1)S(1)}, u32[]{:S(2)}, u32[]{:S(2)}) collective-permute-start(bf16[2,128,768]{2,1,0:T(8,128)(2,1)} %get-tuple-element.111), channel_id=1, source_target_pairs={{0,16},{1,17},{2,18},{3,19},{4,20},{5,21},{6,22},{7,23},{8,24},{9,... | collective-permute-start | bytes 1179656 | tf_op jit(solution)/shard_map/ppermute | solution.py:26
  82.1 19.8 %collective-permute-start.15 = (bf16[2,128,768]{2,1,0:T(8,128)(2,1)}, bf16[2,128,768]{2,1,0:T(8,128)(2,1)S(1)}, u32[]{:S(2)}, u32[]{:S(2)}) collective-permute-start(bf16[2,128,768]{2,1,0:T(8,128)(2,1)} %get-tuple-element.112), channel_id=1, source_target_pairs={{0,32},{1,33},{2,34},{3,35},{4,36},{5,37},{6,38},{7,39},{8,40},{9,... | collective-permute-start | bytes 1179656 | tf_op jit(solution)/shard_map/ppermute | solution.py:26
  85.3 16.6 %collective-permute-start.16 = (bf16[2,128,768]{2,1,0:T(8,128)(2,1)}, bf16[2,128,768]{2,1,0:T(8,128)(2,1)S(1)}, u32[]{:S(2)}, u32[]{:S(2)}) collective-permute-start(bf16[2,128,768]{2,1,0:T(8,128)(2,1)} %get-tuple-element.113), channel_id=1, source_target_pairs={{0,48},{1,49},{2,50},{3,51},{4,52},{5,53},{6,54},{7,55},{8,56},{9,... | collective-permute-start | bytes 1179656 | tf_op jit(solution)/shard_map/ppermute | solution.py:26
  102.8 13.8 %collective-permute-start.17 = (bf16[1,128,768]{2,1,0:T(8,128)(2,1)}, bf16[1,128,768]{2,1,0:T(8,128)(2,1)S(1)}, u32[]{:S(2)}, u32[]{:S(2)}) collective-permute-start(bf16[1,128,768]{2,1,0:T(8,128)(2,1)} %get-tuple-element.133), channel_id=1, source_target_pairs={{0,16},{1,17},{2,18},{3,19},{4,20},{5,21},{6,22},{7,23},{8,24},{9,... | collective-permute-start | bytes 589832 | tf_op jit(solution)/shard_map/ppermute | solution.py:26
  121.6 22.4 %collective-permute-start.20 = (bf16[2,768,128]{2,1,0:T(8,128)(2,1)}, bf16[2,768,128]{2,1,0:T(8,128)(2,1)S(1)}, u32[]{:S(2)}, u32[]{:S(2)}) collective-permute-start(bf16[2,768,128]{2,1,0:T(8,128)(2,1)} %get-tuple-element.172.here_ref), channel_id=1, source_target_pairs={{0,8},{1,9},{2,10},{3,11},{4,12},{5,13},{6,14},{7,15},{8,0},{9,1},... | collective-permute-start | bytes 1179656 | tf_op jit(solution)/shard_map/ppermute | solution.py:26
  147.7 54.7 %all-to-all-start.1 = ((bf16[16,768,128]{2,1,0:T(8,128)(2,1)}), bf16[16,768,128]{2,1,0:T(8,128)(2,1)}, u32[]{:S(2)}, u32[]{:S(2)}) async-start(bf16[16,768,128]{2,1,0:T(8,128)(2,1)} %shard_map.96), calls=%async_computation.1 | async-start | bytes 6291456 | tf_op jit(solution)/shard_map/all_to_all | solution.py:162
  152.8 19.4 %collective-permute-start.24 = (bf16[2,128,768]{2,1,0:T(8,128)(2,1)S(1)}, bf16[2,128,768]{2,1,0:T(8,128)(2,1)S(1)}, u32[]{:S(2)}, u32[]{:S(2)}) collective-permute-start(bf16[2,128,768]{2,1,0:T(8,128)(2,1)S(1)} %copy-done.27), channel_id=1, source_target_pairs={{0,64},{1,65},{2,66},{3,67},{4,68},{5,69},{6,70},{7,71},{8,72},{9,... | collective-permute-start | bytes 1179656 | tf_op jit(solution)/shard_map/ppermute | solution.py:26
  152.8 20.6 %collective-permute-start.25 = (bf16[2,128,768]{2,1,0:T(8,128)(2,1)S(1)}, bf16[2,128,768]{2,1,0:T(8,128)(2,1)S(1)}, u32[]{:S(2)}, u32[]{:S(2)}) collective-permute-start(bf16[2,128,768]{2,1,0:T(8,128)(2,1)S(1)} %copy-done.27), channel_id=1, source_target_pairs={{0,128},{1,129},{2,130},{3,131},{4,132},{5,133},{6,134},{7,135},{8... | collective-permute-start | bytes 1179656 | tf_op jit(solution)/shard_map/ppermute | solution.py:26
  177.8 12.6 %collective-permute-start.27 = (bf16[2,128,768]{2,1,0:T(8,128)(2,1)}, bf16[2,128,768]{2,1,0:T(8,128)(2,1)S(1)}, u32[]{:S(2)}, u32[]{:S(2)}) collective-permute-start(bf16[2,128,768]{2,1,0:T(8,128)(2,1)} %get-tuple-element.160), channel_id=1, source_target_pairs={{0,16},{1,17},{2,18},{3,19},{4,20},{5,21},{6,22},{7,23},{8,24},{9,... | collective-permute-start | bytes 1179656 | tf_op jit(solution)/shard_map/ppermute | solution.py:26
  179.1 19.5 %collective-permute-start.28 = (bf16[2,128,768]{2,1,0:T(8,128)(2,1)}, bf16[2,128,768]{2,1,0:T(8,128)(2,1)S(1)}, u32[]{:S(2)}, u32[]{:S(2)}) collective-permute-start(bf16[2,128,768]{2,1,0:T(8,128)(2,1)} %get-tuple-element.161), channel_id=1, source_target_pairs={{0,32},{1,33},{2,34},{3,35},{4,36},{5,37},{6,38},{7,39},{8,40},{9,... | collective-permute-start | bytes 1179656 | tf_op jit(solution)/shard_map/ppermute | solution.py:26
  181.9 16.7 %collective-permute-start.29 = (bf16[2,128,768]{2,1,0:T(8,128)(2,1)}, bf16[2,128,768]{2,1,0:T(8,128)(2,1)S(1)}, u32[]{:S(2)}, u32[]{:S(2)}) collective-permute-start(bf16[2,128,768]{2,1,0:T(8,128)(2,1)} %get-tuple-element.162), channel_id=1, source_target_pairs={{0,48},{1,49},{2,50},{3,51},{4,52},{5,53},{6,54},{7,55},{8,56},{9,... | collective-permute-start | bytes 1179656 | tf_op jit(solution)/shard_map/ppermute | solution.py:26
  198.6 12.9 %collective-permute-start.30 = (bf16[1,128,768]{2,1,0:T(8,128)(2,1)}, bf16[1,128,768]{2,1,0:T(8,128)(2,1)S(1)}, u32[]{:S(2)}, u32[]{:S(2)}) collective-permute-start(bf16[1,128,768]{2,1,0:T(8,128)(2,1)} %get-tuple-element.175), channel_id=1, source_target_pairs={{0,16},{1,17},{2,18},{3,19},{4,20},{5,21},{6,22},{7,23},{8,24},{9,... | collective-permute-start | bytes 589832 | tf_op jit(solution)/shard_map/ppermute | solution.py:26
  199.1 12.5 %collective-permute-start.31 = (bf16[1,128,768]{2,1,0:T(8,128)(2,1)}, bf16[1,128,768]{2,1,0:T(8,128)(2,1)S(1)}, u32[]{:S(2)}, u32[]{:S(2)}) collective-permute-start(bf16[1,128,768]{2,1,0:T(8,128)(2,1)} %get-tuple-element.176), channel_id=1, source_target_pairs={{0,32},{1,33},{2,34},{3,35},{4,36},{5,37},{6,38},{7,39},{8,40},{9,... | collective-permute-start | bytes 589832 | tf_op jit(solution)/shard_map/ppermute | solution.py:26
  (39 other events, 455.4 us)

commit v8 on v7

--- a/solution.py
+++ b/solution.py
@@ -273,45 +273,53 @@
     )
 
 
-def finish_kernel(second):
-    def kernel(ids, hot, sel, part_ref, ham_ref, *refs):
+def hot_kernel(ids, hot, sel, part_ref, ham_ref, *refs):
+    slabs, row_ref, col_ref = refs[:4], refs[4], refs[5]
+    r, c = ids[0], ids[1]
+    stacked = jnp.concatenate([ref[0] for ref in slabs], axis=0)
+    for h in range(2):
+        at = pl.ds(start(hot[r, h]), B)
+        total = part_ref[at, :] + jnp.dot(ham_ref[at, :], stacked, preferred_element_type=f32)
+        row_ref[h] = (total * scale).astype(bf16)
+        at = pl.ds(start(hot[c, h]), B)
+        some = jnp.concatenate([ref[0, :, at] for ref in slabs], axis=0)
+        total = part_ref[:, at] + jnp.dot(ham_ref[...], some, preferred_element_type=f32)
+        col_ref[h] = (total * scale).astype(bf16)
+    choose_rows(ids, sel, 0, row_ref, refs[6:])
+
+
+def finish_hot(ids, hot, sel, part, ham, slabs):
+    return call(
+        hot_kernel,
+        (ids, hot, sel),
+        (1,),
+        [whole((T, T)), pl.BlockSpec((T, 512), lambda i, *_: (0, 3))] + [whole((1, B, T))] * 4,
+        [whole(s.shape) for s in send_shapes],
+        send_shapes,
+        (part, ham, *slabs),
+        flops=2 * T * 512 * 512,
+        moved=6 << 20,
+        room=32,
+    )
+
+
+def finish_kernel(factor):
+    def kernel(part_ref, ham_ref, *refs):
         stacked = jnp.concatenate([ref[0] for ref in refs[:4]], axis=0)
-        out_ref = refs[4]
         total = part_ref[...] + jnp.dot(ham_ref[...], stacked, preferred_element_type=f32)
-        if second:
-            out_ref[...] = total * (2.0 * scale)
-            return
-        row_ref, col_ref = refs[5:7]
-        out_ref[...] = total * scale
-        i, r, c = pl.program_id(0), ids[0], ids[1]
-        for h in range(2):
-            col_ref[h] = out_ref[:, pl.ds(start(hot[c, h]), B)].astype(bf16)
-            block = hot[r, h]
-
-            @pl.when(block // 2 == i)
-            def _(h=h, block=block):
-                row_ref[h] = out_ref[pl.ds(start(block % 2), B), :].astype(bf16)
-
-        @pl.when(i == T // R - 1)
-        def _():
-            choose_rows(ids, sel, 0, row_ref, refs[7:11])
+        refs[4][...] = total * factor
 
     return kernel
 
 
-def finish(ids, hot, sel, part, ham, slabs, second):
-    out_specs, out_shape = rows, shape((T, T), f32)
-    if not second:
-        out_specs = [rows, whole((2, B, T)), pl.BlockSpec((2, R, B), lambda i, *_: (0, i, 0))]
-        out_specs += [whole((1, B, T))] * 4
-        out_shape = [out_shape] + send_shapes
-    return call(
-        finish_kernel(second),
-        (ids, hot, sel),
+def finish(part, ham, slabs, factor):
+    return call(
+        finish_kernel(factor),
+        (),
         (T // R,),
         [rows, pl.BlockSpec((R, 512), lambda i, *_: (i, 3))] + [whole((1, B, T))] * 4,
-        out_specs,
-        out_shape,
+        rows,
+        shape((T, T), f32),
         (part, ham, *slabs),
         flops=2 * T * T * 512,
         moved=6 << 20,
@@ -331,13 +339,11 @@
     zh = permute(col, zh_flip)
     piece = permute(after(piece, row), mirror)
     near = [sends[0]] + [permute(sends[n], x_shift(n)) for n in (1, 2)]
-    near.append(permute(after(sends[3], near[1]), x_shift(3)))
-    pieces = [piece, permute(after(piece, zh), z_xor(1))]
+    near.append(permute(after(sends[3], [near[1], piece]), x_shift(3)))
+    pieces = [piece, permute(after(piece, [zh, near]), z_xor(1))]
     pieces += [permute(piece, z_xor(n)) for n in (2, 3)]
     ham = dense(ids, lists, counts, (ham_blocks,), False)
-    quarter, row, col, zh, near, ham, dr, dc = barrier(
-        jnp.concatenate(pieces), row, col, zh, near, ham, dr, dc
-    )
+    quarter, row, col, zh, near = barrier(jnp.concatenate(pieces), row, col, zh, near)
     ham_t = None
     outs = []
     value = start_vector
@@ -346,13 +352,14 @@
         if not first:
             zh = permute(col, zh_flip)
             near = over_x(sends)
-            row, col, zh, near = barrier(row, col, zh, near)
+            row, col, zh, near, value = barrier(row, col, zh, near, value)
+            outs.append(value)
         z1 = permute(row, z_xor(1))
         z2 = permute(row, z_xor(2))
         yk = over_yk(choose_cols(ids, sel, col, zh))
         hams = over_x([quarter] * 4) if first else []
         far = next_rows(ids, sel, [z1, z2], (1, 2))
-        row, far, hams = barrier(row, far, hams)
+        row, far, hams, ham, dr, dc = barrier(row, far, hams, ham, dr, dc)
         z3 = permute(row, z_xor(3))
         x12 = over_x(far)
         if first:
@@ -362,12 +369,11 @@
         x3 = over_x(far)
         before = () if first else (start_vector,)
         part = first_products(ham_t, ham, value, dr, dc, near, x12, yk, *before)
-        result = finish(ids, hot, sel, part, ham, x3, not first)
         if first:
-            value, *sent = result
-            row, col, sends = barrier(sent[0], sent[1], sent[2:])
-            result = value
-        outs.append(result)
+            row, col, *sends = finish_hot(ids, hot, sel, part, ham, x3)
+            value = finish(part, ham, x3, scale)
+        else:
+            outs.append(finish(part, ham, x3, 2.0 * scale))
     return tuple(outs)
 
 

time: 215 us -> 219 us (1.019)
  waiting for transfers between devices: 73.4 us -> 63.5 us
  local copies, waits for them, and re-layouts: 7.58 us -> 14.7 us
  Pallas kernels: 48.9 us -> 53.2 us
    ppermute x33, waiting for transfers between devices: 73.4 us -> 63.5 us  [permute(): return lax.ppermute(value, axes, pairs)]
    unnamed x58 -> x68, local copies, waits for them, and re-layouts: 5.18 us -> 10.1 us
    pallas_call x13 -> x14, Pallas kernels: 48.9 us -> 53.2 us  [call(): pl.pallas_call(kernel, grid_spec=pltpu.PrefetchScalarGridSpec(num_scalar_...]
    all_to_all x2, starting transfers between devices: 9.99 us -> 12.5 us  [over_yk(): return lax.all_to_all(chosen, ('y', 'k'), 0, 0, tiled=True)]
  transfers between devices with their start and end apart: 35 -> 35, of which waited for: 15 -> 17; matrix products, arithmetic and copies ran while one was open for 1% -> 2% of each run, Pallas kernels for 15% -> 18%
where the time goes in v8:
time: 219 us; the launch traced here: 218 us
  starting transfers between devices  85.4 us (39%)
  waiting for transfers between devices  63.5 us (29%)
  Pallas kernels  53.2 us (24%)
  local copies, waits for them, and re-layouts  14.7 us (7%)
    ppermute x33, starting transfers between devices, permute(): return lax.ppermute(value, axes, pairs)  72.8 us
    ppermute x33, waiting for transfers between devices, permute(): return lax.ppermute(value, axes, pairs)  63.5 us
    pallas_call x14, Pallas kernels, call(): pl.pallas_call(kernel, grid_spec=pltpu.PrefetchScalarGridSpec(num_scalar_...  53.2 us
    all_to_all x2, starting transfers between devices, over_yk(): return lax.all_to_all(chosen, ('y', 'k'), 0, 0, tiled=True)  12.5 us
    unnamed x68, local copies, waits for them, and re-layouts  10.1 us
  transfers between devices with their start and end apart: 35, of which 17 were waited for; matrix products, arithmetic and copies ran while one was open for 2% of the time, Pallas kernels for 18%

profile of v8, /device:TPU:8, one launch (start us, length us, event | category | flops | bytes accessed | tf_op | source)
XLA Modules:
  0.0 217.8 jit_solution(5586158724724454099)
XLA Ops:
  7.3 7.2 %collective-permute-start.1 = (bf16[2,768,128]{2,1,0:T(8,128)(2,1)}, bf16[2,768,128]{2,1,0:T(8,128)(2,1)S(1)}, u32[]{:S(2)}, u32[]{:S(2)}) collective-permute-start(bf16[2,768,128]{2,1,0:T(8,128)(2,1)} %get-tuple-element.127.here_ref), channel_id=1, source_target_pairs={{0,8},{1,9},{2,10},{3,11},{4,12},{5,13},{6,14},{7,15},{8,0},{9,1},... | collective-permute-start | bytes 1179656 | tf_op jit(solution)/shard_map/ppermute | solution.py:26
  14.7 4.5 %collective-permute-start = (bf16[3,128,128]{2,1,0:T(8,128)(2,1)S(1)}, bf16[3,128,128]{2,1,0:T(8,128)(2,1)S(1)}, u32[]{:S(2)}, u32[]{:S(2)}) collective-permute-start(bf16[3,128,128]{2,1,0:T(8,128)(2,1)S(1)} %bitcast.3), channel_id=1, source_target_pairs={{0,0},{1,16},{2,32},{3,48},{4,64},{5,80},{6,96},{7,112},{8,128},{9... | collective-permute-start | bytes 294920 | tf_op jit(solution)/shard_map/ppermute | solution.py:26
  19.3 5.3 %collective-permute-done = bf16[3,128,128]{2,1,0:T(8,128)(2,1)S(1)} collective-permute-done((bf16[3,128,128]{2,1,0:T(8,128)(2,1)S(1)}, bf16[3,128,128]{2,1,0:T(8,128)(2,1)S(1)}, u32[]{:S(2)}, u32[]{:S(2)}) %collective-permute-start) | collective-permute-done | bytes 98336 | tf_op jit(solution)/shard_map/ppermute | solution.py:26
  24.7 15.3 %collective-permute-start.6 = (bf16[3,128,128]{2,1,0:T(8,128)(2,1)S(1)}, bf16[3,128,128]{2,1,0:T(8,128)(2,1)S(1)}, u32[]{:S(2)}, u32[]{:S(2)}) collective-permute-start(bf16[3,128,128]{2,1,0:T(8,128)(2,1)S(1)} %collective-permute-done), channel_id=1, source_target_pairs={{0,128},{1,129},{2,130},{3,131},{4,132},{5,133},{6,134},{7,135},{8... | collective-permute-start | bytes 294920 | tf_op jit(solution)/shard_map/ppermute | solution.py:26
  51.5 7.6 %all-to-all-start = ((bf16[16,768,128]{2,1,0:T(8,128)(2,1)}), bf16[16,768,128]{2,1,0:T(8,128)(2,1)}, u32[]{:S(2)}, u32[]{:S(2)}) async-start(bf16[16,768,128]{2,1,0:T(8,128)(2,1)} %shard_map.91), calls=%async_computation | async-start | bytes 6291456 | tf_op jit(solution)/shard_map/all_to_all | solution.py:162
  59.9 3.3 %collective-permute-start.9 = (bf16[2,128,768]{2,1,0:T(8,128)(2,1)}, bf16[2,128,768]{2,1,0:T(8,128)(2,1)S(1)}, u32[]{:S(2)}, u32[]{:S(2)}) collective-permute-start(bf16[2,128,768]{2,1,0:T(8,128)(2,1)} %get-tuple-element.102), channel_id=1, source_target_pairs={{0,128},{1,129},{2,130},{3,131},{4,132},{5,133},{6,134},{7,135},{8... | collective-permute-start | bytes 1179656 | tf_op jit(solution)/shard_map/ppermute | solution.py:26
  71.0 4.4 %shard_map.88.ham_ref = bf16[768,2048]{1,0:T(8,128)(2,1)} custom-call(s32[2]{0:T(128)S(1)} %copy-done.13, s32[3,16,64]{2,1,0:T(8,128)S(1)} %copy-done.10, s32[16]{0:T(128)S(1)} %copy-done.17, bf16[48,128,128]{2,1,0:T(8,128)(2,1)S(1)} %copy-done.3), custom_call_target="tpu_custom_call" | custom-call | flops 4194304 | bytes 5242880 | tf_op jit(solution)/shard_map/pallas_call | solution.py:59
  75.4 3.6 %collective-permute-done.8.refs_0_ = bf16[2,128,768]{2,1,0:T(8,128)(2,1)S(1)} collective-permute-done((bf16[2,128,768]{2,1,0:T(8,128)(2,1)}, bf16[2,128,768]{2,1,0:T(8,128)(2,1)S(1)}, u32[]{:S(2)}, u32[]{:S(2)}) %collective-permute-start.8) | collective-permute-done | bytes 393248 | tf_op jit(solution)/shard_map/ppermute | solution.py:26
  93.0 6.4 %shard_map.90.ham_t_ref = bf16[2048,768]{1,0:T(8,128)(2,1)} custom-call(s32[2]{0:T(128)S(1)} %copy-done.14, s32[3,16,64]{2,1,0:T(8,128)S(1)} %copy-done.11, s32[16]{0:T(128)S(1)} %copy-done.18, bf16[12,128,128]{2,1,0:T(8,128)(2,1)S(1)} %pad_maximum_fusion.refs_0_, bf16[12,128,128]{2,1,0:T(8,128)(2,1)S(1)} %collective-permute-done.10.refs_1_, ...), custom_call_target="tpu_custom_call" | custom-call | flops 4194304 | bytes 5242880 | tf_op jit(solution)/shard_map/pallas_call | solution.py:59
  101.1 4.6 %collective-permute-done.15.refs_6_ = bf16[2,128,768]{2,1,0:T(8,128)(2,1)S(1)} collective-permute-done((bf16[2,128,768]{2,1,0:T(8,128)(2,1)}, bf16[2,128,768]{2,1,0:T(8,128)(2,1)S(1)}, u32[]{:S(2)}, u32[]{:S(2)}) %collective-permute-start.15) | collective-permute-done | bytes 393248 | tf_op jit(solution)/shard_map/ppermute | solution.py:26
  107.1 3.8 %collective-permute-start.18 = (bf16[1,128,768]{2,1,0:T(8,128)(2,1)}, bf16[1,128,768]{2,1,0:T(8,128)(2,1)}, u32[]{:S(2)}, u32[]{:S(2)}) collective-permute-start(bf16[1,128,768]{2,1,0:T(8,128)(2,1)} %get-tuple-element.131), channel_id=1, source_target_pairs={{0,32},{1,33},{2,34},{3,35},{4,36},{5,37},{6,38},{7,39},{8,40},{9,... | collective-permute-start | bytes 589832 | tf_op jit(solution)/shard_map/ppermute | solution.py:26
  110.9 8.3 %shard_map.92.part_ref = f32[768,768]{1,0:T(8,128)S(1)} custom-call(bf16[2048,768]{1,0:T(8,128)(2,1)} %shard_map.90.ham_t_ref, bf16[768,2048]{1,0:T(8,128)(2,1)} %shard_map.88.ham_ref, f32[768,768]{1,0:T(8,128)} %refs_9_.1, f32[768,1]{1,0:T(8,128)} %copy.14.dr_ref, f32[1,768]{1,0:T(1,128)} %reshape.11.dc_ref, ...), custom_call_target="tpu_custom_call" | custom-call | flops 4227858432 | bytes 20971520 | tf_op jit(solution)/shard_map/pallas_call | solution.py:59
  120.2 3.6 %shard_map.93 = (bf16[2,128,768]{2,1,0:T(8,128)(2,1)}, bf16[2,768,128]{2,1,0:T(8,128)(2,1)}, bf16[1,128,768]{2,1,0:T(8,128)(2,1)}, bf16[1,128,768]{2,1,0:T(8,128...) custom-call(s32[2]{0:T(128)S(1)} %copy-done.15, s32[16,2]{1,0:T(8,128)S(1)} %copy.15.hot, ...), custom_call_target="tpu_custom_call" | custom-call | flops 402653184 | bytes 6291456 | tf_op jit(solution)/shard_map/pallas_call | solution.py:59
  123.8 4.8 %collective-permute-start.20 = (bf16[2,768,128]{2,1,0:T(8,128)(2,1)}, bf16[2,768,128]{2,1,0:T(8,128)(2,1)S(1)}, u32[]{:S(2)}, u32[]{:S(2)}) collective-permute-start(bf16[2,768,128]{2,1,0:T(8,128)(2,1)} %get-tuple-element.166.here_ref), channel_id=1, source_target_pairs={{0,8},{1,9},{2,10},{3,11},{4,12},{5,13},{6,14},{7,15},{8,0},{9,1},... | collective-permute-start | bytes 1179656 | tf_op jit(solution)/shard_map/ppermute | solution.py:26
  133.1 3.6 %shard_map.94.x_ref = f32[768,768]{1,0:T(8,128)} custom-call(f32[768,768]{1,0:T(8,128)S(1)} %shard_map.92.part_ref, bf16[768,2048]{1,0:T(8,128)(2,1)S(1)} %copy-done, bf16[1,128,768]{2,1,0:T(8,128)(2,1)S(1)} %copy-done.4, bf16[1,128,768]{2,1,0:T(8,128)(2,1)S(1)} %collective-permute-done.17.refs_1_, bf16[1,128,768]{2,1,0:T(8,128)(2,1)} %collective-permute-done.18.refs_2_, ...), custom_call_target="tpu_custom_call" | custom-call | flops 603979776 | bytes 6291456 | tf_op jit(solution)/shard_map/pallas_call | solution.py:59
  136.7 4.4 %collective-permute-done.22.refs_2_ = bf16[1,128,768]{2,1,0:T(8,128)(2,1)S(1)} collective-permute-done((bf16[1,128,768]{2,1,0:T(8,128)(2,1)}, bf16[1,128,768]{2,1,0:T(8,128)(2,1)S(1)}, u32[]{:S(2)}, u32[]{:S(2)}) %collective-permute-start.22) | collective-permute-done | bytes 196640 | tf_op jit(solution)/shard_map/ppermute | solution.py:26
  141.1 5.5 %collective-permute-done.20.there_ref = bf16[2,768,128]{2,1,0:T(8,128)(2,1)S(1)} collective-permute-done((bf16[2,768,128]{2,1,0:T(8,128)(2,1)}, bf16[2,768,128]{2,1,0:T(8,128)(2,1)S(1)}, u32[]{:S(2)}, u32[]{:S(2)}) %collective-permute-start.20) | collective-permute-done | bytes 393248 | tf_op jit(solution)/shard_map/ppermute | solution.py:26
  149.3 5.0 %all-to-all-start.1 = ((bf16[16,768,128]{2,1,0:T(8,128)(2,1)}), bf16[16,768,128]{2,1,0:T(8,128)(2,1)}, u32[]{:S(2)}, u32[]{:S(2)}) async-start(bf16[16,768,128]{2,1,0:T(8,128)(2,1)} %shard_map.97), calls=%async_computation.1 | async-start | bytes 6291456 | tf_op jit(solution)/shard_map/all_to_all | solution.py:162
  157.5 16.1 %collective-permute-done.24.refs_0_ = bf16[2,128,768]{2,1,0:T(8,128)(2,1)S(1)} collective-permute-done((bf16[2,128,768]{2,1,0:T(8,128)(2,1)S(1)}, bf16[2,128,768]{2,1,0:T(8,128)(2,1)S(1)}, u32[]{:S(2)}, u32[]{:S(2)}) %collective-permute-start.24) | collective-permute-done | bytes 393248 | tf_op jit(solution)/shard_map/ppermute | solution.py:26
  184.7 3.4 %collective-permute-done.26.refs_0_ = bf16[2,128,768]{2,1,0:T(8,128)(2,1)S(1)} collective-permute-done((bf16[2,128,768]{2,1,0:T(8,128)(2,1)S(1)}, bf16[2,128,768]{2,1,0:T(8,128)(2,1)S(1)}, u32[]{:S(2)}, u32[]{:S(2)}) %collective-permute-start.26) | collective-permute-done | bytes 393248 | tf_op jit(solution)/shard_map/ppermute | solution.py:26
  191.9 8.6 %collective-permute-done.28.refs_6_ = bf16[2,128,768]{2,1,0:T(8,128)(2,1)S(1)} collective-permute-done((bf16[2,128,768]{2,1,0:T(8,128)(2,1)}, bf16[2,128,768]{2,1,0:T(8,128)(2,1)S(1)}, u32[]{:S(2)}, u32[]{:S(2)}) %collective-permute-start.28) | collective-permute-done | bytes 393248 | tf_op jit(solution)/shard_map/ppermute | solution.py:26
  201.5 3.3 %collective-permute-start.31 = (bf16[1,128,768]{2,1,0:T(8,128)(2,1)}, bf16[1,128,768]{2,1,0:T(8,128)(2,1)}, u32[]{:S(2)}, u32[]{:S(2)}) collective-permute-start(bf16[1,128,768]{2,1,0:T(8,128)(2,1)} %get-tuple-element.170), channel_id=1, source_target_pairs={{0,32},{1,33},{2,34},{3,35},{4,36},{5,37},{6,38},{7,39},{8,40},{9,... | collective-permute-start | bytes 589832 | tf_op jit(solution)/shard_map/ppermute | solution.py:26
  204.9 8.8 %shard_map.98.part_ref = f32[768,768]{1,0:T(8,128)S(1)} custom-call(bf16[2048,768]{1,0:T(8,128)(2,1)} %shard_map.90.ham_t_ref, bf16[768,2048]{1,0:T(8,128)(2,1)} %shard_map.88.ham_ref, f32[768,768]{1,0:T(8,128)} %shard_map.94.x_ref, f32[768,1]{1,0:T(8,128)} %copy.16.dr_ref, f32[1,768]{1,0:T(1,128)} %reshape.11.dc_ref, ...), custom_call_target="tpu_custom_call" | custom-call | flops 4227858432 | bytes 20971520 | tf_op jit(solution)/shard_map/pallas_call | solution.py:59
  214.2 3.6 %shard_map.99 = f32[768,768]{1,0:T(8,128)} custom-call(f32[768,768]{1,0:T(8,128)S(1)} %shard_map.98.part_ref, bf16[768,2048]{1,0:T(8,128)(2,1)S(1)} %copy-done.1, bf16[1,128,768]{2,1,0:T(8,128)(2,1)S(1)} %copy-done.9, bf16[1,128,768]{2,1,0:T(8,128)(2,1)S(1)} %collective-permute-done.30.refs_1_, bf16[1,128,768]{2,1,0:T(8,128)(2,1)} %collective-permute-done.31.refs_2_, ...), custom_call_target="tpu_custom_call" | custom-call | flops 603979776 | bytes 6291456 | tf_op jit(solution)/shard_map/pallas_call | solution.py:59
  (136 shorter events, 71.7 us)
Async XLA Ops:
  5.8 18.8 %collective-permute-start.2 = (bf16[1,128,768]{2,1,0:T(8,128)(2,1)}, bf16[1,128,768]{2,1,0:T(8,128)(2,1)S(1)}, u32[]{:S(2)}, u32[]{:S(2)}) collective-permute-start(bf16[1,128,768]{2,1,0:T(8,128)(2,1)} %get-tuple-element.91), channel_id=1, source_target_pairs={{0,16},{1,17},{2,18},{3,19},{4,20},{5,21},{6,22},{7,23},{8,24},{9,... | collective-permute-start | bytes 589832 | tf_op jit(solution)/shard_map/ppermute | solution.py:26
  7.3 34.3 %collective-permute-start.1 = (bf16[2,768,128]{2,1,0:T(8,128)(2,1)}, bf16[2,768,128]{2,1,0:T(8,128)(2,1)S(1)}, u32[]{:S(2)}, u32[]{:S(2)}) collective-permute-start(bf16[2,768,128]{2,1,0:T(8,128)(2,1)} %get-tuple-element.127.here_ref), channel_id=1, source_target_pairs={{0,8},{1,9},{2,10},{3,11},{4,12},{5,13},{6,14},{7,15},{8,0},{9,1},... | collective-permute-start | bytes 1179656 | tf_op jit(solution)/shard_map/ppermute | solution.py:26
  19.2 22.4 %collective-permute-start.3 = (bf16[1,128,768]{2,1,0:T(8,128)(2,1)}, bf16[1,128,768]{2,1,0:T(8,128)(2,1)S(1)}, u32[]{:S(2)}, u32[]{:S(2)}) collective-permute-start(bf16[1,128,768]{2,1,0:T(8,128)(2,1)} %get-tuple-element.92), channel_id=1, source_target_pairs={{0,32},{1,33},{2,34},{3,35},{4,36},{5,37},{6,38},{7,39},{8,40},{9,... | collective-permute-start | bytes 589832 | tf_op jit(solution)/shard_map/ppermute | solution.py:26
  24.6 17.0 %collective-permute-start.4 = (bf16[1,128,768]{2,1,0:T(8,128)(2,1)}, bf16[1,128,768]{2,1,0:T(8,128)(2,1)S(1)}, u32[]{:S(2)}, u32[]{:S(2)}) collective-permute-start(bf16[1,128,768]{2,1,0:T(8,128)(2,1)} %get-tuple-element.94), channel_id=1, source_target_pairs={{0,48},{1,49},{2,50},{3,51},{4,52},{5,53},{6,54},{7,55},{8,56},{9,... | collective-permute-start | bytes 589832 | tf_op jit(solution)/shard_map/ppermute | solution.py:26
  24.7 22.5 %collective-permute-start.6 = (bf16[3,128,128]{2,1,0:T(8,128)(2,1)S(1)}, bf16[3,128,128]{2,1,0:T(8,128)(2,1)S(1)}, u32[]{:S(2)}, u32[]{:S(2)}) collective-permute-start(bf16[3,128,128]{2,1,0:T(8,128)(2,1)S(1)} %collective-permute-done), channel_id=1, source_target_pairs={{0,128},{1,129},{2,130},{3,131},{4,132},{5,133},{6,134},{7,135},{8... | collective-permute-start | bytes 294920 | tf_op jit(solution)/shard_map/ppermute | solution.py:26
  51.5 59.3 %all-to-all-start = ((bf16[16,768,128]{2,1,0:T(8,128)(2,1)}), bf16[16,768,128]{2,1,0:T(8,128)(2,1)}, u32[]{:S(2)}, u32[]{:S(2)}) async-start(bf16[16,768,128]{2,1,0:T(8,128)(2,1)} %shard_map.91), calls=%async_computation | async-start | bytes 6291456 | tf_op jit(solution)/shard_map/all_to_all | solution.py:162
  59.1 19.8 %collective-permute-start.8 = (bf16[2,128,768]{2,1,0:T(8,128)(2,1)}, bf16[2,128,768]{2,1,0:T(8,128)(2,1)S(1)}, u32[]{:S(2)}, u32[]{:S(2)}) collective-permute-start(bf16[2,128,768]{2,1,0:T(8,128)(2,1)} %get-tuple-element.102), channel_id=1, source_target_pairs={{0,64},{1,65},{2,66},{3,67},{4,68},{5,69},{6,70},{7,71},{8,72},{9,... | collective-permute-start | bytes 1179656 | tf_op jit(solution)/shard_map/ppermute | solution.py:26
  59.9 19.0 %collective-permute-start.9 = (bf16[2,128,768]{2,1,0:T(8,128)(2,1)}, bf16[2,128,768]{2,1,0:T(8,128)(2,1)S(1)}, u32[]{:S(2)}, u32[]{:S(2)}) collective-permute-start(bf16[2,128,768]{2,1,0:T(8,128)(2,1)} %get-tuple-element.102), channel_id=1, source_target_pairs={{0,128},{1,129},{2,130},{3,131},{4,132},{5,133},{6,134},{7,135},{8... | collective-permute-start | bytes 1179656 | tf_op jit(solution)/shard_map/ppermute | solution.py:26
  63.2 17.6 %collective-permute-start.10 = (bf16[12,128,128]{2,1,0:T(8,128)(2,1)S(1)}, bf16[12,128,128]{2,1,0:T(8,128)(2,1)S(1)}, u32[]{:S(2)}, u32[]{:S(2)}) collective-permute-start(bf16[12,128,128]{2,1,0:T(8,128)(2,1)S(1)} %pad_maximum_fusion.refs_0_), channel_id=1, source_target_pairs={{0,16},{1,17},{2,18},{3,19},{4,20},{5,21},{6,22},{7,23},{8,24},{9,... | collective-permute-start | bytes 1179656 | tf_op jit(solution)/shard_map/ppermute | solution.py:26
  63.3 20.2 %collective-permute-start.11 = (bf16[12,128,128]{2,1,0:T(8,128)(2,1)S(1)}, bf16[12,128,128]{2,1,0:T(8,128)(2,1)S(1)}, u32[]{:S(2)}, u32[]{:S(2)}) collective-permute-start(bf16[12,128,128]{2,1,0:T(8,128)(2,1)S(1)} %pad_maximum_fusion.refs_0_), channel_id=1, source_target_pairs={{0,32},{1,33},{2,34},{3,35},{4,36},{5,37},{6,38},{7,39},{8,40},{9,... | collective-permute-start | bytes 1179656 | tf_op jit(solution)/shard_map/ppermute | solution.py:26
  66.4 17.8 %collective-permute-start.12 = (bf16[12,128,128]{2,1,0:T(8,128)(2,1)S(1)}, bf16[12,128,128]{2,1,0:T(8,128)(2,1)}, u32[]{:S(2)}, u32[]{:S(2)}) collective-permute-start(bf16[12,128,128]{2,1,0:T(8,128)(2,1)S(1)} %pad_maximum_fusion.refs_0_), channel_id=1, source_target_pairs={{0,48},{1,49},{2,50},{3,51},{4,52},{5,53},{6,54},{7,55},{8,56},{9,... | collective-permute-start | bytes 1179656 | tf_op jit(solution)/shard_map/ppermute | solution.py:26
  84.2 15.2 %collective-permute-start.13 = (bf16[2,128,768]{2,1,0:T(8,128)(2,1)}, bf16[2,128,768]{2,1,0:T(8,128)(2,1)S(1)}, u32[]{:S(2)}, u32[]{:S(2)}) collective-permute-start(bf16[2,128,768]{2,1,0:T(8,128)(2,1)} %get-tuple-element.102), channel_id=1, source_target_pairs={{0,192},{1,193},{2,194},{3,195},{4,196},{5,197},{6,198},{7,199},{8... | collective-permute-start | bytes 1179656 | tf_op jit(solution)/shard_map/ppermute | solution.py:26
  85.8 15.3 %collective-permute-start.14 = (bf16[2,128,768]{2,1,0:T(8,128)(2,1)}, bf16[2,128,768]{2,1,0:T(8,128)(2,1)S(1)}, u32[]{:S(2)}, u32[]{:S(2)}) collective-permute-start(bf16[2,128,768]{2,1,0:T(8,128)(2,1)} %get-tuple-element.108), channel_id=1, source_target_pairs={{0,16},{1,17},{2,18},{3,19},{4,20},{5,21},{6,22},{7,23},{8,24},{9,... | collective-permute-start | bytes 1179656 | tf_op jit(solution)/shard_map/ppermute | solution.py:26
  85.8 19.9 %collective-permute-start.15 = (bf16[2,128,768]{2,1,0:T(8,128)(2,1)}, bf16[2,128,768]{2,1,0:T(8,128)(2,1)S(1)}, u32[]{:S(2)}, u32[]{:S(2)}) collective-permute-start(bf16[2,128,768]{2,1,0:T(8,128)(2,1)} %get-tuple-element.109), channel_id=1, source_target_pairs={{0,32},{1,33},{2,34},{3,35},{4,36},{5,37},{6,38},{7,39},{8,40},{9,... | collective-permute-start | bytes 1179656 | tf_op jit(solution)/shard_map/ppermute | solution.py:26
  88.7 17.4 %collective-permute-start.16 = (bf16[2,128,768]{2,1,0:T(8,128)(2,1)}, bf16[2,128,768]{2,1,0:T(8,128)(2,1)S(1)}, u32[]{:S(2)}, u32[]{:S(2)}) collective-permute-start(bf16[2,128,768]{2,1,0:T(8,128)(2,1)} %get-tuple-element.110), channel_id=1, source_target_pairs={{0,48},{1,49},{2,50},{3,51},{4,52},{5,53},{6,54},{7,55},{8,56},{9,... | collective-permute-start | bytes 1179656 | tf_op jit(solution)/shard_map/ppermute | solution.py:26
  106.8 12.4 %collective-permute-start.17 = (bf16[1,128,768]{2,1,0:T(8,128)(2,1)}, bf16[1,128,768]{2,1,0:T(8,128)(2,1)S(1)}, u32[]{:S(2)}, u32[]{:S(2)}) collective-permute-start(bf16[1,128,768]{2,1,0:T(8,128)(2,1)} %get-tuple-element.130), channel_id=1, source_target_pairs={{0,16},{1,17},{2,18},{3,19},{4,20},{5,21},{6,22},{7,23},{8,24},{9,... | collective-permute-start | bytes 589832 | tf_op jit(solution)/shard_map/ppermute | solution.py:26
  107.1 13.1 %collective-permute-start.18 = (bf16[1,128,768]{2,1,0:T(8,128)(2,1)}, bf16[1,128,768]{2,1,0:T(8,128)(2,1)}, u32[]{:S(2)}, u32[]{:S(2)}) collective-permute-start(bf16[1,128,768]{2,1,0:T(8,128)(2,1)} %get-tuple-element.131), channel_id=1, source_target_pairs={{0,32},{1,33},{2,34},{3,35},{4,36},{5,37},{6,38},{7,39},{8,40},{9,... | collective-permute-start | bytes 589832 | tf_op jit(solution)/shard_map/ppermute | solution.py:26
  123.8 22.8 %collective-permute-start.20 = (bf16[2,768,128]{2,1,0:T(8,128)(2,1)}, bf16[2,768,128]{2,1,0:T(8,128)(2,1)S(1)}, u32[]{:S(2)}, u32[]{:S(2)}) collective-permute-start(bf16[2,768,128]{2,1,0:T(8,128)(2,1)} %get-tuple-element.166.here_ref), channel_id=1, source_target_pairs={{0,8},{1,9},{2,10},{3,11},{4,12},{5,13},{6,14},{7,15},{8,0},{9,1},... | collective-permute-start | bytes 1179656 | tf_op jit(solution)/shard_map/ppermute | solution.py:26
  149.3 55.6 %all-to-all-start.1 = ((bf16[16,768,128]{2,1,0:T(8,128)(2,1)}), bf16[16,768,128]{2,1,0:T(8,128)(2,1)}, u32[]{:S(2)}, u32[]{:S(2)}) async-start(bf16[16,768,128]{2,1,0:T(8,128)(2,1)} %shard_map.97), calls=%async_computation.1 | async-start | bytes 6291456 | tf_op jit(solution)/shard_map/all_to_all | solution.py:162
  154.3 19.4 %collective-permute-start.24 = (bf16[2,128,768]{2,1,0:T(8,128)(2,1)S(1)}, bf16[2,128,768]{2,1,0:T(8,128)(2,1)S(1)}, u32[]{:S(2)}, u32[]{:S(2)}) collective-permute-start(bf16[2,128,768]{2,1,0:T(8,128)(2,1)S(1)} %copy-done.32), channel_id=1, source_target_pairs={{0,64},{1,65},{2,66},{3,67},{4,68},{5,69},{6,70},{7,71},{8,72},{9,... | collective-permute-start | bytes 1179656 | tf_op jit(solution)/shard_map/ppermute | solution.py:26
  154.3 20.9 %collective-permute-start.25 = (bf16[2,128,768]{2,1,0:T(8,128)(2,1)S(1)}, bf16[2,128,768]{2,1,0:T(8,128)(2,1)S(1)}, u32[]{:S(2)}, u32[]{:S(2)}) collective-permute-start(bf16[2,128,768]{2,1,0:T(8,128)(2,1)S(1)} %copy-done.32), channel_id=1, source_target_pairs={{0,128},{1,129},{2,130},{3,131},{4,132},{5,133},{6,134},{7,135},{8... | collective-permute-start | bytes 1179656 | tf_op jit(solution)/shard_map/ppermute | solution.py:26
  180.6 19.9 %collective-permute-start.28 = (bf16[2,128,768]{2,1,0:T(8,128)(2,1)}, bf16[2,128,768]{2,1,0:T(8,128)(2,1)S(1)}, u32[]{:S(2)}, u32[]{:S(2)}) collective-permute-start(bf16[2,128,768]{2,1,0:T(8,128)(2,1)} %get-tuple-element.152), channel_id=1, source_target_pairs={{0,32},{1,33},{2,34},{3,35},{4,36},{5,37},{6,38},{7,39},{8,40},{9,... | collective-permute-start | bytes 1179656 | tf_op jit(solution)/shard_map/ppermute | solution.py:26
  183.8 16.7 %collective-permute-start.29 = (bf16[2,128,768]{2,1,0:T(8,128)(2,1)}, bf16[2,128,768]{2,1,0:T(8,128)(2,1)S(1)}, u32[]{:S(2)}, u32[]{:S(2)}) collective-permute-start(bf16[2,128,768]{2,1,0:T(8,128)(2,1)} %get-tuple-element.153), channel_id=1, source_target_pairs={{0,48},{1,49},{2,50},{3,51},{4,52},{5,53},{6,54},{7,55},{8,56},{9,... | collective-permute-start | bytes 1179656 | tf_op jit(solution)/shard_map/ppermute | solution.py:26
  201.5 12.7 %collective-permute-start.31 = (bf16[1,128,768]{2,1,0:T(8,128)(2,1)}, bf16[1,128,768]{2,1,0:T(8,128)(2,1)}, u32[]{:S(2)}, u32[]{:S(2)}) collective-permute-start(bf16[1,128,768]{2,1,0:T(8,128)(2,1)} %get-tuple-element.170), channel_id=1, source_target_pairs={{0,32},{1,33},{2,34},{3,35},{4,36},{5,37},{6,38},{7,39},{8,40},{9,... | collective-permute-start | bytes 589832 | tf_op jit(solution)/shard_map/ppermute | solution.py:26
  (44 other events, 432.0 us)

commit v9 on v8

--- a/solution.py
+++ b/solution.py
@@ -338,10 +338,9 @@
     row, col, *sends = pack(ids, hot, sel, start_vector)
     zh = permute(col, zh_flip)
     piece = permute(after(piece, row), mirror)
-    near = [sends[0]] + [permute(sends[n], x_shift(n)) for n in (1, 2)]
-    near.append(permute(after(sends[3], [near[1], piece]), x_shift(3)))
-    pieces = [piece, permute(after(piece, [zh, near]), z_xor(1))]
-    pieces += [permute(piece, z_xor(n)) for n in (2, 3)]
+    near = over_x(sends)
+    pieces = [piece, permute(after(piece, [zh, near[3]]), z_xor(1))]
+    pieces += [permute(after(piece, near[n - 1]), z_xor(n)) for n in (2, 3)]
     ham = dense(ids, lists, counts, (ham_blocks,), False)
     quarter, row, col, zh, near = barrier(jnp.concatenate(pieces), row, col, zh, near)
     ham_t = None

time: 219 us -> 214 us (0.977)
  starting transfers between devices: 85.4 us -> 82.2 us
    all_to_all x2, starting transfers between devices: 12.5 us -> 9.73 us  [over_yk(): return lax.all_to_all(chosen, ('y', 'k'), 0, 0, tiled=True)]
  transfers between devices with their start and end apart: 35 -> 35, of which waited for: 17 -> 14; matrix products, arithmetic and copies ran while one was open for 2% -> 2% of each run, Pallas kernels for 18% -> 19%
where the time goes in v9:
time: 214 us
  starting transfers between devices  82.2 us (38%)
  waiting for transfers between devices  61.7 us (29%)
  Pallas kernels  54.1 us (25%)
  local copies, waits for them, and re-layouts  14.7 us (7%)
    ppermute x33, starting transfers between devices, permute(): return lax.ppermute(value, axes, pairs)  72.5 us
    ppermute x33, waiting for transfers between devices, permute(): return lax.ppermute(value, axes, pairs)  61.7 us
    pallas_call x14, Pallas kernels, call(): pl.pallas_call(kernel, grid_spec=pltpu.PrefetchScalarGridSpec(num_scalar_...  54.1 us
    unnamed x68, local copies, waits for them, and re-layouts  10.1 us
    all_to_all x2, starting transfers between devices, over_yk(): return lax.all_to_all(chosen, ('y', 'k'), 0, 0, tiled=True)  9.73 us
  transfers between devices with their start and end apart: 35, of which 14 were waited for; matrix products, arithmetic and copies ran while one was open for 2% of the time, Pallas kernels for 19%

profile of v9, /device:TPU:8, one launch (start us, length us, event | category | flops | bytes accessed | tf_op | source)
XLA Modules:
  0.0 213.6 jit_solution(1469004538098499345)
XLA Ops:
  5.8 7.2 %collective-permute-start.1 = (bf16[2,768,128]{2,1,0:T(8,128)(2,1)}, bf16[2,768,128]{2,1,0:T(8,128)(2,1)S(1)}, u32[]{:S(2)}, u32[]{:S(2)}) collective-permute-start(bf16[2,768,128]{2,1,0:T(8,128)(2,1)} %get-tuple-element.129.here_ref), channel_id=1, source_target_pairs={{0,8},{1,9},{2,10},{3,11},{4,12},{5,13},{6,14},{7,15},{8,0},{9,1},... | collective-permute-start | bytes 1179656 | tf_op jit(solution)/shard_map/ppermute | solution.py:26
  13.0 2.8 %collective-permute-start.2 = (bf16[1,128,768]{2,1,0:T(8,128)(2,1)}, bf16[1,128,768]{2,1,0:T(8,128)(2,1)S(1)}, u32[]{:S(2)}, u32[]{:S(2)}) collective-permute-start(bf16[1,128,768]{2,1,0:T(8,128)(2,1)} %get-tuple-element.91), channel_id=1, source_target_pairs={{0,48},{1,49},{2,50},{3,51},{4,52},{5,53},{6,54},{7,55},{8,56},{9,... | collective-permute-start | bytes 589832 | tf_op jit(solution)/shard_map/ppermute | solution.py:26
  18.2 3.0 %collective-permute-start = (bf16[3,128,128]{2,1,0:T(8,128)(2,1)S(1)}, bf16[3,128,128]{2,1,0:T(8,128)(2,1)S(1)}, u32[]{:S(2)}, u32[]{:S(2)}) collective-permute-start(bf16[3,128,128]{2,1,0:T(8,128)(2,1)S(1)} %bitcast.3), channel_id=1, source_target_pairs={{0,0},{1,16},{2,32},{3,48},{4,64},{5,80},{6,96},{7,112},{8,128},{9... | collective-permute-start | bytes 294920 | tf_op jit(solution)/shard_map/ppermute | solution.py:26
  21.3 6.3 %collective-permute-done = bf16[3,128,128]{2,1,0:T(8,128)(2,1)S(1)} collective-permute-done((bf16[3,128,128]{2,1,0:T(8,128)(2,1)S(1)}, bf16[3,128,128]{2,1,0:T(8,128)(2,1)S(1)}, u32[]{:S(2)}, u32[]{:S(2)}) %collective-permute-start) | collective-permute-done | bytes 98336 | tf_op jit(solution)/shard_map/ppermute | solution.py:26
  27.6 11.4 %collective-permute-start.5 = (bf16[3,128,128]{2,1,0:T(8,128)(2,1)S(1)}, bf16[3,128,128]{2,1,0:T(8,128)(2,1)S(1)}, u32[]{:S(2)}, u32[]{:S(2)}) collective-permute-start(bf16[3,128,128]{2,1,0:T(8,128)(2,1)S(1)} %collective-permute-done), channel_id=1, source_target_pairs={{0,128},{1,129},{2,130},{3,131},{4,132},{5,133},{6,134},{7,135},{8... | collective-permute-start | bytes 294920 | tf_op jit(solution)/shard_map/ppermute | solution.py:26
  40.9 5.6 %collective-permute-done.5 = bf16[3,128,128]{2,1,0:T(8,128)(2,1)S(1)} collective-permute-done((bf16[3,128,128]{2,1,0:T(8,128)(2,1)S(1)}, bf16[3,128,128]{2,1,0:T(8,128)(2,1)S(1)}, u32[]{:S(2)}, u32[]{:S(2)}) %collective-permute-start.5) | collective-permute-done | bytes 98336 | tf_op jit(solution)/shard_map/ppermute | solution.py:26
  50.9 4.8 %all-to-all-start = ((bf16[16,768,128]{2,1,0:T(8,128)(2,1)}), bf16[16,768,128]{2,1,0:T(8,128)(2,1)}, u32[]{:S(2)}, u32[]{:S(2)}) async-start(bf16[16,768,128]{2,1,0:T(8,128)(2,1)} %shard_map.91), calls=%async_computation | async-start | bytes 6291456 | tf_op jit(solution)/shard_map/all_to_all | solution.py:162
  59.8 3.4 %collective-permute-start.11 = (bf16[12,128,128]{2,1,0:T(8,128)(2,1)S(1)}, bf16[12,128,128]{2,1,0:T(8,128)(2,1)S(1)}, u32[]{:S(2)}, u32[]{:S(2)}) collective-permute-start(bf16[12,128,128]{2,1,0:T(8,128)(2,1)S(1)} %pad_maximum_fusion.refs_0_), channel_id=1, source_target_pairs={{0,32},{1,33},{2,34},{3,35},{4,36},{5,37},{6,38},{7,39},{8,40},{9,... | collective-permute-start | bytes 1179656 | tf_op jit(solution)/shard_map/ppermute | solution.py:26
  68.8 4.5 %shard_map.88.ham_ref = bf16[768,2048]{1,0:T(8,128)(2,1)} custom-call(s32[2]{0:T(128)S(1)} %copy-done.13, s32[3,16,64]{2,1,0:T(8,128)S(1)} %copy-done.10, s32[16]{0:T(128)S(1)} %copy-done.17, bf16[48,128,128]{2,1,0:T(8,128)(2,1)S(1)} %copy-done.3), custom_call_target="tpu_custom_call" | custom-call | flops 4194304 | bytes 5242880 | tf_op jit(solution)/shard_map/pallas_call | solution.py:59
  83.2 3.2 %collective-permute-start.15 = (bf16[2,128,768]{2,1,0:T(8,128)(2,1)}, bf16[2,128,768]{2,1,0:T(8,128)(2,1)S(1)}, u32[]{:S(2)}, u32[]{:S(2)}) collective-permute-start(bf16[2,128,768]{2,1,0:T(8,128)(2,1)} %get-tuple-element.111), channel_id=1, source_target_pairs={{0,32},{1,33},{2,34},{3,35},{4,36},{5,37},{6,38},{7,39},{8,40},{9,... | collective-permute-start | bytes 1179656 | tf_op jit(solution)/shard_map/ppermute | solution.py:26
  91.7 7.3 %shard_map.90.ham_t_ref = bf16[2048,768]{1,0:T(8,128)(2,1)} custom-call(s32[2]{0:T(128)S(1)} %copy-done.14, s32[3,16,64]{2,1,0:T(8,128)S(1)} %copy-done.11, s32[16]{0:T(128)S(1)} %copy-done.18, bf16[12,128,128]{2,1,0:T(8,128)(2,1)S(1)} %pad_maximum_fusion.refs_0_, bf16[12,128,128]{2,1,0:T(8,128)(2,1)S(1)} %collective-permute-done.10.refs_1_, ...), custom_call_target="tpu_custom_call" | custom-call | flops 4194304 | bytes 5242880 | tf_op jit(solution)/shard_map/pallas_call | solution.py:59
  109.1 8.3 %shard_map.92.part_ref = f32[768,768]{1,0:T(8,128)S(1)} custom-call(bf16[2048,768]{1,0:T(8,128)(2,1)} %shard_map.90.ham_t_ref, bf16[768,2048]{1,0:T(8,128)(2,1)} %shard_map.88.ham_ref, f32[768,768]{1,0:T(8,128)} %refs_9_.1, f32[768,1]{1,0:T(8,128)} %copy.14.dr_ref, f32[1,768]{1,0:T(1,128)} %reshape.11.dc_ref, ...), custom_call_target="tpu_custom_call" | custom-call | flops 4227858432 | bytes 20971520 | tf_op jit(solution)/shard_map/pallas_call | solution.py:59
  117.5 3.6 %shard_map.93 = (bf16[2,128,768]{2,1,0:T(8,128)(2,1)}, bf16[2,768,128]{2,1,0:T(8,128)(2,1)}, bf16[1,128,768]{2,1,0:T(8,128)(2,1)}, bf16[1,128,768]{2,1,0:T(8,128...) custom-call(s32[2]{0:T(128)S(1)} %copy-done.15, s32[16,2]{1,0:T(8,128)S(1)} %copy.15.hot, ...), custom_call_target="tpu_custom_call" | custom-call | flops 402653184 | bytes 6291456 | tf_op jit(solution)/shard_map/pallas_call | solution.py:59
  121.1 5.1 %collective-permute-start.20 = (bf16[2,768,128]{2,1,0:T(8,128)(2,1)}, bf16[2,768,128]{2,1,0:T(8,128)(2,1)S(1)}, u32[]{:S(2)}, u32[]{:S(2)}) collective-permute-start(bf16[2,768,128]{2,1,0:T(8,128)(2,1)} %get-tuple-element.168.here_ref), channel_id=1, source_target_pairs={{0,8},{1,9},{2,10},{3,11},{4,12},{5,13},{6,14},{7,15},{8,0},{9,1},... | collective-permute-start | bytes 1179656 | tf_op jit(solution)/shard_map/ppermute | solution.py:26
  130.7 3.6 %shard_map.94.x_ref = f32[768,768]{1,0:T(8,128)} custom-call(f32[768,768]{1,0:T(8,128)S(1)} %shard_map.92.part_ref, bf16[768,2048]{1,0:T(8,128)(2,1)S(1)} %copy-done, bf16[1,128,768]{2,1,0:T(8,128)(2,1)S(1)} %copy-done.4, bf16[1,128,768]{2,1,0:T(8,128)(2,1)S(1)} %collective-permute-done.17.refs_1_, bf16[1,128,768]{2,1,0:T(8,128)(2,1)} %collective-permute-done.18.refs_2_, ...), custom_call_target="tpu_custom_call" | custom-call | flops 603979776 | bytes 6291456 | tf_op jit(solution)/shard_map/pallas_call | solution.py:59
  134.3 4.3 %collective-permute-done.22.refs_2_ = bf16[1,128,768]{2,1,0:T(8,128)(2,1)S(1)} collective-permute-done((bf16[1,128,768]{2,1,0:T(8,128)(2,1)}, bf16[1,128,768]{2,1,0:T(8,128)(2,1)S(1)}, u32[]{:S(2)}, u32[]{:S(2)}) %collective-permute-start.22) | collective-permute-done | bytes 196640 | tf_op jit(solution)/shard_map/ppermute | solution.py:26
  138.5 5.0 %collective-permute-done.20.there_ref = bf16[2,768,128]{2,1,0:T(8,128)(2,1)S(1)} collective-permute-done((bf16[2,768,128]{2,1,0:T(8,128)(2,1)}, bf16[2,768,128]{2,1,0:T(8,128)(2,1)S(1)}, u32[]{:S(2)}, u32[]{:S(2)}) %collective-permute-start.20) | collective-permute-done | bytes 393248 | tf_op jit(solution)/shard_map/ppermute | solution.py:26
  146.2 4.9 %all-to-all-start.1 = ((bf16[16,768,128]{2,1,0:T(8,128)(2,1)}), bf16[16,768,128]{2,1,0:T(8,128)(2,1)}, u32[]{:S(2)}, u32[]{:S(2)}) async-start(bf16[16,768,128]{2,1,0:T(8,128)(2,1)} %shard_map.97), calls=%async_computation.1 | async-start | bytes 6291456 | tf_op jit(solution)/shard_map/all_to_all | solution.py:162
  151.3 17.3 %collective-permute-done.24.refs_0_ = bf16[2,128,768]{2,1,0:T(8,128)(2,1)S(1)} collective-permute-done((bf16[2,128,768]{2,1,0:T(8,128)(2,1)S(1)}, bf16[2,128,768]{2,1,0:T(8,128)(2,1)S(1)}, u32[]{:S(2)}, u32[]{:S(2)}) %collective-permute-start.24) | collective-permute-done | bytes 393248 | tf_op jit(solution)/shard_map/ppermute | solution.py:26
  168.6 3.1 %collective-permute-done.25.refs_1_ = bf16[2,128,768]{2,1,0:T(8,128)(2,1)S(1)} collective-permute-done((bf16[2,128,768]{2,1,0:T(8,128)(2,1)S(1)}, bf16[2,128,768]{2,1,0:T(8,128)(2,1)S(1)}, u32[]{:S(2)}, u32[]{:S(2)}) %collective-permute-start.25) | collective-permute-done | bytes 393248 | tf_op jit(solution)/shard_map/ppermute | solution.py:26
  180.9 4.9 %collective-permute-done.26.refs_0_ = bf16[2,128,768]{2,1,0:T(8,128)(2,1)S(1)} collective-permute-done((bf16[2,128,768]{2,1,0:T(8,128)(2,1)S(1)}, bf16[2,128,768]{2,1,0:T(8,128)(2,1)S(1)}, u32[]{:S(2)}, u32[]{:S(2)}) %collective-permute-start.26) | collective-permute-done | bytes 393248 | tf_op jit(solution)/shard_map/ppermute | solution.py:26
  187.4 6.3 %collective-permute-done.27.refs_5_ = bf16[2,128,768]{2,1,0:T(8,128)(2,1)S(1)} collective-permute-done((bf16[2,128,768]{2,1,0:T(8,128)(2,1)}, bf16[2,128,768]{2,1,0:T(8,128)(2,1)S(1)}, u32[]{:S(2)}, u32[]{:S(2)}) %collective-permute-start.27) | collective-permute-done | bytes 393248 | tf_op jit(solution)/shard_map/ppermute | solution.py:26
  201.2 8.8 %shard_map.98.part_ref = f32[768,768]{1,0:T(8,128)S(1)} custom-call(bf16[2048,768]{1,0:T(8,128)(2,1)} %shard_map.90.ham_t_ref, bf16[768,2048]{1,0:T(8,128)(2,1)} %shard_map.88.ham_ref, f32[768,768]{1,0:T(8,128)} %shard_map.94.x_ref, f32[768,1]{1,0:T(8,128)} %copy.16.dr_ref, f32[1,768]{1,0:T(1,128)} %reshape.11.dc_ref, ...), custom_call_target="tpu_custom_call" | custom-call | flops 4227858432 | bytes 20971520 | tf_op jit(solution)/shard_map/pallas_call | solution.py:59
  210.0 3.6 %shard_map.99 = f32[768,768]{1,0:T(8,128)} custom-call(f32[768,768]{1,0:T(8,128)S(1)} %shard_map.98.part_ref, bf16[768,2048]{1,0:T(8,128)(2,1)S(1)} %copy-done.1, bf16[1,128,768]{2,1,0:T(8,128)(2,1)S(1)} %copy-done.9, bf16[1,128,768]{2,1,0:T(8,128)(2,1)S(1)} %collective-permute-done.30.refs_1_, bf16[1,128,768]{2,1,0:T(8,128)(2,1)} %collective-permute-done.31.refs_2_, ...), custom_call_target="tpu_custom_call" | custom-call | flops 603979776 | bytes 6291456 | tf_op jit(solution)/shard_map/pallas_call | solution.py:59
  (136 shorter events, 74.5 us)
Async XLA Ops:
  5.8 34.7 %collective-permute-start.1 = (bf16[2,768,128]{2,1,0:T(8,128)(2,1)}, bf16[2,768,128]{2,1,0:T(8,128)(2,1)S(1)}, u32[]{:S(2)}, u32[]{:S(2)}) collective-permute-start(bf16[2,768,128]{2,1,0:T(8,128)(2,1)} %get-tuple-element.129.here_ref), channel_id=1, source_target_pairs={{0,8},{1,9},{2,10},{3,11},{4,12},{5,13},{6,14},{7,15},{8,0},{9,1},... | collective-permute-start | bytes 1179656 | tf_op jit(solution)/shard_map/ppermute | solution.py:26
  13.0 27.5 %collective-permute-start.2 = (bf16[1,128,768]{2,1,0:T(8,128)(2,1)}, bf16[1,128,768]{2,1,0:T(8,128)(2,1)S(1)}, u32[]{:S(2)}, u32[]{:S(2)}) collective-permute-start(bf16[1,128,768]{2,1,0:T(8,128)(2,1)} %get-tuple-element.91), channel_id=1, source_target_pairs={{0,48},{1,49},{2,50},{3,51},{4,52},{5,53},{6,54},{7,55},{8,56},{9,... | collective-permute-start | bytes 589832 | tf_op jit(solution)/shard_map/ppermute | solution.py:26
  15.8 23.3 %collective-permute-start.6 = (bf16[1,128,768]{2,1,0:T(8,128)(2,1)}, bf16[1,128,768]{2,1,0:T(8,128)(2,1)S(1)}, u32[]{:S(2)}, u32[]{:S(2)}) collective-permute-start(bf16[1,128,768]{2,1,0:T(8,128)(2,1)} %get-tuple-element.95), channel_id=1, source_target_pairs={{0,32},{1,33},{2,34},{3,35},{4,36},{5,37},{6,38},{7,39},{8,40},{9,... | collective-permute-start | bytes 589832 | tf_op jit(solution)/shard_map/ppermute | solution.py:26
  27.6 18.8 %collective-permute-start.5 = (bf16[3,128,128]{2,1,0:T(8,128)(2,1)S(1)}, bf16[3,128,128]{2,1,0:T(8,128)(2,1)S(1)}, u32[]{:S(2)}, u32[]{:S(2)}) collective-permute-start(bf16[3,128,128]{2,1,0:T(8,128)(2,1)S(1)} %collective-permute-done), channel_id=1, source_target_pairs={{0,128},{1,129},{2,130},{3,131},{4,132},{5,133},{6,134},{7,135},{8... | collective-permute-start | bytes 294920 | tf_op jit(solution)/shard_map/ppermute | solution.py:26
  50.9 58.2 %all-to-all-start = ((bf16[16,768,128]{2,1,0:T(8,128)(2,1)}), bf16[16,768,128]{2,1,0:T(8,128)(2,1)}, u32[]{:S(2)}, u32[]{:S(2)}) async-start(bf16[16,768,128]{2,1,0:T(8,128)(2,1)} %shard_map.91), calls=%async_computation | async-start | bytes 6291456 | tf_op jit(solution)/shard_map/all_to_all | solution.py:162
  55.7 19.8 %collective-permute-start.8 = (bf16[2,128,768]{2,1,0:T(8,128)(2,1)}, bf16[2,128,768]{2,1,0:T(8,128)(2,1)S(1)}, u32[]{:S(2)}, u32[]{:S(2)}) collective-permute-start(bf16[2,128,768]{2,1,0:T(8,128)(2,1)} %get-tuple-element.104), channel_id=1, source_target_pairs={{0,64},{1,65},{2,66},{3,67},{4,68},{5,69},{6,70},{7,71},{8,72},{9,... | collective-permute-start | bytes 1179656 | tf_op jit(solution)/shard_map/ppermute | solution.py:26
  57.0 18.5 %collective-permute-start.9 = (bf16[2,128,768]{2,1,0:T(8,128)(2,1)}, bf16[2,128,768]{2,1,0:T(8,128)(2,1)S(1)}, u32[]{:S(2)}, u32[]{:S(2)}) collective-permute-start(bf16[2,128,768]{2,1,0:T(8,128)(2,1)} %get-tuple-element.104), channel_id=1, source_target_pairs={{0,128},{1,129},{2,130},{3,131},{4,132},{5,133},{6,134},{7,135},{8... | collective-permute-start | bytes 1179656 | tf_op jit(solution)/shard_map/ppermute | solution.py:26
  59.5 18.0 %collective-permute-start.10 = (bf16[12,128,128]{2,1,0:T(8,128)(2,1)S(1)}, bf16[12,128,128]{2,1,0:T(8,128)(2,1)S(1)}, u32[]{:S(2)}, u32[]{:S(2)}) collective-permute-start(bf16[12,128,128]{2,1,0:T(8,128)(2,1)S(1)} %pad_maximum_fusion.refs_0_), channel_id=1, source_target_pairs={{0,16},{1,17},{2,18},{3,19},{4,20},{5,21},{6,22},{7,23},{8,24},{9,... | collective-permute-start | bytes 1179656 | tf_op jit(solution)/shard_map/ppermute | solution.py:26
  59.8 20.4 %collective-permute-start.11 = (bf16[12,128,128]{2,1,0:T(8,128)(2,1)S(1)}, bf16[12,128,128]{2,1,0:T(8,128)(2,1)S(1)}, u32[]{:S(2)}, u32[]{:S(2)}) collective-permute-start(bf16[12,128,128]{2,1,0:T(8,128)(2,1)S(1)} %pad_maximum_fusion.refs_0_), channel_id=1, source_target_pairs={{0,32},{1,33},{2,34},{3,35},{4,36},{5,37},{6,38},{7,39},{8,40},{9,... | collective-permute-start | bytes 1179656 | tf_op jit(solution)/shard_map/ppermute | solution.py:26
  63.2 17.3 %collective-permute-start.12 = (bf16[12,128,128]{2,1,0:T(8,128)(2,1)S(1)}, bf16[12,128,128]{2,1,0:T(8,128)(2,1)}, u32[]{:S(2)}, u32[]{:S(2)}) collective-permute-start(bf16[12,128,128]{2,1,0:T(8,128)(2,1)S(1)} %pad_maximum_fusion.refs_0_), channel_id=1, source_target_pairs={{0,48},{1,49},{2,50},{3,51},{4,52},{5,53},{6,54},{7,55},{8,56},{9,... | collective-permute-start | bytes 1179656 | tf_op jit(solution)/shard_map/ppermute | solution.py:26
  80.5 18.5 %collective-permute-start.13 = (bf16[2,128,768]{2,1,0:T(8,128)(2,1)}, bf16[2,128,768]{2,1,0:T(8,128)(2,1)S(1)}, u32[]{:S(2)}, u32[]{:S(2)}) collective-permute-start(bf16[2,128,768]{2,1,0:T(8,128)(2,1)} %get-tuple-element.104), channel_id=1, source_target_pairs={{0,192},{1,193},{2,194},{3,195},{4,196},{5,197},{6,198},{7,199},{8... | collective-permute-start | bytes 1179656 | tf_op jit(solution)/shard_map/ppermute | solution.py:26
  82.7 17.9 %collective-permute-start.14 = (bf16[2,128,768]{2,1,0:T(8,128)(2,1)}, bf16[2,128,768]{2,1,0:T(8,128)(2,1)S(1)}, u32[]{:S(2)}, u32[]{:S(2)}) collective-permute-start(bf16[2,128,768]{2,1,0:T(8,128)(2,1)} %get-tuple-element.110), channel_id=1, source_target_pairs={{0,16},{1,17},{2,18},{3,19},{4,20},{5,21},{6,22},{7,23},{8,24},{9,... | collective-permute-start | bytes 1179656 | tf_op jit(solution)/shard_map/ppermute | solution.py:26
  83.2 19.8 %collective-permute-start.15 = (bf16[2,128,768]{2,1,0:T(8,128)(2,1)}, bf16[2,128,768]{2,1,0:T(8,128)(2,1)S(1)}, u32[]{:S(2)}, u32[]{:S(2)}) collective-permute-start(bf16[2,128,768]{2,1,0:T(8,128)(2,1)} %get-tuple-element.111), channel_id=1, source_target_pairs={{0,32},{1,33},{2,34},{3,35},{4,36},{5,37},{6,38},{7,39},{8,40},{9,... | collective-permute-start | bytes 1179656 | tf_op jit(solution)/shard_map/ppermute | solution.py:26
  86.4 16.6 %collective-permute-start.16 = (bf16[2,128,768]{2,1,0:T(8,128)(2,1)}, bf16[2,128,768]{2,1,0:T(8,128)(2,1)S(1)}, u32[]{:S(2)}, u32[]{:S(2)}) collective-permute-start(bf16[2,128,768]{2,1,0:T(8,128)(2,1)} %get-tuple-element.112), channel_id=1, source_target_pairs={{0,48},{1,49},{2,50},{3,51},{4,52},{5,53},{6,54},{7,55},{8,56},{9,... | collective-permute-start | bytes 1179656 | tf_op jit(solution)/shard_map/ppermute | solution.py:26
  103.8 13.6 %collective-permute-start.17 = (bf16[1,128,768]{2,1,0:T(8,128)(2,1)}, bf16[1,128,768]{2,1,0:T(8,128)(2,1)S(1)}, u32[]{:S(2)}, u32[]{:S(2)}) collective-permute-start(bf16[1,128,768]{2,1,0:T(8,128)(2,1)} %get-tuple-element.132), channel_id=1, source_target_pairs={{0,16},{1,17},{2,18},{3,19},{4,20},{5,21},{6,22},{7,23},{8,24},{9,... | collective-permute-start | bytes 589832 | tf_op jit(solution)/shard_map/ppermute | solution.py:26
  121.1 22.4 %collective-permute-start.20 = (bf16[2,768,128]{2,1,0:T(8,128)(2,1)}, bf16[2,768,128]{2,1,0:T(8,128)(2,1)S(1)}, u32[]{:S(2)}, u32[]{:S(2)}) collective-permute-start(bf16[2,768,128]{2,1,0:T(8,128)(2,1)} %get-tuple-element.168.here_ref), channel_id=1, source_target_pairs={{0,8},{1,9},{2,10},{3,11},{4,12},{5,13},{6,14},{7,15},{8,0},{9,1},... | collective-permute-start | bytes 1179656 | tf_op jit(solution)/shard_map/ppermute | solution.py:26
  146.2 55.0 %all-to-all-start.1 = ((bf16[16,768,128]{2,1,0:T(8,128)(2,1)}), bf16[16,768,128]{2,1,0:T(8,128)(2,1)}, u32[]{:S(2)}, u32[]{:S(2)}) async-start(bf16[16,768,128]{2,1,0:T(8,128)(2,1)} %shard_map.97), calls=%async_computation.1 | async-start | bytes 6291456 | tf_op jit(solution)/shard_map/all_to_all | solution.py:162
  151.1 17.5 %collective-permute-start.24 = (bf16[2,128,768]{2,1,0:T(8,128)(2,1)S(1)}, bf16[2,128,768]{2,1,0:T(8,128)(2,1)S(1)}, u32[]{:S(2)}, u32[]{:S(2)}) collective-permute-start(bf16[2,128,768]{2,1,0:T(8,128)(2,1)S(1)} %copy-done.32), channel_id=1, source_target_pairs={{0,64},{1,65},{2,66},{3,67},{4,68},{5,69},{6,70},{7,71},{8,72},{9,... | collective-permute-start | bytes 1179656 | tf_op jit(solution)/shard_map/ppermute | solution.py:26
  151.3 20.4 %collective-permute-start.25 = (bf16[2,128,768]{2,1,0:T(8,128)(2,1)S(1)}, bf16[2,128,768]{2,1,0:T(8,128)(2,1)S(1)}, u32[]{:S(2)}, u32[]{:S(2)}) collective-permute-start(bf16[2,128,768]{2,1,0:T(8,128)(2,1)S(1)} %copy-done.32), channel_id=1, source_target_pairs={{0,128},{1,129},{2,130},{3,131},{4,132},{5,133},{6,134},{7,135},{8... | collective-permute-start | bytes 1179656 | tf_op jit(solution)/shard_map/ppermute | solution.py:26
  175.0 18.7 %collective-permute-start.27 = (bf16[2,128,768]{2,1,0:T(8,128)(2,1)}, bf16[2,128,768]{2,1,0:T(8,128)(2,1)S(1)}, u32[]{:S(2)}, u32[]{:S(2)}) collective-permute-start(bf16[2,128,768]{2,1,0:T(8,128)(2,1)} %get-tuple-element.153), channel_id=1, source_target_pairs={{0,16},{1,17},{2,18},{3,19},{4,20},{5,21},{6,22},{7,23},{8,24},{9,... | collective-permute-start | bytes 1179656 | tf_op jit(solution)/shard_map/ppermute | solution.py:26
  177.3 16.4 %collective-permute-start.28 = (bf16[2,128,768]{2,1,0:T(8,128)(2,1)}, bf16[2,128,768]{2,1,0:T(8,128)(2,1)S(1)}, u32[]{:S(2)}, u32[]{:S(2)}) collective-permute-start(bf16[2,128,768]{2,1,0:T(8,128)(2,1)} %get-tuple-element.154), channel_id=1, source_target_pairs={{0,32},{1,33},{2,34},{3,35},{4,36},{5,37},{6,38},{7,39},{8,40},{9,... | collective-permute-start | bytes 1179656 | tf_op jit(solution)/shard_map/ppermute | solution.py:26
  179.2 15.2 %collective-permute-start.29 = (bf16[2,128,768]{2,1,0:T(8,128)(2,1)}, bf16[2,128,768]{2,1,0:T(8,128)(2,1)S(1)}, u32[]{:S(2)}, u32[]{:S(2)}) collective-permute-start(bf16[2,128,768]{2,1,0:T(8,128)(2,1)} %get-tuple-element.155), channel_id=1, source_target_pairs={{0,48},{1,49},{2,50},{3,51},{4,52},{5,53},{6,54},{7,55},{8,56},{9,... | collective-permute-start | bytes 1179656 | tf_op jit(solution)/shard_map/ppermute | solution.py:26
  195.1 14.9 %collective-permute-start.30 = (bf16[1,128,768]{2,1,0:T(8,128)(2,1)}, bf16[1,128,768]{2,1,0:T(8,128)(2,1)S(1)}, u32[]{:S(2)}, u32[]{:S(2)}) collective-permute-start(bf16[1,128,768]{2,1,0:T(8,128)(2,1)} %get-tuple-element.171), channel_id=1, source_target_pairs={{0,16},{1,17},{2,18},{3,19},{4,20},{5,21},{6,22},{7,23},{8,24},{9,... | collective-permute-start | bytes 589832 | tf_op jit(solution)/shard_map/ppermute | solution.py:26
  197.5 12.5 %collective-permute-start.31 = (bf16[1,128,768]{2,1,0:T(8,128)(2,1)}, bf16[1,128,768]{2,1,0:T(8,128)(2,1)}, u32[]{:S(2)}, u32[]{:S(2)}) collective-permute-start(bf16[1,128,768]{2,1,0:T(8,128)(2,1)} %get-tuple-element.172), channel_id=1, source_target_pairs={{0,32},{1,33},{2,34},{3,35},{4,36},{5,37},{6,38},{7,39},{8,40},{9,... | collective-permute-start | bytes 589832 | tf_op jit(solution)/shard_map/ppermute | solution.py:26
  (44 other events, 442.2 us)

commit v10 on v9

--- a/solution.py
+++ b/solution.py
@@ -335,9 +335,9 @@
     dc = lax.dynamic_slice_in_dim(diagonal, col_index * T, T).reshape(1, T)
 
     piece = lax.dynamic_slice_in_dim(ham_blocks, col_index * 3, 3).transpose(0, 2, 1)
-    row, col, *sends = pack(ids, hot, sel, start_vector)
+    piece = permute(piece, mirror)
+    row, col, *sends = pack(ids, hot, sel, after(start_vector, piece))
     zh = permute(col, zh_flip)
-    piece = permute(after(piece, row), mirror)
     near = over_x(sends)
     pieces = [piece, permute(after(piece, [zh, near[3]]), z_xor(1))]
     pieces += [permute(after(piece, near[n - 1]), z_xor(n)) for n in (2, 3)]

time: 214 us -> 221 us (1.033)
  waiting for transfers between devices: 61.7 us -> 74.9 us
  starting transfers between devices: 82.2 us -> 74.9 us
    ppermute x33, waiting for transfers between devices: 61.7 us -> 74.9 us  [permute(): return lax.ppermute(value, axes, pairs)]
    ppermute x33, starting transfers between devices: 72.5 us -> 62.6 us  [permute(): return lax.ppermute(value, axes, pairs)]
    all_to_all x2, starting transfers between devices: 9.73 us -> 12.2 us  [over_yk(): return lax.all_to_all(chosen, ('y', 'k'), 0, 0, tiled=True)]
  transfers between devices with their start and end apart: 35 -> 35, of which waited for: 14 -> 15; matrix products, arithmetic and copies ran while one was open for 2% -> 2% of each run, Pallas kernels for 19% -> 18%
where the time goes in v10:
time: 221 us; the launch traced here: 220 us
  starting transfers between devices  74.9 us (34%)
  waiting for transfers between devices  74.9 us (34%)
  Pallas kernels  53.5 us (24%)
  local copies, waits for them, and re-layouts  15.6 us (7%)
    ppermute x33, waiting for transfers between devices, permute(): return lax.ppermute(value, axes, pairs)  74.9 us
    ppermute x33, starting transfers between devices, permute(): return lax.ppermute(value, axes, pairs)  62.6 us
    pallas_call x14, Pallas kernels, call(): pl.pallas_call(kernel, grid_spec=pltpu.PrefetchScalarGridSpec(num_scalar_...  53.5 us
    all_to_all x2, starting transfers between devices, over_yk(): return lax.all_to_all(chosen, ('y', 'k'), 0, 0, tiled=True)  12.2 us
    unnamed x68, local copies, waits for them, and re-layouts  10.1 us
  transfers between devices with their start and end apart: 35, of which 15 were waited for; matrix products, arithmetic and copies ran while one was open for 2% of the time, Pallas kernels for 18%

profile of v10, /device:TPU:8, one launch (start us, length us, event | category | flops | bytes accessed | tf_op | source)
XLA Modules:
  0.0 219.8 jit_solution(14660939276991244349)
XLA Ops:
  1.7 4.8 %collective-permute-start = (bf16[3,128,128]{2,1,0:T(8,128)(2,1)S(1)}, bf16[3,128,128]{2,1,0:T(8,128)(2,1)S(1)}, u32[]{:S(2)}, u32[]{:S(2)}) collective-permute-start(bf16[3,128,128]{2,1,0:T(8,128)(2,1)S(1)} %bitcast.3), channel_id=1, source_target_pairs={{0,0},{1,16},{2,32},{3,48},{4,64},{5,80},{6,96},{7,112},{8,128},{9... | collective-permute-start | bytes 294920 | tf_op jit(solution)/shard_map/ppermute | solution.py:26
  7.4 4.3 %collective-permute-done = bf16[3,128,128]{2,1,0:T(8,128)(2,1)S(1)} collective-permute-done((bf16[3,128,128]{2,1,0:T(8,128)(2,1)S(1)}, bf16[3,128,128]{2,1,0:T(8,128)(2,1)S(1)}, u32[]{:S(2)}, u32[]{:S(2)}) %collective-permute-start) | collective-permute-done | bytes 98336 | tf_op jit(solution)/shard_map/ppermute | solution.py:26
  16.1 10.9 %collective-permute-start.1 = (bf16[2,768,128]{2,1,0:T(8,128)(2,1)}, bf16[2,768,128]{2,1,0:T(8,128)(2,1)S(1)}, u32[]{:S(2)}, u32[]{:S(2)}) collective-permute-start(bf16[2,768,128]{2,1,0:T(8,128)(2,1)} %get-tuple-element.129.here_ref), channel_id=1, source_target_pairs={{0,8},{1,9},{2,10},{3,11},{4,12},{5,13},{6,14},{7,15},{8,0},{9,1},... | collective-permute-start | bytes 1179656 | tf_op jit(solution)/shard_map/ppermute | solution.py:26
  27.5 2.7 %collective-permute-start.2 = (bf16[1,128,768]{2,1,0:T(8,128)(2,1)}, bf16[1,128,768]{2,1,0:T(8,128)(2,1)S(1)}, u32[]{:S(2)}, u32[]{:S(2)}) collective-permute-start(bf16[1,128,768]{2,1,0:T(8,128)(2,1)} %get-tuple-element.90), channel_id=1, source_target_pairs={{0,48},{1,49},{2,50},{3,51},{4,52},{5,53},{6,54},{7,55},{8,56},{9,... | collective-permute-start | bytes 589832 | tf_op jit(solution)/shard_map/ppermute | solution.py:26
  30.2 8.2 %collective-permute-done.4.refs_1_ = bf16[1,128,768]{2,1,0:T(8,128)(2,1)S(1)} collective-permute-done((bf16[1,128,768]{2,1,0:T(8,128)(2,1)}, bf16[1,128,768]{2,1,0:T(8,128)(2,1)S(1)}, u32[]{:S(2)}, u32[]{:S(2)}) %collective-permute-start.4) | collective-permute-done | bytes 196640 | tf_op jit(solution)/shard_map/ppermute | solution.py:26
  39.6 6.1 %collective-permute-done.1.there_ref = bf16[2,768,128]{2,1,0:T(8,128)(2,1)S(1)} collective-permute-done((bf16[2,768,128]{2,1,0:T(8,128)(2,1)}, bf16[2,768,128]{2,1,0:T(8,128)(2,1)S(1)}, u32[]{:S(2)}, u32[]{:S(2)}) %collective-permute-start.1) | collective-permute-done | bytes 393248 | tf_op jit(solution)/shard_map/ppermute | solution.py:26
  45.8 3.7 %collective-permute-done.5 = bf16[3,128,128]{2,1,0:T(8,128)(2,1)S(1)} collective-permute-done((bf16[3,128,128]{2,1,0:T(8,128)(2,1)S(1)}, bf16[3,128,128]{2,1,0:T(8,128)(2,1)S(1)}, u32[]{:S(2)}, u32[]{:S(2)}) %collective-permute-start.5) | collective-permute-done | bytes 98336 | tf_op jit(solution)/shard_map/ppermute | solution.py:26
  54.5 7.3 %all-to-all-start = ((bf16[16,768,128]{2,1,0:T(8,128)(2,1)}), bf16[16,768,128]{2,1,0:T(8,128)(2,1)}, u32[]{:S(2)}, u32[]{:S(2)}) async-start(bf16[16,768,128]{2,1,0:T(8,128)(2,1)} %shard_map.91), calls=%async_computation | async-start | bytes 6291456 | tf_op jit(solution)/shard_map/all_to_all | solution.py:162
  73.7 5.3 %shard_map.88.ham_ref = bf16[768,2048]{1,0:T(8,128)(2,1)} custom-call(s32[2]{0:T(128)S(1)} %copy-done.13, s32[3,16,64]{2,1,0:T(8,128)S(1)} %copy-done.10, s32[16]{0:T(128)S(1)} %copy-done.17, bf16[48,128,128]{2,1,0:T(8,128)(2,1)S(1)} %copy-done.3), custom_call_target="tpu_custom_call" | custom-call | flops 4194304 | bytes 5242880 | tf_op jit(solution)/shard_map/pallas_call | solution.py:59
  97.0 5.8 %shard_map.90.ham_t_ref = bf16[2048,768]{1,0:T(8,128)(2,1)} custom-call(s32[2]{0:T(128)S(1)} %copy-done.14, s32[3,16,64]{2,1,0:T(8,128)S(1)} %copy-done.11, s32[16]{0:T(128)S(1)} %copy-done.18, bf16[12,128,128]{2,1,0:T(8,128)(2,1)S(1)} %pad_maximum_fusion.refs_0_, bf16[12,128,128]{2,1,0:T(8,128)(2,1)S(1)} %collective-permute-done.10.refs_1_, ...), custom_call_target="tpu_custom_call" | custom-call | flops 4194304 | bytes 5242880 | tf_op jit(solution)/shard_map/pallas_call | solution.py:59
  104.5 4.2 %collective-permute-done.15.refs_6_ = bf16[2,128,768]{2,1,0:T(8,128)(2,1)S(1)} collective-permute-done((bf16[2,128,768]{2,1,0:T(8,128)(2,1)}, bf16[2,128,768]{2,1,0:T(8,128)(2,1)S(1)}, u32[]{:S(2)}, u32[]{:S(2)}) %collective-permute-start.15) | collective-permute-done | bytes 393248 | tf_op jit(solution)/shard_map/ppermute | solution.py:26
  114.4 8.3 %shard_map.92.part_ref = f32[768,768]{1,0:T(8,128)S(1)} custom-call(bf16[2048,768]{1,0:T(8,128)(2,1)} %shard_map.90.ham_t_ref, bf16[768,2048]{1,0:T(8,128)(2,1)} %shard_map.88.ham_ref, f32[768,768]{1,0:T(8,128)} %refs_9_.1, f32[768,1]{1,0:T(8,128)} %copy.14.dr_ref, f32[1,768]{1,0:T(1,128)} %reshape.11.dc_ref, ...), custom_call_target="tpu_custom_call" | custom-call | flops 4227858432 | bytes 20971520 | tf_op jit(solution)/shard_map/pallas_call | solution.py:59
  122.8 3.6 %shard_map.93 = (bf16[2,128,768]{2,1,0:T(8,128)(2,1)}, bf16[2,768,128]{2,1,0:T(8,128)(2,1)}, bf16[1,128,768]{2,1,0:T(8,128)(2,1)}, bf16[1,128,768]{2,1,0:T(8,128...) custom-call(s32[2]{0:T(128)S(1)} %copy-done.15, s32[16,2]{1,0:T(8,128)S(1)} %copy.15.hot, ...), custom_call_target="tpu_custom_call" | custom-call | flops 402653184 | bytes 6291456 | tf_op jit(solution)/shard_map/pallas_call | solution.py:59
  126.4 3.1 %collective-permute-start.20 = (bf16[2,768,128]{2,1,0:T(8,128)(2,1)}, bf16[2,768,128]{2,1,0:T(8,128)(2,1)S(1)}, u32[]{:S(2)}, u32[]{:S(2)}) collective-permute-start(bf16[2,768,128]{2,1,0:T(8,128)(2,1)} %get-tuple-element.168.here_ref), channel_id=1, source_target_pairs={{0,8},{1,9},{2,10},{3,11},{4,12},{5,13},{6,14},{7,15},{8,0},{9,1},... | collective-permute-start | bytes 1179656 | tf_op jit(solution)/shard_map/ppermute | solution.py:26
  134.0 3.6 %shard_map.94.x_ref = f32[768,768]{1,0:T(8,128)} custom-call(f32[768,768]{1,0:T(8,128)S(1)} %shard_map.92.part_ref, bf16[768,2048]{1,0:T(8,128)(2,1)S(1)} %copy-done, bf16[1,128,768]{2,1,0:T(8,128)(2,1)S(1)} %copy-done.4, bf16[1,128,768]{2,1,0:T(8,128)(2,1)S(1)} %collective-permute-done.17.refs_1_, bf16[1,128,768]{2,1,0:T(8,128)(2,1)} %collective-permute-done.18.refs_2_, ...), custom_call_target="tpu_custom_call" | custom-call | flops 603979776 | bytes 6291456 | tf_op jit(solution)/shard_map/pallas_call | solution.py:59
  137.6 4.0 %collective-permute-done.22.refs_2_ = bf16[1,128,768]{2,1,0:T(8,128)(2,1)S(1)} collective-permute-done((bf16[1,128,768]{2,1,0:T(8,128)(2,1)}, bf16[1,128,768]{2,1,0:T(8,128)(2,1)S(1)}, u32[]{:S(2)}, u32[]{:S(2)}) %collective-permute-start.22) | collective-permute-done | bytes 196640 | tf_op jit(solution)/shard_map/ppermute | solution.py:26
  141.7 7.0 %collective-permute-done.20.there_ref = bf16[2,768,128]{2,1,0:T(8,128)(2,1)S(1)} collective-permute-done((bf16[2,768,128]{2,1,0:T(8,128)(2,1)}, bf16[2,768,128]{2,1,0:T(8,128)(2,1)S(1)}, u32[]{:S(2)}, u32[]{:S(2)}) %collective-permute-start.20) | collective-permute-done | bytes 393248 | tf_op jit(solution)/shard_map/ppermute | solution.py:26
  151.3 4.9 %all-to-all-start.1 = ((bf16[16,768,128]{2,1,0:T(8,128)(2,1)}), bf16[16,768,128]{2,1,0:T(8,128)(2,1)}, u32[]{:S(2)}, u32[]{:S(2)}) async-start(bf16[16,768,128]{2,1,0:T(8,128)(2,1)} %shard_map.97), calls=%async_computation.1 | async-start | bytes 6291456 | tf_op jit(solution)/shard_map/all_to_all | solution.py:162
  156.3 3.0 %collective-permute-start.25 = (bf16[2,128,768]{2,1,0:T(8,128)(2,1)S(1)}, bf16[2,128,768]{2,1,0:T(8,128)(2,1)S(1)}, u32[]{:S(2)}, u32[]{:S(2)}) collective-permute-start(bf16[2,128,768]{2,1,0:T(8,128)(2,1)S(1)} %copy-done.32), channel_id=1, source_target_pairs={{0,128},{1,129},{2,130},{3,131},{4,132},{5,133},{6,134},{7,135},{8... | collective-permute-start | bytes 1179656 | tf_op jit(solution)/shard_map/ppermute | solution.py:26
  159.2 16.4 %collective-permute-done.24.refs_0_ = bf16[2,128,768]{2,1,0:T(8,128)(2,1)S(1)} collective-permute-done((bf16[2,128,768]{2,1,0:T(8,128)(2,1)S(1)}, bf16[2,128,768]{2,1,0:T(8,128)(2,1)S(1)}, u32[]{:S(2)}, u32[]{:S(2)}) %collective-permute-start.24) | collective-permute-done | bytes 393248 | tf_op jit(solution)/shard_map/ppermute | solution.py:26
  186.7 3.2 %collective-permute-done.26.refs_0_ = bf16[2,128,768]{2,1,0:T(8,128)(2,1)S(1)} collective-permute-done((bf16[2,128,768]{2,1,0:T(8,128)(2,1)S(1)}, bf16[2,128,768]{2,1,0:T(8,128)(2,1)S(1)}, u32[]{:S(2)}, u32[]{:S(2)}) %collective-permute-start.26) | collective-permute-done | bytes 393248 | tf_op jit(solution)/shard_map/ppermute | solution.py:26
  191.6 9.6 %collective-permute-done.27.refs_5_ = bf16[2,128,768]{2,1,0:T(8,128)(2,1)S(1)} collective-permute-done((bf16[2,128,768]{2,1,0:T(8,128)(2,1)}, bf16[2,128,768]{2,1,0:T(8,128)(2,1)S(1)}, u32[]{:S(2)}, u32[]{:S(2)}) %collective-permute-start.27) | collective-permute-done | bytes 393248 | tf_op jit(solution)/shard_map/ppermute | solution.py:26
  207.4 8.8 %shard_map.98.part_ref = f32[768,768]{1,0:T(8,128)S(1)} custom-call(bf16[2048,768]{1,0:T(8,128)(2,1)} %shard_map.90.ham_t_ref, bf16[768,2048]{1,0:T(8,128)(2,1)} %shard_map.88.ham_ref, f32[768,768]{1,0:T(8,128)} %shard_map.94.x_ref, f32[768,1]{1,0:T(8,128)} %copy.16.dr_ref, f32[1,768]{1,0:T(1,128)} %reshape.11.dc_ref, ...), custom_call_target="tpu_custom_call" | custom-call | flops 4227858432 | bytes 20971520 | tf_op jit(solution)/shard_map/pallas_call | solution.py:59
  216.3 3.6 %shard_map.99 = f32[768,768]{1,0:T(8,128)} custom-call(f32[768,768]{1,0:T(8,128)S(1)} %shard_map.98.part_ref, bf16[768,2048]{1,0:T(8,128)(2,1)S(1)} %copy-done.1, bf16[1,128,768]{2,1,0:T(8,128)(2,1)S(1)} %copy-done.9, bf16[1,128,768]{2,1,0:T(8,128)(2,1)S(1)} %collective-permute-done.30.refs_1_, bf16[1,128,768]{2,1,0:T(8,128)(2,1)} %collective-permute-done.31.refs_2_, ...), custom_call_target="tpu_custom_call" | custom-call | flops 603979776 | bytes 6291456 | tf_op jit(solution)/shard_map/pallas_call | solution.py:59
  (136 shorter events, 76.5 us)
Async XLA Ops:
  16.1 29.7 %collective-permute-start.1 = (bf16[2,768,128]{2,1,0:T(8,128)(2,1)}, bf16[2,768,128]{2,1,0:T(8,128)(2,1)S(1)}, u32[]{:S(2)}, u32[]{:S(2)}) collective-permute-start(bf16[2,768,128]{2,1,0:T(8,128)(2,1)} %get-tuple-element.129.here_ref), channel_id=1, source_target_pairs={{0,8},{1,9},{2,10},{3,11},{4,12},{5,13},{6,14},{7,15},{8,0},{9,1},... | collective-permute-start | bytes 1179656 | tf_op jit(solution)/shard_map/ppermute | solution.py:26
  27.0 11.4 %collective-permute-start.6 = (bf16[1,128,768]{2,1,0:T(8,128)(2,1)}, bf16[1,128,768]{2,1,0:T(8,128)(2,1)S(1)}, u32[]{:S(2)}, u32[]{:S(2)}) collective-permute-start(bf16[1,128,768]{2,1,0:T(8,128)(2,1)} %get-tuple-element.94), channel_id=1, source_target_pairs={{0,32},{1,33},{2,34},{3,35},{4,36},{5,37},{6,38},{7,39},{8,40},{9,... | collective-permute-start | bytes 589832 | tf_op jit(solution)/shard_map/ppermute | solution.py:26
  27.5 12.1 %collective-permute-start.2 = (bf16[1,128,768]{2,1,0:T(8,128)(2,1)}, bf16[1,128,768]{2,1,0:T(8,128)(2,1)S(1)}, u32[]{:S(2)}, u32[]{:S(2)}) collective-permute-start(bf16[1,128,768]{2,1,0:T(8,128)(2,1)} %get-tuple-element.90), channel_id=1, source_target_pairs={{0,48},{1,49},{2,50},{3,51},{4,52},{5,53},{6,54},{7,55},{8,56},{9,... | collective-permute-start | bytes 589832 | tf_op jit(solution)/shard_map/ppermute | solution.py:26
  54.5 59.9 %all-to-all-start = ((bf16[16,768,128]{2,1,0:T(8,128)(2,1)}), bf16[16,768,128]{2,1,0:T(8,128)(2,1)}, u32[]{:S(2)}, u32[]{:S(2)}) async-start(bf16[16,768,128]{2,1,0:T(8,128)(2,1)} %shard_map.91), calls=%async_computation | async-start | bytes 6291456 | tf_op jit(solution)/shard_map/all_to_all | solution.py:162
  61.9 19.6 %collective-permute-start.8 = (bf16[2,128,768]{2,1,0:T(8,128)(2,1)}, bf16[2,128,768]{2,1,0:T(8,128)(2,1)S(1)}, u32[]{:S(2)}, u32[]{:S(2)}) collective-permute-start(bf16[2,128,768]{2,1,0:T(8,128)(2,1)} %get-tuple-element.104), channel_id=1, source_target_pairs={{0,64},{1,65},{2,66},{3,67},{4,68},{5,69},{6,70},{7,71},{8,72},{9,... | collective-permute-start | bytes 1179656 | tf_op jit(solution)/shard_map/ppermute | solution.py:26
  63.4 20.5 %collective-permute-start.9 = (bf16[2,128,768]{2,1,0:T(8,128)(2,1)}, bf16[2,128,768]{2,1,0:T(8,128)(2,1)S(1)}, u32[]{:S(2)}, u32[]{:S(2)}) collective-permute-start(bf16[2,128,768]{2,1,0:T(8,128)(2,1)} %get-tuple-element.104), channel_id=1, source_target_pairs={{0,128},{1,129},{2,130},{3,131},{4,132},{5,133},{6,134},{7,135},{8... | collective-permute-start | bytes 1179656 | tf_op jit(solution)/shard_map/ppermute | solution.py:26
  64.4 21.4 %collective-permute-start.10 = (bf16[12,128,128]{2,1,0:T(8,128)(2,1)S(1)}, bf16[12,128,128]{2,1,0:T(8,128)(2,1)S(1)}, u32[]{:S(2)}, u32[]{:S(2)}) collective-permute-start(bf16[12,128,128]{2,1,0:T(8,128)(2,1)S(1)} %pad_maximum_fusion.refs_0_), channel_id=1, source_target_pairs={{0,16},{1,17},{2,18},{3,19},{4,20},{5,21},{6,22},{7,23},{8,24},{9,... | collective-permute-start | bytes 1179656 | tf_op jit(solution)/shard_map/ppermute | solution.py:26
  65.3 20.5 %collective-permute-start.11 = (bf16[12,128,128]{2,1,0:T(8,128)(2,1)S(1)}, bf16[12,128,128]{2,1,0:T(8,128)(2,1)S(1)}, u32[]{:S(2)}, u32[]{:S(2)}) collective-permute-start(bf16[12,128,128]{2,1,0:T(8,128)(2,1)S(1)} %pad_maximum_fusion.refs_0_), channel_id=1, source_target_pairs={{0,32},{1,33},{2,34},{3,35},{4,36},{5,37},{6,38},{7,39},{8,40},{9,... | collective-permute-start | bytes 1179656 | tf_op jit(solution)/shard_map/ppermute | solution.py:26
  67.5 18.4 %collective-permute-start.12 = (bf16[12,128,128]{2,1,0:T(8,128)(2,1)S(1)}, bf16[12,128,128]{2,1,0:T(8,128)(2,1)}, u32[]{:S(2)}, u32[]{:S(2)}) collective-permute-start(bf16[12,128,128]{2,1,0:T(8,128)(2,1)S(1)} %pad_maximum_fusion.refs_0_), channel_id=1, source_target_pairs={{0,48},{1,49},{2,50},{3,51},{4,52},{5,53},{6,54},{7,55},{8,56},{9,... | collective-permute-start | bytes 1179656 | tf_op jit(solution)/shard_map/ppermute | solution.py:26
  85.8 17.0 %collective-permute-start.13 = (bf16[2,128,768]{2,1,0:T(8,128)(2,1)}, bf16[2,128,768]{2,1,0:T(8,128)(2,1)S(1)}, u32[]{:S(2)}, u32[]{:S(2)}) collective-permute-start(bf16[2,128,768]{2,1,0:T(8,128)(2,1)} %get-tuple-element.104), channel_id=1, source_target_pairs={{0,192},{1,193},{2,194},{3,195},{4,196},{5,197},{6,198},{7,199},{8... | collective-permute-start | bytes 1179656 | tf_op jit(solution)/shard_map/ppermute | solution.py:26
  88.3 16.1 %collective-permute-start.14 = (bf16[2,128,768]{2,1,0:T(8,128)(2,1)}, bf16[2,128,768]{2,1,0:T(8,128)(2,1)S(1)}, u32[]{:S(2)}, u32[]{:S(2)}) collective-permute-start(bf16[2,128,768]{2,1,0:T(8,128)(2,1)} %get-tuple-element.110), channel_id=1, source_target_pairs={{0,16},{1,17},{2,18},{3,19},{4,20},{5,21},{6,22},{7,23},{8,24},{9,... | collective-permute-start | bytes 1179656 | tf_op jit(solution)/shard_map/ppermute | solution.py:26
  89.3 19.4 %collective-permute-start.15 = (bf16[2,128,768]{2,1,0:T(8,128)(2,1)}, bf16[2,128,768]{2,1,0:T(8,128)(2,1)S(1)}, u32[]{:S(2)}, u32[]{:S(2)}) collective-permute-start(bf16[2,128,768]{2,1,0:T(8,128)(2,1)} %get-tuple-element.111), channel_id=1, source_target_pairs={{0,32},{1,33},{2,34},{3,35},{4,36},{5,37},{6,38},{7,39},{8,40},{9,... | collective-permute-start | bytes 1179656 | tf_op jit(solution)/shard_map/ppermute | solution.py:26
  91.4 17.2 %collective-permute-start.16 = (bf16[2,128,768]{2,1,0:T(8,128)(2,1)}, bf16[2,128,768]{2,1,0:T(8,128)(2,1)S(1)}, u32[]{:S(2)}, u32[]{:S(2)}) collective-permute-start(bf16[2,128,768]{2,1,0:T(8,128)(2,1)} %get-tuple-element.112), channel_id=1, source_target_pairs={{0,48},{1,49},{2,50},{3,51},{4,52},{5,53},{6,54},{7,55},{8,56},{9,... | collective-permute-start | bytes 1179656 | tf_op jit(solution)/shard_map/ppermute | solution.py:26
  109.6 13.2 %collective-permute-start.17 = (bf16[1,128,768]{2,1,0:T(8,128)(2,1)}, bf16[1,128,768]{2,1,0:T(8,128)(2,1)S(1)}, u32[]{:S(2)}, u32[]{:S(2)}) collective-permute-start(bf16[1,128,768]{2,1,0:T(8,128)(2,1)} %get-tuple-element.132), channel_id=1, source_target_pairs={{0,16},{1,17},{2,18},{3,19},{4,20},{5,21},{6,22},{7,23},{8,24},{9,... | collective-permute-start | bytes 589832 | tf_op jit(solution)/shard_map/ppermute | solution.py:26
  111.1 11.7 %collective-permute-start.18 = (bf16[1,128,768]{2,1,0:T(8,128)(2,1)}, bf16[1,128,768]{2,1,0:T(8,128)(2,1)}, u32[]{:S(2)}, u32[]{:S(2)}) collective-permute-start(bf16[1,128,768]{2,1,0:T(8,128)(2,1)} %get-tuple-element.133), channel_id=1, source_target_pairs={{0,32},{1,33},{2,34},{3,35},{4,36},{5,37},{6,38},{7,39},{8,40},{9,... | collective-permute-start | bytes 589832 | tf_op jit(solution)/shard_map/ppermute | solution.py:26
  126.4 22.2 %collective-permute-start.20 = (bf16[2,768,128]{2,1,0:T(8,128)(2,1)}, bf16[2,768,128]{2,1,0:T(8,128)(2,1)S(1)}, u32[]{:S(2)}, u32[]{:S(2)}) collective-permute-start(bf16[2,768,128]{2,1,0:T(8,128)(2,1)} %get-tuple-element.168.here_ref), channel_id=1, source_target_pairs={{0,8},{1,9},{2,10},{3,11},{4,12},{5,13},{6,14},{7,15},{8,0},{9,1},... | collective-permute-start | bytes 1179656 | tf_op jit(solution)/shard_map/ppermute | solution.py:26
  151.3 56.0 %all-to-all-start.1 = ((bf16[16,768,128]{2,1,0:T(8,128)(2,1)}), bf16[16,768,128]{2,1,0:T(8,128)(2,1)}, u32[]{:S(2)}, u32[]{:S(2)}) async-start(bf16[16,768,128]{2,1,0:T(8,128)(2,1)} %shard_map.97), calls=%async_computation.1 | async-start | bytes 6291456 | tf_op jit(solution)/shard_map/all_to_all | solution.py:162
  156.3 19.3 %collective-permute-start.24 = (bf16[2,128,768]{2,1,0:T(8,128)(2,1)S(1)}, bf16[2,128,768]{2,1,0:T(8,128)(2,1)S(1)}, u32[]{:S(2)}, u32[]{:S(2)}) collective-permute-start(bf16[2,128,768]{2,1,0:T(8,128)(2,1)S(1)} %copy-done.32), channel_id=1, source_target_pairs={{0,64},{1,65},{2,66},{3,67},{4,68},{5,69},{6,70},{7,71},{8,72},{9,... | collective-permute-start | bytes 1179656 | tf_op jit(solution)/shard_map/ppermute | solution.py:26
  156.3 20.6 %collective-permute-start.25 = (bf16[2,128,768]{2,1,0:T(8,128)(2,1)S(1)}, bf16[2,128,768]{2,1,0:T(8,128)(2,1)S(1)}, u32[]{:S(2)}, u32[]{:S(2)}) collective-permute-start(bf16[2,128,768]{2,1,0:T(8,128)(2,1)S(1)} %copy-done.32), channel_id=1, source_target_pairs={{0,128},{1,129},{2,130},{3,131},{4,132},{5,133},{6,134},{7,135},{8... | collective-permute-start | bytes 1179656 | tf_op jit(solution)/shard_map/ppermute | solution.py:26
  181.2 19.9 %collective-permute-start.27 = (bf16[2,128,768]{2,1,0:T(8,128)(2,1)}, bf16[2,128,768]{2,1,0:T(8,128)(2,1)S(1)}, u32[]{:S(2)}, u32[]{:S(2)}) collective-permute-start(bf16[2,128,768]{2,1,0:T(8,128)(2,1)} %get-tuple-element.153), channel_id=1, source_target_pairs={{0,16},{1,17},{2,18},{3,19},{4,20},{5,21},{6,22},{7,23},{8,24},{9,... | collective-permute-start | bytes 1179656 | tf_op jit(solution)/shard_map/ppermute | solution.py:26
  183.1 18.0 %collective-permute-start.28 = (bf16[2,128,768]{2,1,0:T(8,128)(2,1)}, bf16[2,128,768]{2,1,0:T(8,128)(2,1)S(1)}, u32[]{:S(2)}, u32[]{:S(2)}) collective-permute-start(bf16[2,128,768]{2,1,0:T(8,128)(2,1)} %get-tuple-element.154), channel_id=1, source_target_pairs={{0,32},{1,33},{2,34},{3,35},{4,36},{5,37},{6,38},{7,39},{8,40},{9,... | collective-permute-start | bytes 1179656 | tf_op jit(solution)/shard_map/ppermute | solution.py:26
  185.1 16.7 %collective-permute-start.29 = (bf16[2,128,768]{2,1,0:T(8,128)(2,1)}, bf16[2,128,768]{2,1,0:T(8,128)(2,1)S(1)}, u32[]{:S(2)}, u32[]{:S(2)}) collective-permute-start(bf16[2,128,768]{2,1,0:T(8,128)(2,1)} %get-tuple-element.155), channel_id=1, source_target_pairs={{0,48},{1,49},{2,50},{3,51},{4,52},{5,53},{6,54},{7,55},{8,56},{9,... | collective-permute-start | bytes 1179656 | tf_op jit(solution)/shard_map/ppermute | solution.py:26
  202.5 13.7 %collective-permute-start.30 = (bf16[1,128,768]{2,1,0:T(8,128)(2,1)}, bf16[1,128,768]{2,1,0:T(8,128)(2,1)S(1)}, u32[]{:S(2)}, u32[]{:S(2)}) collective-permute-start(bf16[1,128,768]{2,1,0:T(8,128)(2,1)} %get-tuple-element.171), channel_id=1, source_target_pairs={{0,16},{1,17},{2,18},{3,19},{4,20},{5,21},{6,22},{7,23},{8,24},{9,... | collective-permute-start | bytes 589832 | tf_op jit(solution)/shard_map/ppermute | solution.py:26
  204.1 12.1 %collective-permute-start.31 = (bf16[1,128,768]{2,1,0:T(8,128)(2,1)}, bf16[1,128,768]{2,1,0:T(8,128)(2,1)}, u32[]{:S(2)}, u32[]{:S(2)}) collective-permute-start(bf16[1,128,768]{2,1,0:T(8,128)(2,1)} %get-tuple-element.172), channel_id=1, source_target_pairs={{0,32},{1,33},{2,34},{3,35},{4,36},{5,37},{6,38},{7,39},{8,40},{9,... | collective-permute-start | bytes 589832 | tf_op jit(solution)/shard_map/ppermute | solution.py:26
  (44 other events, 437.9 us)
